TPU v7x, 32 devices: a whole 2x2x4 slice. The times are simulated.
32 devices in a mesh: dp: 4 (over y, core), vocab: 8 (over z, x).
Axes of the slice: x: 2, y: 2, z: 4, core: 2. Of those that a mesh axis runs over, the one named last changes fastest.
Arguments:
- token_ids: int32 [16384], P(('dp', 'vocab')), may hold values from 0 to 50303
- seq_lengths: int32 [32, 4], P(('dp', 'vocab')), may hold values from 0 to 512, as said below
- pick_rows: int32 [2048], P(('dp', 'vocab')), may hold values from 0 to 511
- targets: int32 [2048], P(('dp', 'vocab')), may hold values from 0 to 50303
- step_count: int32 [1], replicated, may hold values from 1 to 20
- block_order: int32 [48], replicated, may hold values from 0 to 47, each once
- slot_weights: float32 [48, 384, 384], P('dp'), may hold values from -0.21875 to 0.21875
- left_stats: float32 [48, 384, 384], P('dp'), as said below
- right_stats: float32 [48, 384, 384], P('dp'), as said below
- left_roots: float32 [48, 384, 384], P('dp'), as said below
- right_roots: float32 [48, 384, 384], P('dp'), as said below
- embedding: float32 [50304, 768], P('vocab', 'dp'), may hold values from -1 to 1
- embedding_first_moment: float32 [50304, 768], P('vocab', 'dp'), may hold values from -2.3841858e-06 to 2.3841858e-06
- emb_second: float32 [50304, 768], P('vocab', 'dp'), may hold values from 1.1566702e-13 to 4.583033e-13
- vectors: float32 [15, 768], replicated, may hold values from 0.5 to 1.5
- vec_first: float32 [15, 768], replicated, may hold values from -9.536743e-06 to 9.536743e-06
- vec_second: float32 [15, 768], replicated, may hold values from 1.8550372e-12 to 7.420149e-12
- feature_maps: float32 [2, 12, 64, 64], replicated, may hold values from -0.75 to 0.75
- map_first: float32 [2, 12, 64, 64], replicated, may hold values from -2.3841858e-06 to 2.3841858e-06
- map_second: float32 [2, 12, 64, 64], replicated, may hold values from 1.1566702e-13 to 4.583033e-13
Outputs:
- loss: float32 [], replicated
- grad_norm: float32 [], replicated
- slot_grads: float32 [48, 384, 384], P('dp')
- new_slot_weights: float32 [48, 384, 384], P('dp')
- new_left_stats: float32 [48, 384, 384], P('dp')
- new_right_stats: float32 [48, 384, 384], P('dp')
- new_embedding: float32 [50304, 768], P('vocab', 'dp')
- new_emb_first: float32 [50304, 768], P('vocab', 'dp')
- new_emb_second: float32 [50304, 768], P('vocab', 'dp')
- new_vectors: float32 [15, 768], replicated
- new_vec_first: float32 [15, 768], replicated
- new_vec_second: float32 [15, 768], replicated
- new_maps: float32 [2, 12, 64, 64], replicated
- new_map_first: float32 [2, 12, 64, 64], replicated
- new_map_second: float32 [2, 12, 64, 64], replicated
Inputs may be any that keep to these rules, and one draw needn't show every extreme that they name: `seq_lengths`: row r holds the document lengths of packed row r in order; they sum to 512, the first is 128 or more, later ones may be 0, and row 0 is a single document. `left_stats`: each slot is symmetric. `right_stats`: each slot is symmetric. `left_roots`: each slot is symmetric. `right_roots`: each slot is symmetric.
All inputs are finite; a program needn't handle non-finite values.
Results may differ from a plain program's by a relative error of at most 0.0017.
The roundings to bfloat16 on the way count: a program that leaves them out, or rounds other values in their place, can miss the bound.
Values may be sent and summed in bfloat16 or wider, within the bound.
No kernel may reach another device: no remote copies, remote signals or barrier semaphores. Data moves between devices by JAX's collectives and lax.ppermute only.
A program may use at most 384 MiB of HBM per device.

v0:
```python
from functools import partial

import jax
import jax.numpy as jnp
from jax import lax
from jax.sharding import PartitionSpec as P

D = 768
HEADS = 12
HD = 64
FF = 3072
BS = 384


NORM_EPSILON = 1e-05
CLIP_NORM = 0.01
DISTILL_WEIGHT = 0.5
BETA_FIRST = 0.9
BETA_SECOND = 0.95
ADAM_EPSILON = 1e-08
DECAY_RATE = 0.01
SHAMPOO_BETA = 0.95
RATE_BLOCKS = 0.1
RATE_TABLE = 0.05
RATE_VECTORS = 0.2
RATE_MAPS = 0.1
FULL_ACCURACY = lax.Precision.HIGHEST


def norm_layer(inputs, gain_row, bias_row):
    centered = inputs - jnp.mean(inputs, -1, keepdims=True)
    variance = jnp.mean(centered * centered, -1, keepdims=True)
    return centered * lax.rsqrt(variance + NORM_EPSILON) * gain_row + bias_row


def gelu_tanh(inputs):
    return (
        0.5
        * inputs
        * (1.0 + jnp.tanh(0.7978845608 * (inputs + 0.044715 * inputs * inputs * inputs)))
    )


def feature(inputs):
    return jnp.concatenate([jax.nn.softmax(inputs, -1), jax.nn.softmax(-inputs, -1)], -1)


def untile(tiles, height, width):
    return (
        tiles.reshape(height // BS, width // BS, BS, BS)
        .transpose(0, 2, 1, 3)
        .reshape(height, width)
    )


def retile(matrix):
    height, width = matrix.shape
    return (
        matrix.reshape(height // BS, BS, width // BS, BS).transpose(0, 2, 1, 3).reshape(-1, BS, BS)
    )


def split_tiles(tiles):
    first_end = 3 * D * D // (BS * BS)
    second_end = first_end + D * D // (BS * BS)
    third_end = second_end + D * FF // (BS * BS)
    return (
        untile(tiles[:first_end], D, 3 * D),
        untile(tiles[first_end:second_end], D, D),
        untile(tiles[second_end:third_end], D, FF),
        untile(tiles[third_end:], FF, D),
    )


def segments(lengths, length_all):
    bounds = jnp.cumsum(lengths)[:-1]
    places = jnp.arange(length_all, dtype=jnp.int32)
    return jnp.sum((places[:, None] >= bounds[None, :]).astype(jnp.int32), axis=1)


def adam_update(weight, first, second, gradient, rate, step_value):
    first_new = BETA_FIRST * first + (1.0 - BETA_FIRST) * gradient
    second_new = BETA_SECOND * second + (1.0 - BETA_SECOND) * gradient * gradient
    first_hat = first_new / (1.0 - BETA_FIRST**step_value)
    second_hat = second_new / (1.0 - BETA_SECOND**step_value)
    return (
        weight - rate * (first_hat / (jnp.sqrt(second_hat) + ADAM_EPSILON) + DECAY_RATE * weight),
        first_new,
        second_new,
    )


def shampoo_update(weights, grads, left_stats, right_stats, left_roots, right_roots):
    new_left = SHAMPOO_BETA * left_stats + (1.0 - SHAMPOO_BETA) * jnp.einsum(
        "nij,nkj->nik", grads, grads, precision=FULL_ACCURACY
    )
    new_right = SHAMPOO_BETA * right_stats + (1.0 - SHAMPOO_BETA) * jnp.einsum(
        "nji,njk->nik", grads, grads, precision=FULL_ACCURACY
    )
    turned = jnp.einsum("nij,njk->nik", grads, right_roots, precision=FULL_ACCURACY)
    direction = jnp.einsum("nij,njk->nik", left_roots, turned, precision=FULL_ACCURACY)
    return (weights - RATE_BLOCKS * (direction + DECAY_RATE * weights), new_left, new_right)


def product(left, right):
    return jnp.dot(left, right, preferred_element_type=jnp.float32)


def inner_rows(left, right):
    return jnp.einsum("ta,tb->ab", left, right, preferred_element_type=jnp.float32)


def against(left, right):
    return jnp.einsum("ta,ba->tb", left, right, preferred_element_type=jnp.float32)


def heads_first(flat):
    return flat.reshape(flat.shape[0], HEADS, HD).transpose(1, 0, 2)


def heads_last(split):
    return split.transpose(1, 0, 2).reshape(split.shape[1], HEADS * HD)


def query_blocks(total_rows):
    tile_height_lines = min(512, total_rows)
    return [(0, tile_height_lines)]


def head_scores(segment, begin_row, row_count, query_head, key_head, phiq_head, phik_head):
    row_index = begin_row + jnp.arange(row_count, dtype=jnp.int32)
    columns = jnp.arange(segment.shape[0], dtype=jnp.int32)
    causal_allowance = (columns[None, :] <= row_index[:, None]) & (
        segment[None, :] == segment[begin_row : begin_row + row_count, None]
    )
    teacher = against(query_head, key_head) * HD ** (-0.5)
    teacher_probs = jax.nn.softmax(jnp.where(causal_allowance, teacher, -1e30), -1)
    affinity_logits = against(phiq_head, phik_head) * causal_allowance
    totals = jnp.sum(affinity_logits, -1, keepdims=True)
    return (causal_allowance, teacher_probs, affinity_logits, totals)


def head_forward(segment, head_parts):
    query_head, key_head, value_head, phiq_head, phik_head = head_parts
    outputs = []
    distill = jnp.zeros((), jnp.float32)
    for begin_row, row_count in query_blocks(segment.shape[0]):
        causal_allowance, teacher_probs, affinity_logits, totals = head_scores(
            segment, begin_row, row_count, query_head, key_head, phiq_head, phik_head
        )
        weights = (affinity_logits / totals).astype(jnp.bfloat16)
        outputs.append(product(weights, value_head))
        distill = jnp.sum(
            -teacher_probs * jnp.log(jnp.where(causal_allowance, affinity_logits, 1.0))
        ) + jnp.sum(jnp.log(totals))
    return (jnp.concatenate(outputs, 0), distill)


def head_backward(segment, coefficient, head_parts):
    query_head, key_head, value_head, phiq_head, phik_head, grad_head = head_parts
    grad_phiq = []
    grad_phik = jnp.zeros(phik_head.shape, jnp.float32)
    grad_value = jnp.zeros(value_head.shape, jnp.float32)
    for begin_row, row_count in query_blocks(segment.shape[0]):
        causal_allowance, teacher_probs, affinity_logits, totals = head_scores(
            segment, begin_row, row_count, query_head, key_head, phiq_head, phik_head
        )
        weights = affinity_logits / totals
        grad_rows = grad_head[begin_row : begin_row + row_count]
        grad_weights = against(grad_rows, value_head)
        grad_value = inner_rows(weights.astype(jnp.bfloat16), grad_rows)
        grad_totals = (coefficient - jnp.sum(grad_weights * weights, -1, keepdims=True)) / totals
        grad_similar = jnp.where(
            causal_allowance,
            grad_weights / totals
            - coefficient * teacher_probs / jnp.where(causal_allowance, affinity_logits, 1.0)
            + grad_totals,
            0.0,
        ).astype(jnp.bfloat16)
        grad_phiq.append(product(grad_similar, phik_head))
        grad_phik = inner_rows(grad_similar, phiq_head)
    return (jnp.concatenate(grad_phiq, 0), grad_phik, grad_value)


def layer_forward(embedded, vector_row_list, maps_low, mats_low, segment):
    wqkv_low, wout_low, wup_low, wdown_low = mats_low
    normed_one = norm_layer(embedded, vector_row_list[0], vector_row_list[1]).astype(jnp.bfloat16)
    mixed = (product(normed_one, wqkv_low) + vector_row_list[8:11].reshape(-1)).astype(jnp.bfloat16)
    query_heads = heads_first(mixed[:, :D])
    key_heads = heads_first(mixed[:, D : 2 * D])
    value_heads = heads_first(mixed[:, 2 * D :])
    feat_query = jnp.einsum(
        "htd,hde->hte", query_heads, maps_low[0], preferred_element_type=jnp.float32
    )
    feat_key = jnp.einsum(
        "htd,hde->hte", key_heads, maps_low[1], preferred_element_type=jnp.float32
    )
    asking_side_lifted = feature(feat_query).astype(jnp.bfloat16)
    lookup_side_lifted = feature(feat_key).astype(jnp.bfloat16)
    attended, distill = lax.map(
        partial(head_forward, segment),
        (query_heads, key_heads, value_heads, asking_side_lifted, lookup_side_lifted),
    )
    attended_low = heads_last(attended).astype(jnp.bfloat16)
    residual_one = embedded + product(attended_low, wout_low) + vector_row_list[6]
    normed_two = norm_layer(residual_one, vector_row_list[2], vector_row_list[3]).astype(
        jnp.bfloat16
    )
    upward = product(normed_two, wup_low) + vector_row_list[11:15].reshape(-1)
    activated = gelu_tanh(upward).astype(jnp.bfloat16)
    residual_two = residual_one + product(activated, wdown_low) + vector_row_list[7]
    kept_values = (
        embedded,
        normed_one,
        query_heads,
        key_heads,
        value_heads,
        feat_query,
        feat_key,
        asking_side_lifted,
        lookup_side_lifted,
        attended_low,
        residual_one,
        normed_two,
        upward,
        activated,
    )
    return (residual_two, jnp.sum(distill), kept_values)


def layer_backward(
    grad_two, vector_row_list, maps_low, mats_low, segment, coefficient, kept_values
):
    (
        embedded,
        normed_one,
        query_heads,
        key_heads,
        value_heads,
        feat_query,
        feat_key,
        asking_side_lifted,
        lookup_side_lifted,
        attended_low,
        residual_one,
        normed_two,
        upward,
        activated,
    ) = kept_values
    wqkv_low, wout_low, wup_low, wdown_low = mats_low
    grad_branch = grad_two.astype(jnp.bfloat16)
    grad_wdown = inner_rows(activated, grad_branch)
    grad_bdown = jnp.sum(grad_branch, 0, dtype=jnp.float32)
    grad_act = against(grad_branch, wdown_low)
    grad_upward = jax.vjp(gelu_tanh, upward)[1](grad_act)[0].astype(jnp.bfloat16)
    grad_wup = inner_rows(normed_two, grad_upward)
    grad_bup = jnp.sum(grad_upward, 0, dtype=jnp.float32)
    norm_pull_two = jax.vjp(norm_layer, residual_one, vector_row_list[2], vector_row_list[3])[1]
    grad_res, grad_gain_two, grad_bias_two = norm_pull_two(against(grad_upward, wup_low))
    grad_one = grad_two + grad_res
    grad_attn = grad_one.astype(jnp.bfloat16)
    grad_wout = inner_rows(attended_low, grad_attn)
    grad_bout = jnp.sum(grad_attn, 0, dtype=jnp.float32)
    grad_heads = heads_first(against(grad_attn, wout_low).astype(jnp.bfloat16))
    grad_phiq, grad_phik, grad_value = lax.map(
        partial(head_backward, segment, coefficient),
        (query_heads, key_heads, value_heads, asking_side_lifted, lookup_side_lifted, grad_heads),
    )
    grad_fq = jax.vjp(feature, feat_query)[1](grad_phiq)[0].astype(jnp.bfloat16)
    grad_fk = jax.vjp(feature, feat_key)[1](grad_phik)[0].astype(jnp.bfloat16)
    grad_query = jnp.einsum(
        "hte,hde->htd", grad_fq, maps_low[0], preferred_element_type=jnp.float32
    )
    grad_key = jnp.einsum("hte,hde->htd", grad_fk, maps_low[1], preferred_element_type=jnp.float32)
    grad_maps = jnp.stack(
        [
            jnp.einsum("htd,hte->hde", query_heads, grad_fq, preferred_element_type=jnp.float32),
            jnp.einsum("htd,hte->hde", key_heads, grad_fk, preferred_element_type=jnp.float32),
        ]
    )
    grad_mixed = jnp.concatenate(
        [heads_last(grad_query), heads_last(grad_key), heads_last(grad_value)], 1
    ).astype(jnp.bfloat16)
    grad_wqkv = inner_rows(normed_one, grad_mixed)
    grad_bqkv = jnp.sum(grad_mixed, 0, dtype=jnp.float32)
    norm_pull_one = jax.vjp(norm_layer, embedded, vector_row_list[0], vector_row_list[1])[1]
    grad_emb, grad_gain_one, grad_bias_one = norm_pull_one(against(grad_mixed, wqkv_low))
    leading = (grad_gain_one, grad_bias_one, grad_gain_two, grad_bias_two)
    trailing = (grad_bout, grad_bdown, grad_bqkv.reshape(3, D), grad_bup.reshape(4, D))
    return (
        grad_one + grad_emb,
        (grad_wqkv, grad_wout, grad_wup, grad_wdown),
        grad_maps,
        leading,
        trailing,
    )


def per_device(
    token_ids,
    seq_lengths,
    pick_rows,
    targets,
    step_count,
    block_order,
    slot_weights,
    left_stats,
    right_stats,
    left_roots,
    right_roots,
    embedding,
    embedding_first_moment,
    emb_second,
    vectors,
    vec_first,
    vec_second,
    feature_maps,
    map_first,
    map_second,
):
    slots_low, table_low = (
        lax.all_gather(slot_weights.astype(jnp.bfloat16), "dp", axis=0, tiled=True),
        lax.all_gather(embedding.astype(jnp.bfloat16), "dp", axis=1, tiled=True),
    )
    block_count = block_order.shape[0]
    inverse = (
        jnp.zeros((block_count,), jnp.int32)
        .at[block_order]
        .set(jnp.arange(block_count, dtype=jnp.int32))
    )
    mats_low = split_tiles(jnp.take(slots_low, inverse, axis=0))
    maps_low = feature_maps.astype(jnp.bfloat16)
    group_ids, group_targets = (
        lax.all_gather(token_ids, "vocab", axis=0, tiled=True),
        lax.all_gather(targets, "vocab", axis=0, tiled=True),
    )
    shard_rows = table_low.shape[0]
    vocab_start = lax.axis_index("vocab") * shard_rows
    local_ids = group_ids - vocab_start
    found_rows = (local_ids >= 0) & (local_ids < shard_rows)
    looked = jnp.take(table_low, jnp.clip(local_ids, 0, shard_rows - 1), axis=0)
    looked_rows = jnp.where(found_rows[:, None], looked, jnp.zeros((), jnp.bfloat16))
    embedded = lax.psum_scatter(looked_rows, "vocab", scatter_dimension=0, tiled=True).astype(
        jnp.float32
    )
    devices_all = lax.axis_size("dp") * lax.axis_size("vocab")
    token_count = token_ids.shape[0]
    pick_count = pick_rows.shape[0]
    total_picks = pick_count * devices_all
    coefficient = DISTILL_WEIGHT / (token_count * devices_all * HEADS)
    segment = segments(seq_lengths[0], token_count)
    residual_two, distill, kept_values = layer_forward(
        embedded, vectors, maps_low, mats_low, segment
    )
    final_norm, final_pull = jax.vjp(norm_layer, residual_two, vectors[4], vectors[5])
    picked = jnp.take(final_norm, pick_rows, axis=0).astype(jnp.bfloat16)
    group_picked = lax.all_gather(picked, "vocab", axis=0, tiled=True)
    logits = against(group_picked, table_low)
    top_logit = lax.pmax(jnp.max(logits, -1), "vocab")
    shifted = jnp.exp(logits - top_logit[:, None])
    local_targets = group_targets - vocab_start
    hit_target = (local_targets >= 0) & (local_targets < shard_rows)
    target_logit = jnp.where(
        hit_target,
        jnp.take_along_axis(logits, jnp.clip(local_targets, 0, shard_rows - 1)[:, None], 1)[:, 0],
        0.0,
    )
    exp_total, target_total = lax.psum((jnp.sum(shifted, -1), target_logit), "vocab")
    losses = top_logit + jnp.log(exp_total) - target_total
    onehot = jnp.arange(shard_rows, dtype=jnp.int32)[None, :] == local_targets[:, None]
    grad_logits = ((shifted / exp_total[:, None] - onehot) / total_picks).astype(jnp.bfloat16)
    grad_picked = lax.psum_scatter(
        product(
            lax.dynamic_slice_in_dim(
                grad_logits, jnp.int32(0), pick_count * lax.axis_size("vocab")
            ),
            table_low,
        ),
        "vocab",
        scatter_dimension=0,
        tiled=True,
    )
    lexicon_derivative = inner_rows(grad_logits, group_picked)
    grad_final = jnp.zeros(final_norm.shape, jnp.float32).at[pick_rows].add(grad_picked)
    grad_two, grad_gain_final, grad_bias_final = final_pull(grad_final)
    grad_embedded, mat_grads, grad_maps, leading, trailing = layer_backward(
        grad_two, vectors, maps_low, mats_low, segment, coefficient, kept_values
    )
    arrived = lax.all_gather(grad_embedded.astype(jnp.bfloat16), "vocab", axis=0, tiled=True)
    arrived_ids = lax.slice_in_dim(group_ids, 0, arrived.shape[0], axis=0) - vocab_start
    target_rows = jnp.where(
        (arrived_ids >= 0) & (arrived_ids < shard_rows), arrived_ids, shard_rows
    )
    lexicon_derivative = lexicon_derivative.at[target_rows].add(
        arrived.astype(jnp.float32), mode="drop"
    )
    emb_grads = lax.psum_scatter(lexicon_derivative, "dp", scatter_dimension=1, tiled=True)
    vec_grads = jnp.concatenate(
        [
            jnp.stack(leading + (grad_gain_final, grad_bias_final, trailing[0], trailing[1])),
            trailing[2],
            trailing[3],
        ],
        0,
    )
    tile_grads = jnp.concatenate([retile(matrix) for matrix in mat_grads], 0)
    slot_grads_all = jnp.take(tile_grads, block_order, axis=0)
    own_losses = lax.dynamic_slice_in_dim(losses, lax.axis_index("vocab") * pick_count, pick_count)
    loss_part = jnp.sum(own_losses) / total_picks + coefficient * distill
    per_owner = slot_weights.shape[0]
    slot_sum, vec_sum, map_sum = lax.psum((slot_grads_all, vec_grads, grad_maps), ("dp", "vocab"))
    owned = lax.dynamic_slice_in_dim(slot_sum, lax.axis_index("dp") * per_owner, per_owner, 0)
    square_sum, loss_total = lax.psum((jnp.sum(emb_grads * emb_grads), loss_part), ("dp", "vocab"))
    square_sum = (
        square_sum
        + jnp.sum(slot_sum * slot_sum)
        + jnp.sum(vec_sum * vec_sum)
        + jnp.sum(map_sum * map_sum)
    )
    grad_norm = jnp.sqrt(square_sum)
    clip_scale = CLIP_NORM / jnp.maximum(grad_norm, CLIP_NORM)
    clipped = owned * clip_scale
    new_slots, new_left, new_right = shampoo_update(
        slot_weights, clipped, left_stats, right_stats, left_roots, right_roots
    )
    step_value = step_count[0].astype(jnp.float32)
    emb_out = adam_update(
        embedding,
        embedding_first_moment,
        emb_second,
        emb_grads * clip_scale,
        RATE_TABLE,
        step_value,
    )
    vec_out = adam_update(
        vectors, vec_first, vec_second, vec_sum * clip_scale, RATE_VECTORS, step_value
    )
    map_out = adam_update(
        feature_maps, map_first, map_second, map_sum * clip_scale, RATE_MAPS, step_value
    )
    return (
        loss_total,
        grad_norm,
        clipped,
        new_slots,
        new_left,
        new_right,
        emb_out[0],
        emb_out[1],
        emb_out[2],
        vec_out[0],
        vec_out[1],
        vec_out[2],
        map_out[0],
        map_out[1],
        map_out[2],
    )


def solution(mesh):
    placed = (
        P(("dp", "vocab")),
        P(("dp", "vocab"), None),
        P(("dp", "vocab")),
        P(("dp", "vocab")),
        P(),
        P(),
        P("dp", None, None),
        P("dp", None, None),
        P("dp", None, None),
        P("dp", None, None),
        P("dp", None, None),
        P("vocab", "dp"),
        P("vocab", "dp"),
        P("vocab", "dp"),
        P(),
        P(),
        P(),
        P(),
        P(),
        P(),
    )
    return jax.shard_map(
        per_device,
        mesh=mesh,
        in_specs=placed,
        out_specs=(
            P(),
            P(),
            P("dp", None, None),
            P("dp", None, None),
            P("dp", None, None),
            P("dp", None, None),
            P("vocab", "dp"),
            P("vocab", "dp"),
            P("vocab", "dp"),
            P(),
            P(),
            P(),
            P(),
            P(),
            P(),
        ),
        check_vma=False,
    )
```

profile of v0, /device:TPU:8, one launch (start us, length us, event | category | flops | bytes accessed | tf_op | source)
XLA Modules:
  0.0 1732.9 jit_solution(2096883179945167799)
XLA Ops:
  17.3 25.0 %all-gather = s32[8,1,512]{2,1,0:T(1,128)S(1)} all-gather(s32[1,1,512]{2,1,0:T(1,128)S(1)} %bitcast.359), channel_id=1, replica_groups=mesh['dp'=4,'vocab'=8] {'vocab'}, dimensions={0}, use_global_device_ids=true | all-gather | bytes 18432 | tf_op jit(solution)/shard_map/all_gather | solution.py:334
  43.0 36.2 %all-gather.5.cloned.1.call-done = bf16[6288,768]{0,1:T(8,128)(2,1)} async-done(((bf16[6288,192]{0,1:T(8,128)(2,1)}), bf16[6288,768]{0,1:T(8,128)(2,1)}) %all-gather.5.cloned.1.call-update) | async-done | bytes 9658384 | tf_op jit(solution)/shard_map/all_gather | solution.py:323
  79.1 13.9 copy.198
  93.1 26.2 %gather_fusion = bf16[4096,768]{1,0:T(8,128)(2,1)} fusion(bf16[6288,768]{1,0:T(8,128)(2,1)} %copy.198, s32[4096]{0:T(1024)S(1)} %get-tuple-element.411), kind=kCustom, calls=%fused_computation | custom fusion | bytes 12599296 | tf_op jit(solution)/shard_map/jit(_take)/gather | solution.py:341
  119.2 8.0 select_select_fusion
  132.6 10.6 all-reduce
  146.4 26.0 %all-gather.7.cloned.1.call-done = bf16[48,384,384]{2,1,0:T(8,128)(2,1)} async-done(((bf16[12,384,384]{2,1,0:T(8,128)(2,1)}), bf16[48,384,384]{2,1,0:T(8,128)(2,1)}) %all-gather.7.cloned.1.call-update) | async-done | bytes 14155792 | tf_op jit(solution)/shard_map/all_gather | solution.py:322
  172.3 12.5 gather_fusion.1
  184.8 7.8 broadcast_select_fusion.1
  198.8 8.1 copy.199
  212.2 7.3 fusion.123
  225.7 7.4 copy.211
  238.8 54.8 %reduce-scatter.6.cloned.1.call-done = bf16[512,768]{1,0:T(8,128)(2,1)} async-done(((bf16[4096,768]{1,0:T(8,128)(2,1)}), bf16[512,768]{1,0:T(8,128)(2,1)}) %reduce-scatter.6.cloned.1.call-update) | async-done | bytes 786448 | tf_op jit(solution)/shard_map/reduce_scatter | solution.py:343
  334.8 118.9 %while.26 = (s32[]{:T(128)}, bf16[12,512,64]{1,2,0:T(8,128)(2,1)}, f32[12]{0:T(128)}, s32[512]{0:T(512)S(1)}, bf16[12,512,128]{2,1,0:T(8,128)(2,1)}, /*index=5*/...) while((s32[]{:T(128)}, bf16[12,512,64]{1,2,0:T(8,128)(2,1)}, ...), condition=%wide.region_20.21_spmd, body=%wide.region_14.20_spmd.sunk | while | flops 139721728 | bytes 6057093 | solution.py:200
  473.4 30.2 %all_gather.21 = bf16[512,768]{1,0:T(8,128)(2,1)S(1)} all-gather(bf16[64,768]{1,0:T(8,128)(2,1)S(1)} %select_convert_fusion.1), channel_id=1, replica_groups=mesh['dp'=4,'vocab'=8] {'vocab'}, dimensions={0}, use_global_device_ids=true | all-gather | bytes 884736 | tf_op jit(solution)/shard_map/all_gather | solution.py:357
  503.6 15.4 fusion.131
  519.0 20.3 %pmax.7 = f32[512]{0:T(512)} all-reduce(f32[512]{0:T(512)} %get-tuple-element.426), channel_id=1, replica_groups=mesh['dp'=4,'vocab'=8] {'vocab'}, use_global_device_ids=true, to_apply=%region_26.27 | all-reduce | flops 512 | bytes 4096 | tf_op jit(solution)/shard_map/pmax | solution.py:359
  539.3 7.0 fusion.56
  546.3 19.1 %gather_fusion.4 = f32[512]{0:T(512)} fusion(f32[512,6288]{0,1:T(8,128)} %get-tuple-element.427, s32[512]{0:T(512)S(1)} %bitcast.304), kind=kCustom, calls=%fused_computation.4 | custom fusion | bytes 8192 | tf_op jit(solution)/shard_map/jit(take_along_axis)/gather | solution.py:365
  566.7 21.2 %all-reduce.3 = (f32[512]{0:T(512)}, f32[512]{0:T(512)S(1)}) all-reduce(f32[512]{0:T(512)} %select_select_fusion.1, f32[512]{0:T(512)} %fusion.56), channel_id=1, replica_groups=mesh['dp'=4,'vocab'=8] {'vocab'}, use_global_device_ids=true, to_apply=%region_29.30 | all-reduce | flops 1024 | bytes 8192 | tf_op jit(solution)/shard_map/psum | solution.py:368
  587.9 7.1 multiply_convert_fusion
  597.8 9.4 fusion.133
  610.1 63.1 %reduce-scatter.8.cloned.1.call-done = f32[64,768]{1,0:T(8,128)} async-done(((f32[512,768]{1,0:T(8,128)}), f32[64,768]{1,0:T(8,128)}) %reduce-scatter.8.cloned.1.call-update) | async-done | bytes 196624 | tf_op jit(solution)/shard_map/reduce_scatter | solution.py:372
  681.3 12.3 convert_reduce_fusion
  705.1 120.3 %while.27 = (s32[]{:T(128)}, f32[12,512,128]{1,2,0:T(8,128)}, f32[12,512,128]{1,2,0:T(8,128)}, bf16[12,512,64]{1,2,0:T(8,128)(2,1)}, s32[512]{0:T(512)S(1)}, /*i...) while((s32[]{:T(128)}, f32[12,512,128]{1,2,0:T(8,128)}, ...), condition=%wide.region_44.45_spmd, body=%wide.region_39.44_spmd.sunk | while | flops 310115328 | bytes 12759157 | solution.py:265
  842.5 6.3 fusion.105
  848.9 9.9 reshape.363
  858.8 13.4 copy.226
  885.6 10.4 fusion.112
  896.0 12.9 reshape.368
  908.9 8.5 copy.229
  918.2 18.5 %pad_maximum_fusion = f32[48,384,384]{2,1,0:T(8,128)} fusion(f32[16,384,384]{2,1,0:T(8,128)} %bitcast.302, f32[16,384,384]{2,1,0:T(8,128)} %bitcast.301, f32[4,384,384]{2,1,0:T(8,128)S(1)} %bitcast.328, f32[12,384,384]{2,1,0:T(8,128)} %bitcast.307), kind=kLoop, calls=%fused_computation.81 | loop fusion | flops 21233664 | bytes 56623104 | tf_op jit(solution)/shard_map/concatenate | solution.py:406
  936.6 21.1 %gather_fusion.3 = f32[48,384,384]{2,1,0:T(8,128)} fusion(f32[48,384,384]{2,1,0:T(8,128)} %pad_maximum_fusion, s32[1024]{0:T(1024)S(1)} %pad_clamp_fusion), kind=kCustom, calls=%fused_computation.3 | custom fusion | bytes 56623296 | tf_op jit(solution)/shard_map/jit(_take)/gather | solution.py:407
  959.4 20.7 %broadcast_select_fusion = f32[48,384,384]{2,1,0:T(8,128)} fusion(f32[48,384,384]{2,1,0:T(8,128)} %gather_fusion.3, pred[48]{0:T(512)(128)(4,1)S(1)} %compare_and_fusion.2), kind=kLoop, calls=%fused_computation.83 | loop fusion | flops 7077888 | bytes 56623152 | tf_op jit(solution)/shard_map/jit(_take)/select_n | solution.py:407
  981.2 12.2 fusion.132
  993.3 42.8 %scatter_custom_fusion.2 = f32[6288,768]{1,0:T(8,128)} fusion(f32[6288,768]{1,0:T(8,128)} %fusion.132, s32[4096]{0:T(1024)} %get-tuple-element.410, bf16[4096,768]{1,0:T(8,128)(2,1)} %all-gather.9.cloned.1.call-done), kind=kCustom, calls=%fused_computation.88 | custom fusion | flops 6291456 | bytes 25608192 | tf_op jit(solution)/shard_map/scatter-add | solution.py:394
  1036.2 20.1 %copy.243 = f32[6288,768]{0,1:T(8,128)} copy(f32[6288,768]{1,0:T(8,128)} %scatter_custom_fusion.2) | data formatting | bytes 38633472
  1056.5 8.2 copy.232
  1069.9 350.3 %all-reduce.6.cloned.1.call-done = (f32[48,384,384]{2,1,0:T(8,128)}, f32[2,12,64,64]{3,2,1,0:T(8,128)}) async-done(((f32[48,384,384]{2,1,0:T(8,128)}, f32[2,12,64,64]{3,2,1,0:T(8,128)}), (f32[48,384,384]{2,1,0:T(8,128)}, f32[2,12,64,64]{3,2,1,0:T(8,128)})) %all-reduce.6.cloned.1.call-update) | async-done | bytes 28704784 | tf_op jit(solution)/shard_map/psum | solution.py:411
  1420.2 14.5 multiply_reduce_fusion.2
  1434.7 133.0 %reduce-scatter.10.cloned.1.call-done = f32[192,6288]{1,0:T(8,128)} async-done(((f32[768,6288]{1,0:T(8,128)}), f32[192,6288]{1,0:T(8,128)}) %reduce-scatter.10.cloned.1.call-update) | async-done | bytes 4829200
  1579.9 39.8 %all-reduce.1 = (f32[]{:T(128)}, f32[]{:T(128)}, f32[15,768]{1,0:T(8,128)S(1)}) all-reduce(f32[]{:T(128)S(6)} %add.318, f32[]{:T(128)} %multiply_reduce_fusion.3, f32[15,768]{1,0:T(8,128)S(1)} %concatenate.22), channel_id=1, replica_groups=mesh['dp'=4,'vocab'=8] {'dp','vocab'}, use_global_device_ids=true, to_apply=%region_32.33 | all-reduce | flops 11522 | bytes 92176 | tf_op jit(solution)/shard_map/psum | solution.py:413
  1629.8 17.2 fusion.135
  1647.0 18.3 %fusion.58 = f32[12,384,384]{1,2,0:T(8,128)} fusion(f32[12,384,384]{1,2,0:T(8,128)S(1)} %bitcast.306, f32[12,384,384]{1,2,0:T(8,128)S(1)} %fusion.135, f32[12,384,384]{2,1,0:T(8,128)} %param.33), kind=kOutput, calls=%fused_computation.98 | convolution fusion | flops 8160804864 | bytes 28311552 | tf_op jit(solution)/shard_map/nij,njk->nik/dot_general | solution.py:101
  1665.3 8.2 copy.235
  1673.5 21.3 %multiply_add_fusion.2 = f32[12,384,384]{2,1,0:T(8,128)} fusion(f32[12,384,384]{2,1,0:T(8,128)} %param.32, f32[12,384,384]{2,1,0:T(8,128)} %copy-done), kind=kOutput, calls=%fused_computation.99 | convolution fusion | flops 8159035392 | bytes 21233664 | tf_op jit(solution)/shard_map/nji,njk->nik/dot_general | solution.py:97
  1694.9 17.9 %multiply_add_fusion.3 = f32[12,384,384]{2,1,0:T(8,128)} fusion(f32[12,384,384]{2,1,0:T(8,128)} %param.31, f32[12,384,384]{2,1,0:T(8,128)S(1)} %bitcast.299), kind=kOutput, calls=%fused_computation.100 | convolution fusion | flops 8159035392 | bytes 21233664 | tf_op jit(solution)/shard_map/nij,nkj->nik/dot_general | solution.py:94
  1715.4 9.1 multiply_subtract_fusion
  (578 shorter events, 410.9 us)
Async XLA Ops:
  7.2 71.9 %all-gather.5.cloned.1.call-start = ((), (), s32[]{:S(2)}) async-start(), calls=%async_computation.3 | async-start | bytes 12288000 | tf_op jit(solution)/shard_map/all_gather | solution.py:323
  11.3 161.0 %all-gather.7.cloned.1.call-start = ((), (), s32[]{:S(2)}) async-start(), calls=%async_computation.5 | async-start | bytes 17694720 | tf_op jit(solution)/shard_map/all_gather | solution.py:322
  16.7 277.0 %reduce-scatter.6.cloned.1.call-start = ((), (), s32[]{:S(2)}) async-start(), calls=%async_computation.4 | async-start | bytes 7077888 | tf_op jit(solution)/shard_map/reduce_scatter | solution.py:343
  127.3 15.9 copy-start.99
  127.3 545.9 %reduce-scatter.8.cloned.1.call-start = ((), (), s32[]{:S(2)}) async-start(), calls=%async_computation.6 | async-start | bytes 1769472 | tf_op jit(solution)/shard_map/reduce_scatter | solution.py:372
  145.8 151.3 %copy-start.54 = (f32[768]{0:T(1024)}, f32[768]{0:T(1024)S(1)}, u32[]{:S(2)}) copy-start(f32[768]{0:T(1024)S(1)} %get-tuple-element.324) | copy-start | bytes 9220
  209.8 87.3 %copy-start.24 = (bf16[288,8,2,384]{3,1,2,0:T(8,128)(2,1)}, bf16[288,8,2,384]{3,1,2,0:T(8,128)(2,1)S(1)}, u32[]{:S(2)}) copy-start(bf16[288,8,2,384]{3,1,2,0:T(8,128)(2,1)S(1)} %copy.287) | copy-start | bytes 10616836
  503.6 15.4 copy-start.40
  607.2 68.6 %copy-start.60 = (f32[512]{0:T(512)S(1)}, f32[512]{0:T(512)}, u32[]{:S(2)}) copy-start(f32[512]{0:T(512)} %copy-done.59) | copy-start | bytes 6148
  607.2 386.1 %all-gather.9.cloned.1.call-start = ((), (), s32[]{:S(2)}) async-start(), calls=%async_computation.7 | async-start | bytes 7077888 | tf_op jit(solution)/shard_map/all_gather | solution.py:389
  679.8 13.8 slice-start.8
  681.2 12.3 copy-start.42
  681.2 12.3 copy-start.20
  681.2 12.3 slice-start.9
  681.2 12.3 copy-start.64
  681.3 12.3 copy-start.75
  681.3 12.3 copy-start.82
  833.0 9.5 copy-start.30
  842.4 577.8 %all-reduce.6.cloned.1.call-start = ((), (), s32[]{:S(2)}) async-start(), calls=%async_computation.9 | async-start | bytes 58195968 | tf_op jit(solution)/shard_map/psum | solution.py:411
  858.8 13.4 copy-start.76
  858.8 13.4 copy-start.83
  858.8 13.4 copy-start.87
  936.6 21.1 %copy-start.13 = (bf16[512,768]{0,1:T(8,128)(2,1)S(1)}, bf16[512,768]{0,1:T(8,128)(2,1)}, u32[]{:S(2)}) copy-start(bf16[512,768]{0,1:T(8,128)(2,1)} %copy-done.12) | copy-start | bytes 2359300
  936.6 21.1 %copy-start.15 = (bf16[12,512,64]{1,2,0:T(8,128)(2,1)S(1)}, bf16[12,512,64]{1,2,0:T(8,128)(2,1)}, u32[]{:S(2)}) copy-start(bf16[12,512,64]{1,2,0:T(8,128)(2,1)} %copy-done.14) | copy-start | bytes 2359300
  936.6 21.4 %copy-start.11 = (bf16[512,768]{0,1:T(8,128)(2,1)S(1)}, bf16[512,768]{0,1:T(8,128)(2,1)}, u32[]{:S(2)}) copy-start(bf16[512,768]{0,1:T(8,128)(2,1)} %copy-done.10) | copy-start | bytes 2359300
  936.6 21.4 %copy-start.17 = (bf16[12,512,64]{1,2,0:T(8,128)(2,1)S(1)}, bf16[12,512,64]{1,2,0:T(8,128)(2,1)}, u32[]{:S(2)}) copy-start(bf16[12,512,64]{1,2,0:T(8,128)(2,1)} %copy-done.16) | copy-start | bytes 2359300
  980.1 587.6 %reduce-scatter.10.cloned.1.call-start = ((), (), s32[]{:S(2)}) async-start(), calls=%async_computation.8 | async-start | bytes 24576000
  1056.4 10.4 copy-start.102
  1056.4 11.7 copy-start.31
  1056.4 11.7 copy-start.33
  1056.4 13.3 copy-start.91
  1056.4 13.3 copy-start.90
  1056.4 13.3 copy-start.80
  1056.4 13.3 copy-start.73
  1056.4 13.4 copy-start.72
  1056.5 13.4 copy-start.71
  1623.0 23.9 %slice-start.2 = ((s8[7077888]{0:T(1024)(128)(4,1)}), s8[4194304]{0:T(1024)(128)(4,1)S(1)}, s32[]{:S(2)}) async-start(s8[7077888]{0:T(1024)(128)(4,1)} %bitcast.305), calls=%async_computation.12 | async-start | bytes 8388608
  1629.8 17.2 slice-start.3
  1665.3 29.5 %slice-start = ((s8[7077888]{0:T(1024)(128)(4,1)}), s8[2883584]{0:T(1024)(128)(4,1)S(1)}, s32[]{:S(2)}) async-start(s8[7077888]{0:T(1024)(128)(4,1)} %bitcast.298), calls=%async_computation.10 | async-start | bytes 5767168
  1673.5 21.3 %slice-start.1 = ((s8[7077888]{0:T(1024)(128)(4,1)}), s8[4194304]{0:T(1024)(128)(4,1)S(1)}, s32[]{:S(2)}) async-start(s8[7077888]{0:T(1024)(128)(4,1)} %bitcast.298), calls=%async_computation.11 | async-start | bytes 8388608
  1673.5 41.9 %slice-start.4 = ((s8[4915200]{0:T(1024)(128)(4,1)}), s8[4194304]{0:T(1024)(128)(4,1)S(1)}, s32[]{:S(2)}) async-start(s8[4915200]{0:T(1024)(128)(4,1)} %bitcast.309), calls=%async_computation.14 | async-start | bytes 8388608
  1673.5 41.9 %slice-start.6 = ((s8[4915200]{0:T(1024)(128)(4,1)}), s8[4194304]{0:T(1024)(128)(4,1)S(1)}, s32[]{:S(2)}) async-start(s8[4915200]{0:T(1024)(128)(4,1)} %bitcast.312), calls=%async_computation.16 | async-start | bytes 8388608
  1694.8 18.0 %copy-start.28 = (f32[2,12,64,64]{3,2,1,0:T(8,128)S(1)}, f32[2,12,64,64]{3,2,1,0:T(8,128)}, u32[]{:S(2)}) copy-start(f32[2,12,64,64]{3,2,1,0:T(8,128)} %param.41) | copy-start | bytes 1179652
  1694.8 18.0 %copy-start.35 = (f32[2,12,64,64]{3,2,1,0:T(8,128)S(1)}, f32[2,12,64,64]{3,2,1,0:T(8,128)}, u32[]{:S(2)}) copy-start(f32[2,12,64,64]{3,2,1,0:T(8,128)} %get-tuple-element.370) | copy-start | bytes 1179652
  1694.8 18.0 %copy-start.38 = (f32[2,12,64,64]{3,2,1,0:T(8,128)S(1)}, f32[2,12,64,64]{3,2,1,0:T(8,128)}, u32[]{:S(2)}) copy-start(f32[2,12,64,64]{3,2,1,0:T(8,128)} %param.43) | copy-start | bytes 1179652
  1694.8 18.0 %copy-start.39 = (f32[2,12,64,64]{3,2,1,0:T(8,128)S(1)}, f32[2,12,64,64]{3,2,1,0:T(8,128)}, u32[]{:S(2)}) copy-start(f32[2,12,64,64]{3,2,1,0:T(8,128)} %param.42) | copy-start | bytes 1179652
  1694.8 20.5 %slice-start.5 = ((s8[4915200]{0:T(1024)(128)(4,1)}), s8[720896]{0:T(1024)(128)(4,1)S(1)}, s32[]{:S(2)}) async-start(s8[4915200]{0:T(1024)(128)(4,1)} %bitcast.309), calls=%async_computation.15 | async-start | bytes 1441792
  1694.9 20.5 %slice-start.7 = ((s8[4915200]{0:T(1024)(128)(4,1)}), s8[720896]{0:T(1024)(128)(4,1)S(1)}, s32[]{:S(2)}) async-start(s8[4915200]{0:T(1024)(128)(4,1)} %bitcast.312), calls=%async_computation.17 | async-start | bytes 1441792
  (78 other events, 272.3 us)
Sparse Core Ops, SparseCore 0:
  11.5 67.6 all-gather.4
  81.3 91.0 all-gather.6
  176.5 117.1 reduce-scatter.5
  607.4 65.8 reduce-scatter.7
  842.5 96.8 all-gather.8
  980.2 439.9 all-reduce.5
  1423.0 144.6 reduce-scatter.9
where the time goes:
time: 1750 us; the launch traced here: 1730 us
  waiting for transfers between devices  663 us (38%)
  matrix products  371 us (21%)
  local copies, waits for them, and re-layouts  296 us (17%)
  other arithmetic  215 us (12%)
  blocking collectives  147 us (8%)
  between operations  22.8 us (1%)
    psum x1, waiting for transfers between devices, per_device(): lax.psum((slot_grads_all, vec_grads, grad_maps), ('dp', 'vocab'))  350 us
    dot_general x65, matrix products, against(): jnp.einsum('ta,ba->tb', left, right, preferred_element_type=jnp.float32)  135 us
    unnamed x8, waiting for transfers between devices  133 us
    unnamed x250, local copies, waits for them, and re-layouts  82.2 us
    dot_general x29, matrix products, inner_rows(): jnp.einsum('ta,tb->ab', left, right, preferred_element_type=jnp.float32)  79.2 us
    dot_general x29, matrix products, product(): return jnp.dot(left, right, preferred_element_type=jnp.float32)  72.5 us
    reduce_scatter x1, waiting for transfers between devices, per_device(): lax.psum_scatter(product(lax.dynamic_slice_in_dim(grad_logits, jnp.int32(...  63.1 us
    reduce_scatter x1, waiting for transfers between devices, per_device(): lax.psum_scatter(looked_rows, 'vocab', scatter_dimension=0, tiled=True)  54.8 us
  transfers between devices with their start and end apart: 7, of which 6 were waited for; matrix products, arithmetic and copies ran while one was open for 21% of the time, Pallas kernels for 0%

commit v1 on v0

v1 whole, which is shorter than its diff:
```python
from functools import partial

import jax
import jax.numpy as jnp
import numpy as np
from jax import lax
from jax.experimental import pallas as pl
from jax.experimental.pallas import tpu as pltpu
from jax.sharding import PartitionSpec as P

D = 768
HEADS = 12
HD = 64
FF = 3072
BS = 384
PAIRS = HEADS // 2

NORM_EPSILON = 1e-05
CLIP_NORM = 0.01
DISTILL_WEIGHT = 0.5
BETA_FIRST = 0.9
BETA_SECOND = 0.95
ADAM_EPSILON = 1e-08
DECAY_RATE = 0.01
SHAMPOO_BETA = 0.95
RATE_BLOCKS = 0.1
RATE_TABLE = 0.05
RATE_VECTORS = 0.2
RATE_MAPS = 0.1

f32 = jnp.float32
bf16 = jnp.bfloat16
i32 = jnp.int32
SMEM = pltpu.SMEM
ANY = pl.ANY


def mm(left, right):
    return lax.dot_general(left, right, (((1,), (0,)), ((), ())), preferred_element_type=f32)


def mm_t(left, right):
    return lax.dot_general(left, right, (((1,), (1,)), ((), ())), preferred_element_type=f32)


def mm_l(left, right):
    return lax.dot_general(left, right, (((0,), (0,)), ((), ())), preferred_element_type=f32)


def split_two(values):
    high = values.astype(bf16)
    return high, (values - high.astype(f32)).astype(bf16)


def full(shape):
    return pl.BlockSpec(shape, lambda *_: (0,) * len(shape))


def cost(flops, bytes_moved, transcendentals=0):
    return pl.CostEstimate(
        flops=int(flops), bytes_accessed=int(bytes_moved), transcendentals=int(transcendentals)
    )


def place_kernel(piece_count, src_ref, off_ref, *refs):
    pieces = refs[:piece_count]
    outs = refs[piece_count : piece_count + 4]
    sems = refs[piece_count + 4]
    base = 0
    for out, rows, cols in zip(outs, (D, D, D, FF), (3 * D, D, FF, D)):
        wide = cols // BS
        count = (rows // BS) * wide

        def go(t, carry, out=out, wide=wide, base=base):
            k = base + t
            r0 = pl.multiple_of((t // wide) * BS, BS)
            c0 = pl.multiple_of((t % wide) * BS, BS)
            for p in range(piece_count):

                @pl.when(src_ref[k] == p)
                def _(p=p):
                    pltpu.make_async_copy(
                        pieces[p].at[off_ref[k]],
                        out.at[pl.ds(r0, BS), pl.ds(c0, BS)],
                        sems.at[k],
                    ).start()

            return carry

        lax.fori_loop(0, count, go, 0)
        base += count
    base = 0
    for out, rows, cols in zip(outs, (D, D, D, FF), (3 * D, D, FF, D)):
        count = (rows // BS) * (cols // BS)

        def done(t, carry, out=out, base=base):
            pltpu.make_async_copy(
                pieces[0].at[0], out.at[pl.ds(0, BS), pl.ds(0, BS)], sems.at[base + t]
            ).wait()
            return carry

        lax.fori_loop(0, count, done, 0)
        base += count


def place_blocks(src, off, pieces):
    count = len(pieces)
    return pl.pallas_call(
        partial(place_kernel, count),
        out_shape=[
            jax.ShapeDtypeStruct(shape, bf16)
            for shape in ((D, 3 * D), (D, D), (D, FF), (FF, D))
        ],
        in_specs=[pl.BlockSpec(memory_space=SMEM)] * 2 + [pl.BlockSpec(memory_space=ANY)] * count,
        out_specs=[pl.BlockSpec(memory_space=pltpu.VMEM)] * 4,
        scratch_shapes=[pltpu.SemaphoreType.DMA((48,))],
        name="place_blocks",
        cost_estimate=cost(0, 2 * 48 * BS * BS * 2),
    )(src, off, *pieces)


def hits_kernel(empty_row, packed_ref, list_ref, count_ref):
    total = packed_ref.shape[0]

    def go(i, n):
        for u in range(16):
            entry = packed_ref[i * 16 + u]
            list_ref[n] = entry
            n = n + 1 + (entry >> 31)
        return n

    n = lax.fori_loop(0, total // 16, go, jnp.int32(0))
    count_ref[0] = n
    for u in range(8):
        list_ref[n + u] = empty_row << 16


def find_hits(packed, empty_row):
    total = packed.shape[0]
    return pl.pallas_call(
        partial(hits_kernel, empty_row),
        out_shape=[
            jax.ShapeDtypeStruct((total + 16,), i32),
            jax.ShapeDtypeStruct((1,), i32),
        ],
        in_specs=[pl.BlockSpec(memory_space=SMEM)],
        out_specs=[pl.BlockSpec(memory_space=SMEM)] * 2,
        name="find_hits",
        cost_estimate=cost(1e10, total * 8),
    )(packed)


def lookup_kernel(rows_all, list_ref, count_ref, table_ref, out_ref, tab, acc):
    total = out_ref.shape[0]
    tab[pl.ds(0, rows_all), :] = table_ref[...].astype(f32)
    tab[pl.ds(rows_all, 8), :] = jnp.zeros((8, tab.shape[1]), f32)
    acc[...] = jnp.zeros(acc.shape, f32)

    def go(i, carry):
        for u in range(8):
            entry = list_ref[i * 8 + u]
            row = entry >> 16
            place = jnp.where(row < rows_all, entry & 0xFFFF, total)
            acc[pl.ds(place, 1), :] = tab[pl.ds(row, 1), :]
        return carry

    lax.fori_loop(0, (count_ref[0] + 7) // 8, go, 0)
    out_ref[...] = acc[pl.ds(0, total), :].astype(bf16)


def lookup(hit_list, hit_count, table, count):
    rows_all, width = table.shape
    return pl.pallas_call(
        partial(lookup_kernel, rows_all),
        out_shape=jax.ShapeDtypeStruct((count, width), bf16),
        in_specs=[pl.BlockSpec(memory_space=SMEM)] * 2 + [pl.BlockSpec(memory_space=pltpu.VMEM)],
        out_specs=pl.BlockSpec(memory_space=pltpu.VMEM),
        scratch_shapes=[
            pltpu.VMEM((rows_all + 8, width), f32),
            pltpu.VMEM((count + 8, width), f32),
        ],
        name="lookup",
        cost_estimate=cost(1e10, rows_all * width * 2),
    )(hit_list, hit_count, table)


def scatter_kernel(piece_count, half, rows_all, *refs):
    lists, counts = refs[0:4:2], refs[1:4:2]
    lex_ref = refs[4]
    pieces = refs[5 : 5 + piece_count]
    out_ref, square_ref, acc, tail, wide, pair = refs[5 + piece_count :]
    acc[...] = jnp.zeros(acc.shape, f32)
    tail[...] = jnp.zeros(tail.shape, f32)
    for k in range(piece_count):
        wide[pl.ds(k * 2 * half, 2 * half), :] = pieces[k][pl.ds(0, 2 * half), :].astype(f32)
        pair[pl.ds(k * half, half), :] = pieces[k][pl.ds(2 * half, half), :].astype(f32)
    upper = lax.broadcasted_iota(i32, (1, 128), 1) >= 64
    for side in range(2):
        own = upper if side else ~upper

        def go(i, carry, side=side, own=own):
            for u in range(8):
                entry = lists[side][i * 8 + u]
                row = entry >> 16
                p = entry & 0xFFFF
                q = (p // half) * half + p + side * half
                acc[pl.ds(row, 1), :] += wide[pl.ds(q, 1), :]
                tail[pl.ds(row, 1), :] += jnp.where(own, pair[pl.ds(p, 1), :], 0.0)
            return carry

        lax.fori_loop(0, (counts[side][0] + 7) // 8, go, 0)
    chunks = rows_all // 128
    rest = rows_all - chunks * 128

    def turn(start, width):
        upright = acc[pl.ds(start, 128), :].T
        lower = tail[pl.ds(start, 128), :].T
        lower = lower[:64] + lower[64:]
        lanes = pl.ds(start, width)
        left = lex_ref[pl.ds(0, 128), lanes] + upright[:, :width]
        right = lex_ref[pl.ds(128, 64), lanes] + lower[:, :width]
        out_ref[pl.ds(0, 128), lanes] = left
        out_ref[pl.ds(128, 64), lanes] = right
        return jnp.sum(left * left, 0, keepdims=True), jnp.sum(right * right, 0, keepdims=True)

    def step(i, carry):
        left, right = turn(pl.multiple_of(i * 128, 128), 128)
        return carry + left + right

    squares = lax.fori_loop(0, chunks, step, jnp.zeros((1, 128), f32))
    total = jnp.sum(squares)
    if rest:
        left, right = turn(chunks * 128, rest)
        total = total + jnp.sum(left) + jnp.sum(right)
    square_ref[0, 0] = total


def scatter_rows(lists, lex, pieces):
    width, rows_all = lex.shape
    half = pieces[0].shape[0] // 3
    count = len(pieces)
    padded = (rows_all // 128 + 1) * 128
    return pl.pallas_call(
        partial(scatter_kernel, count, half, rows_all),
        out_shape=[
            jax.ShapeDtypeStruct((width, rows_all), f32),
            jax.ShapeDtypeStruct((1, 1), f32),
        ],
        in_specs=[pl.BlockSpec(memory_space=SMEM)] * 4
        + [pl.BlockSpec(memory_space=pltpu.VMEM)] * (count + 1),
        out_specs=[
            pl.BlockSpec(memory_space=pltpu.VMEM),
            pl.BlockSpec(memory_space=SMEM),
        ],
        scratch_shapes=[
            pltpu.VMEM((padded, 128), f32),
            pltpu.VMEM((padded, 128), f32),
            pltpu.VMEM((count * 2 * half, 128), f32),
            pltpu.VMEM((count * half, 128), f32),
        ],
        name="scatter_rows",
        cost_estimate=cost(1.5e10, rows_all * width * 8),
    )(*lists, lex, *pieces)


def norm_parts(inputs):
    centered = inputs - jnp.mean(inputs, -1, keepdims=True)
    scale = lax.rsqrt(jnp.mean(centered * centered, -1, keepdims=True) + NORM_EPSILON)
    return centered, scale


def norm_pull(inputs, gain_row, grads):
    centered, scale = norm_parts(inputs)
    unit = centered * scale
    pulled = grads * gain_row
    lead = jnp.mean(pulled, -1, keepdims=True)
    along = jnp.mean(pulled * unit, -1, keepdims=True)
    grad_in = scale * (pulled - lead - unit * along)
    return (
        grad_in,
        jnp.sum(grads * unit, 0, keepdims=True),
        jnp.sum(grads, 0, keepdims=True),
    )


def qkv_kernel(x_ref, w_ref, vec_ref, h_ref, mixed_ref):
    j = pl.program_id(0)

    @pl.when(j == 0)
    def _():
        centered, scale = norm_parts(x_ref[...].astype(f32))
        h_ref[...] = (centered * scale * vec_ref[0:1, :] + vec_ref[1:2, :]).astype(bf16)

    mixed_ref[...] = (mm(h_ref[...], w_ref[...]) + vec_ref[pl.ds(8 + j, 1), :]).astype(bf16)


def qkv_forward(x0, wqkv, vectors):
    tokens = x0.shape[0]
    return pl.pallas_call(
        qkv_kernel,
        grid=(3,),
        out_shape=[
            jax.ShapeDtypeStruct((tokens, D), bf16),
            jax.ShapeDtypeStruct((tokens, 3 * D), bf16),
        ],
        in_specs=[
            full((tokens, D)),
            pl.BlockSpec((D, D), lambda j: (0, j)),
            full(vectors.shape),
        ],
        out_specs=[full((tokens, D)), pl.BlockSpec((tokens, D), lambda j: (0, j))],
        name="qkv_forward",
        cost_estimate=cost(2 * tokens * D * 3 * D, 8e6),
    )(x0, wqkv, vectors)


def feature_parts(values, lift, low_half):
    raw = mm(values, lift)
    top_a = jnp.max(jnp.where(low_half, raw, -jnp.inf), -1, keepdims=True)
    top_b = jnp.max(jnp.where(low_half, -jnp.inf, raw), -1, keepdims=True)
    grown = jnp.exp(raw - jnp.where(low_half, top_a, top_b))
    sum_a = jnp.sum(jnp.where(low_half, grown, 0.0), -1, keepdims=True)
    sum_b = jnp.sum(jnp.where(low_half, 0.0, grown), -1, keepdims=True)
    return grown / jnp.where(low_half, sum_a, sum_b)


def feature_pull(soft, grads, low_half):
    weighed = soft * grads
    sum_a = jnp.sum(jnp.where(low_half, weighed, 0.0), -1, keepdims=True)
    sum_b = jnp.sum(jnp.where(low_half, 0.0, weighed), -1, keepdims=True)
    pulled = soft * (grads - jnp.where(low_half, sum_a, sum_b))
    return (pulled - pltpu.roll(pulled, HD, 1)).astype(bf16)


def fill_allowed(len_ref, allow_ref):
    tokens = allow_ref.shape[0]
    first = len_ref[0, 0]
    second = first + len_ref[0, 1]
    third = second + len_ref[0, 2]

    def document(places):
        return (
            (places >= first).astype(i32)
            + (places >= second).astype(i32)
            + (places >= third).astype(i32)
        )

    rows = lax.broadcasted_iota(i32, (tokens, tokens), 0)
    cols = lax.broadcasted_iota(i32, (tokens, tokens), 1)
    allow_ref[...] = ((cols <= rows) & (document(rows) == document(cols))).astype(f32)


ROWS = 256


def attend_kernel(
    len_ref, q_ref, k_ref, v_ref, fq_ref, fk_ref, y_ref, distill_ref, allow_ref, lift_q, lift_k
):
    tokens = q_ref.shape[0]

    @pl.when(pl.program_id(0) == 0)
    def _():
        fill_allowed(len_ref, allow_ref)
        distill_ref[...] = jnp.zeros_like(distill_ref)

    low_half = lax.broadcasted_iota(i32, (1, 2 * HD), 1) < HD
    low_rows = lax.broadcasted_iota(i32, (ROWS, 2 * HD), 1) < HD
    total = jnp.zeros((1, 1), f32)
    for h in range(2):
        lift_q[h] = feature_parts(q_ref[...], fq_ref[h], low_half).astype(bf16)
        lift_k[h] = feature_parts(k_ref[...], fk_ref[h], low_half).astype(bf16)
    for begin in range(0, tokens, ROWS):
        width = begin + ROWS
        ok = allow_ref[pl.ds(begin, ROWS), pl.ds(0, width)] > 0.5
        queries = q_ref[pl.ds(begin, ROWS), :] * jnp.asarray(HD**-0.5, bf16)
        keys = k_ref[pl.ds(0, width), :]
        values = v_ref[pl.ds(0, width), :]
        parts = []
        for h in range(2):
            own = low_rows if h == 0 else ~low_rows
            scores = mm_t(jnp.where(own, queries, jnp.zeros_like(queries)), keys)
            scores = jnp.where(ok, scores, -1e30)
            grown = jnp.exp(scores - jnp.max(scores, -1, keepdims=True))
            inverse = 1.0 / jnp.sum(grown, -1, keepdims=True)
            similar = mm_t(lift_q[h, pl.ds(begin, ROWS), :], lift_k[h, pl.ds(0, width), :])
            kept = jnp.where(ok, similar, 0.0)
            sums = jnp.sum(kept, -1, keepdims=True)
            weights = (kept * (1.0 / sums)).astype(bf16)
            parts.append(mm(weights, values))
            logs = jnp.log(jnp.where(ok, similar, 1.0))
            row_terms = jnp.log(sums) - jnp.sum(grown * logs, -1, keepdims=True) * inverse
            total = total + jnp.sum(row_terms, 0, keepdims=True)
        y_ref[pl.ds(begin, ROWS), :] = jnp.where(low_rows, parts[0], parts[1]).astype(bf16)
    distill_ref[...] += jnp.broadcast_to(total, distill_ref.shape)


def attend(lengths, mixed, lift_maps):
    tokens = mixed.shape[0]
    column = lambda base: pl.BlockSpec((tokens, 2 * HD), lambda g: (0, base + g))
    maps = pl.BlockSpec((2, 2 * HD, 2 * HD), lambda g: (g, 0, 0))
    return pl.pallas_call(
        attend_kernel,
        grid=(PAIRS,),
        out_shape=[
            jax.ShapeDtypeStruct((tokens, D), bf16),
            jax.ShapeDtypeStruct((8, 128), f32),
        ],
        in_specs=[
            pl.BlockSpec(memory_space=SMEM),
            column(0),
            column(PAIRS),
            column(2 * PAIRS),
            maps,
            maps,
        ],
        out_specs=[column(0), full((8, 128))],
        scratch_shapes=[
            pltpu.VMEM((tokens, tokens), f32),
            pltpu.VMEM((2, tokens, 2 * HD), bf16),
            pltpu.VMEM((2, tokens, 2 * HD), bf16),
        ],
        name="attend",
        cost_estimate=cost(1.2e10, 4e6, 6e6),
    )(lengths, mixed, mixed, mixed, lift_maps[0], lift_maps[1])


def attend_back_kernel(
    coefficient,
    later,
    len_ref,
    q_ref,
    k_ref,
    v_ref,
    gy_ref,
    fq_ref,
    fk_ref,
    *refs,
):
    g_ref, gq_map_ref, gk_map_ref, allow_ref, soft_q, soft_k, grad_q, grad_k, grad_v = refs[later:]
    tokens = q_ref.shape[0]

    @pl.when(pl.program_id(0) == 0)
    def _():
        fill_allowed(len_ref, allow_ref)

    low_half = lax.broadcasted_iota(i32, (1, 2 * HD), 1) < HD
    low_rows = lax.broadcasted_iota(i32, (ROWS, 2 * HD), 1) < HD
    for h in range(2):
        soft_q[h] = feature_parts(q_ref[...], fq_ref[h], low_half)
        soft_k[h] = feature_parts(k_ref[...], fk_ref[h], low_half)
    for step, begin in enumerate(reversed(range(0, tokens, ROWS))):
        width = begin + ROWS
        ok = allow_ref[pl.ds(begin, ROWS), pl.ds(0, width)] > 0.5
        queries = q_ref[pl.ds(begin, ROWS), :] * jnp.asarray(HD**-0.5, bf16)
        keys = k_ref[pl.ds(0, width), :]
        values = v_ref[pl.ds(0, width), :]
        grads = gy_ref[pl.ds(begin, ROWS), :]
        value_sum = None
        for h in range(2):
            own = low_rows if h == 0 else ~low_rows
            scores = mm_t(jnp.where(own, queries, jnp.zeros_like(queries)), keys)
            scores = jnp.where(ok, scores, -1e30)
            grown = jnp.exp(scores - jnp.max(scores, -1, keepdims=True))
            teach = grown * (coefficient / jnp.sum(grown, -1, keepdims=True))
            phi_q = soft_q[h, pl.ds(begin, ROWS), :].astype(bf16)
            phi_k = soft_k[h, pl.ds(0, width), :].astype(bf16)
            similar = mm_t(phi_q, phi_k)
            kept = jnp.where(ok, similar, 0.0)
            inverse = 1.0 / jnp.sum(kept, -1, keepdims=True)
            weights = kept * inverse
            own_grads = jnp.where(own, grads, jnp.zeros_like(grads))
            grad_w = mm_t(own_grads, values)
            row_sum = jnp.sum(grad_w * weights, -1, keepdims=True)
            grad_sums = (coefficient - row_sum) * inverse
            grad_sim = jnp.where(
                ok,
                grad_w * inverse - teach / jnp.where(ok, similar, 1.0) + grad_sums,
                0.0,
            ).astype(bf16)
            grad_q[h, pl.ds(begin, ROWS), :] = mm(grad_sim, phi_k)
            part_k = mm_l(grad_sim, phi_q)
            part_v = mm_l(weights.astype(bf16), own_grads)
            value_sum = part_v if value_sum is None else value_sum + part_v
            if step == 0:
                grad_k[h] = part_k
            else:
                grad_k[h, pl.ds(0, width), :] += part_k
        if step == 0:
            grad_v[...] = value_sum
        else:
            grad_v[pl.ds(0, width), :] += value_sum
    for slot, own_ref, map_ref, soft, grad, out in (
        (0, q_ref, fq_ref, soft_q, grad_q, gq_map_ref),
        (1, k_ref, fk_ref, soft_k, grad_k, gk_map_ref),
    ):
        result = None
        for h in range(2):
            pulled = feature_pull(soft[h], grad[h], low_half)
            back = mm_t(pulled, map_ref[h]) * 0.5
            result = back if result is None else result + back
            out[h] = mm_l(own_ref[...], pulled)[h * HD : (h + 1) * HD, :HD]
        g_ref[slot] = result.astype(bf16)
    g_ref[2] = grad_v[...].astype(bf16)


def attend_back(lengths, mixed, grad_y, lift_maps, coefficient, start, pairs, before):
    tokens = mixed.shape[0]
    column = lambda base: pl.BlockSpec((tokens, 2 * HD), lambda g: (0, base + start + g))
    maps = pl.BlockSpec((2, 2 * HD, 2 * HD), lambda g: (start + g, 0, 0))
    small = pl.BlockSpec((2, HD, HD), lambda g: (g, 0, 0))
    wide = (2, tokens, 2 * HD)
    later = before is not None
    return pl.pallas_call(
        partial(attend_back_kernel, coefficient, int(later)),
        grid=(pairs,),
        out_shape=[
            jax.ShapeDtypeStruct((3, tokens, D), bf16),
            jax.ShapeDtypeStruct((2 * pairs, HD, HD), f32),
            jax.ShapeDtypeStruct((2 * pairs, HD, HD), f32),
        ],
        in_specs=[
            pl.BlockSpec(memory_space=SMEM),
            column(0),
            column(PAIRS),
            column(2 * PAIRS),
            column(0),
            maps,
            maps,
        ]
        + [pl.BlockSpec(memory_space=ANY)] * later,
        out_specs=[
            pl.BlockSpec((3, tokens, 2 * HD), lambda g: (0, 0, start + g)),
            small,
            small,
        ],
        scratch_shapes=[
            pltpu.VMEM((tokens, tokens), f32),
            pltpu.VMEM(wide, f32),
            pltpu.VMEM(wide, f32),
            pltpu.VMEM(wide, f32),
            pltpu.VMEM(wide, f32),
            pltpu.VMEM((tokens, 2 * HD), f32),
        ],
        input_output_aliases={7: 0} if later else {},
        name="attend_back",
        cost_estimate=cost(1.2e10, 4e6, 3e6),
    )(lengths, mixed, mixed, mixed, grad_y, lift_maps[0], lift_maps[1], *([before] * later))


FSTEPS = FF // D


def mlp_kernel(
    x_ref,
    y_ref,
    wo_ref,
    wup_ref,
    wdown_ref,
    vec_ref,
    pick_ref,
    x1_ref,
    h_ref,
    up_ref,
    act_ref,
    x2_ref,
    hp_ref,
):
    j = pl.program_id(0)

    @pl.when(j == 0)
    def _():
        x1 = x_ref[...].astype(f32) + mm(y_ref[...], wo_ref[...]) + vec_ref[6:7, :]
        x1_ref[...] = x1
        centered, scale = norm_parts(x1)
        h_ref[...] = (centered * scale * vec_ref[2:3, :] + vec_ref[3:4, :]).astype(bf16)
        x2_ref[...] = x1 + vec_ref[7:8, :]

    up = mm(h_ref[...], wup_ref[...]) + vec_ref[pl.ds(11 + j, 1), :]
    up_ref[...] = up
    act = (0.5 * up * (1.0 + jnp.tanh(0.7978845608 * (up + 0.044715 * up * up * up)))).astype(bf16)
    act_ref[...] = act
    x2_ref[...] += mm(act, wdown_ref[...])

    @pl.when(j == FSTEPS - 1)
    def _():
        centered, scale = norm_parts(x2_ref[...])
        last = (centered * scale * vec_ref[4:5, :] + vec_ref[5:6, :]).astype(bf16)
        tokens = last.shape[0]
        places = lax.broadcasted_iota(i32, (pick_ref.shape[0], tokens), 1)
        chosen = (places == pick_ref[...]).astype(bf16)
        hp_ref[...] = mm(chosen, last).astype(bf16)


def mlp_forward(x0, y, wo, wup, wdown, vectors, picks):
    tokens = x0.shape[0]
    count = picks.shape[0]
    wide = pl.BlockSpec((tokens, D), lambda j: (0, j))
    shape = lambda cols, kind: jax.ShapeDtypeStruct((tokens, cols), kind)
    return pl.pallas_call(
        mlp_kernel,
        grid=(FSTEPS,),
        out_shape=[
            shape(D, f32),
            shape(D, bf16),
            shape(FF, f32),
            shape(FF, bf16),
            shape(D, f32),
            jax.ShapeDtypeStruct((count, D), bf16),
        ],
        in_specs=[
            full((tokens, D)),
            full((tokens, D)),
            full((D, D)),
            pl.BlockSpec((D, D), lambda j: (0, j)),
            pl.BlockSpec((D, D), lambda j: (j, 0)),
            full(vectors.shape),
            full((count, 1)),
        ],
        out_specs=[
            full((tokens, D)),
            full((tokens, D)),
            wide,
            wide,
            full((tokens, D)),
            full((count, D)),
        ],
        name="mlp_forward",
        cost_estimate=cost(2 * tokens * D * (2 * FF + D), 3e7, tokens * FF),
    )(x0, y, wo, wup, wdown, vectors, picks.reshape(count, 1))


def halve(core, tile, outs, slot, row, col):
    half = BS // 2
    near = pl.multiple_of(row * BS + core * half, half)
    far = pl.multiple_of(row * BS + (1 - core) * half, half)
    for start, out, top in ((near, outs[0], outs[2]), (far, outs[1], outs[3])):
        values = tile[pl.ds(start, half), pl.ds(col * BS, BS)]
        out[slot] = values
        top[slot] = jnp.max(jnp.abs(values), 0, keepdims=True)


def mlp_back_kernel(
    core_ref,
    ghp_ref,
    pick_ref,
    x2_ref,
    act_ref,
    up_ref,
    h_ref,
    x1_ref,
    wdown_ref,
    wup_ref,
    wo_ref,
    vec_ref,
    mine_ref,
    theirs_ref,
    mine_top_ref,
    theirs_top_ref,
    gx1_ref,
    ga_ref,
    gy_ref,
    vg_ref,
    gx2,
    gm,
    gh,
    tile_a,
    tile_b,
):
    j = pl.program_id(0)
    core = core_ref[0]
    tokens = x2_ref.shape[0]
    outs = (mine_ref, theirs_ref, mine_top_ref, theirs_top_ref)

    @pl.when(j == 0)
    def _():
        vg_ref[...] = jnp.zeros_like(vg_ref)
        places = lax.broadcasted_iota(i32, (tokens, pick_ref.shape[1]), 0)
        chosen = (places == pick_ref[...]).astype(bf16)
        rest = ghp_ref[...]
        spread = jnp.zeros((tokens, D), f32)
        for _ in range(3):
            part = rest.astype(bf16)
            rest = rest - part.astype(f32)
            spread = spread + mm(chosen, part)
        grad, gain, bias = norm_pull(x2_ref[...], vec_ref[4:5, :], spread)
        gx2[...] = grad
        low = grad.astype(bf16)
        gm[...] = low
        vg_ref[4:5, :] = gain
        vg_ref[5:6, :] = bias
        vg_ref[7:8, :] = jnp.sum(low.astype(f32), 0, keepdims=True)

    grad_act = mm_t(gm[...], wdown_ref[...])
    up = up_ref[...]
    turn = jnp.tanh(0.7978845608 * (up + 0.044715 * up * up * up))
    slope = 0.5 * (1.0 + turn) + 0.5 * up * (1.0 - turn * turn) * (
        0.7978845608 * (1.0 + 3.0 * 0.044715 * up * up)
    )
    gup = (grad_act * slope).astype(bf16)
    vg_ref[pl.ds(11 + j, 1), :] = jnp.sum(gup.astype(f32), 0, keepdims=True)
    part = mm_t(gup, wup_ref[...])

    @pl.when(j == 0)
    def _():
        gh[...] = part

    @pl.when(j > 0)
    def _():
        gh[...] += part

    tile_a[...] = mm_l(h_ref[...], gup)
    tile_b[...] = mm_l(act_ref[...], gm[...])
    for r in range(2):
        for c in range(2):
            halve(core, tile_a, outs, 2 * r + c, r, c)
            halve(core, tile_b, outs, 4 + 2 * r + c, r, c)

    @pl.when(j == FSTEPS - 1)
    def _():
        grad, gain, bias = norm_pull(x1_ref[...], vec_ref[2:3, :], gh[...])
        vg_ref[2:3, :] = gain
        vg_ref[3:4, :] = bias
        grad = grad + gx2[...]
        gx1_ref[...] = grad
        low = grad.astype(bf16)
        ga_ref[...] = low
        vg_ref[6:7, :] = jnp.sum(low.astype(f32), 0, keepdims=True)
        gy_ref[...] = mm_t(low, wo_ref[...]).astype(bf16)


def mlp_back(core, ghp, picks, x2, act, up, h2, x1, wdown, wup, wo, vectors):
    tokens = x2.shape[0]
    count = picks.shape[0]
    wide = pl.BlockSpec((tokens, D), lambda j: (0, j))
    flat = full((tokens, D))
    tiles = pl.BlockSpec((8, BS // 2, BS), lambda j: (j, 0, 0))
    tops = pl.BlockSpec((8, 1, BS), lambda j: (j, 0, 0))
    halves = jax.ShapeDtypeStruct((8 * FSTEPS, BS // 2, BS), f32)
    highs = jax.ShapeDtypeStruct((8 * FSTEPS, 1, BS), f32)
    return pl.pallas_call(
        mlp_back_kernel,
        grid=(FSTEPS,),
        out_shape=[
            halves,
            halves,
            highs,
            highs,
            jax.ShapeDtypeStruct((tokens, D), f32),
            jax.ShapeDtypeStruct((tokens, D), bf16),
            jax.ShapeDtypeStruct((tokens, D), bf16),
            jax.ShapeDtypeStruct((16, D), f32),
        ],
        in_specs=[
            pl.BlockSpec(memory_space=SMEM),
            full((count, D)),
            full((1, count)),
            flat,
            wide,
            wide,
            flat,
            flat,
            pl.BlockSpec((D, D), lambda j: (j, 0)),
            pl.BlockSpec((D, D), lambda j: (0, j)),
            full((D, D)),
            full(vectors.shape),
        ],
        out_specs=[tiles, tiles, tops, tops, flat, flat, flat, full((16, D))],
        scratch_shapes=[
            pltpu.VMEM((tokens, D), f32),
            pltpu.VMEM((tokens, D), bf16),
            pltpu.VMEM((tokens, D), f32),
            pltpu.VMEM((D, D), f32),
            pltpu.VMEM((D, D), f32),
        ],
        name="mlp_back",
        cost_estimate=cost(8 * tokens * D * FF, 5e7, tokens * FF),
    )(core, ghp, picks.reshape(1, count), x2, act, up, h2, x1, wdown, wup, wo, vectors)


def qkv_back_kernel(g_ref, w_ref, x_ref, gx1_ref, vec_ref, gx0_ref, vg_ref, gh):
    j = pl.program_id(0)
    part = mm_t(g_ref[0], w_ref[...])

    @pl.when(j == 0)
    def _():
        vg_ref[...] = jnp.zeros_like(vg_ref)
        gh[...] = part

    @pl.when(j > 0)
    def _():
        gh[...] += part

    vg_ref[pl.ds(8 + j, 1), :] = jnp.sum(g_ref[0].astype(f32), 0, keepdims=True)

    @pl.when(j == 2)
    def _():
        grad, gain, bias = norm_pull(x_ref[...].astype(f32), vec_ref[0:1, :], gh[...])
        vg_ref[0:1, :] = gain
        vg_ref[1:2, :] = bias
        gx0_ref[...] = (gx1_ref[...] + grad).astype(bf16)


def qkv_back(grads, wqkv, x0, gx1, vectors):
    tokens = x0.shape[0]
    flat = full((tokens, D))
    return pl.pallas_call(
        qkv_back_kernel,
        grid=(3,),
        out_shape=[
            jax.ShapeDtypeStruct((tokens, D), bf16),
            jax.ShapeDtypeStruct((16, D), f32),
        ],
        in_specs=[
            pl.BlockSpec((1, tokens, D), lambda j: (j, 0, 0)),
            pl.BlockSpec((D, D), lambda j: (0, j)),
            flat,
            flat,
            full(vectors.shape),
        ],
        out_specs=[flat, full((16, D))],
        scratch_shapes=[pltpu.VMEM((tokens, D), f32)],
        name="qkv_back",
        cost_estimate=cost(2 * tokens * D * 3 * D, 1e7),
    )(grads, wqkv, x0, gx1, vectors)


def qkv_weights_kernel(
    core_ref, h_ref, g_ref, y_ref, ga_ref, small_ref, mine_ref, theirs_ref, mtop_ref, ttop_ref, tile
):
    j = pl.program_id(0)
    core = core_ref[0]
    outs = (mine_ref, theirs_ref, mtop_ref, ttop_ref)

    @pl.when(j < 3)
    def _():
        tile[...] = mm_l(h_ref[...], g_ref[0])

    @pl.when(j == 3)
    def _():
        tile[...] = mm_l(y_ref[...], ga_ref[...])

    @pl.when(j < 4)
    def _():
        for r in range(2):
            for c in range(2):
                halve(core, tile, outs, 4 * j + 2 * r + c, r, c)

    @pl.when(j == 4)
    def _():
        halve(core, small_ref, outs, 16, 0, 0)


def qkv_weights(core, h1, grads, y, ga, small):
    tokens = h1.shape[0]
    flat = full((tokens, D))
    halves = (17, BS // 2, BS)
    highs = (17, 1, BS)
    shapes = (halves, halves, highs, highs)
    return pl.pallas_call(
        qkv_weights_kernel,
        grid=(5,),
        out_shape=[jax.ShapeDtypeStruct(shape, f32) for shape in shapes],
        in_specs=[
            pl.BlockSpec(memory_space=SMEM),
            flat,
            pl.BlockSpec((1, tokens, D), lambda j: (jnp.minimum(j, 2), 0, 0)),
            flat,
            flat,
            full((BS, BS)),
        ],
        out_specs=[full(shape) for shape in shapes],
        scratch_shapes=[pltpu.VMEM((D, D), f32)],
        name="qkv_weights",
        cost_estimate=cost(2 * tokens * D * 4 * D, 2e7),
    )(core, h1, grads, y, ga, small)


def comm_positions():
    order = []
    for j in range(FSTEPS):
        order += [16 + r * 8 + 2 * j + c for r in range(2) for c in range(2)]
        order += [32 + (2 * j + r) * 2 + c for r in range(2) for c in range(2)]
    for j in range(3):
        order += [r * 6 + 2 * j + c for r in range(2) for c in range(2)]
    order += [12 + r * 2 + c for r in range(2) for c in range(2)]
    positions = np.zeros(48, np.int32)
    positions[np.array(order)] = np.arange(48)
    return positions


def three(left, right, product):
    left_high, left_low = left
    right_high, right_low = right
    return (
        product(left_high, right_high)
        + product(left_high, right_low)
        + product(left_low, right_high)
    )


def shampoo_kernel(count, strip, places_ref, clip_ref, *refs):
    pieces = refs[:count]
    w_ref, ls_ref, rs_ref, lr_ref, rr_ref = refs[count : count + 5]
    g_ref, nw_ref, nl_ref, nr_ref = refs[count + 5 :]
    clip = clip_ref[0]
    for k in range(count):
        for half in range(2):
            place = pl.multiple_of(places_ref[2 * k + half], strip)
            g_ref[0, pl.ds(place, strip), :] = pieces[k][0, half] * clip
    grads = split_two(g_ref[0])
    nl_ref[0] = SHAMPOO_BETA * ls_ref[0] + (1.0 - SHAMPOO_BETA) * three(grads, grads, mm_t)
    nr_ref[0] = SHAMPOO_BETA * rs_ref[0] + (1.0 - SHAMPOO_BETA) * three(grads, grads, mm_l)
    turned = split_two(three(grads, split_two(rr_ref[0]), mm))
    direction = three(split_two(lr_ref[0]), turned, mm)
    weights = w_ref[0]
    nw_ref[0] = weights - RATE_BLOCKS * (direction + DECAY_RATE * weights)


def shampoo(places, clip, pieces, weights, left_stats, right_stats, left_roots, right_roots):
    slots = weights.shape[0]
    count = len(pieces)
    strip = pieces[0].shape[2]
    block = pl.BlockSpec((1, BS, BS), lambda s: (s, 0, 0))
    shape = jax.ShapeDtypeStruct((slots, BS, BS), f32)
    return pl.pallas_call(
        partial(shampoo_kernel, count, strip),
        grid=(slots,),
        out_shape=[shape] * 4,
        in_specs=[pl.BlockSpec(memory_space=SMEM)] * 2
        + [pl.BlockSpec((1, 2, strip, BS), lambda s: (s, 0, 0, 0))] * count
        + [block] * 5,
        out_specs=[block] * 4,
        name="shampoo",
        cost_estimate=cost(slots * 24 * BS**3, slots * BS * BS * 40),
    )(places, clip, *pieces, weights, left_stats, right_stats, left_roots, right_roots)


def adam_update(weight, first, second, gradient, rate, step_value):
    first_new = BETA_FIRST * first + (1.0 - BETA_FIRST) * gradient
    second_new = BETA_SECOND * second + (1.0 - BETA_SECOND) * gradient * gradient
    first_hat = first_new / (1.0 - BETA_FIRST**step_value)
    second_hat = second_new / (1.0 - BETA_SECOND**step_value)
    return (
        weight - rate * (first_hat / (jnp.sqrt(second_hat) + ADAM_EPSILON) + DECAY_RATE * weight),
        first_new,
        second_new,
    )


def tie(values, *others):
    return lax.optimization_barrier((values,) + others)[0]


LEVEL = 32768.0


def encode(values, bound):
    return (values * (LEVEL / jnp.maximum(bound, 1e-30))).astype(jnp.float16)


def decode(coded, bound):
    return coded.astype(f32) * (jnp.maximum(bound, 1e-30) * (1.0 / LEVEL))


def per_device(
    sizes,
    token_ids,
    seq_lengths,
    pick_rows,
    targets,
    step_count,
    block_order,
    slot_weights,
    left_stats,
    right_stats,
    left_roots,
    right_roots,
    embedding,
    embedding_first_moment,
    emb_second,
    vectors,
    vec_first,
    vec_second,
    feature_maps,
    map_first,
    map_second,
):
    ny, nc, n1, n0 = sizes
    n_dp, n_voc = ny * nc, n1 * n0
    dp_index, voc_index = lax.axis_index("dp"), lax.axis_index("vocab")
    y_at, c_at = dp_index // nc, dp_index % nc
    i1, i0 = voc_index // n0, voc_index % n0

    def over_dp(values, dy, dc):
        pairs = [
            (a * nc + b, ((a + dy) % ny) * nc + (b + dc) % nc) for a in range(ny) for b in range(nc)
        ]
        return lax.ppermute(values, "dp", pairs)

    def over_voc(values, d1, d0):
        pairs = [
            (a * n0 + b, ((a + d1) % n1) * n0 + (b + d0) % n0) for a in range(n1) for b in range(n0)
        ]
        return lax.ppermute(values, "vocab", pairs)

    def gather_voc(values):
        near = [values] + [over_voc(values, k, 0) for k in range(1, n1)]
        return [[part] + [over_voc(part, 0, k) for k in range(1, n0)] for part in near]

    def flat_gather(values):
        return [part for line in gather_voc(values) for part in line]

    def gather_y(values):
        return [values] + [over_dp(values, k, 0) for k in range(1, ny)]

    def line_up(parts, at):
        size = len(parts)
        return jnp.take(jnp.stack(parts), (at - jnp.arange(size)) % size, axis=0)

    tokens = token_ids.shape[0]
    picks_own = pick_rows.shape[0]
    devices_all = n_dp * n_voc
    total_picks = picks_own * devices_all
    coefficient = DISTILL_WEIGHT / (tokens * devices_all * HEADS)
    shard_rows, cols_own = embedding.shape
    cols_y = cols_own * nc
    vocab_start = (voc_index * shard_rows).astype(i32)
    per_owner = slot_weights.shape[0]
    block_count = block_order.shape[0]
    table_own = embedding.T
    relative = [((y_at - ky) % ny) * nc + (c_at + kc) % nc for kc in range(nc) for ky in range(ny)]
    relative = jnp.stack(relative)
    canonical = jnp.stack(
        [
            ((j % nc - c_at) % nc) * ny + (y_at - j // nc) % ny
            for j in range(n_dp)
        ]
    )

    ids_y = jnp.stack(gather_y(token_ids))
    ids_rows = jnp.concatenate(flat_gather(ids_y), 0).reshape(-1)
    targets_all = jnp.concatenate(flat_gather(targets), 0)
    local_ids = ids_rows - vocab_start
    packed_ids = jnp.where(
        (local_ids >= 0) & (local_ids < shard_rows),
        (local_ids << 16) | jnp.arange(ids_rows.shape[0], dtype=i32),
        -1,
    )
    hit_list, hit_count = find_hits(packed_ids, shard_rows)

    low_own = table_own.astype(bf16)
    low_other = over_dp(low_own, 0, 1)
    first_core = c_at == 0
    upright = jnp.concatenate(
        [jnp.where(first_core, low_own, low_other), jnp.where(first_core, low_other, low_own)], 0
    ).T

    slots_y = gather_y(slot_weights.astype(bf16))

    found = lookup(hit_list, hit_count, upright, ids_rows.shape[0])
    found = found.reshape(n1, n0, ny, tokens, cols_y)
    by_one = []
    for a in list(range(1, n1)) + [0]:
        part = found[a, 0]
        for b in range(1, n0):
            part = part + over_voc(found[a, b], 0, -b)
        by_one.append(part)
    mine = by_one[-1]
    for a in range(1, n1):
        mine = mine + over_voc(by_one[a - 1], -a, 0)

    slots_y = [slots_y[0]] + [tie(part, *by_one[:-1]) for part in slots_y[1:]]
    slots_core = [over_dp(part, 0, 1) for part in slots_y]
    inverse = (
        jnp.zeros((block_count,), i32).at[block_order].set(jnp.arange(block_count, dtype=i32))
    )
    owner = inverse // per_owner
    src = ((c_at - owner % nc) % nc) * ny + (y_at - owner // nc) % ny
    wqkv, wo, wup, wdown = place_blocks(
        src.astype(i32), inverse % per_owner, slots_y + slots_core
    )

    low_sent = tie(low_own, *slots_y[1:])
    low_y = [over_dp(low_sent, k, 0) for k in range(1, ny)]

    row_parts = [mine[0]] + [over_dp(mine[k], -k, 0) for k in range(1, ny)]
    if ny == 2:
        first = y_at == 0
        x0 = jnp.concatenate(
            [
                jnp.where(first, row_parts[0], row_parts[1]),
                jnp.where(first, row_parts[1], row_parts[0]),
            ],
            1,
        )
    else:
        stacked = jnp.stack(row_parts)
        x0 = jnp.concatenate(
            [jnp.take(stacked, (j - y_at) % ny, axis=0) for j in range(ny)], axis=1
        )

    maps_low = feature_maps.astype(bf16)
    both = jnp.concatenate([maps_low, -maps_low], -1).reshape(2, PAIRS, 2, HD, 2 * HD)
    empty = jnp.zeros_like(both[:, :, 0])
    lift_maps = jnp.stack(
        [
            jnp.concatenate([both[:, :, 0], empty], -2),
            jnp.concatenate([empty, both[:, :, 1]], -2),
        ],
        2,
    ).reshape(2, HEADS, 2 * HD, 2 * HD)
    h1, mixed = qkv_forward(x0, wqkv, vectors)
    y, distill = attend(seq_lengths, mixed, lift_maps)
    x1, h2, up, act, x2, picked = mlp_forward(x0, y, wo, wup, wdown, vectors, pick_rows)

    low_y = [tie(part, picked) for part in low_y]
    low_y_other = [over_dp(part, 0, 1) for part in low_y]
    table = jnp.concatenate([low_own] + low_y + [low_other] + low_y_other, 0)
    picked = jnp.take(picked.reshape(picks_own, n_dp, cols_own), relative, axis=1)
    picked = picked.reshape(picks_own, D)
    group = jnp.concatenate(flat_gather(picked), 0)
    local_targets = targets_all - vocab_start
    logits = mm(group, table)
    hit = jnp.arange(shard_rows, dtype=i32)[None, :] == local_targets[:, None]
    top = jnp.max(logits, 1)
    exp_sum = jnp.sum(jnp.exp(logits - top[:, None]), 1)
    chosen = jnp.sum(jnp.where(hit, logits, 0.0), 1)
    stats = jnp.stack([top, exp_sum, chosen]).reshape(3, n1, n0, picks_own)
    stats_all = gather_voc(stats)
    lined = jnp.stack(
        [jnp.roll(stats_all[a][b], (a, b), (1, 2)) for a in range(n1) for b in range(n0)]
    ).reshape(n_voc, 3, n_voc * picks_own)
    top_all = jnp.max(lined[:, 0], 0)
    sum_all = jnp.sum(lined[:, 1] * jnp.exp(lined[:, 0] - top_all[None]), 0)
    losses = top_all + jnp.log(sum_all) - jnp.sum(lined[:, 2], 0)
    loss_part = jnp.sum(losses[:picks_own]) / total_picks + coefficient * distill[0, 0]
    grad_logits = (
        (jnp.exp(logits - top_all[:, None]) * (1.0 / sum_all)[:, None] - hit) / total_picks
    ).astype(bf16)
    grad_group = mm_t(grad_logits, table).reshape(n1, n0, picks_own, D)
    by_one = []
    for a in list(range(1, n1)) + [0]:
        part = grad_group[a, 0]
        for b in range(1, n0):
            part = part + over_voc(grad_group[a, b], 0, -b)
        by_one.append(part)
    near_parts = [over_voc(by_one[a - 1], -a, 0) for a in range(1, n1)]

    lex_theirs = mm_l(group[:, D // nc :], grad_logits)
    lex_arrived = over_dp(lex_theirs, 0, 1)
    near_parts = [tie(part, lex_theirs) for part in near_parts]
    ghp = by_one[-1]
    for part in near_parts:
        ghp = ghp + part
    ghp = jnp.take(ghp.reshape(picks_own, n_dp, cols_own), canonical, axis=1)
    ghp = ghp.reshape(picks_own, D)
    lex_sums = mm_l(group[:, : D // nc], grad_logits) + lex_arrived
    lex = lex_sums[:cols_own]
    for k in range(1, ny):
        lex = lex + over_dp(lex_sums[k * cols_own : (k + 1) * cols_own], -k, 0)

    core = c_at.astype(i32).reshape(1)

    def reduce_blocks(mine_half, their_half, mine_top, their_top):
        part = mine_half + over_dp(their_half, 0, 1)
        bound = mine_top + over_dp(their_top, 0, 1)
        for size, at, far in ((n0, i0, 0), (n1, i1, 1)):
            rows = part.shape[1] // size
            total = lax.dynamic_slice_in_dim(part, at * rows, rows, 1)
            bound_next = bound
            for k in range(1, size):
                d1, d0 = (k, 0) if far else (0, k)
                piece = lax.dynamic_slice_in_dim(part, ((at + k) % size) * rows, rows, 1)
                coded = over_voc(encode(piece, bound), d1, d0)
                theirs = over_voc(bound, d1, d0)
                total = total + decode(coded, theirs)
                bound_next = bound_next + theirs
            part, bound = total, bound_next
        return part

    *halves_a, gx1, ga, gy, vg_a = mlp_back(
        core, ghp, pick_rows, x2, act, up, h2, x1, wdown, wup, wo, vectors
    )
    blocks_a = reduce_blocks(*halves_a)
    half_pairs = PAIRS // 2
    gqkv, map_q_a, map_k_a = attend_back(
        seq_lengths, mixed, gy, lift_maps, coefficient, 0, half_pairs, None
    )
    gqkv, map_q_b, map_k_b = attend_back(
        seq_lengths, mixed, gy, lift_maps, coefficient, half_pairs, half_pairs, gqkv
    )
    gx0, vg_b = qkv_back(gqkv, wqkv, x0, gx1, vectors)

    map_grads = jnp.concatenate([map_q_a, map_q_b, map_k_a, map_k_b], 0)
    vec_grads = (vg_a + vg_b)[:15]
    small_count = map_grads.size + vec_grads.size
    small = jnp.concatenate(
        [
            map_grads.reshape(-1),
            vec_grads.reshape(-1),
            jnp.zeros((BS * BS - small_count,), f32),
        ]
    ).reshape(BS, BS)
    blocks_b = reduce_blocks(*qkv_weights(core, h1, gqkv, y, ga, small))

    gx0_cols = gx0.reshape(tokens, ny, cols_y)
    arrived = [jnp.take(gx0_cols, y_at, axis=1)] + [
        over_dp(jnp.take(gx0_cols, (y_at + k) % ny, axis=1), k, 0) for k in range(1, ny)
    ]
    arrived = jnp.concatenate(arrived, 0).reshape(ny * tokens, nc, cols_own)
    rows_mine = jnp.take(arrived, c_at, axis=1)
    rows_other = over_dp(jnp.take(arrived, (c_at + 1) % nc, axis=1), 0, 1)
    if cols_own == 192:
        packed = jnp.concatenate(
            [
                rows_mine[:, :128],
                rows_other[:, :128],
                jnp.concatenate([rows_mine[:, 128:], rows_other[:, 128:]], 1),
            ],
            0,
        )
        pieces = flat_gather(packed)
        lists = (hit_list, hit_count, over_dp(hit_list, 0, 1), over_dp(hit_count, 0, 1))
        emb_grads, emb_square = scatter_rows(lists, lex, pieces)
        emb_square = emb_square[0, 0]
    else:
        packed = jnp.stack([rows_mine, rows_other])
        pieces = jnp.stack(flat_gather(packed), 1).reshape(-1, cols_own)
        local = jnp.concatenate([ids_rows, over_dp(ids_rows, 0, 1)]) - vocab_start
        local = jnp.where((local >= 0) & (local < shard_rows), local, shard_rows)
        emb_grads = lex.T.at[local].add(pieces.astype(f32), mode="drop").T
        emb_square = jnp.sum(emb_grads * emb_grads)

    blocks = jnp.concatenate([blocks_a, blocks_b], 0)
    slot_places = jnp.take(jnp.asarray(comm_positions()), block_order).reshape(
        ny, nc * per_owner
    )

    def slots_of(k):
        places = jnp.take(slot_places, (y_at + k) % ny, axis=0)
        return jnp.take(blocks, places, axis=0)

    strips = slots_of(0)
    small_parts = [blocks[block_count:]]
    for k in range(1, ny):
        moved = over_dp(jnp.concatenate([slots_of(k), blocks[block_count:]], 0), k, 0)
        strips = strips + moved[:-1]
        small_parts.append(moved[-1:])
    if ny == 2:
        small_sum = small_parts[0] + small_parts[1]
    else:
        small_sum = jnp.sum(line_up(small_parts, y_at), 0)
    strip_rows = strips.shape[1]
    strips = strips.reshape(nc, per_owner, strip_rows, BS)

    def with_small(k):
        return jnp.concatenate([jnp.take(strips, (c_at + k) % nc, axis=0), small_sum], 0)

    own_strips = jnp.stack([with_small(0), over_dp(with_small(1), 0, 1)], 1)
    strip_bound = jnp.max(jnp.abs(own_strips), 2, keepdims=True)
    coded_all = flat_gather(encode(own_strips, strip_bound))
    bound_all = flat_gather(strip_bound)
    strip_pieces = [decode(part, bound) for part, bound in zip(coded_all, bound_all)]

    square = emb_square + jnp.sum(strips * strips)
    square = square + jnp.where(y_at == 0, jnp.sum(small_sum * small_sum), 0.0)
    sums = jnp.pad(jnp.stack([square, loss_part]).reshape(1, 2), ((0, 7), (0, 126)))
    sums = sums + over_dp(sums, 0, 1)
    sums = jnp.sum(line_up(gather_y(sums), y_at), 0)
    sums = jnp.sum(line_up([sums] + [over_voc(sums, 0, k) for k in range(1, n0)], i0), 0)
    sums = jnp.sum(line_up([sums] + [over_voc(sums, k, 0) for k in range(1, n1)], i1), 0)
    grad_norm = jnp.sqrt(sums[0, 0])
    loss_total = sums[0, 1]
    clip_scale = CLIP_NORM / jnp.maximum(grad_norm, CLIP_NORM)

    small_all = jnp.stack([part[per_owner] for part in strip_pieces])
    small_all = small_all.reshape(n1, n0, nc, strip_rows, BS)
    small_all = jnp.take(small_all, (i1 - jnp.arange(n1)) % n1, axis=0)
    small_all = jnp.take(small_all, (i0 - jnp.arange(n0)) % n0, axis=1)
    small_all = jnp.take(small_all, (c_at - jnp.arange(nc)) % nc, axis=2)
    small_all = small_all.transpose(2, 1, 0, 3, 4).reshape(-1)
    map_sum = small_all[: map_grads.size].reshape(feature_maps.shape)
    vec_sum = small_all[map_grads.size : small_count].reshape(vectors.shape)

    strip_half = BS // nc
    if strip_rows % 8:
        whole = jnp.stack(strip_pieces).reshape(n1, n0, per_owner + 1, nc, strip_rows, BS)
        whole = jnp.take(whole, (i1 - jnp.arange(n1)) % n1, axis=0)
        whole = jnp.take(whole, (i0 - jnp.arange(n0)) % n0, axis=1)
        strip_pieces = [
            whole.transpose(2, 3, 1, 0, 4, 5).reshape(per_owner + 1, nc, strip_half, BS)
        ]
        bases = [0]
    else:
        bases = [
            ((i0 - b) % n0) * (strip_half // n0) + ((i1 - a) % n1) * strip_rows
            for a in range(n1)
            for b in range(n0)
        ]
    places = []
    for base in bases:
        places += [c_at * strip_half + base, ((c_at + 1) % nc) * strip_half + base]
    places = jnp.stack(places).astype(i32)
    clipped, new_slots, new_left, new_right = shampoo(
        places,
        clip_scale.reshape(1),
        strip_pieces,
        slot_weights,
        left_stats,
        right_stats,
        left_roots,
        right_roots,
    )
    step_value = step_count[0].astype(f32)
    emb_out = adam_update(
        table_own,
        embedding_first_moment.T,
        emb_second.T,
        emb_grads * clip_scale,
        RATE_TABLE,
        step_value,
    )
    vec_out = adam_update(
        vectors, vec_first, vec_second, vec_sum * clip_scale, RATE_VECTORS, step_value
    )
    map_out = adam_update(
        feature_maps, map_first, map_second, map_sum * clip_scale, RATE_MAPS, step_value
    )
    return (
        loss_total,
        grad_norm,
        clipped,
        new_slots,
        new_left,
        new_right,
        emb_out[0].T,
        emb_out[1].T,
        emb_out[2].T,
        vec_out[0],
        vec_out[1],
        vec_out[2],
        map_out[0],
        map_out[1],
        map_out[2],
    )


def solution(mesh):
    n_dp, n_voc = mesh.shape["dp"], mesh.shape["vocab"]
    sizes = (n_dp // 2, 2, 4, n_voc // 4)
    rows = P(("dp", "vocab"))
    blocks = P("dp", None, None)
    table = P("vocab", "dp")
    placed = (
        (rows, P(("dp", "vocab"), None), rows, rows, P(), P())
        + (blocks,) * 5
        + (table,) * 3
        + (P(),) * 6
    )
    return jax.shard_map(
        partial(per_device, sizes),
        mesh=mesh,
        in_specs=placed,
        out_specs=(P(), P()) + (blocks,) * 4 + (table,) * 3 + (P(),) * 6,
        check_vma=False,
    )
```

time: 1750 us -> 1050 us (0.60)
  matrix products: 371 us -> 43.1 us
  Pallas kernels: 0 us -> 233 us
  waiting for transfers between devices: 663 us -> 430 us
  local copies, waits for them, and re-layouts: 296 us -> 73.4 us
  blocking collectives: 147 us -> 0 us
  starting transfers between devices: 0.29 us -> 135 us
  other arithmetic: 215 us -> 114 us
    ppermute x0 -> x105, waiting for transfers between devices: none -> 430 us  [the longest x83 330 us: over_voc(): return lax.ppermute(values, 'vocab', pairs)]
    psum x1 -> x0, waiting for transfers between devices: 350 us -> none  [per_device(): lax.psum((slot_grads_all, vec_grads, grad_maps), ('dp', 'vocab'))]
    dot_general x131 -> x4, matrix products: 363 us -> 43.1 us  [the longest x2 19.2 us: mm_l(): lax.dot_general(left, right, (((0,), (0,)), ((), ())), preferred_element_...]
    pallas_call x0 -> x13, Pallas kernels: none -> 233 us  [the longest x2 38.3 us: attend_back(): pl.pallas_call(partial(attend_back_kernel, coefficient, int(later)), grid...]
    ppermute x0 -> x105, starting transfers between devices: none -> 135 us  [the longest x83 125 us: over_voc(): return lax.ppermute(values, 'vocab', pairs)]
    unnamed x8 -> x0, waiting for transfers between devices: 133 us -> none
    reduce_scatter x2 -> x0, waiting for transfers between devices: 118 us -> none  [the longest x1 63.1 us: per_device(): lax.psum_scatter(product(lax.dynamic_slice_in_dim(grad_logits, jnp.int32(...]
    gather x5 -> x15, local copies, waits for them, and re-layouts: 81.6 us -> 7.83 us  [the longest x3 1.77 us: line_up(): return jnp.take(jnp.stack(parts), (at - jnp.arange(size)) % size, axis=0)]
  transfers between devices with their start and end apart: 7 -> 105, of which waited for: 6 -> 53; matrix products, arithmetic and copies ran while one was open for 21% -> 16% of each run, Pallas kernels for 0% -> 19%
where the time goes in v1:
time: 1050 us; the launch traced here: 1040 us
  waiting for transfers between devices  430 us (41%)
  Pallas kernels  233 us (22%)
  starting transfers between devices  135 us (13%)
  other arithmetic  114 us (11%)
  local copies, waits for them, and re-layouts  73.4 us (7%)
  matrix products  43.1 us (4%)
    ppermute x83, waiting for transfers between devices, over_voc(): return lax.ppermute(values, 'vocab', pairs)  330 us
    ppermute x83, starting transfers between devices, over_voc(): return lax.ppermute(values, 'vocab', pairs)  125 us
    ppermute x22, waiting for transfers between devices, over_dp(): return lax.ppermute(values, 'dp', pairs)  101 us
    pallas_call x2, Pallas kernels, attend_back(): pl.pallas_call(partial(attend_back_kernel, coefficient, int(later)), grid...  38.3 us
    pallas_call x1, Pallas kernels, shampoo(): pl.pallas_call(partial(shampoo_kernel, count, strip), grid=(slots,), out_...  35.7 us
    pallas_call x1, Pallas kernels, mlp_back(): pl.pallas_call(mlp_back_kernel, grid=(FSTEPS,), out_shape=[halves, halves...  27.1 us
    unnamed x177, local copies, waits for them, and re-layouts  24.9 us
    pallas_call x1, Pallas kernels, scatter_rows(): pl.pallas_call(partial(scatter_kernel, count, half, rows_all), out_shape=...  24.6 us
  transfers between devices with their start and end apart: 105, of which 53 were waited for; matrix products, arithmetic and copies ran while one was open for 16% of the time, Pallas kernels for 19%

profile of v1, /device:TPU:8, one launch (start us, length us, event | category | flops | bytes accessed | tf_op | source)
XLA Modules:
  0.0 1037.5 jit_solution(16620428656000230385)
XLA Ops:
  27.5 24.4 %find_hits.1 = (s32[8208]{0:T(1024)}, s32[1]{0:T(128)}) custom-call(s32[8192]{0:T(1024)} %or_select_fusion.packed_ref), custom_call_target="tpu_custom_call" | custom-call | flops 10000000000 | bytes 65536 | tf_op jit(solution)/shard_map/find_hits/pallas_call | solution.py:140
  58.1 7.4 copy.117.table_ref
  65.5 11.7 %lookup.1 = bf16[8192,384]{1,0:T(8,128)(2,1)} custom-call(s32[8208]{0:T(1024)} %get-tuple-element.69.list_ref.refs_0_, s32[1]{0:T(128)} %get-tuple-element.70.count_ref.refs_1_, bf16[6288,384]{1,0:T(8,128)(2,1)} %copy.117.table_ref), custom_call_target="tpu_custom_call" | custom-call | flops 10000000000 | bytes 4829184 | tf_op jit(solution)/shard_map/lookup/pallas_call | solution.py:173
  79.5 5.7 collective-permute-start.12
  87.2 16.4 %collective-permute-done.12 = bf16[2,512,384]{2,1,0:T(8,128)(2,1)S(1)} collective-permute-done((bf16[2,512,384]{2,1,0:T(8,128)(2,1)S(1)}, bf16[2,512,384]{2,1,0:T(8,128)(2,1)S(1)}, u32[]{:S(2)}, u32[]{:S(2)}) %collective-permute-start.12) | collective-permute-done | bytes 786464 | tf_op jit(solution)/shard_map/ppermute | solution.py:1004
  103.7 16.9 %collective-permute-done.14 = bf16[2,512,384]{2,1,0:T(8,128)(2,1)S(1)} collective-permute-done((bf16[2,512,384]{2,1,0:T(8,128)(2,1)S(1)}, bf16[2,512,384]{2,1,0:T(8,128)(2,1)S(1)}, u32[]{:S(2)}, u32[]{:S(2)}) %collective-permute-start.14) | collective-permute-done | bytes 786464 | tf_op jit(solution)/shard_map/ppermute | solution.py:1004
  120.5 13.0 %collective-permute-done.16 = bf16[2,512,384]{2,1,0:T(8,128)(2,1)S(1)} collective-permute-done((bf16[2,512,384]{2,1,0:T(8,128)(2,1)S(1)}, bf16[2,512,384]{2,1,0:T(8,128)(2,1)S(1)}, u32[]{:S(2)}, u32[]{:S(2)}) %collective-permute-start.16) | collective-permute-done | bytes 786464 | tf_op jit(solution)/shard_map/ppermute | solution.py:1004
  136.7 17.2 %collective-permute-done.11 = bf16[2,512,384]{2,1,0:T(8,128)(2,1)S(1)} collective-permute-done((bf16[2,512,384]{2,1,0:T(8,128)(2,1)S(1)}, bf16[2,512,384]{2,1,0:T(8,128)(2,1)S(1)}, u32[]{:S(2)}, u32[]{:S(2)}) %collective-permute-start.11) | collective-permute-done | bytes 786464 | tf_op jit(solution)/shard_map/ppermute | solution.py:1004
  154.2 35.6 %collective-permute-done.13 = bf16[2,512,384]{2,1,0:T(8,128)(2,1)S(1)} collective-permute-done((bf16[2,512,384]{2,1,0:T(8,128)(2,1)S(1)}, bf16[2,512,384]{2,1,0:T(8,128)(2,1)S(1)}, u32[]{:S(2)}, u32[]{:S(2)}) %collective-permute-start.13) | collective-permute-done | bytes 786464 | tf_op jit(solution)/shard_map/ppermute | solution.py:1004
  189.8 12.2 %collective-permute-done.17 = bf16[2,512,384]{2,1,0:T(8,128)(2,1)S(1)} collective-permute-done((bf16[2,512,384]{2,1,0:T(8,128)(2,1)S(1)}, bf16[2,512,384]{2,1,0:T(8,128)(2,1)S(1)}, u32[]{:S(2)}, u32[]{:S(2)}) %collective-permute-start.17) | collective-permute-done | bytes 786464 | tf_op jit(solution)/shard_map/ppermute | solution.py:1004
  211.6 4.6 collective-permute-done.18
  218.4 11.5 %place_blocks.1 = (bf16[768,2304]{1,0:T(8,128)(2,1)}, bf16[768,768]{1,0:T(8,128)(2,1)}, bf16[768,3072]{1,0:T(8,128)(2,1)}, bf16[3072,768]{1,0:T(8,128)(2,1)}) custom-call(s32[48]{0:T(128)} %get-tuple-element.253.src_ref, s32[48]{0:T(128)} %get-tuple-element.252.off_ref, bf16[12,384,384]{2,1,0:T(8,128)(2,1)} %copy-done.5, ...), custom_call_target="tpu_custom_call" | custom-call | bytes 28311552 | tf_op jit(solution)/shard_map/place_blocks/pallas_call | solution.py:108
  229.8 6.2 qkv_forward.1
  236.0 20.0 %attend.1 = (bf16[512,768]{1,0:T(8,128)(2,1)}, f32[8,128]{1,0:T(8,128)}) custom-call(s32[1,4]{1,0:T(1,128)} %len_ref.5, bf16[512,2304]{1,0:T(8,128)(2,1)} %get-tuple-element.73.q_ref.k_ref.v_ref, bf16[512,2304]{1,0:T(8,128)(2,1)} %get-tuple-element.73.q_ref.k_ref.v_ref, bf16[512,2304]{1,0:T(8,128)(2,1)} %get-tuple-element.73.q_ref.k_ref.v_ref, ...), custom_call_target="tpu_custom_call" | custom-call | flops 12000000000 | bytes 4000000 | tf_op jit(solution)/shard_map/attend/pallas_call | solution.py:401
  256.0 14.8 %mlp_forward.1 = (f32[512,768]{1,0:T(8,128)}, bf16[512,768]{1,0:T(8,128)(2,1)}, f32[512,3072]{1,0:T(8,128)}, bf16[512,3072]{1,0:T(8,128)(2,1)}, f32[512,768]{1,0:T(8,128)}, /*index=5*/bf16[64,768]{1,0:T(8,128)(2,1)}) custom-call(bf16[512,768]{1,0:T(8,128)(2,1)} %pad_maximum_fusion.6.x_ref, bf16[512,768]{1,0:T(8,128)(2,1)} %get-tuple-element.74.y_ref, ...), custom_call_target="tpu_custom_call" | custom-call | flops 5435817984 | bytes 30000000 | tf_op jit(solution)/shard_map/mlp_forward/pallas_call | solution.py:599
  274.4 4.3 collective-permute-start.34
  303.1 11.0 %fusion.72 = (f32[512]{0:T(512)S(1)}, f32[512,6288]{0,1:T(8,128)}) fusion(bf16[512,768]{1,0:T(8,128)(2,1)S(1)} %constant_dynamic-update-slice_fusion, bf16[192,6288]{1,0:T(8,128)(2,1)} %collective-permute-done.30, bf16[192,6288]{1,0:T(8,128)(2,1)} %collective-permute-done.10, bf16[192,6288]{1,0:T(8,128)(2,1)} %collective-permute-done.29, ...), kind=kOutput, calls=%fused_computation.348 | convolution fusion | flops 4986936832 | bytes 23324672 | tf_op jit(solution)/shard_map/dot_general | solution.py:39
  314.2 6.8 exponential_reduce_fusion
  337.8 7.1 multiply_convert_fusion
  344.9 12.9 %fusion.4 = f32[512,768]{1,0:T(8,128)S(1)} fusion(bf16[512,6288]{0,1:T(8,128)(2,1)S(1)} %multiply_convert_fusion, bf16[192,6288]{1,0:T(8,128)(2,1)} %collective-permute-done.30, bf16[192,6288]{1,0:T(8,128)(2,1)} %collective-permute-done.10, bf16[192,6288]{1,0:T(8,128)(2,1)} %collective-permute-done.29, bf16[192,6288]{1,0:T(8,128)(2,1)} %bitcast_convert_fusion), kind=kOutput, calls=%fused_computation.35 | convolution fusion | flops 4983717888 | bytes 17670144 | tf_op jit(solution)/shard_map/dot_general | solution.py:43
  373.4 10.1 fusion.18
  385.5 27.1 %mlp_back.1 = (f32[32,192,384]{2,1,0:T(8,128)}, f32[32,192,384]{2,1,0:T(8,128)}, f32[32,1,384]{2,1,0:T(1,128)}, f32[32,1,384]{2,1,0:T(1,128)}, f32[512,768]{1,0:...) custom-call(s32[1]{0:T(128)} %bitcast.37.core_ref, ...), custom_call_target="tpu_custom_call" | custom-call | flops 9663676416 | bytes 50000000 | tf_op jit(solution)/shard_map/mlp_back/pallas_call | solution.py:740
  413.2 19.2 %attend_back.2 = (bf16[3,512,768]{2,1,0:T(8,128)(2,1)}, f32[6,64,64]{2,1,0:T(8,128)}, f32[6,64,64]{2,1,0:T(8,128)}) custom-call(s32[1,4]{1,0:T(1,128)} %len_ref.5, bf16[512,2304]{1,0:T(8,128)(2,1)} %get-tuple-element.73.q_ref.k_ref.v_ref, bf16[512,2304]{1,0:T(8,128)(2,1)} %get-tuple-element.73.q_ref.k_ref.v_ref, ...), custom_call_target="tpu_custom_call" | custom-call | flops 12000000000 | bytes 4000000 | tf_op jit(solution)/shard_map/attend_back/pallas_call | solution.py:513
  432.5 19.0 %attend_back.3 = (bf16[3,512,768]{2,1,0:T(8,128)(2,1)}, f32[6,64,64]{2,1,0:T(8,128)}, f32[6,64,64]{2,1,0:T(8,128)}) custom-call(s32[1,4]{1,0:T(1,128)} %len_ref.5, bf16[512,2304]{1,0:T(8,128)(2,1)} %get-tuple-element.73.q_ref.k_ref.v_ref, bf16[512,2304]{1,0:T(8,128)(2,1)} %get-tuple-element.73.q_ref.k_ref.v_ref, ...), custom_call_target="tpu_custom_call", output_to_operand_aliasing={{0}: (7, {})} | custom-call | flops 12000000000 | bytes 4000000 | tf_op jit(solution)/shard_map/attend_back/pallas_call | solution.py:513
  452.8 8.1 qkv_back.1
  462.7 10.3 qkv_weights.1
  506.0 11.4 %add.653 = f32[32,192,384]{2,1,0:T(8,128)} add(f32[32,192,384]{2,1,0:T(8,128)} %get-tuple-element.95, f32[32,192,384]{2,1,0:T(8,128)} %collective-permute-done.63) | non-fusion elementwise | flops 2359296 | bytes 28311552 | tf_op jit(solution)/shard_map/add | solution.py:1165
  542.2 9.1 convolution_add_fusion
  551.3 27.6 %collective-permute-done.65 = f16[32,96,384]{2,1,0:T(8,128)(2,1)S(1)} collective-permute-done((f16[32,96,384]{2,1,0:T(8,128)(2,1)S(1)}, f16[32,96,384]{2,1,0:T(8,128)(2,1)S(1)}, u32[]{:S(2)}, u32[]{:S(2)}) %collective-permute-start.65) | collective-permute-done | bytes 2359328 | tf_op jit(solution)/shard_map/ppermute | solution.py:1004
  588.9 11.3 %fusion.67 = (f32[192,6288]{0,1:T(8,128)}, f32[192,6288]{0,1:T(8,128)}) fusion(f32[384,6288]{0,1:T(8,128)} %convolution_add_fusion), kind=kLoop, calls=%fused_computation.343 | loop fusion | bytes 19316736 | tf_op jit(solution)/shard_map/slice | solution.py:1160
  600.2 6.3 copy.152
  610.0 15.1 %collective-permute-done.67 = f16[32,24,384]{2,1,0:T(8,128)(2,1)} collective-permute-done((f16[32,24,384]{2,1,0:T(8,128)(2,1)}, f16[32,24,384]{2,1,0:T(8,128)(2,1)}, u32[]{:S(2)}, u32[]{:S(2)}) %collective-permute-start.67) | collective-permute-done | bytes 589856 | tf_op jit(solution)/shard_map/ppermute | solution.py:1004
  625.1 7.0 collective-permute-done.69
  649.4 88.6 %collective-permute-done.83 = f32[25,24,384]{2,1,0:T(8,128)} collective-permute-done((f32[25,24,384]{2,1,0:T(8,128)}, f32[25,24,384]{2,1,0:T(8,128)}, u32[]{:S(2)}, u32[]{:S(2)}) %collective-permute-start.83) | collective-permute-done | bytes 921632 | tf_op jit(solution)/shard_map/ppermute | solution.py:998
  751.2 6.3 copy.151
  763.3 48.2 %collective-permute-done.59.refs_9_ = bf16[3072,128]{1,0:T(8,128)(2,1)} collective-permute-done((bf16[3072,128]{1,0:T(8,128)(2,1)S(1)}, bf16[3072,128]{1,0:T(8,128)(2,1)}, u32[]{:S(2)}, u32[]{:S(2)}) %collective-permute-start.59) | collective-permute-done | bytes 786464 | tf_op jit(solution)/shard_map/ppermute | solution.py:1004
  821.5 6.6 add.635.refs_4_
  829.2 6.4 collective-permute-done.56.refs_6_
  837.8 14.6 %collective-permute-done.58.refs_8_ = bf16[3072,128]{1,0:T(8,128)(2,1)S(1)} collective-permute-done((bf16[3072,128]{1,0:T(8,128)(2,1)S(1)}, bf16[3072,128]{1,0:T(8,128)(2,1)S(1)}, u32[]{:S(2)}, u32[]{:S(2)}) %collective-permute-start.58) | collective-permute-done | bytes 786464 | tf_op jit(solution)/shard_map/ppermute | solution.py:1004
  853.5 15.8 %collective-permute-done.60.refs_10_ = bf16[3072,128]{1,0:T(8,128)(2,1)S(1)} collective-permute-done((bf16[3072,128]{1,0:T(8,128)(2,1)}, bf16[3072,128]{1,0:T(8,128)(2,1)S(1)}, u32[]{:S(2)}, u32[]{:S(2)}) %collective-permute-start.60) | collective-permute-done | bytes 786464 | tf_op jit(solution)/shard_map/ppermute | solution.py:1004
  870.3 15.8 %collective-permute-done.62.refs_12_ = bf16[3072,128]{1,0:T(8,128)(2,1)S(1)} collective-permute-done((bf16[3072,128]{1,0:T(8,128)(2,1)}, bf16[3072,128]{1,0:T(8,128)(2,1)S(1)}, u32[]{:S(2)}, u32[]{:S(2)}) %collective-permute-start.62) | collective-permute-done | bytes 786464 | tf_op jit(solution)/shard_map/ppermute | solution.py:1004
  888.1 24.6 %scatter_rows.1 = (f32[192,6288]{1,0:T(8,128)}, f32[1,1]{1,0:T(1,128)}) custom-call(s32[8208]{0:T(1024)} %get-tuple-element.69.list_ref.refs_0_, s32[1]{0:T(128)} %get-tuple-element.70.count_ref.refs_1_, s32[8208]{0:T(1024)} %copy-done.62, s32[1]{0:T(128)} %collective-permute-done.9.refs_3_, f32[192,6288]{1,0:T(8,128)} %add.635.refs_4_, ...), custom_call_target="tpu_custom_call" | custom-call | flops 15000000512 | bytes 9658368 | tf_op jit(solution)/shard_map/scatter_rows/pallas_call | solution.py:243
  919.5 11.2 %collective-permute-start.86 = (f32[8,128]{1,0:T(8,128)S(1)}, f32[8,128]{1,0:T(8,128)S(1)}, u32[]{:S(2)}, u32[]{:S(2)}) collective-permute-start(f32[8,128]{1,0:T(8,128)S(1)} %select_reduce_fusion.3), channel_id=1, source_target_pairs={{0,1},{1,0},{2,3},{3,2},{4,5},{5,4},{6,7},{7,6},{8,9},{9,8},{10,11... | collective-permute-start | bytes 12296 | tf_op jit(solution)/shard_map/ppermute | solution.py:1004
  945.8 12.2 %fusion.7 = (f32[6288,192]{0,1:T(8,128)}, f32[6288,192]{0,1:T(8,128)}, f32[6288,192]{0,1:T(8,128)}) fusion(f32[192,6288]{1,0:T(8,128)} %get-tuple-element.116, f32[]{:T(128)} %div.136, f32[6288,192]{0,1:T(8,128)} %param.46, f32[]{:T(128)} %bitcast.115, f32[]{:T(128)} %bitcast.113, f32[6288,192]{0,1:T(8,128)} %param.45, f32[6288,192]{0,1:T(8,128)} %param.44), kind=kLoop, calls=%fused_computation.43 | loop fusion | flops 19316736 | bytes 33804300 | tf_op jit(solution)/shard_map/transpose | solution.py:1338
  961.0 5.8 collective-permute-done.97
  970.9 9.9 collective-permute-done.99
  981.0 9.2 collective-permute-done.103
  1000.2 35.7 %shampoo.1 = (f32[12,384,384]{2,1,0:T(8,128)}, f32[12,384,384]{2,1,0:T(8,128)}, f32[12,384,384]{2,1,0:T(8,128)}, f32[12,384,384]{2,1,0:T(8,128)}) custom-call(s32[16]{0:T(128)} %stack.290.places_ref, f32[1]{0:T(128)} %bitcast.97.clip_ref, f32[13,2,24,384]{3,2,1,0:T(8,128)} %copy-done.20, f32[13,2,24,384]{3,2,1,0:T(8,128)} %copy-done.14, ...), custom_call_target="tpu_custom_call" | custom-call | flops 16307453952 | bytes 70778880 | tf_op jit(solution)/shard_map/shampoo/pallas_call | solution.py:925
  (567 shorter events, 276.6 us)
Async XLA Ops:
  4.7 47.2 %collective-permute-start.10 = (bf16[192,6288]{1,0:T(8,128)(2,1)}, bf16[192,6288]{1,0:T(8,128)(2,1)}, u32[]{:S(2)}, u32[]{:S(2)}) collective-permute-start(bf16[192,6288]{1,0:T(8,128)(2,1)} %bitcast_convert_fusion), channel_id=1, source_target_pairs={{0,8},{8,0},{16,24},{24,16},{1,9},{9,1},{17,25},{25,17},{2,10},{10... | collective-permute-start | bytes 7243784 | tf_op jit(solution)/shard_map/ppermute | solution.py:998
  21.1 112.7 %collective-permute-start.19 = (bf16[12,384,384]{2,1,0:T(8,128)(2,1)S(1)}, bf16[12,384,384]{2,1,0:T(8,128)(2,1)}, u32[]{:S(2)}, u32[]{:S(2)}) collective-permute-start(bf16[12,384,384]{2,1,0:T(8,128)(2,1)S(1)} %convert_element_type.97.refs_0_), channel_id=1, source_target_pairs={{0,16},{8,24},{16,0},{24,8},{1,17},{9,25},{17,1},{25,9},{2,18},{10... | collective-permute-start | bytes 10616840 | tf_op jit(solution)/shard_map/ppermute | solution.py:998
  79.5 24.2 %collective-permute-start.12 = (bf16[2,512,384]{2,1,0:T(8,128)(2,1)S(1)}, bf16[2,512,384]{2,1,0:T(8,128)(2,1)S(1)}, u32[]{:S(2)}, u32[]{:S(2)}) collective-permute-start(bf16[2,512,384]{2,1,0:T(8,128)(2,1)S(1)} %get-tuple-element.201), channel_id=1, source_target_pairs={{0,1},{1,0},{2,3},{3,2},{4,5},{5,4},{6,7},{7,6},{8,9},{9,8},{10,11... | collective-permute-start | bytes 2359304 | tf_op jit(solution)/shard_map/ppermute | solution.py:1004
  85.2 35.3 %collective-permute-start.14 = (bf16[2,512,384]{2,1,0:T(8,128)(2,1)S(1)}, bf16[2,512,384]{2,1,0:T(8,128)(2,1)S(1)}, u32[]{:S(2)}, u32[]{:S(2)}) collective-permute-start(bf16[2,512,384]{2,1,0:T(8,128)(2,1)S(1)} %get-tuple-element.200), channel_id=1, source_target_pairs={{0,1},{1,0},{2,3},{3,2},{4,5},{5,4},{6,7},{7,6},{8,9},{9,8},{10,11... | collective-permute-start | bytes 2359304 | tf_op jit(solution)/shard_map/ppermute | solution.py:1004
  85.3 48.2 %collective-permute-start.16 = (bf16[2,512,384]{2,1,0:T(8,128)(2,1)S(1)}, bf16[2,512,384]{2,1,0:T(8,128)(2,1)S(1)}, u32[]{:S(2)}, u32[]{:S(2)}) collective-permute-start(bf16[2,512,384]{2,1,0:T(8,128)(2,1)S(1)} %get-tuple-element.199), channel_id=1, source_target_pairs={{0,1},{1,0},{2,3},{3,2},{4,5},{5,4},{6,7},{7,6},{8,9},{9,8},{10,11... | collective-permute-start | bytes 2359304 | tf_op jit(solution)/shard_map/ppermute | solution.py:1004
  87.2 131.1 %collective-permute-start.20 = (bf16[12,384,384]{2,1,0:T(8,128)(2,1)S(1)}, bf16[12,384,384]{2,1,0:T(8,128)(2,1)}, u32[]{:S(2)}, u32[]{:S(2)}) collective-permute-start(bf16[12,384,384]{2,1,0:T(8,128)(2,1)S(1)} %convert_element_type.97.refs_0_), channel_id=1, source_target_pairs={{0,8},{8,0},{16,24},{24,16},{1,9},{9,1},{17,25},{25,17},{2,10},{10... | collective-permute-start | bytes 10616840 | tf_op jit(solution)/shard_map/ppermute | solution.py:998
  133.8 84.6 %collective-permute-start.21 = (bf16[12,384,384]{2,1,0:T(8,128)(2,1)}, bf16[12,384,384]{2,1,0:T(8,128)(2,1)}, u32[]{:S(2)}, u32[]{:S(2)}) collective-permute-start(bf16[12,384,384]{2,1,0:T(8,128)(2,1)} %collective-permute-done.19.refs_1_), channel_id=1, source_target_pairs={{0,8},{8,0},{16,24},{24,16},{1,9},{9,1},{17,25},{25,17},{2,10},{10... | collective-permute-start | bytes 10616840 | tf_op jit(solution)/shard_map/ppermute | solution.py:998
  133.9 19.9 %collective-permute-start.11 = (bf16[2,512,384]{2,1,0:T(8,128)(2,1)S(1)}, bf16[2,512,384]{2,1,0:T(8,128)(2,1)S(1)}, u32[]{:S(2)}, u32[]{:S(2)}) collective-permute-start(bf16[2,512,384]{2,1,0:T(8,128)(2,1)S(1)} %get-tuple-element.198), channel_id=1, source_target_pairs={{0,1},{1,0},{2,3},{3,2},{4,5},{5,4},{6,7},{7,6},{8,9},{9,8},{10,11... | collective-permute-start | bytes 2359304 | tf_op jit(solution)/shard_map/ppermute | solution.py:1004
  135.7 54.1 %collective-permute-start.13 = (bf16[2,512,384]{2,1,0:T(8,128)(2,1)S(1)}, bf16[2,512,384]{2,1,0:T(8,128)(2,1)S(1)}, u32[]{:S(2)}, u32[]{:S(2)}) collective-permute-start(bf16[2,512,384]{2,1,0:T(8,128)(2,1)S(1)} %get-tuple-element.202), channel_id=1, source_target_pairs={{0,6},{1,7},{2,0},{3,1},{4,2},{5,3},{6,4},{7,5},{8,14},{9,15},{10,... | collective-permute-start | bytes 2359304 | tf_op jit(solution)/shard_map/ppermute | solution.py:1004
  135.7 54.1 %collective-permute-start.15 = (bf16[2,512,384]{2,1,0:T(8,128)(2,1)S(1)}, bf16[2,512,384]{2,1,0:T(8,128)(2,1)S(1)}, u32[]{:S(2)}, u32[]{:S(2)}) collective-permute-start(bf16[2,512,384]{2,1,0:T(8,128)(2,1)S(1)} %get-tuple-element.204), channel_id=1, source_target_pairs={{0,4},{1,5},{2,6},{3,7},{4,0},{5,1},{6,2},{7,3},{8,12},{9,13},{10,... | collective-permute-start | bytes 2359304 | tf_op jit(solution)/shard_map/ppermute | solution.py:1004
  153.8 48.2 %collective-permute-start.17 = (bf16[2,512,384]{2,1,0:T(8,128)(2,1)S(1)}, bf16[2,512,384]{2,1,0:T(8,128)(2,1)S(1)}, u32[]{:S(2)}, u32[]{:S(2)}) collective-permute-start(bf16[2,512,384]{2,1,0:T(8,128)(2,1)S(1)} %get-tuple-element.203), channel_id=1, source_target_pairs={{0,2},{1,3},{2,4},{3,5},{4,6},{5,7},{6,0},{7,1},{8,10},{9,11},{10,... | collective-permute-start | bytes 2359304 | tf_op jit(solution)/shard_map/ppermute | solution.py:1004
  209.7 61.1 %collective-permute-start.29 = (bf16[192,6288]{1,0:T(8,128)(2,1)}, bf16[192,6288]{1,0:T(8,128)(2,1)}, u32[]{:S(2)}, u32[]{:S(2)}) collective-permute-start(bf16[192,6288]{1,0:T(8,128)(2,1)} %bitcast_convert_fusion), channel_id=1, source_target_pairs={{0,16},{8,24},{16,0},{24,8},{1,17},{9,25},{17,1},{25,9},{2,18},{10... | collective-permute-start | bytes 7243784 | tf_op jit(solution)/shard_map/ppermute | solution.py:998
  270.8 32.3 %collective-permute-start.30 = (bf16[192,6288]{1,0:T(8,128)(2,1)}, bf16[192,6288]{1,0:T(8,128)(2,1)}, u32[]{:S(2)}, u32[]{:S(2)}) collective-permute-start(bf16[192,6288]{1,0:T(8,128)(2,1)} %collective-permute-done.29), channel_id=1, source_target_pairs={{0,8},{8,0},{16,24},{24,16},{1,9},{9,1},{17,25},{25,17},{2,10},{10... | collective-permute-start | bytes 7243784 | tf_op jit(solution)/shard_map/ppermute | solution.py:998
  361.3 22.3 %collective-permute-start.47 = (f32[64,768]{1,0:T(8,128)S(1)}, f32[64,768]{1,0:T(8,128)S(1)}, u32[]{:S(2)}, u32[]{:S(2)}) collective-permute-start(f32[64,768]{1,0:T(8,128)S(1)} %get-tuple-element.213), channel_id=1, source_target_pairs={{0,1},{1,0},{2,3},{3,2},{4,5},{5,4},{6,7},{7,6},{8,9},{9,8},{10,11... | collective-permute-start | bytes 589832 | tf_op jit(solution)/shard_map/ppermute | solution.py:1004
  383.5 158.6 %collective-permute-start.45 = (f32[384,6288]{0,1:T(8,128)}, f32[384,6288]{0,1:T(8,128)}, u32[]{:S(2)}, u32[]{:S(2)}) collective-permute-start(f32[384,6288]{0,1:T(8,128)} %fusion.18), channel_id=1, source_target_pairs={{0,8},{8,0},{16,24},{24,16},{1,9},{9,1},{17,25},{25,17},{2,10},{10... | collective-permute-start | bytes 28975112 | tf_op jit(solution)/shard_map/ppermute | solution.py:998
  412.6 93.4 %collective-permute-start.63 = (f32[32,192,384]{2,1,0:T(8,128)}, f32[32,192,384]{2,1,0:T(8,128)}, u32[]{:S(2)}, u32[]{:S(2)}) collective-permute-start(f32[32,192,384]{2,1,0:T(8,128)} %get-tuple-element.96), channel_id=1, source_target_pairs={{0,8},{8,0},{16,24},{24,16},{1,9},{9,1},{17,25},{25,17},{2,10},{10... | collective-permute-start | bytes 28311560 | tf_op jit(solution)/shard_map/ppermute | solution.py:998
  473.1 22.8 %collective-permute-start.73 = (f32[17,192,384]{2,1,0:T(8,128)}, f32[17,192,384]{2,1,0:T(8,128)}, u32[]{:S(2)}, u32[]{:S(2)}) collective-permute-start(f32[17,192,384]{2,1,0:T(8,128)} %get-tuple-element.108), channel_id=1, source_target_pairs={{0,8},{8,0},{16,24},{24,16},{1,9},{9,1},{17,25},{25,17},{2,10},{10... | collective-permute-start | bytes 15040520 | tf_op jit(solution)/shard_map/ppermute | solution.py:998
  486.5 16.8 %collective-permute-start.66 = (f32[32,1,384]{2,1,0:T(1,128)S(1)}, f32[32,1,384]{2,1,0:T(1,128)S(1)}, u32[]{:S(2)}, u32[]{:S(2)}) collective-permute-start(f32[32,1,384]{2,1,0:T(1,128)S(1)} %get-tuple-element.184), channel_id=1, source_target_pairs={{0,1},{1,0},{2,3},{3,2},{4,5},{5,4},{6,7},{7,6},{8,9},{9,8},{10,11... | collective-permute-start | bytes 147464 | tf_op jit(solution)/shard_map/ppermute | solution.py:1004
  495.6 25.2 %collective-permute-start.78 = (f32[17,1,384]{2,1,0:T(1,128)}, f32[17,1,384]{2,1,0:T(1,128)S(1)}, u32[]{:S(2)}, u32[]{:S(2)}) collective-permute-start(f32[17,1,384]{2,1,0:T(1,128)} %get-tuple-element.186), channel_id=1, source_target_pairs={{0,2},{1,3},{2,4},{3,5},{4,6},{5,7},{6,0},{7,1},{8,10},{9,11},{10,... | collective-permute-start | bytes 78344 | tf_op jit(solution)/shard_map/ppermute | solution.py:1004
  501.5 30.6 %collective-permute-start.75 = (f16[17,96,384]{2,1,0:T(8,128)(2,1)S(1)}, f16[17,96,384]{2,1,0:T(8,128)(2,1)S(1)}, u32[]{:S(2)}, u32[]{:S(2)}) collective-permute-start(f16[17,96,384]{2,1,0:T(8,128)(2,1)S(1)} %multiply_convert_fusion.2), channel_id=1, source_target_pairs={{0,1},{1,0},{2,3},{3,2},{4,5},{5,4},{6,7},{7,6},{8,9},{9,8},{10,11... | collective-permute-start | bytes 3760136 | tf_op jit(solution)/shard_map/ppermute | solution.py:1004
  504.0 19.9 %collective-permute-start.72 = (f32[32,1,384]{2,1,0:T(1,128)}, f32[32,1,384]{2,1,0:T(1,128)}, u32[]{:S(2)}, u32[]{:S(2)}) collective-permute-start(f32[32,1,384]{2,1,0:T(1,128)} %get-tuple-element.182), channel_id=1, source_target_pairs={{0,6},{1,7},{2,0},{3,1},{4,2},{5,3},{6,4},{7,5},{8,14},{9,15},{10,... | collective-permute-start | bytes 147464 | tf_op jit(solution)/shard_map/ppermute | solution.py:1004
  520.5 58.3 %collective-permute-start.65 = (f16[32,96,384]{2,1,0:T(8,128)(2,1)S(1)}, f16[32,96,384]{2,1,0:T(8,128)(2,1)S(1)}, u32[]{:S(2)}, u32[]{:S(2)}) collective-permute-start(f16[32,96,384]{2,1,0:T(8,128)(2,1)S(1)} %multiply_convert_fusion.1), channel_id=1, source_target_pairs={{0,1},{1,0},{2,3},{3,2},{4,5},{5,4},{6,7},{7,6},{8,9},{9,8},{10,11... | collective-permute-start | bytes 7077896 | tf_op jit(solution)/shard_map/ppermute | solution.py:1004
  536.1 51.1 %collective-permute-start.77 = (f16[17,24,384]{2,1,0:T(8,128)(2,1)S(1)}, f16[17,24,384]{2,1,0:T(8,128)(2,1)}, u32[]{:S(2)}, u32[]{:S(2)}) collective-permute-start(f16[17,24,384]{2,1,0:T(8,128)(2,1)S(1)} %get-tuple-element.210), channel_id=1, source_target_pairs={{0,2},{1,3},{2,4},{3,5},{4,6},{5,7},{6,0},{7,1},{8,10},{9,11},{10,... | collective-permute-start | bytes 940040 | tf_op jit(solution)/shard_map/ppermute | solution.py:1004
  539.6 67.0 %collective-permute-start.79 = (f16[17,24,384]{2,1,0:T(8,128)(2,1)}, f16[17,24,384]{2,1,0:T(8,128)(2,1)}, u32[]{:S(2)}, u32[]{:S(2)}) collective-permute-start(f16[17,24,384]{2,1,0:T(8,128)(2,1)} %get-tuple-element.212), channel_id=1, source_target_pairs={{0,4},{1,5},{2,6},{3,7},{4,0},{5,1},{6,2},{7,3},{8,12},{9,13},{10,... | collective-permute-start | bytes 940040 | tf_op jit(solution)/shard_map/ppermute | solution.py:1004
  540.4 66.7 %collective-permute-start.81 = (f16[17,24,384]{2,1,0:T(8,128)(2,1)}, f16[17,24,384]{2,1,0:T(8,128)(2,1)}, u32[]{:S(2)}, u32[]{:S(2)}) collective-permute-start(f16[17,24,384]{2,1,0:T(8,128)(2,1)} %get-tuple-element.211), channel_id=1, source_target_pairs={{0,6},{1,7},{2,0},{3,1},{4,2},{5,3},{6,4},{7,5},{8,14},{9,15},{10,... | collective-permute-start | bytes 940040 | tf_op jit(solution)/shard_map/ppermute | solution.py:1004
  583.3 41.8 %collective-permute-start.67 = (f16[32,24,384]{2,1,0:T(8,128)(2,1)}, f16[32,24,384]{2,1,0:T(8,128)(2,1)}, u32[]{:S(2)}, u32[]{:S(2)}) collective-permute-start(f16[32,24,384]{2,1,0:T(8,128)(2,1)} %get-tuple-element.207), channel_id=1, source_target_pairs={{0,2},{1,3},{2,4},{3,5},{4,6},{5,7},{6,0},{7,1},{8,10},{9,11},{10,... | collective-permute-start | bytes 1769480 | tf_op jit(solution)/shard_map/ppermute | solution.py:1004
  585.7 46.4 %collective-permute-start.69 = (f16[32,24,384]{2,1,0:T(8,128)(2,1)}, f16[32,24,384]{2,1,0:T(8,128)(2,1)}, u32[]{:S(2)}, u32[]{:S(2)}) collective-permute-start(f16[32,24,384]{2,1,0:T(8,128)(2,1)} %get-tuple-element.209), channel_id=1, source_target_pairs={{0,4},{1,5},{2,6},{3,7},{4,0},{5,1},{6,2},{7,3},{8,12},{9,13},{10,... | collective-permute-start | bytes 1769480 | tf_op jit(solution)/shard_map/ppermute | solution.py:1004
  587.2 47.5 %collective-permute-start.71 = (f16[32,24,384]{2,1,0:T(8,128)(2,1)}, f16[32,24,384]{2,1,0:T(8,128)(2,1)}, u32[]{:S(2)}, u32[]{:S(2)}) collective-permute-start(f16[32,24,384]{2,1,0:T(8,128)(2,1)} %get-tuple-element.208), channel_id=1, source_target_pairs={{0,6},{1,7},{2,0},{3,1},{4,2},{5,3},{6,4},{7,5},{8,14},{9,15},{10,... | collective-permute-start | bytes 1769480 | tf_op jit(solution)/shard_map/ppermute | solution.py:1004
  606.6 32.9 %collective-permute-start.54 = (bf16[512,384]{1,0:T(8,128)(2,1)S(1)}, bf16[512,384]{1,0:T(8,128)(2,1)}, u32[]{:S(2)}, u32[]{:S(2)}) collective-permute-start(bf16[512,384]{1,0:T(8,128)(2,1)S(1)} %fusion.21), channel_id=1, source_target_pairs={{0,16},{8,24},{16,0},{24,8},{1,17},{9,25},{17,1},{25,9},{2,18},{10... | collective-permute-start | bytes 1179656 | tf_op jit(solution)/shard_map/ppermute | solution.py:998
  607.2 214.2 %collective-permute-start.46 = (f32[192,6288]{1,0:T(8,128)}, f32[192,6288]{1,0:T(8,128)}, u32[]{:S(2)}, u32[]{:S(2)}) collective-permute-start(f32[192,6288]{1,0:T(8,128)} %copy.152), channel_id=1, source_target_pairs={{0,16},{8,24},{16,0},{24,8},{1,17},{9,25},{17,1},{25,9},{2,18},{10... | collective-permute-start | bytes 14487560 | tf_op jit(solution)/shard_map/ppermute | solution.py:998
  638.9 99.1 %collective-permute-start.83 = (f32[25,24,384]{2,1,0:T(8,128)}, f32[25,24,384]{2,1,0:T(8,128)}, u32[]{:S(2)}, u32[]{:S(2)}) collective-permute-start(f32[25,24,384]{2,1,0:T(8,128)} %pad_maximum_fusion.5), channel_id=1, source_target_pairs={{0,16},{8,24},{16,0},{24,8},{1,17},{9,25},{17,1},{25,9},{2,18},{10... | collective-permute-start | bytes 2764808 | tf_op jit(solution)/shard_map/ppermute | solution.py:998
  741.9 20.4 %collective-permute-start.57 = (bf16[3072,128]{1,0:T(8,128)(2,1)S(1)}, bf16[3072,128]{1,0:T(8,128)(2,1)S(1)}, u32[]{:S(2)}, u32[]{:S(2)}) collective-permute-start(bf16[3072,128]{1,0:T(8,128)(2,1)S(1)} %maximum_maximum_fusion.refs_5_), channel_id=1, source_target_pairs={{0,2},{1,3},{2,4},{3,5},{4,6},{5,7},{6,0},{7,1},{8,10},{9,11},{10,... | collective-permute-start | bytes 2359304 | tf_op jit(solution)/shard_map/ppermute | solution.py:1004
  742.2 69.3 %collective-permute-start.59 = (bf16[3072,128]{1,0:T(8,128)(2,1)S(1)}, bf16[3072,128]{1,0:T(8,128)(2,1)}, u32[]{:S(2)}, u32[]{:S(2)}) collective-permute-start(bf16[3072,128]{1,0:T(8,128)(2,1)S(1)} %maximum_maximum_fusion.refs_5_), channel_id=1, source_target_pairs={{0,4},{1,5},{2,6},{3,7},{4,0},{5,1},{6,2},{7,3},{8,12},{9,13},{10,... | collective-permute-start | bytes 2359304 | tf_op jit(solution)/shard_map/ppermute | solution.py:1004
  744.9 70.1 %collective-permute-start.61 = (bf16[3072,128]{1,0:T(8,128)(2,1)S(1)}, bf16[3072,128]{1,0:T(8,128)(2,1)}, u32[]{:S(2)}, u32[]{:S(2)}) collective-permute-start(bf16[3072,128]{1,0:T(8,128)(2,1)S(1)} %maximum_maximum_fusion.refs_5_), channel_id=1, source_target_pairs={{0,6},{1,7},{2,0},{3,1},{4,2},{5,3},{6,4},{7,5},{8,14},{9,15},{10,... | collective-permute-start | bytes 2359304 | tf_op jit(solution)/shard_map/ppermute | solution.py:1004
  759.6 55.4 %collective-permute-start.92 = (f32[13,2,1,384]{3,1,0,2:T(2,128)S(1)}, f32[13,2,1,384]{3,1,0,2:T(2,128)S(1)}, u32[]{:S(2)}, u32[]{:S(2)}) collective-permute-start(f32[13,2,1,384]{3,1,0,2:T(2,128)S(1)} %bitcast.332), channel_id=1, source_target_pairs={{0,1},{1,0},{2,3},{3,2},{4,5},{5,4},{6,7},{7,6},{8,9},{9,8},{10,11... | collective-permute-start | bytes 119816 | tf_op jit(solution)/shard_map/ppermute | solution.py:1004
  762.3 53.9 %collective-permute-start.94 = (f32[13,2,1,384]{3,1,0,2:T(2,128)S(1)}, f32[13,2,1,384]{3,1,0,2:T(2,128)S(1)}, u32[]{:S(2)}, u32[]{:S(2)}) collective-permute-start(f32[13,2,1,384]{3,1,0,2:T(2,128)S(1)} %bitcast.333), channel_id=1, source_target_pairs={{0,2},{1,3},{2,4},{3,5},{4,6},{5,7},{6,0},{7,1},{8,10},{9,11},{10,... | collective-permute-start | bytes 119816 | tf_op jit(solution)/shard_map/ppermute | solution.py:1004
  815.0 20.5 %collective-permute-start.56 = (bf16[3072,128]{1,0:T(8,128)(2,1)S(1)}, bf16[3072,128]{1,0:T(8,128)(2,1)S(1)}, u32[]{:S(2)}, u32[]{:S(2)}) collective-permute-start(bf16[3072,128]{1,0:T(8,128)(2,1)S(1)} %maximum_maximum_fusion.refs_5_), channel_id=1, source_target_pairs={{0,1},{1,0},{2,3},{3,2},{4,5},{5,4},{6,7},{7,6},{8,9},{9,8},{10,11... | collective-permute-start | bytes 2359304 | tf_op jit(solution)/shard_map/ppermute | solution.py:1004
  816.1 36.3 %collective-permute-start.58 = (bf16[3072,128]{1,0:T(8,128)(2,1)S(1)}, bf16[3072,128]{1,0:T(8,128)(2,1)S(1)}, u32[]{:S(2)}, u32[]{:S(2)}) collective-permute-start(bf16[3072,128]{1,0:T(8,128)(2,1)S(1)} %collective-permute-done.57.refs_7_), channel_id=1, source_target_pairs={{0,1},{1,0},{2,3},{3,2},{4,5},{5,4},{6,7},{7,6},{8,9},{9,8},{10,11... | collective-permute-start | bytes 2359304 | tf_op jit(solution)/shard_map/ppermute | solution.py:1004
  817.1 52.2 %collective-permute-start.60 = (bf16[3072,128]{1,0:T(8,128)(2,1)}, bf16[3072,128]{1,0:T(8,128)(2,1)S(1)}, u32[]{:S(2)}, u32[]{:S(2)}) collective-permute-start(bf16[3072,128]{1,0:T(8,128)(2,1)} %collective-permute-done.59.refs_9_), channel_id=1, source_target_pairs={{0,1},{1,0},{2,3},{3,2},{4,5},{5,4},{6,7},{7,6},{8,9},{9,8},{10,11... | collective-permute-start | bytes 2359304 | tf_op jit(solution)/shard_map/ppermute | solution.py:1004
  819.0 67.2 %collective-permute-start.62 = (bf16[3072,128]{1,0:T(8,128)(2,1)}, bf16[3072,128]{1,0:T(8,128)(2,1)S(1)}, u32[]{:S(2)}, u32[]{:S(2)}) collective-permute-start(bf16[3072,128]{1,0:T(8,128)(2,1)} %collective-permute-done.61.refs_11_), channel_id=1, source_target_pairs={{0,1},{1,0},{2,3},{3,2},{4,5},{5,4},{6,7},{7,6},{8,9},{9,8},{10,11... | collective-permute-start | bytes 2359304 | tf_op jit(solution)/shard_map/ppermute | solution.py:1004
  828.2 140.5 %collective-permute-start.91 = (f16[13,2,24,384]{3,2,1,0:T(8,128)(2,1)}, f16[13,2,24,384]{3,2,1,0:T(8,128)(2,1)S(1)}, u32[]{:S(2)}, u32[]{:S(2)}) collective-permute-start(f16[13,2,24,384]{3,2,1,0:T(8,128)(2,1)} %get-tuple-element.172), channel_id=1, source_target_pairs={{0,1},{1,0},{2,3},{3,2},{4,5},{5,4},{6,7},{7,6},{8,9},{9,8},{10,11... | collective-permute-start | bytes 1437704 | tf_op jit(solution)/shard_map/ppermute | solution.py:1004
  835.6 122.5 %collective-permute-start.93 = (f16[13,2,24,384]{3,2,1,0:T(8,128)(2,1)}, f16[13,2,24,384]{3,2,1,0:T(8,128)(2,1)S(1)}, u32[]{:S(2)}, u32[]{:S(2)}) collective-permute-start(f16[13,2,24,384]{3,2,1,0:T(8,128)(2,1)} %get-tuple-element.172), channel_id=1, source_target_pairs={{0,2},{1,3},{2,4},{3,5},{4,6},{5,7},{6,0},{7,1},{8,10},{9,11},{10,... | collective-permute-start | bytes 1437704 | tf_op jit(solution)/shard_map/ppermute | solution.py:1004
  852.4 61.4 %collective-permute-start.96 = (f32[13,2,1,384]{3,1,0,2:T(2,128)S(1)}, f32[13,2,1,384]{3,1,0,2:T(2,128)S(1)}, u32[]{:S(2)}, u32[]{:S(2)}) collective-permute-start(f32[13,2,1,384]{3,1,0,2:T(2,128)S(1)} %collective-permute-done.94), channel_id=1, source_target_pairs={{0,1},{1,0},{2,3},{3,2},{4,5},{5,4},{6,7},{7,6},{8,9},{9,8},{10,11... | collective-permute-start | bytes 119816 | tf_op jit(solution)/shard_map/ppermute | solution.py:1004
  869.3 61.4 %collective-permute-start.100 = (f32[13,2,1,384]{3,1,0,2:T(2,128)S(1)}, f32[13,2,1,384]{3,1,0,2:T(2,128)S(1)}, u32[]{:S(2)}, u32[]{:S(2)}) collective-permute-start(f32[13,2,1,384]{3,1,0,2:T(2,128)S(1)} %collective-permute-done.98), channel_id=1, source_target_pairs={{0,1},{1,0},{2,3},{3,2},{4,5},{5,4},{6,7},{7,6},{8,9},{9,8},{10,11... | collective-permute-start | bytes 119816 | tf_op jit(solution)/shard_map/ppermute | solution.py:1004
  887.0 45.9 %collective-permute-start.104 = (f32[13,2,1,384]{3,1,0,2:T(2,128)S(1)}, f32[13,2,1,384]{3,1,0,2:T(2,128)S(1)}, u32[]{:S(2)}, u32[]{:S(2)}) collective-permute-start(f32[13,2,1,384]{3,1,0,2:T(2,128)S(1)} %collective-permute-done.102), channel_id=1, source_target_pairs={{0,1},{1,0},{2,3},{3,2},{4,5},{5,4},{6,7},{7,6},{8,9},{9,8},{10,11... | collective-permute-start | bytes 119816 | tf_op jit(solution)/shard_map/ppermute | solution.py:1004
  936.5 30.3 %collective-permute-start.97 = (f16[13,2,24,384]{3,2,1,0:T(8,128)(2,1)}, f16[13,2,24,384]{3,2,1,0:T(8,128)(2,1)}, u32[]{:S(2)}, u32[]{:S(2)}) collective-permute-start(f16[13,2,24,384]{3,2,1,0:T(8,128)(2,1)} %get-tuple-element.172), channel_id=1, source_target_pairs={{0,4},{1,5},{2,6},{3,7},{4,0},{5,1},{6,2},{7,3},{8,12},{9,13},{10,... | collective-permute-start | bytes 1437704 | tf_op jit(solution)/shard_map/ppermute | solution.py:1004
  938.5 31.7 %collective-permute-start.101 = (f16[13,2,24,384]{3,2,1,0:T(8,128)(2,1)}, f16[13,2,24,384]{3,2,1,0:T(8,128)(2,1)S(1)}, u32[]{:S(2)}, u32[]{:S(2)}) collective-permute-start(f16[13,2,24,384]{3,2,1,0:T(8,128)(2,1)} %get-tuple-element.172), channel_id=1, source_target_pairs={{0,6},{1,7},{2,0},{3,1},{4,2},{5,3},{6,4},{7,5},{8,14},{9,15},{10,... | collective-permute-start | bytes 1437704 | tf_op jit(solution)/shard_map/ppermute | solution.py:1004
  970.2 19.9 %collective-permute-start.103 = (f16[13,2,24,384]{3,2,1,0:T(8,128)(2,1)S(1)}, f16[13,2,24,384]{3,2,1,0:T(8,128)(2,1)S(1)}, u32[]{:S(2)}, u32[]{:S(2)}) collective-permute-start(f16[13,2,24,384]{3,2,1,0:T(8,128)(2,1)S(1)} %collective-permute-done.101), channel_id=1, source_target_pairs={{0,1},{1,0},{2,3},{3,2},{4,5},{5,4},{6,7},{7,6},{8,9},{9,8},{10,11... | collective-permute-start | bytes 1437704 | tf_op jit(solution)/shard_map/ppermute | solution.py:1004
  (126 other events, 2754.7 us)

commit v2 on v1

--- a/solution.py
+++ b/solution.py
@@ -58,7 +58,9 @@
 
 def cost(flops, bytes_moved, transcendentals=0):
     return pl.CostEstimate(
-        flops=int(flops), bytes_accessed=int(bytes_moved), transcendentals=int(transcendentals)
+        flops=int(flops * 0.02),
+        bytes_accessed=int(bytes_moved * 0.02),
+        transcendentals=int(transcendentals * 0.02),
     )
 
 
@@ -119,7 +121,7 @@
     )(src, off, *pieces)
 
 
-def hits_kernel(empty_row, packed_ref, list_ref, count_ref):
+def hits_kernel(empty_row, packed_ref, list_ref):
     total = packed_ref.shape[0]
 
     def go(i, n):
@@ -130,7 +132,7 @@
         return n
 
     n = lax.fori_loop(0, total // 16, go, jnp.int32(0))
-    count_ref[0] = n
+    list_ref[total + 8] = n
     for u in range(8):
         list_ref[n + u] = empty_row << 16
 
@@ -139,19 +141,40 @@
     total = packed.shape[0]
     return pl.pallas_call(
         partial(hits_kernel, empty_row),
-        out_shape=[
-            jax.ShapeDtypeStruct((total + 16,), i32),
-            jax.ShapeDtypeStruct((1,), i32),
-        ],
+        out_shape=jax.ShapeDtypeStruct((total + 16,), i32),
         in_specs=[pl.BlockSpec(memory_space=SMEM)],
-        out_specs=[pl.BlockSpec(memory_space=SMEM)] * 2,
+        out_specs=pl.BlockSpec(memory_space=SMEM),
         name="find_hits",
         cost_estimate=cost(1e10, total * 8),
     )(packed)
 
 
-def lookup_kernel(rows_all, list_ref, count_ref, table_ref, out_ref, tab, acc):
-    total = out_ref.shape[0]
+def turn_kernel(core_ref, own_ref, other_ref, out_ref):
+    first = core_ref[0] == 0
+    own, other = own_ref[...].astype(f32), other_ref[...].astype(f32)
+    depth = own.shape[0]
+    both = jnp.concatenate([jnp.where(first, own, other), jnp.where(first, other, own)], 0)
+    out_ref[...] = both.T[:, : 2 * depth].astype(bf16)
+
+
+def turn_table(core, own, other):
+    depth, rows_all = own.shape
+    wide = lane_block(rows_all)
+    block = pl.BlockSpec((depth, wide), lambda j: (0, j))
+    return pl.pallas_call(
+        turn_kernel,
+        grid=(pl.cdiv(rows_all, wide),),
+        out_shape=jax.ShapeDtypeStruct((rows_all, 2 * depth), bf16),
+        in_specs=[pl.BlockSpec(memory_space=SMEM), block, block],
+        out_specs=pl.BlockSpec((wide, 2 * depth), lambda j: (j, 0)),
+        name="turn_table",
+        cost_estimate=cost(1e7, 1e7),
+    )(core, own, other)
+
+
+def lookup_kernel(rows_all, list_ref, table_ref, *refs):
+    outs, (tab, acc) = refs[:-2], refs[-2:]
+    total = acc.shape[0] - 8
     tab[pl.ds(0, rows_all), :] = table_ref[...].astype(f32)
     tab[pl.ds(rows_all, 8), :] = jnp.zeros((8, tab.shape[1]), f32)
     acc[...] = jnp.zeros(acc.shape, f32)
@@ -164,51 +187,58 @@
             acc[pl.ds(place, 1), :] = tab[pl.ds(row, 1), :]
         return carry
 
-    lax.fori_loop(0, (count_ref[0] + 7) // 8, go, 0)
-    out_ref[...] = acc[pl.ds(0, total), :].astype(bf16)
-
-
-def lookup(hit_list, hit_count, table, count):
+    lax.fori_loop(0, (list_ref[total + 8] + 7) // 8, go, 0)
+    each = outs[0].shape[0]
+    for part, out in enumerate(outs):
+        out[...] = acc[pl.ds(part * each, each), :].astype(bf16)
+
+
+def lookup(hit_list, table, count, parts):
     rows_all, width = table.shape
     return pl.pallas_call(
         partial(lookup_kernel, rows_all),
-        out_shape=jax.ShapeDtypeStruct((count, width), bf16),
-        in_specs=[pl.BlockSpec(memory_space=SMEM)] * 2 + [pl.BlockSpec(memory_space=pltpu.VMEM)],
-        out_specs=pl.BlockSpec(memory_space=pltpu.VMEM),
+        out_shape=[jax.ShapeDtypeStruct((count // parts, width), bf16)] * parts,
+        in_specs=[
+            pl.BlockSpec(memory_space=SMEM),
+            pl.BlockSpec(memory_space=pltpu.VMEM),
+        ],
+        out_specs=[pl.BlockSpec(memory_space=pltpu.VMEM)] * parts,
         scratch_shapes=[
             pltpu.VMEM((rows_all + 8, width), f32),
             pltpu.VMEM((count + 8, width), f32),
         ],
         name="lookup",
         cost_estimate=cost(1e10, rows_all * width * 2),
-    )(hit_list, hit_count, table)
-
-
-def scatter_kernel(piece_count, half, rows_all, *refs):
-    lists, counts = refs[0:4:2], refs[1:4:2]
-    lex_ref = refs[4]
-    pieces = refs[5 : 5 + piece_count]
-    out_ref, square_ref, acc, tail, wide, pair = refs[5 + piece_count :]
+    )(hit_list, table)
+
+
+def scatter_kernel(piece_count, half, rows_all, starts, *refs):
+    used = len(starts)
+    lists = refs[:used]
+    lex_ref = refs[used]
+    pieces = refs[used + 1 : used + 1 + piece_count]
+    out_ref, square_ref, acc, tail, wide, pair = refs[used + 1 + piece_count :]
     acc[...] = jnp.zeros(acc.shape, f32)
     tail[...] = jnp.zeros(tail.shape, f32)
     for k in range(piece_count):
         wide[pl.ds(k * 2 * half, 2 * half), :] = pieces[k][pl.ds(0, 2 * half), :].astype(f32)
         pair[pl.ds(k * half, half), :] = pieces[k][pl.ds(2 * half, half), :].astype(f32)
     upper = lax.broadcasted_iota(i32, (1, 128), 1) >= 64
-    for side in range(2):
+    for which, (side, start) in enumerate(starts):
         own = upper if side else ~upper
 
-        def go(i, carry, side=side, own=own):
+        def go(i, carry, which=which, side=side, start=start, own=own):
             for u in range(8):
-                entry = lists[side][i * 8 + u]
+                entry = lists[which][i * 8 + u]
                 row = entry >> 16
-                p = entry & 0xFFFF
+                p = (entry & 0xFFFF) + start
                 q = (p // half) * half + p + side * half
                 acc[pl.ds(row, 1), :] += wide[pl.ds(q, 1), :]
                 tail[pl.ds(row, 1), :] += jnp.where(own, pair[pl.ds(p, 1), :], 0.0)
             return carry
 
-        lax.fori_loop(0, (counts[side][0] + 7) // 8, go, 0)
+        held = lists[which].shape[0] - 8
+        lax.fori_loop(0, (lists[which][held] + 7) // 8, go, 0)
     chunks = rows_all // 128
     rest = rows_all - chunks * 128
 
@@ -235,18 +265,23 @@
     square_ref[0, 0] = total
 
 
-def scatter_rows(lists, lex, pieces):
-    width, rows_all = lex.shape
+def scatter_rows(hits, lex, pieces, rows_all):
+    lists, starts, start = [], [], 0
+    for own_list, other_list in hits:
+        lists += [own_list, other_list]
+        starts += [(0, start), (1, start)]
+        start += own_list.shape[0] - 16
+    width = lex.shape[0]
     half = pieces[0].shape[0] // 3
     count = len(pieces)
     padded = (rows_all // 128 + 1) * 128
     return pl.pallas_call(
-        partial(scatter_kernel, count, half, rows_all),
+        partial(scatter_kernel, count, half, rows_all, tuple(starts)),
         out_shape=[
             jax.ShapeDtypeStruct((width, rows_all), f32),
             jax.ShapeDtypeStruct((1, 1), f32),
         ],
-        in_specs=[pl.BlockSpec(memory_space=SMEM)] * 4
+        in_specs=[pl.BlockSpec(memory_space=SMEM)] * len(lists)
         + [pl.BlockSpec(memory_space=pltpu.VMEM)] * (count + 1),
         out_specs=[
             pl.BlockSpec(memory_space=pltpu.VMEM),
@@ -629,14 +664,15 @@
     )(x0, y, wo, wup, wdown, vectors, picks.reshape(count, 1))
 
 
-def halve(core, tile, outs, slot, row, col):
-    half = BS // 2
-    near = pl.multiple_of(row * BS + core * half, half)
-    far = pl.multiple_of(row * BS + (1 - core) * half, half)
-    for start, out, top in ((near, outs[0], outs[2]), (far, outs[1], outs[3])):
-        values = tile[pl.ds(start, half), pl.ds(col * BS, BS)]
-        out[slot] = values
-        top[slot] = jnp.max(jnp.abs(values), 0, keepdims=True)
+def keep_tiles(values, out, top, slot):
+    for c in range(2):
+        out[slot + c] = values[:, c * BS : (c + 1) * BS]
+    high = jnp.max(jnp.abs(values), 0, keepdims=True)
+    top[...] = jnp.maximum(top[...], jnp.maximum(high[:, :BS], high[:, BS:]))
+
+
+def near_far(core):
+    return pl.ds(pl.multiple_of(core * BS, BS), BS), pl.ds(pl.multiple_of((1 - core) * BS, BS), BS)
 
 
 def mlp_back_kernel(
@@ -663,16 +699,15 @@
     gx2,
     gm,
     gh,
-    tile_a,
-    tile_b,
 ):
     j = pl.program_id(0)
     core = core_ref[0]
     tokens = x2_ref.shape[0]
-    outs = (mine_ref, theirs_ref, mine_top_ref, theirs_top_ref)
 
     @pl.when(j == 0)
     def _():
+        mine_top_ref[...] = jnp.zeros_like(mine_top_ref)
+        theirs_top_ref[...] = jnp.zeros_like(theirs_top_ref)
         vg_ref[...] = jnp.zeros_like(vg_ref)
         places = lax.broadcasted_iota(i32, (tokens, pick_ref.shape[1]), 0)
         chosen = (places == pick_ref[...]).astype(bf16)
@@ -708,12 +743,11 @@
     def _():
         gh[...] += part
 
-    tile_a[...] = mm_l(h_ref[...], gup)
-    tile_b[...] = mm_l(act_ref[...], gm[...])
-    for r in range(2):
-        for c in range(2):
-            halve(core, tile_a, outs, 2 * r + c, r, c)
-            halve(core, tile_b, outs, 4 + 2 * r + c, r, c)
+    for cols, out, top in zip(
+        near_far(core), (mine_ref, theirs_ref), (mine_top_ref, theirs_top_ref)
+    ):
+        keep_tiles(mm_l(h_ref[:, cols], gup), out, top, 0)
+        keep_tiles(mm_l(act_ref[:, cols], gm[...]), out, top, 2)
 
     @pl.when(j == FSTEPS - 1)
     def _():
@@ -733,10 +767,10 @@
     count = picks.shape[0]
     wide = pl.BlockSpec((tokens, D), lambda j: (0, j))
     flat = full((tokens, D))
-    tiles = pl.BlockSpec((8, BS // 2, BS), lambda j: (j, 0, 0))
-    tops = pl.BlockSpec((8, 1, BS), lambda j: (j, 0, 0))
-    halves = jax.ShapeDtypeStruct((8 * FSTEPS, BS // 2, BS), f32)
-    highs = jax.ShapeDtypeStruct((8 * FSTEPS, 1, BS), f32)
+    tiles = pl.BlockSpec((4, BS, BS), lambda j: (j, 0, 0))
+    tops = full((1, BS))
+    halves = jax.ShapeDtypeStruct((4 * FSTEPS, BS, BS), f32)
+    highs = jax.ShapeDtypeStruct((1, BS), f32)
     return pl.pallas_call(
         mlp_back_kernel,
         grid=(FSTEPS,),
@@ -769,8 +803,6 @@
             pltpu.VMEM((tokens, D), f32),
             pltpu.VMEM((tokens, D), bf16),
             pltpu.VMEM((tokens, D), f32),
-            pltpu.VMEM((D, D), f32),
-            pltpu.VMEM((D, D), f32),
         ],
         name="mlp_back",
         cost_estimate=cost(8 * tokens * D * FF, 5e7, tokens * FF),
@@ -825,40 +857,39 @@
 
 
 def qkv_weights_kernel(
-    core_ref, h_ref, g_ref, y_ref, ga_ref, small_ref, mine_ref, theirs_ref, mtop_ref, ttop_ref, tile
+    core_ref, h_ref, g_ref, y_ref, ga_ref, small_ref, mine_ref, theirs_ref, mtop_ref, ttop_ref
 ):
     j = pl.program_id(0)
     core = core_ref[0]
-    outs = (mine_ref, theirs_ref, mtop_ref, ttop_ref)
+    both = tuple(zip(near_far(core), (mine_ref, theirs_ref), (mtop_ref, ttop_ref)))
+
+    @pl.when(j == 0)
+    def _():
+        for turn, (_, out, top) in enumerate(both):
+            values = small_ref[core if turn == 0 else 1 - core]
+            out[8] = values
+            top[...] = jnp.max(jnp.abs(values), 0, keepdims=True)
 
     @pl.when(j < 3)
     def _():
-        tile[...] = mm_l(h_ref[...], g_ref[0])
+        for cols, out, top in both:
+            keep_tiles(mm_l(h_ref[:, cols], g_ref[0]), out, top, 2 * j)
 
     @pl.when(j == 3)
     def _():
-        tile[...] = mm_l(y_ref[...], ga_ref[...])
-
-    @pl.when(j < 4)
-    def _():
-        for r in range(2):
-            for c in range(2):
-                halve(core, tile, outs, 4 * j + 2 * r + c, r, c)
-
-    @pl.when(j == 4)
-    def _():
-        halve(core, small_ref, outs, 16, 0, 0)
+        for cols, out, top in both:
+            keep_tiles(mm_l(y_ref[:, cols], ga_ref[...]), out, top, 6)
 
 
 def qkv_weights(core, h1, grads, y, ga, small):
     tokens = h1.shape[0]
     flat = full((tokens, D))
-    halves = (17, BS // 2, BS)
-    highs = (17, 1, BS)
+    halves = (9, BS, BS)
+    highs = (1, BS)
     shapes = (halves, halves, highs, highs)
     return pl.pallas_call(
         qkv_weights_kernel,
-        grid=(5,),
+        grid=(4,),
         out_shape=[jax.ShapeDtypeStruct(shape, f32) for shape in shapes],
         in_specs=[
             pl.BlockSpec(memory_space=SMEM),
@@ -866,26 +897,189 @@
             pl.BlockSpec((1, tokens, D), lambda j: (jnp.minimum(j, 2), 0, 0)),
             flat,
             flat,
-            full((BS, BS)),
+            full((2, BS, BS)),
         ],
         out_specs=[full(shape) for shape in shapes],
-        scratch_shapes=[pltpu.VMEM((D, D), f32)],
         name="qkv_weights",
         cost_estimate=cost(2 * tokens * D * 4 * D, 2e7),
     )(core, h1, grads, y, ga, small)
 
 
 def comm_positions():
-    order = []
-    for j in range(FSTEPS):
-        order += [16 + r * 8 + 2 * j + c for r in range(2) for c in range(2)]
-        order += [32 + (2 * j + r) * 2 + c for r in range(2) for c in range(2)]
-    for j in range(3):
-        order += [r * 6 + 2 * j + c for r in range(2) for c in range(2)]
-    order += [12 + r * 2 + c for r in range(2) for c in range(2)]
-    positions = np.zeros(48, np.int32)
-    positions[np.array(order)] = np.arange(48)
-    return positions
+    side = np.zeros(48, np.int32)
+    place = np.zeros(48, np.int32)
+    for r in range(2):
+        for c in range(2):
+            for j in range(FSTEPS):
+                place[16 + r * 8 + 2 * j + c] = 4 * j + c
+                place[32 + (2 * j + r) * 2 + c] = 4 * j + 2 + c
+                side[16 + r * 8 + 2 * j + c] = side[32 + (2 * j + r) * 2 + c] = r
+            for j in range(3):
+                place[r * 6 + 2 * j + c] = 16 + 2 * j + c
+                side[r * 6 + 2 * j + c] = r
+            place[12 + r * 2 + c] = 22 + c
+            side[12 + r * 2 + c] = r
+    return side, place
+
+
+def lane_block(rows_all):
+    return min(1280, (rows_all // 128 + 1) * 128)
+
+
+def fill_table(places_ref, pieces, tab, valid):
+    depth = pieces[0].shape[0]
+    for p, piece in enumerate(pieces):
+        start = pl.multiple_of(places_ref[p], depth)
+        tab[pl.ds(start, depth), :] = jnp.where(valid, piece[...], jnp.zeros((), bf16))
+
+
+def logits_kernel(rows_all, count, places_ref, group_ref, target_ref, *refs):
+    pieces = refs[:count]
+    logit_ref, stat_ref, tab, top, total, chosen = refs[count:]
+    j = pl.program_id(0)
+    wide = tab.shape[1]
+    lane = lax.broadcasted_iota(i32, (1, wide), 1) + j * wide
+    valid = lane < rows_all
+    fill_table(places_ref, pieces, tab, valid)
+
+    @pl.when(j == 0)
+    def _():
+        top[...] = jnp.full(top.shape, -jnp.inf, f32)
+        total[...] = jnp.zeros(total.shape, f32)
+        chosen[...] = jnp.zeros(chosen.shape, f32)
+
+    logits = mm(group_ref[...], tab[...])
+    logit_ref[...] = logits
+    kept = jnp.where(valid, logits, -jnp.inf)
+    before = top[...]
+    after = jnp.maximum(before, jnp.max(kept, -1, keepdims=True))
+    top[...] = after
+    total[...] = total[...] * jnp.exp(before - after) + jnp.sum(
+        jnp.exp(kept - after), -1, keepdims=True
+    )
+    hit = (lane == target_ref[...]) & valid
+    chosen[...] += jnp.sum(jnp.where(hit, logits, 0.0), -1, keepdims=True)
+
+    @pl.when(j == pl.num_programs(0) - 1)
+    def _():
+        spot = lax.broadcasted_iota(i32, (1, 128), 1)
+        merged = jnp.where(
+            spot == 0, top[...], jnp.where(spot == 1, total[...], chosen[...])
+        )
+        stat_ref[...] = merged.T[:8]
+
+
+def table_specs(pieces, wide):
+    return [pl.BlockSpec((pieces[0].shape[0], wide), lambda j: (0, j))] * len(pieces)
+
+
+def vocabulary_logits(places, group, local_targets, pieces):
+    count, rows_all = group.shape[0], pieces[0].shape[1]
+    wide = lane_block(rows_all)
+    return pl.pallas_call(
+        partial(logits_kernel, rows_all, len(pieces)),
+        grid=(pl.cdiv(rows_all, wide),),
+        out_shape=[
+            jax.ShapeDtypeStruct((count, rows_all), f32),
+            jax.ShapeDtypeStruct((8, count), f32),
+        ],
+        in_specs=[pl.BlockSpec(memory_space=SMEM), full((count, D)), full((count, 1))]
+        + table_specs(pieces, wide),
+        out_specs=[pl.BlockSpec((count, wide), lambda j: (0, j)), full((8, count))],
+        scratch_shapes=[pltpu.VMEM((D, wide), bf16)] + [pltpu.VMEM((count, 1), f32)] * 3,
+        name="vocabulary_logits",
+        cost_estimate=cost(2 * count * D * rows_all, 2e7, count * rows_all),
+    )(places, group, local_targets.reshape(count, 1), *pieces)
+
+
+def vocabulary_back_kernel(
+    rows_all, count, scale, places_ref, logit_ref, stat_ref, target_ref, *refs
+):
+    pieces = refs[:count]
+    grad_ref, ghp_ref, tab, stat = refs[count:]
+    j = pl.program_id(0)
+    wide = tab.shape[1]
+    lane = lax.broadcasted_iota(i32, (1, wide), 1) + j * wide
+    valid = lane < rows_all
+    fill_table(places_ref, pieces, tab, valid)
+
+    @pl.when(j == 0)
+    def _():
+        stat[...] = stat_ref[...].T
+        ghp_ref[...] = jnp.zeros_like(ghp_ref)
+
+    hit = (lane == target_ref[...]).astype(f32)
+    soft = jnp.exp(logit_ref[...] - stat[:, 0:1]) * stat[:, 1:2]
+    grads = jnp.where(valid, (soft - hit) * scale, 0.0).astype(bf16)
+    grad_ref[...] = grads
+    ghp_ref[...] += mm_t(grads, tab[...])
+
+
+def vocabulary_back(places, logits, stats, local_targets, pieces, scale):
+    count, rows_all = logits.shape
+    wide = lane_block(rows_all)
+    block = pl.BlockSpec((count, wide), lambda j: (0, j))
+    return pl.pallas_call(
+        partial(vocabulary_back_kernel, rows_all, len(pieces), scale),
+        grid=(pl.cdiv(rows_all, wide),),
+        out_shape=[
+            jax.ShapeDtypeStruct((count, pl.cdiv(rows_all, wide) * wide), bf16),
+            jax.ShapeDtypeStruct((count, D), f32),
+        ],
+        in_specs=[
+            pl.BlockSpec(memory_space=SMEM),
+            block,
+            full(stats.shape),
+            full((count, 1)),
+        ]
+        + table_specs(pieces, wide),
+        out_specs=[block, full((count, D))],
+        scratch_shapes=[pltpu.VMEM((D, wide), bf16), pltpu.VMEM((count, stats.shape[0]), f32)],
+        name="vocabulary_back",
+        cost_estimate=cost(2 * count * D * rows_all, 3e7, count * rows_all),
+    )(places, logits, stats, local_targets.reshape(count, 1), *pieces)
+
+
+def lexicon_kernel(
+    depth, places_ref, turned_ref, grad_ref, mine_ref, theirs_ref, mtop_ref, ttop_ref, sel
+):
+    j = pl.program_id(0)
+    half = mine_ref.shape[0]
+
+    @pl.when(j == 0)
+    def _():
+        for p in range(sel.shape[0] // depth):
+            start = pl.multiple_of(places_ref[p], depth)
+            sel[pl.ds(p * depth, depth), :] = turned_ref[pl.ds(start, depth), :]
+        mtop_ref[...] = jnp.zeros_like(mtop_ref)
+        ttop_ref[...] = jnp.zeros_like(ttop_ref)
+
+    for start, out, top in ((0, mine_ref, mtop_ref), (half, theirs_ref, ttop_ref)):
+        part = mm(sel[pl.ds(start, half), :], grad_ref[...])
+        out[...] = part
+        top[...] = jnp.maximum(top[...], jnp.max(jnp.abs(part), 0, keepdims=True))
+
+
+def lexicon(places, turned, grads, depth, rows_all):
+    count, padded = grads.shape
+    wide = lane_block(rows_all)
+    half = D // 2
+    block = pl.BlockSpec((half, wide), lambda j: (0, j))
+    return pl.pallas_call(
+        partial(lexicon_kernel, depth),
+        grid=(padded // wide,),
+        out_shape=[jax.ShapeDtypeStruct((half, padded), f32)] * 2
+        + [jax.ShapeDtypeStruct((1, wide), f32)] * 2,
+        in_specs=[
+            pl.BlockSpec(memory_space=SMEM),
+            full((D, count)),
+            pl.BlockSpec((count, wide), lambda j: (0, j)),
+        ],
+        out_specs=[block, block, full((1, wide)), full((1, wide))],
+        scratch_shapes=[pltpu.VMEM((D, count), bf16)],
+        name="lexicon",
+        cost_estimate=cost(2 * count * D * padded, 3e7),
+    )(places, turned, grads)
 
 
 def three(left, right, product):
@@ -904,12 +1098,13 @@
     g_ref, nw_ref, nl_ref, nr_ref = refs[count + 5 :]
     clip = clip_ref[0]
     for k in range(count):
-        for half in range(2):
-            place = pl.multiple_of(places_ref[2 * k + half], strip)
-            g_ref[0, pl.ds(place, strip), :] = pieces[k][0, half] * clip
+        place = pl.multiple_of(places_ref[k], strip)
+        g_ref[0, pl.ds(place, strip), :] = pieces[k][0] * clip
     grads = split_two(g_ref[0])
-    nl_ref[0] = SHAMPOO_BETA * ls_ref[0] + (1.0 - SHAMPOO_BETA) * three(grads, grads, mm_t)
-    nr_ref[0] = SHAMPOO_BETA * rs_ref[0] + (1.0 - SHAMPOO_BETA) * three(grads, grads, mm_l)
+    for old, new, product in ((ls_ref, nl_ref, mm_t), (rs_ref, nr_ref, mm_l)):
+        cross = product(grads[0], grads[1])
+        outer = product(grads[0], grads[0]) + (cross + cross.T)
+        new[0] = SHAMPOO_BETA * old[0] + (1.0 - SHAMPOO_BETA) * outer
     turned = split_two(three(grads, split_two(rr_ref[0]), mm))
     direction = three(split_two(lr_ref[0]), turned, mm)
     weights = w_ref[0]
@@ -919,7 +1114,7 @@
 def shampoo(places, clip, pieces, weights, left_stats, right_stats, left_roots, right_roots):
     slots = weights.shape[0]
     count = len(pieces)
-    strip = pieces[0].shape[2]
+    strip = pieces[0].shape[1]
     block = pl.BlockSpec((1, BS, BS), lambda s: (s, 0, 0))
     shape = jax.ShapeDtypeStruct((slots, BS, BS), f32)
     return pl.pallas_call(
@@ -927,7 +1122,7 @@
         grid=(slots,),
         out_shape=[shape] * 4,
         in_specs=[pl.BlockSpec(memory_space=SMEM)] * 2
-        + [pl.BlockSpec((1, 2, strip, BS), lambda s: (s, 0, 0, 0))] * count
+        + [pl.BlockSpec((1, strip, BS), lambda s: (s, 0, 0))] * count
         + [block] * 5,
         out_specs=[block] * 4,
         name="shampoo",
@@ -951,15 +1146,36 @@
     return lax.optimization_barrier((values,) + others)[0]
 
 
-LEVEL = 32768.0
+def exponent(bound):
+    return jnp.floor(jnp.log2(jnp.maximum(bound, 1e-30))) + 1.0
 
 
 def encode(values, bound):
-    return (values * (LEVEL / jnp.maximum(bound, 1e-30))).astype(jnp.float16)
-
-
-def decode(coded, bound):
-    return coded.astype(f32) * (jnp.maximum(bound, 1e-30) * (1.0 / LEVEL))
+    level = exponent(bound)
+    coded = (values * jnp.exp2(15.0 - level)).astype(jnp.float16)
+    return coded.reshape(-1, values.shape[-1]), level.astype(jnp.float16)
+
+
+def pack(values, bound):
+    coded, level = encode(values, bound)
+    return jnp.concatenate([coded, jnp.broadcast_to(level, (16, coded.shape[1]))], 0)
+
+
+def unpack(payload, shape):
+    level = payload[-1, 0].astype(f32)
+    values = payload[:-16].reshape(shape).astype(f32) * jnp.exp2(level - 15.0)
+    return values, jnp.exp2(level)
+
+
+def pack_lanes(values, bound):
+    coded, level = encode(values, bound)
+    lane = lax.broadcasted_iota(i32, coded.shape, 1)
+    return jnp.where(lane == coded.shape[1] - 1, level, coded)
+
+
+def unpack_lanes(payload):
+    level = payload[0, -1].astype(f32)
+    return payload.astype(f32) * jnp.exp2(level - 15.0)
 
 
 def per_device(
@@ -1007,6 +1223,10 @@
         near = [values] + [over_voc(values, k, 0) for k in range(1, n1)]
         return [[part] + [over_voc(part, 0, k) for k in range(1, n0)] for part in near]
 
+    def gather_stacked(values):
+        near = jnp.stack([values] + [over_voc(values, 0, k) for k in range(1, n0)])
+        return jnp.stack([near] + [over_voc(near, k, 0) for k in range(1, n1)])
+
     def flat_gather(values):
         return [part for line in gather_voc(values) for part in line]
 
@@ -1028,48 +1248,49 @@
     per_owner = slot_weights.shape[0]
     block_count = block_order.shape[0]
     table_own = embedding.T
-    relative = [((y_at - ky) % ny) * nc + (c_at + kc) % nc for kc in range(nc) for ky in range(ny)]
-    relative = jnp.stack(relative)
-    canonical = jnp.stack(
+    core = c_at.astype(i32).reshape(1)
+    piece_places = jnp.stack(
         [
-            ((j % nc - c_at) % nc) * ny + (y_at - j // nc) % ny
-            for j in range(n_dp)
+            (((y_at - ky) % ny) * nc + (c_at + kc) % nc) * cols_own
+            for kc in range(nc)
+            for ky in range(ny)
         ]
-    )
-
-    ids_y = jnp.stack(gather_y(token_ids))
-    ids_rows = jnp.concatenate(flat_gather(ids_y), 0).reshape(-1)
-    targets_all = jnp.concatenate(flat_gather(targets), 0)
-    local_ids = ids_rows - vocab_start
-    packed_ids = jnp.where(
-        (local_ids >= 0) & (local_ids < shard_rows),
-        (local_ids << 16) | jnp.arange(ids_rows.shape[0], dtype=i32),
-        -1,
-    )
-    hit_list, hit_count = find_hits(packed_ids, shard_rows)
+    ).astype(i32)
 
     low_own = table_own.astype(bf16)
     low_other = over_dp(low_own, 0, 1)
-    first_core = c_at == 0
-    upright = jnp.concatenate(
-        [jnp.where(first_core, low_own, low_other), jnp.where(first_core, low_other, low_own)], 0
-    ).T
-
-    slots_y = gather_y(slot_weights.astype(bf16))
-
-    found = lookup(hit_list, hit_count, upright, ids_rows.shape[0])
-    found = found.reshape(n1, n0, ny, tokens, cols_y)
-    by_one = []
-    for a in list(range(1, n1)) + [0]:
-        part = found[a, 0]
+    upright = turn_table(core, low_own, low_other)
+
+    ids_y = gather_y(token_ids)
+    numbers = jnp.concatenate(ids_y + [targets])
+
+    slots_y = gather_y(tie(slot_weights.astype(bf16), numbers))
+    numbers = gather_stacked(numbers)
+    targets_all = numbers[:, :, ny * tokens :].reshape(-1)
+    piece_order = [(a, b) for b in list(range(1, n0)) + [0] for a in list(range(1, n1)) + [0]]
+    early = (n0 - 1) * n1
+    ids_order = [numbers[a, b, : ny * tokens] for a, b in piece_order]
+    halves, hits = [], []
+    for first, last in ((0, early), (early, n0 * n1)):
+        ids_rows = jnp.concatenate(ids_order[first:last])
+        local_ids = ids_rows - vocab_start
+        packed_ids = jnp.where(
+            (local_ids >= 0) & (local_ids < shard_rows),
+            (local_ids << 16) | jnp.arange(ids_rows.shape[0], dtype=i32),
+            -1,
+        )
+        hits.append(find_hits(tie(packed_ids, upright), shard_rows))
+        halves += lookup(hits[-1], upright, ids_rows.shape[0], 2 * (last - first) // n1)
+
+    def near_half(h, *before):
+        part = halves[2 * (n0 - 1) + h]
         for b in range(1, n0):
-            part = part + over_voc(found[a, b], 0, -b)
-        by_one.append(part)
-    mine = by_one[-1]
-    for a in range(1, n1):
-        mine = mine + over_voc(by_one[a - 1], -a, 0)
-
-    slots_y = [slots_y[0]] + [tie(part, *by_one[:-1]) for part in slots_y[1:]]
+            moved = over_voc(tie(halves[2 * (b - 1) + h], *before[:1]), 0, -b)
+            part = part + tie(moved, *before)
+        return [line for line in part.reshape(n1 // 2, ny, tokens, cols_y)]
+
+    by_one = near_half(0)
+    slots_y = [tie(part, by_one[0]) for part in slots_y]
     slots_core = [over_dp(part, 0, 1) for part in slots_y]
     inverse = (
         jnp.zeros((block_count,), i32).at[block_order].set(jnp.arange(block_count, dtype=i32))
@@ -1080,9 +1301,11 @@
         src.astype(i32), inverse % per_owner, slots_y + slots_core
     )
 
-    low_sent = tie(low_own, *slots_y[1:])
-    low_y = [over_dp(low_sent, k, 0) for k in range(1, ny)]
-
+    by_one = by_one + near_half(1, by_one[0], wup)
+    far_parts = [over_voc(by_one[a - 1], -a, 0) for a in range(1, n1)]
+    mine = by_one[-1]
+    for part in far_parts:
+        mine = mine + part
     row_parts = [mine[0]] + [over_dp(mine[k], -k, 0) for k in range(1, ny)]
     if ny == 2:
         first = y_at == 0
@@ -1099,6 +1322,9 @@
             [jnp.take(stacked, (j - y_at) % ny, axis=0) for j in range(ny)], axis=1
         )
 
+    low_sent = tie(low_own, x0)
+    low_y = [over_dp(low_sent, k, 0) for k in range(1, ny)]
+
     maps_low = feature_maps.astype(bf16)
     both = jnp.concatenate([maps_low, -maps_low], -1).reshape(2, PAIRS, 2, HD, 2 * HD)
     empty = jnp.zeros_like(both[:, :, 0])
@@ -1109,35 +1335,34 @@
         ],
         2,
     ).reshape(2, HEADS, 2 * HD, 2 * HD)
-    h1, mixed = qkv_forward(x0, wqkv, vectors)
+    their_hits = [over_dp(own, 0, 1) for own in hits]
+    h1, mixed = qkv_forward(tie(x0, *their_hits), wqkv, vectors)
     y, distill = attend(seq_lengths, mixed, lift_maps)
     x1, h2, up, act, x2, picked = mlp_forward(x0, y, wo, wup, wdown, vectors, pick_rows)
 
     low_y = [tie(part, picked) for part in low_y]
     low_y_other = [over_dp(part, 0, 1) for part in low_y]
-    table = jnp.concatenate([low_own] + low_y + [low_other] + low_y_other, 0)
-    picked = jnp.take(picked.reshape(picks_own, n_dp, cols_own), relative, axis=1)
-    picked = picked.reshape(picks_own, D)
+    pieces = [low_own] + low_y + [low_other] + low_y_other
     group = jnp.concatenate(flat_gather(picked), 0)
     local_targets = targets_all - vocab_start
-    logits = mm(group, table)
-    hit = jnp.arange(shard_rows, dtype=i32)[None, :] == local_targets[:, None]
-    top = jnp.max(logits, 1)
-    exp_sum = jnp.sum(jnp.exp(logits - top[:, None]), 1)
-    chosen = jnp.sum(jnp.where(hit, logits, 0.0), 1)
-    stats = jnp.stack([top, exp_sum, chosen]).reshape(3, n1, n0, picks_own)
-    stats_all = gather_voc(stats)
+    logits, stats = vocabulary_logits(piece_places, group, local_targets, pieces)
+    stats_all = gather_stacked(stats)
     lined = jnp.stack(
-        [jnp.roll(stats_all[a][b], (a, b), (1, 2)) for a in range(n1) for b in range(n0)]
+        [
+            jnp.roll(stats_all[a, b, :3].reshape(3, n1, n0, picks_own), (a, b), (1, 2))
+            for a in range(n1)
+            for b in range(n0)
+        ]
     ).reshape(n_voc, 3, n_voc * picks_own)
     top_all = jnp.max(lined[:, 0], 0)
     sum_all = jnp.sum(lined[:, 1] * jnp.exp(lined[:, 0] - top_all[None]), 0)
     losses = top_all + jnp.log(sum_all) - jnp.sum(lined[:, 2], 0)
     loss_part = jnp.sum(losses[:picks_own]) / total_picks + coefficient * distill[0, 0]
-    grad_logits = (
-        (jnp.exp(logits - top_all[:, None]) * (1.0 / sum_all)[:, None] - hit) / total_picks
-    ).astype(bf16)
-    grad_group = mm_t(grad_logits, table).reshape(n1, n0, picks_own, D)
+    shares = jnp.pad(jnp.stack([top_all, 1.0 / sum_all]), ((0, 126), (0, 0)))
+    grad_logits, grad_group = vocabulary_back(
+        piece_places, logits, shares, local_targets, pieces, 1.0 / total_picks
+    )
+    grad_group = grad_group.reshape(n1, n0, picks_own, D)
     by_one = []
     for a in list(range(1, n1)) + [0]:
         part = grad_group[a, 0]
@@ -1146,49 +1371,62 @@
         by_one.append(part)
     near_parts = [over_voc(by_one[a - 1], -a, 0) for a in range(1, n1)]
 
-    lex_theirs = mm_l(group[:, D // nc :], grad_logits)
+    lex_mine, lex_theirs, mine_high, theirs_high = lexicon(
+        piece_places, group.T, tie(grad_logits, *by_one[:-1]), cols_own, shard_rows
+    )
     lex_arrived = over_dp(lex_theirs, 0, 1)
-    near_parts = [tie(part, lex_theirs) for part in near_parts]
+    lex_high = jnp.max(mine_high) + jnp.max(over_dp(theirs_high, 0, 1))
     ghp = by_one[-1]
     for part in near_parts:
-        ghp = ghp + part
-    ghp = jnp.take(ghp.reshape(picks_own, n_dp, cols_own), canonical, axis=1)
-    ghp = ghp.reshape(picks_own, D)
-    lex_sums = mm_l(group[:, : D // nc], grad_logits) + lex_arrived
-    lex = lex_sums[:cols_own]
-    for k in range(1, ny):
-        lex = lex + over_dp(lex_sums[k * cols_own : (k + 1) * cols_own], -k, 0)
-
-    core = c_at.astype(i32).reshape(1)
-
-    def reduce_blocks(mine_half, their_half, mine_top, their_top):
-        part = mine_half + over_dp(their_half, 0, 1)
-        bound = mine_top + over_dp(their_top, 0, 1)
-        for size, at, far in ((n0, i0, 0), (n1, i1, 1)):
-            rows = part.shape[1] // size
-            total = lax.dynamic_slice_in_dim(part, at * rows, rows, 1)
-            bound_next = bound
-            for k in range(1, size):
-                d1, d0 = (k, 0) if far else (0, k)
-                piece = lax.dynamic_slice_in_dim(part, ((at + k) % size) * rows, rows, 1)
-                coded = over_voc(encode(piece, bound), d1, d0)
-                theirs = over_voc(bound, d1, d0)
-                total = total + decode(coded, theirs)
-                bound_next = bound_next + theirs
-            part, bound = total, bound_next
-        return part
+        ghp = ghp + tie(part, lex_theirs)
+
+    def lex_lines(k):
+        lines = slice(k * cols_own, (k + 1) * cols_own)
+        return lex_mine[lines] + lex_arrived[lines]
+
+    lex_sent = [pack_lanes(lex_lines(k), lex_high) for k in range(1, ny)]
+
+
+    def core_parts(mine_part, their_part, mine_top, their_top, *later):
+        arrived = tie(over_dp(their_part, 0, 1), *later)
+        bound = jnp.max(mine_top) + jnp.max(over_dp(their_top, 0, 1))
+        return coded_parts((mine_part, arrived), bound, False) + (bound,)
+
+    def coded_parts(parts, bound, far):
+        size, at = (n1, i1) if far else (n0, i0)
+        rows = parts[0].shape[1] // size
+
+        def lines(k):
+            cut = [
+                lax.dynamic_slice_in_dim(part, ((at + k) % size) * rows, rows, 1) for part in parts
+            ]
+            return sum(cut[1:], cut[0])
+
+        return lines(0), [pack(lines(k), bound) for k in range(1, size)]
+
+    def exchange(own, sent, bound, far, *later):
+        total, high = own, bound
+        for k, coded in enumerate(sent, 1):
+            d1, d0 = (k, 0) if far else (0, k)
+            values, top = unpack(tie(over_voc(coded, d1, d0), *later), own.shape)
+            total = total + values
+            high = high + top
+        return total, high
 
     *halves_a, gx1, ga, gy, vg_a = mlp_back(
         core, ghp, pick_rows, x2, act, up, h2, x1, wdown, wup, wo, vectors
     )
-    blocks_a = reduce_blocks(*halves_a)
     half_pairs = PAIRS // 2
+    gy = tie(gy, *lex_sent)
     gqkv, map_q_a, map_k_a = attend_back(
         seq_lengths, mixed, gy, lift_maps, coefficient, 0, half_pairs, None
     )
+    own_a, sent_a, bound_a = core_parts(*halves_a, gqkv)
+    gy = tie(gy, own_a, *sent_a)
     gqkv, map_q_b, map_k_b = attend_back(
         seq_lengths, mixed, gy, lift_maps, coefficient, half_pairs, half_pairs, gqkv
     )
+    lex_parts = [over_dp(part, -k, 0) for k, part in enumerate(lex_sent, 1)]
     gx0, vg_b = qkv_back(gqkv, wqkv, x0, gx1, vectors)
 
     map_grads = jnp.concatenate([map_q_a, map_q_b, map_k_a, map_k_b], 0)
@@ -1198,17 +1436,17 @@
         [
             map_grads.reshape(-1),
             vec_grads.reshape(-1),
-            jnp.zeros((BS * BS - small_count,), f32),
+            jnp.zeros((2 * BS * BS - small_count,), f32),
         ]
-    ).reshape(BS, BS)
-    blocks_b = reduce_blocks(*qkv_weights(core, h1, gqkv, y, ga, small))
-
+    ).reshape(2, BS, BS)
     gx0_cols = gx0.reshape(tokens, ny, cols_y)
+    cols_sent = [jnp.take(gx0_cols, (y_at + k) % ny, axis=1) for k in range(1, ny)]
     arrived = [jnp.take(gx0_cols, y_at, axis=1)] + [
-        over_dp(jnp.take(gx0_cols, (y_at + k) % ny, axis=1), k, 0) for k in range(1, ny)
+        over_dp(part, k, 0) for k, part in enumerate(cols_sent, 1)
     ]
     arrived = jnp.concatenate(arrived, 0).reshape(ny * tokens, nc, cols_own)
     rows_mine = jnp.take(arrived, c_at, axis=1)
+    moved_a = [over_voc(part, 0, k) for k, part in enumerate(sent_a, 1)]
     rows_other = over_dp(jnp.take(arrived, (c_at + 1) % nc, axis=1), 0, 1)
     if cols_own == 192:
         packed = jnp.concatenate(
@@ -1219,51 +1457,82 @@
             ],
             0,
         )
-        pieces = flat_gather(packed)
-        lists = (hit_list, hit_count, over_dp(hit_list, 0, 1), over_dp(hit_count, 0, 1))
-        emb_grads, emb_square = scatter_rows(lists, lex, pieces)
+    else:
+        packed = jnp.stack([rows_mine, rows_other])
+    halves_b = qkv_weights(core, tie(h1, packed, *moved_a, *lex_parts), gqkv, y, ga, small)
+    total_a, high_a = own_a, bound_a
+    for part in moved_a:
+        values, top = unpack(tie(part, halves_b[0]), own_a.shape)
+        total_a, high_a = total_a + values, high_a + top
+    own_b, sent_b, bound_b = core_parts(*halves_b, packed)
+    total_b, high_b = exchange(own_b, sent_b, bound_b, False)
+    total = jnp.concatenate([total_a, total_b], 0)
+    high = jnp.maximum(high_a, high_b)
+    own, sent = coded_parts((total,), high, True)
+    near_rows = [packed] + [tie(over_voc(packed, k, 0), *sent) for k in range(1, n1)]
+    gathered = [[packed] + [over_voc(packed, 0, k) for k in range(1, n0)]]
+    sent = [tie(part, *near_rows, *gathered[0]) for part in sent]
+    gathered += [[part] + [over_voc(part, 0, k) for k in range(1, n0)] for part in near_rows[1:]]
+    blocks = exchange(own, sent, high, True, *(line[-1] for line in gathered))[0]
+
+    per_side = blocks.shape[0]
+    both = jnp.concatenate([blocks, over_dp(blocks, 0, 1)], 0)
+    side, place = comm_positions()
+    side = jnp.concatenate([jnp.take(jnp.asarray(side), block_order), jnp.arange(2, dtype=i32)])
+    place = jnp.concatenate(
+        [jnp.take(jnp.asarray(place), block_order), jnp.full((2,), per_side - 1, i32)]
+    )
+    at_place = ((side - c_at) % nc) * per_side + place
+    smalls = at_place[block_count:]
+    at_place = at_place[:block_count].reshape(ny, nc, per_owner)
+
+    def slots_of(k):
+        mine = jnp.take(jnp.take(at_place, c_at, axis=1), (y_at + k) % ny, axis=0)
+        return jnp.take(both, jnp.concatenate([mine, smalls]), axis=0)
+
+    own_slots = slots_of(0)
+    strips, small_parts = own_slots[:per_owner], []
+    strip_rows = own_slots.shape[1]
+    tail = own_slots[per_owner:]
+    values, _ = unpack(pack(tail, jnp.max(jnp.abs(own_slots))), tail.shape)
+    small_parts.append(values)
+    slots_sent = []
+    for k in range(1, ny):
+        moved = slots_of(k)
+        high = jnp.maximum(jnp.max(jnp.abs(moved)), jnp.max(jnp.abs(own_slots)))
+        slots_sent.append(pack(moved, high))
+    lex = lex_lines(0)
+    for part in lex_parts:
+        lex = lex + unpack_lanes(part)
+    lex = tie(lex, *slots_sent)
+    if cols_own == 192:
+        pieces = [gathered[a][b] for a, b in piece_order]
+        emb_grads, emb_square = scatter_rows(
+            list(zip(hits, their_hits)), lex, pieces, shard_rows
+        )
         emb_square = emb_square[0, 0]
     else:
-        packed = jnp.stack([rows_mine, rows_other])
-        pieces = jnp.stack(flat_gather(packed), 1).reshape(-1, cols_own)
+        pieces = jnp.stack([gathered[a][b] for a, b in piece_order], 1).reshape(-1, cols_own)
+        ids_rows = jnp.concatenate(ids_order)
         local = jnp.concatenate([ids_rows, over_dp(ids_rows, 0, 1)]) - vocab_start
         local = jnp.where((local >= 0) & (local < shard_rows), local, shard_rows)
-        emb_grads = lex.T.at[local].add(pieces.astype(f32), mode="drop").T
+        emb_grads = lex[:, :shard_rows].T.at[local].add(pieces.astype(f32), mode="drop").T
         emb_square = jnp.sum(emb_grads * emb_grads)
 
-    blocks = jnp.concatenate([blocks_a, blocks_b], 0)
-    slot_places = jnp.take(jnp.asarray(comm_positions()), block_order).reshape(
-        ny, nc * per_owner
-    )
-
-    def slots_of(k):
-        places = jnp.take(slot_places, (y_at + k) % ny, axis=0)
-        return jnp.take(blocks, places, axis=0)
-
-    strips = slots_of(0)
-    small_parts = [blocks[block_count:]]
-    for k in range(1, ny):
-        moved = over_dp(jnp.concatenate([slots_of(k), blocks[block_count:]], 0), k, 0)
-        strips = strips + moved[:-1]
-        small_parts.append(moved[-1:])
+    for k, sent in enumerate(slots_sent, 1):
+        moved, _ = unpack(over_dp(sent, k, 0), own_slots.shape)
+        strips = strips + moved[:per_owner]
+        small_parts.append(moved[per_owner:])
     if ny == 2:
         small_sum = small_parts[0] + small_parts[1]
     else:
         small_sum = jnp.sum(line_up(small_parts, y_at), 0)
-    strip_rows = strips.shape[1]
-    strips = strips.reshape(nc, per_owner, strip_rows, BS)
-
-    def with_small(k):
-        return jnp.concatenate([jnp.take(strips, (c_at + k) % nc, axis=0), small_sum], 0)
-
-    own_strips = jnp.stack([with_small(0), over_dp(with_small(1), 0, 1)], 1)
-    strip_bound = jnp.max(jnp.abs(own_strips), 2, keepdims=True)
-    coded_all = flat_gather(encode(own_strips, strip_bound))
-    bound_all = flat_gather(strip_bound)
-    strip_pieces = [decode(part, bound) for part, bound in zip(coded_all, bound_all)]
+    own_strips = jnp.concatenate([strips, small_sum], 0)
+    coded_all = flat_gather(pack(own_strips, jnp.max(jnp.abs(own_strips))))
+    strip_pieces = [unpack(part, own_strips.shape)[0] for part in coded_all]
 
     square = emb_square + jnp.sum(strips * strips)
-    square = square + jnp.where(y_at == 0, jnp.sum(small_sum * small_sum), 0.0)
+    square = square + jnp.where(dp_index == 0, jnp.sum(small_sum * small_sum), 0.0)
     sums = jnp.pad(jnp.stack([square, loss_part]).reshape(1, 2), ((0, 7), (0, 126)))
     sums = sums + over_dp(sums, 0, 1)
     sums = jnp.sum(line_up(gather_y(sums), y_at), 0)
@@ -1273,33 +1542,19 @@
     loss_total = sums[0, 1]
     clip_scale = CLIP_NORM / jnp.maximum(grad_norm, CLIP_NORM)
 
-    small_all = jnp.stack([part[per_owner] for part in strip_pieces])
-    small_all = small_all.reshape(n1, n0, nc, strip_rows, BS)
+    small_all = jnp.stack([part[per_owner:] for part in strip_pieces])
+    small_all = small_all.reshape(n1, n0, 2, strip_rows, BS)
     small_all = jnp.take(small_all, (i1 - jnp.arange(n1)) % n1, axis=0)
     small_all = jnp.take(small_all, (i0 - jnp.arange(n0)) % n0, axis=1)
-    small_all = jnp.take(small_all, (c_at - jnp.arange(nc)) % nc, axis=2)
     small_all = small_all.transpose(2, 1, 0, 3, 4).reshape(-1)
     map_sum = small_all[: map_grads.size].reshape(feature_maps.shape)
     vec_sum = small_all[map_grads.size : small_count].reshape(vectors.shape)
 
-    strip_half = BS // nc
-    if strip_rows % 8:
-        whole = jnp.stack(strip_pieces).reshape(n1, n0, per_owner + 1, nc, strip_rows, BS)
-        whole = jnp.take(whole, (i1 - jnp.arange(n1)) % n1, axis=0)
-        whole = jnp.take(whole, (i0 - jnp.arange(n0)) % n0, axis=1)
-        strip_pieces = [
-            whole.transpose(2, 3, 1, 0, 4, 5).reshape(per_owner + 1, nc, strip_half, BS)
-        ]
-        bases = [0]
-    else:
-        bases = [
-            ((i0 - b) % n0) * (strip_half // n0) + ((i1 - a) % n1) * strip_rows
-            for a in range(n1)
-            for b in range(n0)
-        ]
-    places = []
-    for base in bases:
-        places += [c_at * strip_half + base, ((c_at + 1) % nc) * strip_half + base]
+    places = [
+        ((i0 - b) % n0) * (BS // n0) + ((i1 - a) % n1) * strip_rows
+        for a in range(n1)
+        for b in range(n0)
+    ]
     places = jnp.stack(places).astype(i32)
     clipped, new_slots, new_left, new_right = shampoo(
         places,

time: 1050 us -> 893 us (0.85)
  waiting for transfers between devices: 430 us -> 315 us
  Pallas kernels: 233 us -> 288 us
  starting transfers between devices: 135 us -> 88.4 us
  matrix products: 43.1 us -> 0 us
  between operations: 8.7 us -> 25.5 us
  local copies, waits for them, and re-layouts: 73.4 us -> 58.6 us
    ppermute x83 -> x50, waiting for transfers between devices: 330 us -> 268 us  [over_voc(): return lax.ppermute(values, 'vocab', pairs)]
    pallas_call x4 -> x10, Pallas kernels: 71 us -> 129 us  [the longest x1 27.2 us: scatter_rows(): pl.pallas_call(partial(scatter_kernel, count, half, rows_all, tuple(start...]
    ppermute x22 -> x23, waiting for transfers between devices: 101 us -> 46.3 us  [over_dp(): return lax.ppermute(values, 'dp', pairs)]
    ppermute x83 -> x50, starting transfers between devices: 125 us -> 76.2 us  [over_voc(): return lax.ppermute(values, 'vocab', pairs)]
    dot_general x4 -> x0, matrix products: 43.1 us -> none  [the longest x2 19.2 us: mm_l(): lax.dot_general(left, right, (((0,), (0,)), ((), ())), preferred_element_...]
    unnamed x177 -> x116, local copies, waits for them, and re-layouts: 24.9 us -> 5.37 us
    add x10 -> x9, other arithmetic: 27.8 us -> 25.8 us  [the longest x1 7.48 us: per_device(): lex = lex + unpack_lanes(part)]
  transfers between devices with their start and end apart: 105 -> 73, of which waited for: 53 -> 43; matrix products, arithmetic and copies ran while one was open for 16% -> 13% of each run, Pallas kernels for 19% -> 23%
where the time goes in v2:
time: 893 us; the launch traced here: 882 us
  waiting for transfers between devices  315 us (35%)
  Pallas kernels  288 us (32%)
  other arithmetic  107 us (12%)
  starting transfers between devices  88.4 us (10%)
  local copies, waits for them, and re-layouts  58.6 us (7%)
  between operations  25.5 us (3%)
    ppermute x50, waiting for transfers between devices, over_voc(): return lax.ppermute(values, 'vocab', pairs)  268 us
    ppermute x50, starting transfers between devices, over_voc(): return lax.ppermute(values, 'vocab', pairs)  76.2 us
    ppermute x23, waiting for transfers between devices, over_dp(): return lax.ppermute(values, 'dp', pairs)  46.3 us
    pallas_call x2, Pallas kernels, attend_back(): pl.pallas_call(partial(attend_back_kernel, coefficient, int(later)), grid...  38.4 us
    pallas_call x1, Pallas kernels, shampoo(): pl.pallas_call(partial(shampoo_kernel, count, strip), grid=(slots,), out_...  34.4 us
    pallas_call x1, Pallas kernels, scatter_rows(): pl.pallas_call(partial(scatter_kernel, count, half, rows_all, tuple(start...  27.2 us
    pallas_call x1, Pallas kernels, mlp_back(): pl.pallas_call(mlp_back_kernel, grid=(FSTEPS,), out_shape=[halves, halves...  26.2 us
    pallas_call x2, Pallas kernels, find_hits(): pl.pallas_call(partial(hits_kernel, empty_row), out_shape=jax.ShapeDtypeS...  25.5 us
  transfers between devices with their start and end apart: 73, of which 43 were waited for; matrix products, arithmetic and copies ran while one was open for 13% of the time, Pallas kernels for 23%

profile of v2, /device:TPU:8, one launch (start us, length us, event | category | flops | bytes accessed | tf_op | source)
XLA Modules:
  0.0 882.1 jit_solution(15650120042803970469)
XLA Ops:
  5.0 5.3 convert_element_type.195.refs_0_
  22.3 7.1 turn_table.1.table_ref
  29.4 12.8 %find_hits.2.list_ref.refs_0_ = s32[4112]{0:T(1024)} custom-call(s32[4096]{0:T(1024)} %get-tuple-element.104.packed_ref), custom_call_target="tpu_custom_call" | custom-call | flops 200000000 | bytes 655 | tf_op jit(solution)/shard_map/find_hits/pallas_call | solution.py:142
  42.2 7.9 lookup.3
  52.8 12.8 %find_hits.3.list_ref.refs_2_ = s32[4112]{0:T(1024)} custom-call(s32[4096]{0:T(1024)} %get-tuple-element.105.packed_ref), custom_call_target="tpu_custom_call" | custom-call | flops 200000000 | bytes 655 | tf_op jit(solution)/shard_map/find_hits/pallas_call | solution.py:142
  65.6 8.1 lookup.2
  73.7 11.1 %collective-permute-done.8 = bf16[2048,384]{1,0:T(8,128)(2,1)S(1)} collective-permute-done((bf16[2048,384]{1,0:T(8,128)(2,1)}, bf16[2048,384]{1,0:T(8,128)(2,1)S(1)}, u32[]{:S(2)}, u32[]{:S(2)}) %collective-permute-start.8) | collective-permute-done | bytes 1572896 | tf_op jit(solution)/shard_map/ppermute | solution.py:1220
  102.5 11.5 %place_blocks.1 = (bf16[768,2304]{1,0:T(8,128)(2,1)}, bf16[768,768]{1,0:T(8,128)(2,1)}, bf16[768,3072]{1,0:T(8,128)(2,1)}, bf16[3072,768]{1,0:T(8,128)(2,1)}) custom-call(s32[48]{0:T(128)} %get-tuple-element.318.src_ref, s32[48]{0:T(128)} %get-tuple-element.317.off_ref, bf16[12,384,384]{2,1,0:T(8,128)(2,1)} %convert_element_type.195.refs_0_, ...), custom_call_target="tpu_custom_call" | custom-call | bytes 566231 | tf_op jit(solution)/shard_map/place_blocks/pallas_call | solution.py:110
  114.0 12.4 %collective-permute-done.9 = bf16[2048,384]{1,0:T(8,128)(2,1)} collective-permute-done((bf16[2048,384]{1,0:T(8,128)(2,1)}, bf16[2048,384]{1,0:T(8,128)(2,1)}, u32[]{:S(2)}, u32[]{:S(2)}) %collective-permute-start.9) | collective-permute-done | bytes 1572896 | tf_op jit(solution)/shard_map/ppermute | solution.py:1220
  131.0 17.2 %collective-permute-done.14 = bf16[2,512,384]{2,1,0:T(8,128)(2,1)} collective-permute-done((bf16[2,512,384]{2,1,0:T(8,128)(2,1)}, bf16[2,512,384]{2,1,0:T(8,128)(2,1)}, u32[]{:S(2)}, u32[]{:S(2)}) %collective-permute-start.14) | collective-permute-done | bytes 786464 | tf_op jit(solution)/shard_map/ppermute | solution.py:1220
  148.2 15.9 %collective-permute-done.15 = bf16[2,512,384]{2,1,0:T(8,128)(2,1)S(1)} collective-permute-done((bf16[2,512,384]{2,1,0:T(8,128)(2,1)S(1)}, bf16[2,512,384]{2,1,0:T(8,128)(2,1)S(1)}, u32[]{:S(2)}, u32[]{:S(2)}) %collective-permute-start.15) | collective-permute-done | bytes 786464 | tf_op jit(solution)/shard_map/ppermute | solution.py:1220
  168.5 9.6 %collective-permute-done.16 = bf16[512,384]{1,0:T(8,128)(2,1)} collective-permute-done((bf16[512,384]{1,0:T(8,128)(2,1)}, bf16[512,384]{1,0:T(8,128)(2,1)}, u32[]{:S(2)}, u32[]{:S(2)}) %collective-permute-start.16) | collective-permute-done | bytes 393248 | tf_op jit(solution)/shard_map/ppermute | solution.py:1214
  184.8 6.1 qkv_forward.1
  190.9 20.0 %attend.1 = (bf16[512,768]{1,0:T(8,128)(2,1)}, f32[8,128]{1,0:T(8,128)}) custom-call(s32[1,4]{1,0:T(1,128)} %len_ref.5, bf16[512,2304]{1,0:T(8,128)(2,1)} %get-tuple-element.118.q_ref.k_ref.v_ref, bf16[512,2304]{1,0:T(8,128)(2,1)} %get-tuple-element.118.q_ref.k_ref.v_ref, bf16[512,2304]{1,0:T(8,128)(2,1)} %get-tuple-element.118.q_ref.k_ref.v_ref, ...), custom_call_target="tpu_custom_call" | custom-call | flops 240000000 | bytes 80000 | tf_op jit(solution)/shard_map/attend/pallas_call | solution.py:436
  211.0 14.7 %mlp_forward.1 = (f32[512,768]{1,0:T(8,128)}, bf16[512,768]{1,0:T(8,128)(2,1)}, f32[512,3072]{1,0:T(8,128)}, bf16[512,3072]{1,0:T(8,128)(2,1)}, f32[512,768]{1,0:T(8,128)}, /*index=5*/bf16[64,768]{1,0:T(8,128)(2,1)}) custom-call(bf16[512,768]{1,0:T(8,128)(2,1)} %pad_maximum_fusion.3.x_ref, bf16[512,768]{1,0:T(8,128)(2,1)} %get-tuple-element.119.y_ref, ...), custom_call_target="tpu_custom_call" | custom-call | flops 108716360 | bytes 600000 | tf_op jit(solution)/shard_map/mlp_forward/pallas_call | solution.py:634
  225.7 9.1 %collective-permute-done.24.refs_1_ = bf16[192,6288]{1,0:T(8,128)(2,1)} collective-permute-done((bf16[192,6288]{1,0:T(8,128)(2,1)S(1)}, bf16[192,6288]{1,0:T(8,128)(2,1)}, u32[]{:S(2)}, u32[]{:S(2)}) %collective-permute-start.24) | collective-permute-done | bytes 2414624 | tf_op jit(solution)/shard_map/ppermute | solution.py:1214
  243.1 9.0 %collective-permute-done.18 = bf16[64,768]{0,1:T(8,128)(2,1)S(1)} collective-permute-done((bf16[64,768]{0,1:T(8,128)(2,1)S(1)}, bf16[64,768]{0,1:T(8,128)(2,1)S(1)}, u32[]{:S(2)}, u32[]{:S(2)}) %collective-permute-start.18) | collective-permute-done | bytes 98336 | tf_op jit(solution)/shard_map/ppermute | solution.py:1220
  271.9 15.8 %vocabulary_logits.1 = (f32[512,6288]{1,0:T(8,128)}, f32[8,512]{1,0:T(8,128)}) custom-call(s32[4]{0:T(128)} %pad_add_fusion.5.places_ref, bf16[512,768]{1,0:T(8,128)(2,1)} %copy.78.group_ref, s32[512,1]{1,0:T(8,128)} %sub.302.target_ref, bf16[192,6288]{1,0:T(8,128)(2,1)} %copy-done.2, bf16[192,6288]{1,0:T(8,128)(2,1)} %collective-permute-done.24.refs_1_, ...), custom_call_target="tpu_custom_call" | custom-call | flops 98901688 | bytes 400000 | tf_op jit(solution)/shard_map/vocabulary_logits/pallas_call | solution.py:979
  302.1 15.3 %vocabulary_back.1 = (bf16[512,6400]{1,0:T(8,128)(2,1)}, f32[512,768]{1,0:T(8,128)}) custom-call(s32[4]{0:T(128)} %pad_add_fusion.5.places_ref, f32[512,6288]{1,0:T(8,128)} %get-tuple-element.125.logit_ref, f32[128,512]{1,0:T(8,128)} %select_maximum_fusion.stat_ref, s32[512,1]{1,0:T(8,128)} %sub.302.target_ref, bf16[192,6288]{1,0:T(8,128)(2,1)} %copy-done.2, ...), custom_call_target="tpu_custom_call" | custom-call | flops 98901688 | bytes 600000 | tf_op jit(solution)/shard_map/vocabulary_back/pallas_call | solution.py:1022
  331.4 11.6 %lexicon.1 = (f32[384,6400]{1,0:T(8,128)}, f32[384,6400]{1,0:T(8,128)}, f32[1,1280]{1,0:T(1,128)}, f32[1,1280]{1,0:T(1,128)}) custom-call(s32[4]{0:T(128)} %pad_add_fusion.5.places_ref, bf16[768,512]{1,0:T(8,128)(2,1)} %bitcast.246, bf16[512,6400]{1,0:T(8,128)(2,1)} %get-tuple-element.129.grad_ref), custom_call_target="tpu_custom_call" | custom-call | flops 100663296 | bytes 600000 | tf_op jit(solution)/shard_map/lexicon/pallas_call | solution.py:1068
  350.7 10.6 %collective-permute-done.38 = f32[64,768]{1,0:T(8,128)S(1)} collective-permute-done((f32[64,768]{1,0:T(8,128)S(1)}, f32[64,768]{1,0:T(8,128)S(1)}, u32[]{:S(2)}, u32[]{:S(2)}) %collective-permute-start.38) | collective-permute-done | bytes 196640 | tf_op jit(solution)/shard_map/ppermute | solution.py:1220
  365.9 26.2 %mlp_back.1 = (f32[16,384,384]{2,1,0:T(8,128)}, f32[16,384,384]{2,1,0:T(8,128)}, f32[1,384]{1,0:T(1,128)}, f32[1,384]{1,0:T(1,128)}, f32[512,768]{1,0:T(8,128)},...) custom-call(s32[1]{0:T(128)} %bitcast.8.core_ref, f32[64,768]{1,0:T(8,128)} %fusion.30.ghp_ref, ...), custom_call_target="tpu_custom_call" | custom-call | flops 193273536 | bytes 1000000 | tf_op jit(solution)/shard_map/mlp_back/pallas_call | solution.py:774
  403.4 6.1 fusion.7
  411.2 19.1 %attend_back.2 = (bf16[3,512,768]{2,1,0:T(8,128)(2,1)}, f32[6,64,64]{2,1,0:T(8,128)}, f32[6,64,64]{2,1,0:T(8,128)}) custom-call(s32[1,4]{1,0:T(1,128)} %len_ref.5, bf16[512,2304]{1,0:T(8,128)(2,1)} %get-tuple-element.118.q_ref.k_ref.v_ref, bf16[512,2304]{1,0:T(8,128)(2,1)} %get-tuple-element.118.q_ref.k_ref.v_ref, ...), custom_call_target="tpu_custom_call" | custom-call | flops 240000000 | bytes 80000 | tf_op jit(solution)/shard_map/attend_back/pallas_call | solution.py:548
  430.3 10.4 %multiply_convert_fusion = (f16[16,192,384]{2,1,0:T(8,128)(2,1)S(1)}, f32[16,192,384]{2,1,0:T(8,128)}) fusion(f32[16,384,384]{2,1,0:T(8,128)} %collective-permute-done.40, s32[]{:T(128)S(6)} %select_n.375, f32[16,384,384]{2,1,0:T(8,128)} %get-tuple-element.142, f32[]{:T(128)S(6)} %exp2.224, s32[]{:T(128)S(6)} %select_n.373), kind=kLoop, calls=%fused_computation.33 | loop fusion | flops 4718592 | bytes 25952268 | tf_op jit(solution)/shard_map/convert_element_type | solution.py:1155
  443.1 19.3 %attend_back.3 = (bf16[3,512,768]{2,1,0:T(8,128)(2,1)}, f32[6,64,64]{2,1,0:T(8,128)}, f32[6,64,64]{2,1,0:T(8,128)}) custom-call(s32[1,4]{1,0:T(1,128)} %len_ref.5, bf16[512,2304]{1,0:T(8,128)(2,1)} %get-tuple-element.118.q_ref.k_ref.v_ref, bf16[512,2304]{1,0:T(8,128)(2,1)} %get-tuple-element.118.q_ref.k_ref.v_ref, ...), custom_call_target="tpu_custom_call", output_to_operand_aliasing={{0}: (7, {})} | custom-call | flops 240000000 | bytes 80000 | tf_op jit(solution)/shard_map/attend_back/pallas_call | solution.py:548
  462.4 7.9 qkv_back.1
  475.1 10.1 %collective-permute-done.43 = bf16[512,384]{1,0:T(8,128)(2,1)S(1)} collective-permute-done((bf16[512,384]{1,0:T(8,128)(2,1)S(1)}, bf16[512,384]{1,0:T(8,128)(2,1)S(1)}, u32[]{:S(2)}, u32[]{:S(2)}) %collective-permute-start.43) | collective-permute-done | bytes 393248 | tf_op jit(solution)/shard_map/ppermute | solution.py:1214
  489.0 7.5 collective-permute-done.42
  496.4 10.1 %qkv_weights.1 = (f32[9,384,384]{2,1,0:T(8,128)}, f32[9,384,384]{2,1,0:T(8,128)}, f32[1,384]{1,0:T(1,128)}, f32[1,384]{1,0:T(1,128)}) custom-call(s32[1]{0:T(128)} %bitcast.8.core_ref, bf16[512,768]{1,0:T(8,128)(2,1)} %get-tuple-element.155.h_ref, bf16[3,512,768]{2,1,0:T(8,128)(2,1)} %get-tuple-element.152.g_ref, bf16[512,768]{1,0:T(8,128)(2,1)} %get-tuple-element.119.y_ref, ...), custom_call_target="tpu_custom_call" | custom-call | flops 48318384 | bytes 400000 | tf_op jit(solution)/shard_map/qkv_weights/pallas_call | solution.py:890
  527.3 5.3 add.586
  532.6 18.6 %collective-permute-done.47 = f16[1744,384]{1,0:T(8,128)(2,1)S(1)} collective-permute-done((f16[1744,384]{1,0:T(8,128)(2,1)S(1)}, f16[1744,384]{1,0:T(8,128)(2,1)S(1)}, u32[]{:S(2)}, u32[]{:S(2)}) %collective-permute-start.47) | collective-permute-done | bytes 1339424 | tf_op jit(solution)/shard_map/ppermute | solution.py:1220
  562.9 24.5 %collective-permute-done.49.refs_10_ = bf16[3072,128]{1,0:T(8,128)(2,1)} collective-permute-done((bf16[3072,128]{1,0:T(8,128)(2,1)}, bf16[3072,128]{1,0:T(8,128)(2,1)}, u32[]{:S(2)}, u32[]{:S(2)}) %collective-permute-start.49) | collective-permute-done | bytes 786464 | tf_op jit(solution)/shard_map/ppermute | solution.py:1220
  596.1 15.6 %collective-permute-done.53.refs_5_ = bf16[3072,128]{1,0:T(8,128)(2,1)} collective-permute-done((bf16[3072,128]{1,0:T(8,128)(2,1)}, bf16[3072,128]{1,0:T(8,128)(2,1)}, u32[]{:S(2)}, u32[]{:S(2)}) %collective-permute-start.53) | collective-permute-done | bytes 786464 | tf_op jit(solution)/shard_map/ppermute | solution.py:1220
  614.7 13.8 %collective-permute-done.54.refs_6_ = bf16[3072,128]{1,0:T(8,128)(2,1)} collective-permute-done((bf16[3072,128]{1,0:T(8,128)(2,1)}, bf16[3072,128]{1,0:T(8,128)(2,1)}, u32[]{:S(2)}, u32[]{:S(2)}) %collective-permute-start.54) | collective-permute-done | bytes 786464 | tf_op jit(solution)/shard_map/ppermute | solution.py:1220
  628.5 14.8 %collective-permute-done.55.refs_7_ = bf16[3072,128]{1,0:T(8,128)(2,1)} collective-permute-done((bf16[3072,128]{1,0:T(8,128)(2,1)}, bf16[3072,128]{1,0:T(8,128)(2,1)}, u32[]{:S(2)}, u32[]{:S(2)}) %collective-permute-start.55) | collective-permute-done | bytes 786464 | tf_op jit(solution)/shard_map/ppermute | solution.py:1220
  643.4 9.0 %collective-permute-done.57 = f16[1216,384]{1,0:T(8,128)(2,1)} collective-permute-done((f16[1216,384]{1,0:T(8,128)(2,1)}, f16[1216,384]{1,0:T(8,128)(2,1)}, u32[]{:S(2)}, u32[]{:S(2)}) %collective-permute-start.57) | collective-permute-done | bytes 933920 | tf_op jit(solution)/shard_map/ppermute | solution.py:1220
  659.1 11.6 %collective-permute-done.52 = f16[1216,384]{1,0:T(8,128)(2,1)S(1)} collective-permute-done((f16[1216,384]{1,0:T(8,128)(2,1)}, f16[1216,384]{1,0:T(8,128)(2,1)S(1)}, u32[]{:S(2)}, u32[]{:S(2)}) %collective-permute-start.52) | collective-permute-done | bytes 933920 | tf_op jit(solution)/shard_map/ppermute | solution.py:1220
  693.3 7.5 fusion.3.refs_4_
  701.6 27.2 %scatter_rows.1 = (f32[192,6288]{1,0:T(8,128)}, f32[1,1]{1,0:T(1,128)}) custom-call(s32[4112]{0:T(1024)} %find_hits.2.list_ref.refs_0_, s32[4112]{0:T(1024)} %copy-done.35, s32[4112]{0:T(1024)} %find_hits.3.list_ref.refs_2_, s32[4112]{0:T(1024)} %copy-done.36, f32[192,6400]{1,0:T(8,128)} %fusion.3.refs_4_, ...), custom_call_target="tpu_custom_call" | custom-call | flops 300000000 | bytes 193167 | tf_op jit(solution)/shard_map/scatter_rows/pallas_call | solution.py:278
  739.8 6.9 collective-permute-start.62
  757.7 6.2 collective-permute-start.69
  763.9 16.9 %collective-permute-done.64 = f32[8,128]{1,0:T(8,128)S(1)} collective-permute-done((f32[8,128]{1,0:T(8,128)S(1)}, f32[8,128]{1,0:T(8,128)S(1)}, u32[]{:S(2)}, u32[]{:S(2)}) %collective-permute-start.64) | collective-permute-done | bytes 4128 | tf_op jit(solution)/shard_map/ppermute | solution.py:1220
  783.0 12.2 %fusion.22 = (f32[6288,192]{0,1:T(8,128)}, f32[6288,192]{0,1:T(8,128)}, f32[6288,192]{0,1:T(8,128)}) fusion(f32[192,6288]{1,0:T(8,128)} %get-tuple-element.185, f32[]{:T(128)} %div.104, f32[6288,192]{0,1:T(8,128)} %param.49, f32[]{:T(128)} %bitcast.126, f32[]{:T(128)} %bitcast.124, f32[6288,192]{0,1:T(8,128)} %param.48, f32[6288,192]{0,1:T(8,128)} %param.47), kind=kLoop, calls=%fused_computation.75 | loop fusion | flops 19316736 | bytes 33804300 | tf_op jit(solution)/shard_map/transpose | solution.py:1593
  810.0 5.5 collective-permute-done.68
  816.7 10.1 %collective-permute-done.70 = f16[688,384]{1,0:T(8,128)(2,1)S(1)} collective-permute-done((f16[688,384]{1,0:T(8,128)(2,1)}, f16[688,384]{1,0:T(8,128)(2,1)S(1)}, u32[]{:S(2)}, u32[]{:S(2)}) %collective-permute-start.70) | collective-permute-done | bytes 528416 | tf_op jit(solution)/shard_map/ppermute | solution.py:1220
  828.0 5.1 collective-permute-done.72
  846.3 34.4 %shampoo.1 = (f32[12,384,384]{2,1,0:T(8,128)}, f32[12,384,384]{2,1,0:T(8,128)}, f32[12,384,384]{2,1,0:T(8,128)}, f32[12,384,384]{2,1,0:T(8,128)}) custom-call(s32[8]{0:T(128)} %stack.255.places_ref, f32[1]{0:T(128)} %bitcast.107.clip_ref, f32[14,48,384]{2,1,0:T(8,128)} %copy-done.6, f32[14,48,384]{2,1,0:T(8,128)} %bitcast.254, f32[14,48,384]{2,1,0:T(8,128)} %bitcast.255, ...), custom_call_target="tpu_custom_call" | custom-call | flops 326149088 | bytes 1415577 | tf_op jit(solution)/shard_map/shampoo/pallas_call | solution.py:1120
  (458 shorter events, 251.0 us)
Async XLA Ops:
  3.3 19.0 %collective-permute-start.5 = (bf16[192,6288]{1,0:T(8,128)(2,1)S(1)}, bf16[192,6288]{1,0:T(8,128)(2,1)}, u32[]{:S(2)}, u32[]{:S(2)}) collective-permute-start(bf16[192,6288]{1,0:T(8,128)(2,1)S(1)} %bitcast_convert_fusion.own_ref.refs_0_), channel_id=1, source_target_pairs={{0,8},{8,0},{16,24},{24,16},{1,9},{9,1},{17,25},{25,17},{2,10},{10... | collective-permute-start | bytes 7243784 | tf_op jit(solution)/shard_map/ppermute | solution.py:1214
  10.3 79.0 %collective-permute-start.10 = (bf16[12,384,384]{2,1,0:T(8,128)(2,1)}, bf16[12,384,384]{2,1,0:T(8,128)(2,1)}, u32[]{:S(2)}, u32[]{:S(2)}) collective-permute-start(bf16[12,384,384]{2,1,0:T(8,128)(2,1)} %convert_element_type.195.refs_0_), channel_id=1, source_target_pairs={{0,16},{8,24},{16,0},{24,8},{1,17},{9,25},{17,1},{25,9},{2,18},{10... | collective-permute-start | bytes 10616840 | tf_op jit(solution)/shard_map/ppermute | solution.py:1214
  50.1 34.7 %collective-permute-start.8 = (bf16[2048,384]{1,0:T(8,128)(2,1)}, bf16[2048,384]{1,0:T(8,128)(2,1)S(1)}, u32[]{:S(2)}, u32[]{:S(2)}) collective-permute-start(bf16[2048,384]{1,0:T(8,128)(2,1)} %get-tuple-element.109), channel_id=1, source_target_pairs={{0,1},{1,0},{2,3},{3,2},{4,5},{5,4},{6,7},{7,6},{8,9},{9,8},{10,11... | collective-permute-start | bytes 4718600 | tf_op jit(solution)/shard_map/ppermute | solution.py:1220
  89.3 11.5 %collective-permute-start.11 = (bf16[12,384,384]{2,1,0:T(8,128)(2,1)}, bf16[12,384,384]{2,1,0:T(8,128)(2,1)S(1)}, u32[]{:S(2)}, u32[]{:S(2)}) collective-permute-start(bf16[12,384,384]{2,1,0:T(8,128)(2,1)} %convert_element_type.195.refs_0_), channel_id=1, source_target_pairs={{0,8},{8,0},{16,24},{24,16},{1,9},{9,1},{17,25},{25,17},{2,10},{10... | collective-permute-start | bytes 10616840 | tf_op jit(solution)/shard_map/ppermute | solution.py:1214
  89.3 11.6 %collective-permute-start.12 = (bf16[12,384,384]{2,1,0:T(8,128)(2,1)}, bf16[12,384,384]{2,1,0:T(8,128)(2,1)}, u32[]{:S(2)}, u32[]{:S(2)}) collective-permute-start(bf16[12,384,384]{2,1,0:T(8,128)(2,1)} %collective-permute-done.10.refs_1_), channel_id=1, source_target_pairs={{0,8},{8,0},{16,24},{24,16},{1,9},{9,1},{17,25},{25,17},{2,10},{10... | collective-permute-start | bytes 10616840 | tf_op jit(solution)/shard_map/ppermute | solution.py:1214
  89.8 36.6 %collective-permute-start.9 = (bf16[2048,384]{1,0:T(8,128)(2,1)}, bf16[2048,384]{1,0:T(8,128)(2,1)}, u32[]{:S(2)}, u32[]{:S(2)}) collective-permute-start(bf16[2048,384]{1,0:T(8,128)(2,1)} %get-tuple-element.110), channel_id=1, source_target_pairs={{0,1},{1,0},{2,3},{3,2},{4,5},{5,4},{6,7},{7,6},{8,9},{9,8},{10,11... | collective-permute-start | bytes 4718600 | tf_op jit(solution)/shard_map/ppermute | solution.py:1220
  93.8 54.4 %collective-permute-start.13 = (bf16[2,512,384]{2,1,0:T(8,128)(2,1)}, bf16[2,512,384]{2,1,0:T(8,128)(2,1)}, u32[]{:S(2)}, u32[]{:S(2)}) collective-permute-start(bf16[2,512,384]{2,1,0:T(8,128)(2,1)} %bitcast.275), channel_id=1, source_target_pairs={{0,6},{1,7},{2,0},{3,1},{4,2},{5,3},{6,4},{7,5},{8,14},{9,15},{10,... | collective-permute-start | bytes 2359304 | tf_op jit(solution)/shard_map/ppermute | solution.py:1220
  94.2 54.0 %collective-permute-start.14 = (bf16[2,512,384]{2,1,0:T(8,128)(2,1)}, bf16[2,512,384]{2,1,0:T(8,128)(2,1)}, u32[]{:S(2)}, u32[]{:S(2)}) collective-permute-start(bf16[2,512,384]{2,1,0:T(8,128)(2,1)} %bitcast.276), channel_id=1, source_target_pairs={{0,4},{1,5},{2,6},{3,7},{4,0},{5,1},{6,2},{7,3},{8,12},{9,13},{10,... | collective-permute-start | bytes 2359304 | tf_op jit(solution)/shard_map/ppermute | solution.py:1220
  128.9 35.2 %collective-permute-start.15 = (bf16[2,512,384]{2,1,0:T(8,128)(2,1)S(1)}, bf16[2,512,384]{2,1,0:T(8,128)(2,1)S(1)}, u32[]{:S(2)}, u32[]{:S(2)}) collective-permute-start(bf16[2,512,384]{2,1,0:T(8,128)(2,1)S(1)} %bitcast.277), channel_id=1, source_target_pairs={{0,2},{1,3},{2,4},{3,5},{4,6},{5,7},{6,0},{7,1},{8,10},{9,11},{10,... | collective-permute-start | bytes 2359304 | tf_op jit(solution)/shard_map/ppermute | solution.py:1220
  167.3 10.8 %collective-permute-start.16 = (bf16[512,384]{1,0:T(8,128)(2,1)}, bf16[512,384]{1,0:T(8,128)(2,1)}, u32[]{:S(2)}, u32[]{:S(2)}) collective-permute-start(bf16[512,384]{1,0:T(8,128)(2,1)} %slice_bitcast_fusion), channel_id=1, source_target_pairs={{0,16},{8,24},{16,0},{24,8},{1,17},{9,25},{17,1},{25,9},{2,18},{10... | collective-permute-start | bytes 1179656 | tf_op jit(solution)/shard_map/ppermute | solution.py:1214
  180.3 54.5 %collective-permute-start.24 = (bf16[192,6288]{1,0:T(8,128)(2,1)S(1)}, bf16[192,6288]{1,0:T(8,128)(2,1)}, u32[]{:S(2)}, u32[]{:S(2)}) collective-permute-start(bf16[192,6288]{1,0:T(8,128)(2,1)S(1)} %copy-done.3), channel_id=1, source_target_pairs={{0,16},{8,24},{16,0},{24,8},{1,17},{9,25},{17,1},{25,9},{2,18},{10... | collective-permute-start | bytes 7243784 | tf_op jit(solution)/shard_map/ppermute | solution.py:1214
  234.8 35.5 %collective-permute-start.25 = (bf16[192,6288]{1,0:T(8,128)(2,1)}, bf16[192,6288]{1,0:T(8,128)(2,1)S(1)}, u32[]{:S(2)}, u32[]{:S(2)}) collective-permute-start(bf16[192,6288]{1,0:T(8,128)(2,1)} %collective-permute-done.24.refs_1_), channel_id=1, source_target_pairs={{0,8},{8,0},{16,24},{24,16},{1,9},{9,1},{17,25},{25,17},{2,10},{10... | collective-permute-start | bytes 7243784 | tf_op jit(solution)/shard_map/ppermute | solution.py:1214
  235.9 16.2 %collective-permute-start.18 = (bf16[64,768]{0,1:T(8,128)(2,1)S(1)}, bf16[64,768]{0,1:T(8,128)(2,1)S(1)}, u32[]{:S(2)}, u32[]{:S(2)}) collective-permute-start(bf16[64,768]{0,1:T(8,128)(2,1)S(1)} %copy.77), channel_id=1, source_target_pairs={{0,2},{1,3},{2,4},{3,5},{4,6},{5,7},{6,0},{7,1},{8,10},{9,11},{10,... | collective-permute-start | bytes 294920 | tf_op jit(solution)/shard_map/ppermute | solution.py:1220
  238.4 17.5 %collective-permute-start.20 = (bf16[64,768]{0,1:T(8,128)(2,1)S(1)}, bf16[64,768]{0,1:T(8,128)(2,1)S(1)}, u32[]{:S(2)}, u32[]{:S(2)}) collective-permute-start(bf16[64,768]{0,1:T(8,128)(2,1)S(1)} %copy.77), channel_id=1, source_target_pairs={{0,4},{1,5},{2,6},{3,7},{4,0},{5,1},{6,2},{7,3},{8,12},{9,13},{10,... | collective-permute-start | bytes 294920 | tf_op jit(solution)/shard_map/ppermute | solution.py:1220
  238.4 17.6 %collective-permute-start.22 = (bf16[64,768]{0,1:T(8,128)(2,1)S(1)}, bf16[64,768]{0,1:T(8,128)(2,1)S(1)}, u32[]{:S(2)}, u32[]{:S(2)}) collective-permute-start(bf16[64,768]{0,1:T(8,128)(2,1)S(1)} %copy.77), channel_id=1, source_target_pairs={{0,6},{1,7},{2,0},{3,1},{4,2},{5,3},{6,4},{7,5},{8,14},{9,15},{10,... | collective-permute-start | bytes 294920 | tf_op jit(solution)/shard_map/ppermute | solution.py:1220
  240.7 18.8 %collective-permute-start.17 = (bf16[64,768]{0,1:T(8,128)(2,1)S(1)}, bf16[64,768]{0,1:T(8,128)(2,1)S(1)}, u32[]{:S(2)}, u32[]{:S(2)}) collective-permute-start(bf16[64,768]{0,1:T(8,128)(2,1)S(1)} %copy.77), channel_id=1, source_target_pairs={{0,1},{1,0},{2,3},{3,2},{4,5},{5,4},{6,7},{7,6},{8,9},{9,8},{10,11... | collective-permute-start | bytes 294920 | tf_op jit(solution)/shard_map/ppermute | solution.py:1220
  256.0 10.7 %collective-permute-start.23 = (bf16[64,768]{0,1:T(8,128)(2,1)S(1)}, bf16[64,768]{0,1:T(8,128)(2,1)}, u32[]{:S(2)}, u32[]{:S(2)}) collective-permute-start(bf16[64,768]{0,1:T(8,128)(2,1)S(1)} %collective-permute-done.22), channel_id=1, source_target_pairs={{0,1},{1,0},{2,3},{3,2},{4,5},{5,4},{6,7},{7,6},{8,9},{9,8},{10,11... | collective-permute-start | bytes 294920 | tf_op jit(solution)/shard_map/ppermute | solution.py:1220
  320.7 9.5 %collective-permute-start.30 = (f32[64,768]{1,0:T(8,128)S(1)}, f32[64,768]{1,0:T(8,128)S(1)}, u32[]{:S(2)}, u32[]{:S(2)}) collective-permute-start(f32[64,768]{1,0:T(8,128)S(1)} %get-tuple-element.263), channel_id=1, source_target_pairs={{0,1},{1,0},{2,3},{3,2},{4,5},{5,4},{6,7},{7,6},{8,9},{9,8},{10,11... | collective-permute-start | bytes 589832 | tf_op jit(solution)/shard_map/ppermute | solution.py:1220
  343.0 60.4 %collective-permute-start.33 = (f32[384,6400]{1,0:T(8,128)}, f32[384,6400]{1,0:T(8,128)}, u32[]{:S(2)}, u32[]{:S(2)}) collective-permute-start(f32[384,6400]{1,0:T(8,128)} %get-tuple-element.131), channel_id=1, source_target_pairs={{0,8},{8,0},{16,24},{24,16},{1,9},{9,1},{17,25},{25,17},{2,10},{10... | collective-permute-start | bytes 29491208 | tf_op jit(solution)/shard_map/ppermute | solution.py:1214
  343.9 17.4 %collective-permute-start.38 = (f32[64,768]{1,0:T(8,128)S(1)}, f32[64,768]{1,0:T(8,128)S(1)}, u32[]{:S(2)}, u32[]{:S(2)}) collective-permute-start(f32[64,768]{1,0:T(8,128)S(1)} %get-tuple-element.265), channel_id=1, source_target_pairs={{0,4},{1,5},{2,6},{3,7},{4,0},{5,1},{6,2},{7,3},{8,12},{9,13},{10,... | collective-permute-start | bytes 589832 | tf_op jit(solution)/shard_map/ppermute | solution.py:1220
  346.8 17.5 %collective-permute-start.37 = (f32[64,768]{1,0:T(8,128)S(1)}, f32[64,768]{1,0:T(8,128)S(1)}, u32[]{:S(2)}, u32[]{:S(2)}) collective-permute-start(f32[64,768]{1,0:T(8,128)S(1)} %get-tuple-element.266), channel_id=1, source_target_pairs={{0,6},{1,7},{2,0},{3,1},{4,2},{5,3},{6,4},{7,5},{8,14},{9,15},{10,... | collective-permute-start | bytes 589832 | tf_op jit(solution)/shard_map/ppermute | solution.py:1220
  348.0 16.3 %collective-permute-start.36 = (f32[64,768]{1,0:T(8,128)S(1)}, f32[64,768]{1,0:T(8,128)S(1)}, u32[]{:S(2)}, u32[]{:S(2)}) collective-permute-start(f32[64,768]{1,0:T(8,128)S(1)} %get-tuple-element.260), channel_id=1, source_target_pairs={{0,1},{1,0},{2,3},{3,2},{4,5},{5,4},{6,7},{7,6},{8,9},{9,8},{10,11... | collective-permute-start | bytes 589832 | tf_op jit(solution)/shard_map/ppermute | solution.py:1220
  392.2 38.1 %collective-permute-start.40 = (f32[16,384,384]{2,1,0:T(8,128)}, f32[16,384,384]{2,1,0:T(8,128)}, u32[]{:S(2)}, u32[]{:S(2)}) collective-permute-start(f32[16,384,384]{2,1,0:T(8,128)} %get-tuple-element.143), channel_id=1, source_target_pairs={{0,8},{8,0},{16,24},{24,16},{1,9},{9,1},{17,25},{25,17},{2,10},{10... | collective-permute-start | bytes 28311560 | tf_op jit(solution)/shard_map/ppermute | solution.py:1214
  409.5 87.0 %collective-permute-start.35 = (f16[192,6400]{1,0:T(8,128)(2,1)}, f16[192,6400]{1,0:T(8,128)(2,1)}, u32[]{:S(2)}, u32[]{:S(2)}) collective-permute-start(f16[192,6400]{1,0:T(8,128)(2,1)} %fusion.7), channel_id=1, source_target_pairs={{0,16},{8,24},{16,0},{24,8},{1,17},{9,25},{17,1},{25,9},{2,18},{10... | collective-permute-start | bytes 7372808 | tf_op jit(solution)/shard_map/ppermute | solution.py:1214
  442.6 53.8 %collective-permute-start.42 = (f16[3088,384]{1,0:T(8,128)(2,1)}, f16[3088,384]{1,0:T(8,128)(2,1)}, u32[]{:S(2)}, u32[]{:S(2)}) collective-permute-start(f16[3088,384]{1,0:T(8,128)(2,1)} %concatenate.140), channel_id=1, source_target_pairs={{0,1},{1,0},{2,3},{3,2},{4,5},{5,4},{6,7},{7,6},{8,9},{9,8},{10,11... | collective-permute-start | bytes 7114760 | tf_op jit(solution)/shard_map/ppermute | solution.py:1220
  474.3 10.9 %collective-permute-start.43 = (bf16[512,384]{1,0:T(8,128)(2,1)S(1)}, bf16[512,384]{1,0:T(8,128)(2,1)S(1)}, u32[]{:S(2)}, u32[]{:S(2)}) collective-permute-start(bf16[512,384]{1,0:T(8,128)(2,1)S(1)} %fusion.25), channel_id=1, source_target_pairs={{0,16},{8,24},{16,0},{24,8},{1,17},{9,25},{17,1},{25,9},{2,18},{10... | collective-permute-start | bytes 1179656 | tf_op jit(solution)/shard_map/ppermute | solution.py:1214
  518.9 32.3 %collective-permute-start.47 = (f16[1744,384]{1,0:T(8,128)(2,1)S(1)}, f16[1744,384]{1,0:T(8,128)(2,1)S(1)}, u32[]{:S(2)}, u32[]{:S(2)}) collective-permute-start(f16[1744,384]{1,0:T(8,128)(2,1)S(1)} %concatenate.146), channel_id=1, source_target_pairs={{0,1},{1,0},{2,3},{3,2},{4,5},{5,4},{6,7},{7,6},{8,9},{9,8},{10,11... | collective-permute-start | bytes 4018184 | tf_op jit(solution)/shard_map/ppermute | solution.py:1220
  519.5 43.5 %collective-permute-start.48 = (bf16[3072,128]{1,0:T(8,128)(2,1)}, bf16[3072,128]{1,0:T(8,128)(2,1)}, u32[]{:S(2)}, u32[]{:S(2)}) collective-permute-start(bf16[3072,128]{1,0:T(8,128)(2,1)} %maximum_maximum_fusion.refs_12_), channel_id=1, source_target_pairs={{0,2},{1,3},{2,4},{3,5},{4,6},{5,7},{6,0},{7,1},{8,10},{9,11},{10,... | collective-permute-start | bytes 2359304 | tf_op jit(solution)/shard_map/ppermute | solution.py:1220
  519.5 68.0 %collective-permute-start.49 = (bf16[3072,128]{1,0:T(8,128)(2,1)}, bf16[3072,128]{1,0:T(8,128)(2,1)}, u32[]{:S(2)}, u32[]{:S(2)}) collective-permute-start(bf16[3072,128]{1,0:T(8,128)(2,1)} %maximum_maximum_fusion.refs_12_), channel_id=1, source_target_pairs={{0,4},{1,5},{2,6},{3,7},{4,0},{5,1},{6,2},{7,3},{8,12},{9,13},{10,... | collective-permute-start | bytes 2359304 | tf_op jit(solution)/shard_map/ppermute | solution.py:1220
  520.1 68.5 %collective-permute-start.50 = (bf16[3072,128]{1,0:T(8,128)(2,1)}, bf16[3072,128]{1,0:T(8,128)(2,1)}, u32[]{:S(2)}, u32[]{:S(2)}) collective-permute-start(bf16[3072,128]{1,0:T(8,128)(2,1)} %maximum_maximum_fusion.refs_12_), channel_id=1, source_target_pairs={{0,6},{1,7},{2,0},{3,1},{4,2},{5,3},{6,4},{7,5},{8,14},{9,15},{10,... | collective-permute-start | bytes 2359304 | tf_op jit(solution)/shard_map/ppermute | solution.py:1220
  522.1 66.5 %collective-permute-start.51 = (bf16[3072,128]{1,0:T(8,128)(2,1)}, bf16[3072,128]{1,0:T(8,128)(2,1)}, u32[]{:S(2)}, u32[]{:S(2)}) collective-permute-start(bf16[3072,128]{1,0:T(8,128)(2,1)} %maximum_maximum_fusion.refs_12_), channel_id=1, source_target_pairs={{0,1},{1,0},{2,3},{3,2},{4,5},{5,4},{6,7},{7,6},{8,9},{9,8},{10,11... | collective-permute-start | bytes 2359304 | tf_op jit(solution)/shard_map/ppermute | solution.py:1220
  588.5 63.9 %collective-permute-start.57 = (f16[1216,384]{1,0:T(8,128)(2,1)}, f16[1216,384]{1,0:T(8,128)(2,1)}, u32[]{:S(2)}, u32[]{:S(2)}) collective-permute-start(f16[1216,384]{1,0:T(8,128)(2,1)} %concatenate.150), channel_id=1, source_target_pairs={{0,6},{1,7},{2,0},{3,1},{4,2},{5,3},{6,4},{7,5},{8,14},{9,15},{10,... | collective-permute-start | bytes 2801672 | tf_op jit(solution)/shard_map/ppermute | solution.py:1220
  588.5 65.8 %collective-permute-start.56 = (f16[1216,384]{1,0:T(8,128)(2,1)}, f16[1216,384]{1,0:T(8,128)(2,1)}, u32[]{:S(2)}, u32[]{:S(2)}) collective-permute-start(f16[1216,384]{1,0:T(8,128)(2,1)} %concatenate.149), channel_id=1, source_target_pairs={{0,4},{1,5},{2,6},{3,7},{4,0},{5,1},{6,2},{7,3},{8,12},{9,13},{10,... | collective-permute-start | bytes 2801672 | tf_op jit(solution)/shard_map/ppermute | solution.py:1220
  590.9 20.8 %collective-permute-start.53 = (bf16[3072,128]{1,0:T(8,128)(2,1)}, bf16[3072,128]{1,0:T(8,128)(2,1)}, u32[]{:S(2)}, u32[]{:S(2)}) collective-permute-start(bf16[3072,128]{1,0:T(8,128)(2,1)} %collective-permute-done.48.refs_9_), channel_id=1, source_target_pairs={{0,1},{1,0},{2,3},{3,2},{4,5},{5,4},{6,7},{7,6},{8,9},{9,8},{10,11... | collective-permute-start | bytes 2359304 | tf_op jit(solution)/shard_map/ppermute | solution.py:1220
  592.4 36.1 %collective-permute-start.54 = (bf16[3072,128]{1,0:T(8,128)(2,1)}, bf16[3072,128]{1,0:T(8,128)(2,1)}, u32[]{:S(2)}, u32[]{:S(2)}) collective-permute-start(bf16[3072,128]{1,0:T(8,128)(2,1)} %collective-permute-done.49.refs_10_), channel_id=1, source_target_pairs={{0,1},{1,0},{2,3},{3,2},{4,5},{5,4},{6,7},{7,6},{8,9},{9,8},{10,11... | collective-permute-start | bytes 2359304 | tf_op jit(solution)/shard_map/ppermute | solution.py:1220
  592.9 50.5 %collective-permute-start.55 = (bf16[3072,128]{1,0:T(8,128)(2,1)}, bf16[3072,128]{1,0:T(8,128)(2,1)}, u32[]{:S(2)}, u32[]{:S(2)}) collective-permute-start(bf16[3072,128]{1,0:T(8,128)(2,1)} %collective-permute-done.50.refs_11_), channel_id=1, source_target_pairs={{0,1},{1,0},{2,3},{3,2},{4,5},{5,4},{6,7},{7,6},{8,9},{9,8},{10,11... | collective-permute-start | bytes 2359304 | tf_op jit(solution)/shard_map/ppermute | solution.py:1220
  611.7 59.0 %collective-permute-start.52 = (f16[1216,384]{1,0:T(8,128)(2,1)}, f16[1216,384]{1,0:T(8,128)(2,1)S(1)}, u32[]{:S(2)}, u32[]{:S(2)}) collective-permute-start(f16[1216,384]{1,0:T(8,128)(2,1)} %concatenate.148), channel_id=1, source_target_pairs={{0,2},{1,3},{2,4},{3,5},{4,6},{5,7},{6,0},{7,1},{8,10},{9,11},{10,... | collective-permute-start | bytes 2801672 | tf_op jit(solution)/shard_map/ppermute | solution.py:1220
  693.0 35.9 %collective-permute-start.59 = (f16[688,384]{1,0:T(8,128)(2,1)S(1)}, f16[688,384]{1,0:T(8,128)(2,1)S(1)}, u32[]{:S(2)}, u32[]{:S(2)}) collective-permute-start(f16[688,384]{1,0:T(8,128)(2,1)S(1)} %concatenate.156), channel_id=1, source_target_pairs={{0,16},{8,24},{16,0},{24,8},{1,17},{9,25},{17,1},{25,9},{2,18},{10... | collective-permute-start | bytes 1585160 | tf_op jit(solution)/shard_map/ppermute | solution.py:1214
  739.8 11.4 %collective-permute-start.62 = (f32[8,128]{1,0:T(8,128)S(1)}, f32[8,128]{1,0:T(8,128)S(1)}, u32[]{:S(2)}, u32[]{:S(2)}) collective-permute-start(f32[8,128]{1,0:T(8,128)S(1)} %select_reduce_fusion.2), channel_id=1, source_target_pairs={{0,1},{1,0},{2,3},{3,2},{4,5},{5,4},{6,7},{7,6},{8,9},{9,8},{10,11... | collective-permute-start | bytes 12296 | tf_op jit(solution)/shard_map/ppermute | solution.py:1220
  747.8 47.5 %collective-permute-start.66 = (f16[688,384]{1,0:T(8,128)(2,1)}, f16[688,384]{1,0:T(8,128)(2,1)S(1)}, u32[]{:S(2)}, u32[]{:S(2)}) collective-permute-start(f16[688,384]{1,0:T(8,128)(2,1)} %concatenate.158), channel_id=1, source_target_pairs={{0,1},{1,0},{2,3},{3,2},{4,5},{5,4},{6,7},{7,6},{8,9},{9,8},{10,11... | collective-permute-start | bytes 1585160 | tf_op jit(solution)/shard_map/ppermute | solution.py:1220
  747.8 48.7 %collective-permute-start.67 = (f16[688,384]{1,0:T(8,128)(2,1)}, f16[688,384]{1,0:T(8,128)(2,1)}, u32[]{:S(2)}, u32[]{:S(2)}) collective-permute-start(f16[688,384]{1,0:T(8,128)(2,1)} %concatenate.158), channel_id=1, source_target_pairs={{0,2},{1,3},{2,4},{3,5},{4,6},{5,7},{6,0},{7,1},{8,10},{9,11},{10,... | collective-permute-start | bytes 1585160 | tf_op jit(solution)/shard_map/ppermute | solution.py:1220
  751.8 29.0 %collective-permute-start.64 = (f32[8,128]{1,0:T(8,128)S(1)}, f32[8,128]{1,0:T(8,128)S(1)}, u32[]{:S(2)}, u32[]{:S(2)}) collective-permute-start(f32[8,128]{1,0:T(8,128)S(1)} %select_reduce_fusion.1), channel_id=1, source_target_pairs={{0,4},{1,5},{2,6},{3,7},{4,0},{5,1},{6,2},{7,3},{8,12},{9,13},{10,... | collective-permute-start | bytes 12296 | tf_op jit(solution)/shard_map/ppermute | solution.py:1220
  753.7 27.4 %collective-permute-start.63 = (f32[8,128]{1,0:T(8,128)S(1)}, f32[8,128]{1,0:T(8,128)S(1)}, u32[]{:S(2)}, u32[]{:S(2)}) collective-permute-start(f32[8,128]{1,0:T(8,128)S(1)} %select_reduce_fusion.1), channel_id=1, source_target_pairs={{0,2},{1,3},{2,4},{3,5},{4,6},{5,7},{6,0},{7,1},{8,10},{9,11},{10,... | collective-permute-start | bytes 12296 | tf_op jit(solution)/shard_map/ppermute | solution.py:1220
  757.7 40.7 %collective-permute-start.69 = (f16[688,384]{1,0:T(8,128)(2,1)}, f16[688,384]{1,0:T(8,128)(2,1)}, u32[]{:S(2)}, u32[]{:S(2)}) collective-permute-start(f16[688,384]{1,0:T(8,128)(2,1)} %concatenate.158), channel_id=1, source_target_pairs={{0,4},{1,5},{2,6},{3,7},{4,0},{5,1},{6,2},{7,3},{8,12},{9,13},{10,... | collective-permute-start | bytes 1585160 | tf_op jit(solution)/shard_map/ppermute | solution.py:1220
  780.8 23.1 %collective-permute-start.71 = (f16[688,384]{1,0:T(8,128)(2,1)}, f16[688,384]{1,0:T(8,128)(2,1)}, u32[]{:S(2)}, u32[]{:S(2)}) collective-permute-start(f16[688,384]{1,0:T(8,128)(2,1)} %concatenate.158), channel_id=1, source_target_pairs={{0,6},{1,7},{2,0},{3,1},{4,2},{5,3},{6,4},{7,5},{8,14},{9,15},{10,... | collective-permute-start | bytes 1585160 | tf_op jit(solution)/shard_map/ppermute | solution.py:1220
  800.3 15.2 %collective-permute-start.68 = (f16[688,384]{1,0:T(8,128)(2,1)}, f16[688,384]{1,0:T(8,128)(2,1)S(1)}, u32[]{:S(2)}, u32[]{:S(2)}) collective-permute-start(f16[688,384]{1,0:T(8,128)(2,1)} %collective-permute-done.67), channel_id=1, source_target_pairs={{0,1},{1,0},{2,3},{3,2},{4,5},{5,4},{6,7},{7,6},{8,9},{9,8},{10,11... | collective-permute-start | bytes 1585160 | tf_op jit(solution)/shard_map/ppermute | solution.py:1220
  802.1 24.8 %collective-permute-start.70 = (f16[688,384]{1,0:T(8,128)(2,1)}, f16[688,384]{1,0:T(8,128)(2,1)S(1)}, u32[]{:S(2)}, u32[]{:S(2)}) collective-permute-start(f16[688,384]{1,0:T(8,128)(2,1)} %collective-permute-done.69), channel_id=1, source_target_pairs={{0,1},{1,0},{2,3},{3,2},{4,5},{5,4},{6,7},{7,6},{8,9},{9,8},{10,11... | collective-permute-start | bytes 1585160 | tf_op jit(solution)/shard_map/ppermute | solution.py:1220
  804.0 29.1 %collective-permute-start.72 = (f16[688,384]{1,0:T(8,128)(2,1)}, f16[688,384]{1,0:T(8,128)(2,1)S(1)}, u32[]{:S(2)}, u32[]{:S(2)}) collective-permute-start(f16[688,384]{1,0:T(8,128)(2,1)} %collective-permute-done.71), channel_id=1, source_target_pairs={{0,1},{1,0},{2,3},{3,2},{4,5},{5,4},{6,7},{7,6},{8,9},{9,8},{10,11... | collective-permute-start | bytes 1585160 | tf_op jit(solution)/shard_map/ppermute | solution.py:1220
  (75 other events, 925.6 us)

commit v3 on v2

--- a/solution.py
+++ b/solution.py
@@ -154,7 +154,7 @@
     own, other = own_ref[...].astype(f32), other_ref[...].astype(f32)
     depth = own.shape[0]
     both = jnp.concatenate([jnp.where(first, own, other), jnp.where(first, other, own)], 0)
-    out_ref[...] = both.T[:, : 2 * depth].astype(bf16)
+    out_ref[...] = both.T
 
 
 def turn_table(core, own, other):
@@ -164,7 +164,7 @@
     return pl.pallas_call(
         turn_kernel,
         grid=(pl.cdiv(rows_all, wide),),
-        out_shape=jax.ShapeDtypeStruct((rows_all, 2 * depth), bf16),
+        out_shape=jax.ShapeDtypeStruct((rows_all, 2 * depth), f32),
         in_specs=[pl.BlockSpec(memory_space=SMEM), block, block],
         out_specs=pl.BlockSpec((wide, 2 * depth), lambda j: (j, 0)),
         name="turn_table",
@@ -172,25 +172,41 @@
     )(core, own, other)
 
 
+def in_chunks(count, size, body):
+    def go(i, carry):
+        body(pl.multiple_of(i * size, size))
+        return carry
+
+    lax.fori_loop(0, count // size, go, 0)
+
+
 def lookup_kernel(rows_all, list_ref, table_ref, *refs):
-    outs, (tab, acc) = refs[:-2], refs[-2:]
+    outs, acc = refs[:-1], refs[-1]
     total = acc.shape[0] - 8
-    tab[pl.ds(0, rows_all), :] = table_ref[...].astype(f32)
-    tab[pl.ds(rows_all, 8), :] = jnp.zeros((8, tab.shape[1]), f32)
-    acc[...] = jnp.zeros(acc.shape, f32)
+    chunk = 128
+
+    def clear(start):
+        acc[pl.ds(start, chunk), :] = jnp.zeros((chunk, acc.shape[1]), f32)
+
+    in_chunks(total, chunk, clear)
 
     def go(i, carry):
         for u in range(8):
             entry = list_ref[i * 8 + u]
             row = entry >> 16
             place = jnp.where(row < rows_all, entry & 0xFFFF, total)
-            acc[pl.ds(place, 1), :] = tab[pl.ds(row, 1), :]
+            row = jnp.minimum(row, rows_all - 1)
+            acc[pl.ds(place, 1), :] = table_ref[pl.ds(row, 1), :]
         return carry
 
     lax.fori_loop(0, (list_ref[total + 8] + 7) // 8, go, 0)
     each = outs[0].shape[0]
     for part, out in enumerate(outs):
-        out[...] = acc[pl.ds(part * each, each), :].astype(bf16)
+
+        def keep(start, part=part, out=out):
+            out[pl.ds(start, chunk), :] = acc[pl.ds(part * each + start, chunk), :].astype(bf16)
+
+        in_chunks(each, chunk, keep)
 
 
 def lookup(hit_list, table, count, parts):
@@ -203,10 +219,7 @@
             pl.BlockSpec(memory_space=pltpu.VMEM),
         ],
         out_specs=[pl.BlockSpec(memory_space=pltpu.VMEM)] * parts,
-        scratch_shapes=[
-            pltpu.VMEM((rows_all + 8, width), f32),
-            pltpu.VMEM((count + 8, width), f32),
-        ],
+        scratch_shapes=[pltpu.VMEM((count + 8, width), f32)],
         name="lookup",
         cost_estimate=cost(1e10, rows_all * width * 2),
     )(hit_list, table)
@@ -218,11 +231,25 @@
     lex_ref = refs[used]
     pieces = refs[used + 1 : used + 1 + piece_count]
     out_ref, square_ref, acc, tail, wide, pair = refs[used + 1 + piece_count :]
-    acc[...] = jnp.zeros(acc.shape, f32)
-    tail[...] = jnp.zeros(tail.shape, f32)
+    chunk = 128
+
+    def clear(start):
+        acc[pl.ds(start, chunk), :] = jnp.zeros((chunk, 128), f32)
+        tail[pl.ds(start, chunk), :] = jnp.zeros((chunk, 128), f32)
+
+    in_chunks(acc.shape[0], chunk, clear)
     for k in range(piece_count):
-        wide[pl.ds(k * 2 * half, 2 * half), :] = pieces[k][pl.ds(0, 2 * half), :].astype(f32)
-        pair[pl.ds(k * half, half), :] = pieces[k][pl.ds(2 * half, half), :].astype(f32)
+
+        def widen(start, k=k):
+            values = pieces[k][pl.ds(start, chunk), :].astype(f32)
+            wide[pl.ds(k * 2 * half + start, chunk), :] = values
+
+        def widen_pair(start, k=k):
+            values = pieces[k][pl.ds(2 * half + start, chunk), :].astype(f32)
+            pair[pl.ds(k * half + start, chunk), :] = values
+
+        in_chunks(2 * half, chunk, widen)
+        in_chunks(half, chunk, widen_pair)
     upper = lax.broadcasted_iota(i32, (1, 128), 1) >= 64
     for which, (side, start) in enumerate(starts):
         own = upper if side else ~upper
@@ -1093,13 +1120,21 @@
 
 
 def shampoo_kernel(count, strip, places_ref, clip_ref, *refs):
-    pieces = refs[:count]
-    w_ref, ls_ref, rs_ref, lr_ref, rr_ref = refs[count : count + 5]
-    g_ref, nw_ref, nl_ref, nr_ref = refs[count + 5 :]
+    pieces, smalls, tails = refs[:count], refs[count : 2 * count], refs[2 * count : 3 * count]
+    w_ref, ls_ref, rs_ref, lr_ref, rr_ref = refs[3 * count : 3 * count + 5]
+    g_ref, nw_ref, nl_ref, nr_ref, small_ref = refs[3 * count + 5 :]
     clip = clip_ref[0]
     for k in range(count):
         place = pl.multiple_of(places_ref[k], strip)
-        g_ref[0, pl.ds(place, strip), :] = pieces[k][0] * clip
+        scale = jnp.exp2(tails[k][0:1, :] - 15.0) * clip
+        g_ref[0, pl.ds(place, strip), :] = pieces[k][...] * scale
+
+        @pl.when(pl.program_id(0) == 0)
+        def _(k=k, place=place, scale=scale):
+            for side in range(2):
+                values = smalls[k][pl.ds(side * strip, strip), :] * scale
+                small_ref[side, pl.ds(place, strip), :] = values
+
     grads = split_two(g_ref[0])
     for old, new, product in ((ls_ref, nl_ref, mm_t), (rs_ref, nr_ref, mm_l)):
         cross = product(grads[0], grads[1])
@@ -1111,23 +1146,25 @@
     nw_ref[0] = weights - RATE_BLOCKS * (direction + DECAY_RATE * weights)
 
 
-def shampoo(places, clip, pieces, weights, left_stats, right_stats, left_roots, right_roots):
-    slots = weights.shape[0]
+def shampoo(places, clip, pieces, strip, kept):
+    slots = kept[0].shape[0]
     count = len(pieces)
-    strip = pieces[0].shape[1]
     block = pl.BlockSpec((1, BS, BS), lambda s: (s, 0, 0))
     shape = jax.ShapeDtypeStruct((slots, BS, BS), f32)
+    small_at, tail_at = slots // 2, (slots + 2) * strip // 16
     return pl.pallas_call(
         partial(shampoo_kernel, count, strip),
         grid=(slots,),
-        out_shape=[shape] * 4,
+        out_shape=[shape] * 4 + [jax.ShapeDtypeStruct((2, BS, BS), f32)],
         in_specs=[pl.BlockSpec(memory_space=SMEM)] * 2
-        + [pl.BlockSpec((1, strip, BS), lambda s: (s, 0, 0))] * count
+        + [pl.BlockSpec((strip, BS), lambda s: (s, 0))] * count
+        + [pl.BlockSpec((2 * strip, BS), lambda s: (small_at, 0))] * count
+        + [pl.BlockSpec((16, BS), lambda s: (tail_at, 0))] * count
         + [block] * 5,
-        out_specs=[block] * 4,
+        out_specs=[block] * 4 + [full((2, BS, BS))],
         name="shampoo",
         cost_estimate=cost(slots * 24 * BS**3, slots * BS * BS * 40),
-    )(places, clip, *pieces, weights, left_stats, right_stats, left_roots, right_roots)
+    )(places, clip, *pieces, *pieces, *pieces, *kept)
 
 
 def adam_update(weight, first, second, gradient, rate, step_value):
@@ -1162,9 +1199,11 @@
 
 
 def unpack(payload, shape):
-    level = payload[-1, 0].astype(f32)
-    values = payload[:-16].reshape(shape).astype(f32) * jnp.exp2(level - 15.0)
-    return values, jnp.exp2(level)
+    count = payload.shape[0] - 16
+    wide = payload.astype(f32)
+    level = wide[count : count + 1]
+    values = wide[:count] * jnp.exp2(level - 15.0)
+    return values.reshape(shape), jnp.exp2(payload[-1, 0].astype(f32))
 
 
 def pack_lanes(values, bound):
@@ -1267,10 +1306,11 @@
     slots_y = gather_y(tie(slot_weights.astype(bf16), numbers))
     numbers = gather_stacked(numbers)
     targets_all = numbers[:, :, ny * tokens :].reshape(-1)
-    piece_order = [(a, b) for b in list(range(1, n0)) + [0] for a in list(range(1, n1)) + [0]]
+    lines = sorted(range(1, n1), key=lambda a: -min(a, n1 - a)) + [0]
+    piece_order = [(a, b) for b in list(range(1, n0)) + [0] for a in lines]
     early = (n0 - 1) * n1
     ids_order = [numbers[a, b, : ny * tokens] for a, b in piece_order]
-    halves, hits = [], []
+    looked, hits = [], []
     for first, last in ((0, early), (early, n0 * n1)):
         ids_rows = jnp.concatenate(ids_order[first:last])
         local_ids = ids_rows - vocab_start
@@ -1280,17 +1320,19 @@
             -1,
         )
         hits.append(find_hits(tie(packed_ids, upright), shard_rows))
-        halves += lookup(hits[-1], upright, ids_rows.shape[0], 2 * (last - first) // n1)
-
-    def near_half(h, *before):
-        part = halves[2 * (n0 - 1) + h]
+        looked += lookup(hits[-1], upright, ids_rows.shape[0], last - first)
+
+    def near_piece(h, sums, *before):
+        part = looked[n1 * (n0 - 1) + h]
         for b in range(1, n0):
-            moved = over_voc(tie(halves[2 * (b - 1) + h], *before[:1]), 0, -b)
-            part = part + tie(moved, *before)
-        return [line for line in part.reshape(n1 // 2, ny, tokens, cols_y)]
-
-    by_one = near_half(0)
-    slots_y = [tie(part, by_one[0]) for part in slots_y]
+            moved = over_voc(tie(looked[(b - 1) * n1 + h], *sums[: max(h - 1, 0)]), 0, -b)
+            part = part + tie(moved, *sums, *before)
+        return part.reshape(ny, tokens, cols_y)
+
+    by_one = []
+    for h in range(n1 - 1):
+        by_one.append(near_piece(h, by_one))
+    slots_y = [tie(part, by_one[1]) for part in slots_y]
     slots_core = [over_dp(part, 0, 1) for part in slots_y]
     inverse = (
         jnp.zeros((block_count,), i32).at[block_order].set(jnp.arange(block_count, dtype=i32))
@@ -1301,11 +1343,12 @@
         src.astype(i32), inverse % per_owner, slots_y + slots_core
     )
 
-    by_one = by_one + near_half(1, by_one[0], wup)
-    far_parts = [over_voc(by_one[a - 1], -a, 0) for a in range(1, n1)]
+    far_parts = [over_voc(by_one[h], -lines[h], 0) for h in range(n1 - 1)]
+    by_one.append(near_piece(n1 - 1, by_one, wup, far_parts[0]))
     mine = by_one[-1]
     for part in far_parts:
         mine = mine + part
+
     row_parts = [mine[0]] + [over_dp(mine[k], -k, 0) for k in range(1, ny)]
     if ny == 2:
         first = y_at == 0
@@ -1340,10 +1383,13 @@
     y, distill = attend(seq_lengths, mixed, lift_maps)
     x1, h2, up, act, x2, picked = mlp_forward(x0, y, wo, wup, wdown, vectors, pick_rows)
 
-    low_y = [tie(part, picked) for part in low_y]
+    near_picked = [picked] + [over_voc(picked, 0, k) for k in range(1, n0)]
+    low_y = [tie(part, *near_picked) for part in low_y]
     low_y_other = [over_dp(part, 0, 1) for part in low_y]
     pieces = [low_own] + low_y + [low_other] + low_y_other
-    group = jnp.concatenate(flat_gather(picked), 0)
+    near_picked = jnp.concatenate(near_picked, 0)
+    group = [near_picked] + [over_voc(near_picked, k, 0) for k in range(1, n1)]
+    group = jnp.concatenate(group, 0)
     local_targets = targets_all - vocab_start
     logits, stats = vocabulary_logits(piece_places, group, local_targets, pieces)
     stats_all = gather_stacked(stats)
@@ -1390,25 +1436,39 @@
     def core_parts(mine_part, their_part, mine_top, their_top, *later):
         arrived = tie(over_dp(their_part, 0, 1), *later)
         bound = jnp.max(mine_top) + jnp.max(over_dp(their_top, 0, 1))
-        return coded_parts((mine_part, arrived), bound, False) + (bound,)
-
-    def coded_parts(parts, bound, far):
-        size, at = (n1, i1) if far else (n0, i0)
-        rows = parts[0].shape[1] // size
-
-        def lines(k):
-            cut = [
-                lax.dynamic_slice_in_dim(part, ((at + k) % size) * rows, rows, 1) for part in parts
-            ]
+        return coded_parts((mine_part, arrived), bound, 0) + (bound,)
+
+    def coded_parts(parts, bound, axis):
+        size = (n0, ny, n1)[axis]
+
+        def lines(part, k):
+            count = part.shape[0]
+            if axis == 1:
+                rows = part.reshape(count, n1, ny, -1, BS)
+                rows = lax.dynamic_index_in_dim(rows, (y_at + k) % ny, 2, False)
+                return rows.reshape(count, -1, BS)
+            rows = part.shape[1] // size
+            at = (i0 if axis == 0 else i1) + k
+            return lax.dynamic_slice_in_dim(part, (at % size) * rows, rows, 1)
+
+        def summed(k):
+            cut = [lines(part, k) for part in parts]
             return sum(cut[1:], cut[0])
 
-        return lines(0), [pack(lines(k), bound) for k in range(1, size)]
-
-    def exchange(own, sent, bound, far, *later):
+        return summed(0), [pack(summed(k), bound) for k in range(1, size)]
+
+    def moved_parts(sent, axis):
+        if axis == 1:
+            return [over_dp(part, k, 0) for k, part in enumerate(sent, 1)]
+        return [
+            over_voc(part, k, 0) if axis == 2 else over_voc(part, 0, k)
+            for k, part in enumerate(sent, 1)
+        ]
+
+    def collect(own, arrived, bound, *later):
         total, high = own, bound
-        for k, coded in enumerate(sent, 1):
-            d1, d0 = (k, 0) if far else (0, k)
-            values, top = unpack(tie(over_voc(coded, d1, d0), *later), own.shape)
+        for part in arrived:
+            values, top = unpack(tie(part, *later), own.shape)
             total = total + values
             high = high + top
         return total, high
@@ -1416,20 +1476,15 @@
     *halves_a, gx1, ga, gy, vg_a = mlp_back(
         core, ghp, pick_rows, x2, act, up, h2, x1, wdown, wup, wo, vectors
     )
-    half_pairs = PAIRS // 2
-    gy = tie(gy, *lex_sent)
-    gqkv, map_q_a, map_k_a = attend_back(
-        seq_lengths, mixed, gy, lift_maps, coefficient, 0, half_pairs, None
-    )
-    own_a, sent_a, bound_a = core_parts(*halves_a, gqkv)
-    gy = tie(gy, own_a, *sent_a)
-    gqkv, map_q_b, map_k_b = attend_back(
-        seq_lengths, mixed, gy, lift_maps, coefficient, half_pairs, half_pairs, gqkv
+    own_a, sent_a, bound_a = core_parts(*halves_a, *lex_sent)
+    gy = tie(gy, *lex_sent, own_a, *sent_a)
+    gqkv, map_q, map_k = attend_back(
+        seq_lengths, mixed, gy, lift_maps, coefficient, 0, PAIRS, None
     )
     lex_parts = [over_dp(part, -k, 0) for k, part in enumerate(lex_sent, 1)]
     gx0, vg_b = qkv_back(gqkv, wqkv, x0, gx1, vectors)
 
-    map_grads = jnp.concatenate([map_q_a, map_q_b, map_k_a, map_k_b], 0)
+    map_grads = jnp.concatenate([map_q, map_k], 0)
     vec_grads = (vg_a + vg_b)[:15]
     small_count = map_grads.size + vec_grads.size
     small = jnp.concatenate(
@@ -1441,13 +1496,17 @@
     ).reshape(2, BS, BS)
     gx0_cols = gx0.reshape(tokens, ny, cols_y)
     cols_sent = [jnp.take(gx0_cols, (y_at + k) % ny, axis=1) for k in range(1, ny)]
+    lex = lex_lines(0)
+    for part in lex_parts:
+        lex = lex + unpack_lanes(part)
     arrived = [jnp.take(gx0_cols, y_at, axis=1)] + [
-        over_dp(part, k, 0) for k, part in enumerate(cols_sent, 1)
+        tie(over_dp(part, k, 0), lex) for k, part in enumerate(cols_sent, 1)
     ]
     arrived = jnp.concatenate(arrived, 0).reshape(ny * tokens, nc, cols_own)
     rows_mine = jnp.take(arrived, c_at, axis=1)
-    moved_a = [over_voc(part, 0, k) for k, part in enumerate(sent_a, 1)]
-    rows_other = over_dp(jnp.take(arrived, (c_at + 1) % nc, axis=1), 0, 1)
+    moved_a = moved_parts(sent_a, 0)
+    rows_sent = jnp.take(arrived, (c_at + 1) % nc, axis=1)
+    rows_other = over_dp(rows_sent, 0, 1)
     if cols_own == 192:
         packed = jnp.concatenate(
             [
@@ -1459,52 +1518,22 @@
         )
     else:
         packed = jnp.stack([rows_mine, rows_other])
-    halves_b = qkv_weights(core, tie(h1, packed, *moved_a, *lex_parts), gqkv, y, ga, small)
-    total_a, high_a = own_a, bound_a
-    for part in moved_a:
-        values, top = unpack(tie(part, halves_b[0]), own_a.shape)
-        total_a, high_a = total_a + values, high_a + top
+    halves_b = qkv_weights(core, tie(h1, rows_sent, *moved_a), gqkv, y, ga, small)
+    total_a, high_a = collect(own_a, moved_a, bound_a, halves_b[0])
     own_b, sent_b, bound_b = core_parts(*halves_b, packed)
-    total_b, high_b = exchange(own_b, sent_b, bound_b, False)
+    near_raw = [over_voc(packed, k, 0) for k in range(1, n1)]
+    total_b, high_b = collect(own_b, moved_parts(sent_b, 0), bound_b, near_raw[0])
     total = jnp.concatenate([total_a, total_b], 0)
     high = jnp.maximum(high_a, high_b)
-    own, sent = coded_parts((total,), high, True)
-    near_rows = [packed] + [tie(over_voc(packed, k, 0), *sent) for k in range(1, n1)]
+    own, sent = coded_parts((total,), high, 1)
+    near_rows = [packed] + [tie(part, *sent) for part in near_raw]
+    total, high = collect(own, moved_parts(sent, 1), high)
+    own, sent = coded_parts((total,), high, 2)
     gathered = [[packed] + [over_voc(packed, 0, k) for k in range(1, n0)]]
     sent = [tie(part, *near_rows, *gathered[0]) for part in sent]
     gathered += [[part] + [over_voc(part, 0, k) for k in range(1, n0)] for part in near_rows[1:]]
-    blocks = exchange(own, sent, high, True, *(line[-1] for line in gathered))[0]
-
-    per_side = blocks.shape[0]
-    both = jnp.concatenate([blocks, over_dp(blocks, 0, 1)], 0)
-    side, place = comm_positions()
-    side = jnp.concatenate([jnp.take(jnp.asarray(side), block_order), jnp.arange(2, dtype=i32)])
-    place = jnp.concatenate(
-        [jnp.take(jnp.asarray(place), block_order), jnp.full((2,), per_side - 1, i32)]
-    )
-    at_place = ((side - c_at) % nc) * per_side + place
-    smalls = at_place[block_count:]
-    at_place = at_place[:block_count].reshape(ny, nc, per_owner)
-
-    def slots_of(k):
-        mine = jnp.take(jnp.take(at_place, c_at, axis=1), (y_at + k) % ny, axis=0)
-        return jnp.take(both, jnp.concatenate([mine, smalls]), axis=0)
-
-    own_slots = slots_of(0)
-    strips, small_parts = own_slots[:per_owner], []
-    strip_rows = own_slots.shape[1]
-    tail = own_slots[per_owner:]
-    values, _ = unpack(pack(tail, jnp.max(jnp.abs(own_slots))), tail.shape)
-    small_parts.append(values)
-    slots_sent = []
-    for k in range(1, ny):
-        moved = slots_of(k)
-        high = jnp.maximum(jnp.max(jnp.abs(moved)), jnp.max(jnp.abs(own_slots)))
-        slots_sent.append(pack(moved, high))
-    lex = lex_lines(0)
-    for part in lex_parts:
-        lex = lex + unpack_lanes(part)
-    lex = tie(lex, *slots_sent)
+    moved_ab = moved_parts(sent, 2)
+    lex = tie(lex, moved_ab[0])
     if cols_own == 192:
         pieces = [gathered[a][b] for a, b in piece_order]
         emb_grads, emb_square = scatter_rows(
@@ -1518,68 +1547,80 @@
         local = jnp.where((local >= 0) & (local < shard_rows), local, shard_rows)
         emb_grads = lex[:, :shard_rows].T.at[local].add(pieces.astype(f32), mode="drop").T
         emb_square = jnp.sum(emb_grads * emb_grads)
-
-    for k, sent in enumerate(slots_sent, 1):
-        moved, _ = unpack(over_dp(sent, k, 0), own_slots.shape)
-        strips = strips + moved[:per_owner]
-        small_parts.append(moved[per_owner:])
-    if ny == 2:
-        small_sum = small_parts[0] + small_parts[1]
-    else:
-        small_sum = jnp.sum(line_up(small_parts, y_at), 0)
-    own_strips = jnp.concatenate([strips, small_sum], 0)
-    coded_all = flat_gather(pack(own_strips, jnp.max(jnp.abs(own_strips))))
-    strip_pieces = [unpack(part, own_strips.shape)[0] for part in coded_all]
-
-    square = emb_square + jnp.sum(strips * strips)
-    square = square + jnp.where(dp_index == 0, jnp.sum(small_sum * small_sum), 0.0)
+    blocks = collect(own, moved_ab, high, emb_grads)[0]
+
+    square = emb_square + jnp.sum(blocks * blocks)
     sums = jnp.pad(jnp.stack([square, loss_part]).reshape(1, 2), ((0, 7), (0, 126)))
     sums = sums + over_dp(sums, 0, 1)
     sums = jnp.sum(line_up(gather_y(sums), y_at), 0)
+    per_side = blocks.shape[0]
+    both = jnp.concatenate([blocks, over_dp(blocks, 0, 1)], 0)
+    side, place = comm_positions()
+    side = jnp.concatenate([jnp.take(jnp.asarray(side), block_order), jnp.arange(2, dtype=i32)])
+    place = jnp.concatenate(
+        [jnp.take(jnp.asarray(place), block_order), jnp.full((2,), per_side - 1, i32)]
+    )
+    at_place = ((side - c_at) % nc) * per_side + place
+    smalls = at_place[block_count:]
+    at_place = at_place[:block_count].reshape(ny, nc, per_owner)
+
+    def slots_of(k):
+        mine = jnp.take(jnp.take(at_place, c_at, axis=1), (y_at + k) % ny, axis=0)
+        return jnp.take(both, jnp.concatenate([mine, smalls]), axis=0)
+
+    moved = [slots_of(k) for k in range(1, ny)]
+    slots_sent = [pack(part, jnp.max(jnp.abs(both))) for part in moved]
+    sums = tie(sums, *slots_sent)
     sums = jnp.sum(line_up([sums] + [over_voc(sums, 0, k) for k in range(1, n0)], i0), 0)
+
+    small_own = unpack(slots_sent[0], moved[0].shape)[0][per_owner:]
+    strip_parts = [jnp.concatenate([slots_of(0)[:per_owner], small_own], 0)]
+    slots_moved = moved_parts(slots_sent, 1)
+    sums = tie(sums, *slots_moved)
+    for part in slots_moved:
+        strip_parts.append(unpack(part, moved[0].shape)[0])
     sums = jnp.sum(line_up([sums] + [over_voc(sums, k, 0) for k in range(1, n1)], i1), 0)
     grad_norm = jnp.sqrt(sums[0, 0])
     loss_total = sums[0, 1]
     clip_scale = CLIP_NORM / jnp.maximum(grad_norm, CLIP_NORM)
-
-    small_all = jnp.stack([part[per_owner:] for part in strip_pieces])
-    small_all = small_all.reshape(n1, n0, 2, strip_rows, BS)
-    small_all = jnp.take(small_all, (i1 - jnp.arange(n1)) % n1, axis=0)
-    small_all = jnp.take(small_all, (i0 - jnp.arange(n0)) % n0, axis=1)
-    small_all = small_all.transpose(2, 1, 0, 3, 4).reshape(-1)
-    map_sum = small_all[: map_grads.size].reshape(feature_maps.shape)
-    vec_sum = small_all[map_grads.size : small_count].reshape(vectors.shape)
-
+    own_strips = line_up(strip_parts, y_at).transpose(1, 0, 2, 3)
+    own_strips = own_strips.reshape(per_owner + 2, -1, BS)
+    strip_rows = own_strips.shape[1]
+    strip_half = BS // n0
     places = [
-        ((i0 - b) % n0) * (BS // n0) + ((i1 - a) % n1) * strip_rows
+        ((i0 - b) % n0) * strip_half + ((i1 - a) % n1) * strip_rows
         for a in range(n1)
         for b in range(n0)
     ]
     places = jnp.stack(places).astype(i32)
-    clipped, new_slots, new_left, new_right = shampoo(
+    strip_sent = tie(pack(own_strips, jnp.max(jnp.abs(own_strips))), sums)
+    strip_pieces = [part.astype(f32) for part in flat_gather(strip_sent)]
+    clipped, new_slots, new_left, new_right, small_all = shampoo(
         places,
         clip_scale.reshape(1),
         strip_pieces,
-        slot_weights,
-        left_stats,
-        right_stats,
-        left_roots,
-        right_roots,
-    )
+        strip_rows,
+        (slot_weights, left_stats, right_stats, left_roots, right_roots),
+    )
+    clip_late = tie(clip_scale, strip_sent)
+    small_all = small_all.reshape(-1)
+    map_grad = small_all[: map_grads.size].reshape(feature_maps.shape)
+    vec_grad = small_all[map_grads.size : small_count].reshape(vectors.shape)
+
     step_value = step_count[0].astype(f32)
     emb_out = adam_update(
         table_own,
         embedding_first_moment.T,
         emb_second.T,
-        emb_grads * clip_scale,
+        emb_grads * clip_late,
         RATE_TABLE,
         step_value,
     )
     vec_out = adam_update(
-        vectors, vec_first, vec_second, vec_sum * clip_scale, RATE_VECTORS, step_value
+        vectors, vec_first, vec_second, vec_grad, RATE_VECTORS, step_value
     )
     map_out = adam_update(
-        feature_maps, map_first, map_second, map_sum * clip_scale, RATE_MAPS, step_value
+        feature_maps, map_first, map_second, map_grad, RATE_MAPS, step_value
     )
     return (
         loss_total,

time: 893 us -> 829 us (0.928)
  waiting for transfers between devices: 315 us -> 265 us
  between operations: 25.5 us -> 16.5 us
    ppermute x50 -> x49, waiting for transfers between devices: 268 us -> 237 us  [over_voc(): return lax.ppermute(values, 'vocab', pairs)]
    ppermute x23 -> x24, waiting for transfers between devices: 46.3 us -> 28.3 us  [over_dp(): return lax.ppermute(values, 'dp', pairs)]
    convert_element_type x0 -> x16, other arithmetic: none -> 13.5 us  [the longest x8 8.47 us: per_device(): strip_pieces = [part.astype(f32) for part in flat_gather(strip_sent)]]
    ppermute x50 -> x49, starting transfers between devices: 76.2 us -> 70.8 us  [over_voc(): return lax.ppermute(values, 'vocab', pairs)]
    pallas_call x2 -> x1, Pallas kernels: 38.4 us -> 35.9 us  [attend_back(): pl.pallas_call(partial(attend_back_kernel, coefficient, int(later)), grid...]
  transfers between devices with their start and end apart: 73 -> 73, of which waited for: 43 -> 37; matrix products, arithmetic and copies ran while one was open for 13% -> 14% of each run, Pallas kernels for 23% -> 25%
where the time goes in v3:
time: 829 us; the launch traced here: 822 us
  Pallas kernels  291 us (35%)
  waiting for transfers between devices  265 us (32%)
  other arithmetic  114 us (14%)
  starting transfers between devices  82.9 us (10%)
  local copies, waits for them, and re-layouts  52.4 us (6%)
  between operations  16.5 us (2%)
    ppermute x49, waiting for transfers between devices, over_voc(): return lax.ppermute(values, 'vocab', pairs)  237 us
    ppermute x49, starting transfers between devices, over_voc(): return lax.ppermute(values, 'vocab', pairs)  70.8 us
    pallas_call x1, Pallas kernels, attend_back(): pl.pallas_call(partial(attend_back_kernel, coefficient, int(later)), grid...  35.9 us
    pallas_call x1, Pallas kernels, shampoo(): pl.pallas_call(partial(shampoo_kernel, count, strip), grid=(slots,), out_...  35.3 us
    ppermute x24, waiting for transfers between devices, over_dp(): return lax.ppermute(values, 'dp', pairs)  28.3 us
    pallas_call x1, Pallas kernels, scatter_rows(): pl.pallas_call(partial(scatter_kernel, count, half, rows_all, tuple(start...  27.9 us
    pallas_call x1, Pallas kernels, mlp_back(): pl.pallas_call(mlp_back_kernel, grid=(FSTEPS,), out_shape=[halves, halves...  26.2 us
    pallas_call x2, Pallas kernels, find_hits(): pl.pallas_call(partial(hits_kernel, empty_row), out_shape=jax.ShapeDtypeS...  25.5 us
  transfers between devices with their start and end apart: 73, of which 37 were waited for; matrix products, arithmetic and copies ran while one was open for 14% of the time, Pallas kernels for 25%

profile of v3, /device:TPU:8, one launch (start us, length us, event | category | flops | bytes accessed | tf_op | source)
XLA Modules:
  0.0 822.0 jit_solution(11134037113143626367)
XLA Ops:
  5.0 5.3 convert_element_type.146.refs_0_
  16.8 4.4 collective-permute-start.2
  23.6 7.4 turn_table.1.table_ref
  31.0 12.8 %find_hits.2.list_ref.refs_0_ = s32[4112]{0:T(1024)} custom-call(s32[4096]{0:T(1024)} %get-tuple-element.114.packed_ref), custom_call_target="tpu_custom_call" | custom-call | flops 200000000 | bytes 655 | tf_op jit(solution)/shard_map/find_hits/pallas_call | solution.py:142
  43.8 9.6 %lookup.3 = (bf16[1024,384]{1,0:T(8,128)(2,1)}, bf16[1024,384]{1,0:T(8,128)(2,1)}, bf16[1024,384]{1,0:T(8,128)(2,1)}, bf16[1024,384]{1,0:T(8,128)(2,1)}) custom-call(s32[4112]{0:T(1024)} %find_hits.2.list_ref.refs_0_, f32[6288,384]{1,0:T(8,128)} %turn_table.1.table_ref), custom_call_target="tpu_custom_call" | custom-call | flops 200000000 | bytes 96583 | tf_op jit(solution)/shard_map/lookup/pallas_call | solution.py:214
  55.4 12.8 %find_hits.3.list_ref.refs_2_ = s32[4112]{0:T(1024)} custom-call(s32[4096]{0:T(1024)} %get-tuple-element.115.packed_ref), custom_call_target="tpu_custom_call" | custom-call | flops 200000000 | bytes 655 | tf_op jit(solution)/shard_map/find_hits/pallas_call | solution.py:142
  68.1 9.6 %lookup.2 = (bf16[1024,384]{1,0:T(8,128)(2,1)}, bf16[1024,384]{1,0:T(8,128)(2,1)}, bf16[1024,384]{1,0:T(8,128)(2,1)}, bf16[1024,384]{1,0:T(8,128)(2,1)}) custom-call(s32[4112]{0:T(1024)} %find_hits.3.list_ref.refs_2_, f32[6288,384]{1,0:T(8,128)} %turn_table.1.table_ref), custom_call_target="tpu_custom_call" | custom-call | flops 200000000 | bytes 96583 | tf_op jit(solution)/shard_map/lookup/pallas_call | solution.py:214
  80.1 6.7 collective-permute-done.9
  94.4 15.6 %collective-permute-done.11 = bf16[1024,384]{1,0:T(8,128)(2,1)S(1)} collective-permute-done((bf16[1024,384]{1,0:T(8,128)(2,1)S(1)}, bf16[1024,384]{1,0:T(8,128)(2,1)S(1)}, u32[]{:S(2)}, u32[]{:S(2)}) %collective-permute-start.11) | collective-permute-done | bytes 786464 | tf_op jit(solution)/shard_map/ppermute | solution.py:1259
  119.1 11.5 %place_blocks.1 = (bf16[768,2304]{1,0:T(8,128)(2,1)}, bf16[768,768]{1,0:T(8,128)(2,1)}, bf16[768,3072]{1,0:T(8,128)(2,1)}, bf16[3072,768]{1,0:T(8,128)(2,1)}) custom-call(s32[48]{0:T(128)} %get-tuple-element.332.src_ref, s32[48]{0:T(128)} %get-tuple-element.331.off_ref, bf16[12,384,384]{2,1,0:T(8,128)(2,1)} %convert_element_type.146.refs_0_, ...), custom_call_target="tpu_custom_call" | custom-call | bytes 566231 | tf_op jit(solution)/shard_map/place_blocks/pallas_call | solution.py:110
  130.6 15.3 %collective-permute-done.15 = bf16[2,512,384]{2,1,0:T(8,128)(2,1)} collective-permute-done((bf16[2,512,384]{2,1,0:T(8,128)(2,1)}, bf16[2,512,384]{2,1,0:T(8,128)(2,1)}, u32[]{:S(2)}, u32[]{:S(2)}) %collective-permute-start.15) | collective-permute-done | bytes 786464 | tf_op jit(solution)/shard_map/ppermute | solution.py:1259
  147.4 15.2 %collective-permute-done.17 = bf16[2,512,384]{2,1,0:T(8,128)(2,1)} collective-permute-done((bf16[2,512,384]{2,1,0:T(8,128)(2,1)}, bf16[2,512,384]{2,1,0:T(8,128)(2,1)}, u32[]{:S(2)}, u32[]{:S(2)}) %collective-permute-start.17) | collective-permute-done | bytes 786464 | tf_op jit(solution)/shard_map/ppermute | solution.py:1259
  167.0 10.6 %collective-permute-done.18 = bf16[512,384]{1,0:T(8,128)(2,1)} collective-permute-done((bf16[512,384]{1,0:T(8,128)(2,1)}, bf16[512,384]{1,0:T(8,128)(2,1)}, u32[]{:S(2)}, u32[]{:S(2)}) %collective-permute-start.18) | collective-permute-done | bytes 393248 | tf_op jit(solution)/shard_map/ppermute | solution.py:1253
  182.8 6.2 qkv_forward.1
  188.9 20.0 %attend.1 = (bf16[512,768]{1,0:T(8,128)(2,1)}, f32[8,128]{1,0:T(8,128)}) custom-call(s32[1,4]{1,0:T(1,128)} %len_ref.3, bf16[512,2304]{1,0:T(8,128)(2,1)} %get-tuple-element.135.q_ref.k_ref.v_ref, bf16[512,2304]{1,0:T(8,128)(2,1)} %get-tuple-element.135.q_ref.k_ref.v_ref, bf16[512,2304]{1,0:T(8,128)(2,1)} %get-tuple-element.135.q_ref.k_ref.v_ref, ...), custom_call_target="tpu_custom_call" | custom-call | flops 240000000 | bytes 80000 | tf_op jit(solution)/shard_map/attend/pallas_call | solution.py:463
  208.9 14.8 %mlp_forward.1 = (f32[512,768]{1,0:T(8,128)}, bf16[512,768]{1,0:T(8,128)(2,1)}, f32[512,3072]{1,0:T(8,128)}, bf16[512,3072]{1,0:T(8,128)(2,1)}, f32[512,768]{1,0:T(8,128)}, /*index=5*/bf16[64,768]{1,0:T(8,128)(2,1)}) custom-call(bf16[512,768]{1,0:T(8,128)(2,1)} %pad_maximum_fusion.4.x_ref, bf16[512,768]{1,0:T(8,128)(2,1)} %get-tuple-element.136.y_ref, ...), custom_call_target="tpu_custom_call" | custom-call | flops 108716360 | bytes 600000 | tf_op jit(solution)/shard_map/mlp_forward/pallas_call | solution.py:661
  226.3 5.4 collective-permute-done.19
  236.9 3.8 collective-permute-start.21
  244.1 10.3 %collective-permute-done.21 = bf16[128,768]{0,1:T(8,128)(2,1)S(1)} collective-permute-done((bf16[128,768]{0,1:T(8,128)(2,1)S(1)}, bf16[128,768]{0,1:T(8,128)(2,1)S(1)}, u32[]{:S(2)}, u32[]{:S(2)}) %collective-permute-start.21) | collective-permute-done | bytes 196640 | tf_op jit(solution)/shard_map/ppermute | solution.py:1259
  262.0 15.9 %vocabulary_logits.1 = (f32[512,6288]{1,0:T(8,128)}, f32[8,512]{1,0:T(8,128)}) custom-call(s32[4]{0:T(128)} %pad_add_fusion.5.places_ref, bf16[512,768]{1,0:T(8,128)(2,1)} %copy.70.group_ref, s32[512,1]{1,0:T(8,128)} %sub.272.target_ref, bf16[192,6288]{1,0:T(8,128)(2,1)} %copy-done.2, bf16[192,6288]{1,0:T(8,128)(2,1)} %collective-permute-done.23.refs_1_, ...), custom_call_target="tpu_custom_call" | custom-call | flops 98901688 | bytes 400000 | tf_op jit(solution)/shard_map/vocabulary_logits/pallas_call | solution.py:1006
  290.4 15.3 %vocabulary_back.1 = (bf16[512,6400]{1,0:T(8,128)(2,1)}, f32[512,768]{1,0:T(8,128)}) custom-call(s32[4]{0:T(128)} %pad_add_fusion.5.places_ref, f32[512,6288]{1,0:T(8,128)} %get-tuple-element.142.logit_ref, f32[128,512]{1,0:T(8,128)} %select_maximum_fusion.stat_ref, s32[512,1]{1,0:T(8,128)} %sub.272.target_ref, bf16[192,6288]{1,0:T(8,128)(2,1)} %copy-done.2, ...), custom_call_target="tpu_custom_call" | custom-call | flops 98901688 | bytes 600000 | tf_op jit(solution)/shard_map/vocabulary_back/pallas_call | solution.py:1049
  310.6 4.3 collective-permute-done.31
  321.0 11.6 %lexicon.1 = (f32[384,6400]{1,0:T(8,128)}, f32[384,6400]{1,0:T(8,128)}, f32[1,1280]{1,0:T(1,128)}, f32[1,1280]{1,0:T(1,128)}) custom-call(s32[4]{0:T(128)} %pad_add_fusion.5.places_ref, bf16[768,512]{1,0:T(8,128)(2,1)} %bitcast.222, bf16[512,6400]{1,0:T(8,128)(2,1)} %get-tuple-element.146.grad_ref), custom_call_target="tpu_custom_call" | custom-call | flops 100663296 | bytes 600000 | tf_op jit(solution)/shard_map/lexicon/pallas_call | solution.py:1095
  340.4 10.6 %collective-permute-done.37 = f32[64,768]{1,0:T(8,128)S(1)} collective-permute-done((f32[64,768]{1,0:T(8,128)S(1)}, f32[64,768]{1,0:T(8,128)S(1)}, u32[]{:S(2)}, u32[]{:S(2)}) %collective-permute-start.37) | collective-permute-done | bytes 196640 | tf_op jit(solution)/shard_map/ppermute | solution.py:1259
  355.3 26.2 %mlp_back.1 = (f32[16,384,384]{2,1,0:T(8,128)}, f32[16,384,384]{2,1,0:T(8,128)}, f32[1,384]{1,0:T(1,128)}, f32[1,384]{1,0:T(1,128)}, f32[512,768]{1,0:T(8,128)},...) custom-call(s32[1]{0:T(128)} %bitcast.8.core_ref, f32[64,768]{1,0:T(8,128)} %fusion.20.ghp_ref, ...), custom_call_target="tpu_custom_call" | custom-call | flops 193273536 | bytes 1000000 | tf_op jit(solution)/shard_map/mlp_back/pallas_call | solution.py:801
  382.9 4.3 collective-permute-done.33
  392.5 6.1 fusion.8
  399.8 10.3 %multiply_convert_fusion = (f16[16,192,384]{2,1,0:T(8,128)(2,1)S(1)}, f32[16,192,384]{2,1,0:T(8,128)}) fusion(f32[16,384,384]{2,1,0:T(8,128)} %collective-permute-done.39, s32[]{:T(128)S(6)} %select_n.372, f32[16,384,384]{2,1,0:T(8,128)} %get-tuple-element.159, f32[]{:T(128)S(6)} %exp2.140, s32[]{:T(128)S(6)} %select_n.370), kind=kLoop, calls=%fused_computation.25 | loop fusion | flops 4718592 | bytes 25952268 | tf_op jit(solution)/shard_map/convert_element_type | solution.py:1192
  413.1 35.9 %attend_back.1 = (bf16[3,512,768]{2,1,0:T(8,128)(2,1)}, f32[12,64,64]{2,1,0:T(8,128)}, f32[12,64,64]{2,1,0:T(8,128)}) custom-call(s32[1,4]{1,0:T(1,128)} %len_ref.3, bf16[512,2304]{1,0:T(8,128)(2,1)} %get-tuple-element.135.q_ref.k_ref.v_ref, bf16[512,2304]{1,0:T(8,128)(2,1)} %get-tuple-element.135.q_ref.k_ref.v_ref, ...), custom_call_target="tpu_custom_call" | custom-call | flops 240000000 | bytes 80000 | tf_op jit(solution)/shard_map/attend_back/pallas_call | solution.py:575
  448.9 7.9 qkv_back.1
  466.3 7.5 fusion.3.refs_4_
  474.5 10.1 %qkv_weights.1 = (f32[9,384,384]{2,1,0:T(8,128)}, f32[9,384,384]{2,1,0:T(8,128)}, f32[1,384]{1,0:T(1,128)}, f32[1,384]{1,0:T(1,128)}) custom-call(s32[1]{0:T(128)} %bitcast.8.core_ref, bf16[512,768]{1,0:T(8,128)(2,1)} %get-tuple-element.171.h_ref, bf16[3,512,768]{2,1,0:T(8,128)(2,1)} %get-tuple-element.167.g_ref, bf16[512,768]{1,0:T(8,128)(2,1)} %get-tuple-element.136.y_ref, ...), custom_call_target="tpu_custom_call" | custom-call | flops 48318384 | bytes 400000 | tf_op jit(solution)/shard_map/qkv_weights/pallas_call | solution.py:917
  486.9 5.3 collective-permute-done.45
  507.3 13.8 %collective-permute-done.47.refs_10_ = bf16[3072,128]{1,0:T(8,128)(2,1)S(1)} collective-permute-done((bf16[3072,128]{1,0:T(8,128)(2,1)S(1)}, bf16[3072,128]{1,0:T(8,128)(2,1)S(1)}, u32[]{:S(2)}, u32[]{:S(2)}) %collective-permute-start.47) | collective-permute-done | bytes 786464 | tf_op jit(solution)/shard_map/ppermute | solution.py:1259
  522.0 7.8 collective-permute-done.46
  548.2 47.7 %collective-permute-done.49.refs_9_ = bf16[3072,128]{1,0:T(8,128)(2,1)} collective-permute-done((bf16[3072,128]{1,0:T(8,128)(2,1)S(1)}, bf16[3072,128]{1,0:T(8,128)(2,1)}, u32[]{:S(2)}, u32[]{:S(2)}) %collective-permute-start.49) | collective-permute-done | bytes 786464 | tf_op jit(solution)/shard_map/ppermute | solution.py:1259
  599.0 4.1 constant_dynamic-slice_fusion.7
  606.8 3.6 bitcast_add_fusion.1
  616.6 10.8 %collective-permute-done.52 = f16[616,384]{1,0:T(8,128)(2,1)S(1)} collective-permute-done((f16[616,384]{1,0:T(8,128)(2,1)}, f16[616,384]{1,0:T(8,128)(2,1)S(1)}, u32[]{:S(2)}, u32[]{:S(2)}) %collective-permute-start.52) | collective-permute-done | bytes 473120 | tf_op jit(solution)/shard_map/ppermute | solution.py:1259
  627.4 11.1 %collective-permute-start.56 = (f16[616,384]{1,0:T(8,128)(2,1)}, f16[616,384]{1,0:T(8,128)(2,1)S(1)}, u32[]{:S(2)}, u32[]{:S(2)}) collective-permute-start(f16[616,384]{1,0:T(8,128)(2,1)} %concatenate.158), channel_id=1, source_target_pairs={{0,4},{1,5},{2,6},{3,7},{4,0},{5,1},{6,2},{7,3},{8,12},{9,13},{10,... | collective-permute-start | bytes 1419272 | tf_op jit(solution)/shard_map/ppermute | solution.py:1259
  640.4 9.0 %collective-permute-done.55.refs_7_ = bf16[3072,128]{1,0:T(8,128)(2,1)} collective-permute-done((bf16[3072,128]{1,0:T(8,128)(2,1)}, bf16[3072,128]{1,0:T(8,128)(2,1)}, u32[]{:S(2)}, u32[]{:S(2)}) %collective-permute-start.55) | collective-permute-done | bytes 786464 | tf_op jit(solution)/shard_map/ppermute | solution.py:1259
  649.3 27.9 %scatter_rows.1 = (f32[192,6288]{1,0:T(8,128)}, f32[1,1]{1,0:T(1,128)}) custom-call(s32[4112]{0:T(1024)} %find_hits.2.list_ref.refs_0_, s32[4112]{0:T(1024)} %copy-done.34, s32[4112]{0:T(1024)} %find_hits.3.list_ref.refs_2_, s32[4112]{0:T(1024)} %copy-done.35, f32[192,6400]{1,0:T(8,128)} %fusion.3.refs_4_, ...), custom_call_target="tpu_custom_call" | custom-call | flops 300000000 | bytes 193167 | tf_op jit(solution)/shard_map/scatter_rows/pallas_call | solution.py:305
  707.9 4.4 collective-permute-start.69
  715.4 27.6 %collective-permute-done.67 = f16[688,384]{1,0:T(8,128)(2,1)S(1)} collective-permute-done((f16[688,384]{1,0:T(8,128)(2,1)S(1)}, f16[688,384]{1,0:T(8,128)(2,1)S(1)}, u32[]{:S(2)}, u32[]{:S(2)}) %collective-permute-start.67) | collective-permute-done | bytes 528416 | tf_op jit(solution)/shard_map/ppermute | solution.py:1259
  743.1 7.4 collective-permute-done.69
  750.5 3.5 collective-permute-done.71
  754.0 12.2 %fusion.10 = (f32[6288,192]{0,1:T(8,128)}, f32[6288,192]{0,1:T(8,128)}, f32[6288,192]{0,1:T(8,128)}) fusion(f32[192,6288]{1,0:T(8,128)} %get-tuple-element.190, f32[]{:T(128)} %div.104, f32[6288,192]{0,1:T(8,128)} %param.49, f32[]{:T(128)} %bitcast.114, f32[]{:T(128)} %bitcast.112, f32[6288,192]{0,1:T(8,128)} %param.48, f32[6288,192]{0,1:T(8,128)} %param.47), kind=kLoop, calls=%fused_computation.43 | loop fusion | flops 19316736 | bytes 33804300 | tf_op jit(solution)/shard_map/transpose | solution.py:1634
  776.0 35.3 %shampoo.1 = (f32[12,384,384]{2,1,0:T(8,128)}, f32[12,384,384]{2,1,0:T(8,128)}, f32[12,384,384]{2,1,0:T(8,128)}, f32[12,384,384]{2,1,0:T(8,128)}, f32[2,384,384]{2,1,0:T(8,128)}) custom-call(s32[8]{0:T(128)} %stack.234.places_ref, f32[1]{0:T(128)} %bitcast.103.clip_ref, f32[688,384]{1,0:T(8,128)} %convert_element_type.180.refs_0_.refs_8_.refs_16_, ...), custom_call_target="tpu_custom_call" | custom-call | flops 326149088 | bytes 1415577 | tf_op jit(solution)/shard_map/shampoo/pallas_call | solution.py:1155
  (445 shorter events, 211.1 us)
Async XLA Ops:
  3.3 20.3 %collective-permute-start.5 = (bf16[192,6288]{1,0:T(8,128)(2,1)S(1)}, bf16[192,6288]{1,0:T(8,128)(2,1)}, u32[]{:S(2)}, u32[]{:S(2)}) collective-permute-start(bf16[192,6288]{1,0:T(8,128)(2,1)S(1)} %bitcast_convert_fusion.own_ref.refs_0_), channel_id=1, source_target_pairs={{0,8},{8,0},{16,24},{24,16},{1,9},{9,1},{17,25},{25,17},{2,10},{10... | collective-permute-start | bytes 7243784 | tf_op jit(solution)/shard_map/ppermute | solution.py:1253
  10.3 79.0 %collective-permute-start.12 = (bf16[12,384,384]{2,1,0:T(8,128)(2,1)}, bf16[12,384,384]{2,1,0:T(8,128)(2,1)}, u32[]{:S(2)}, u32[]{:S(2)}) collective-permute-start(bf16[12,384,384]{2,1,0:T(8,128)(2,1)} %convert_element_type.146.refs_0_), channel_id=1, source_target_pairs={{0,16},{8,24},{16,0},{24,8},{1,17},{9,25},{17,1},{25,9},{2,18},{10... | collective-permute-start | bytes 10616840 | tf_op jit(solution)/shard_map/ppermute | solution.py:1253
  53.3 24.4 %collective-permute-start.8 = (bf16[1024,384]{1,0:T(8,128)(2,1)}, bf16[1024,384]{1,0:T(8,128)(2,1)S(1)}, u32[]{:S(2)}, u32[]{:S(2)}) collective-permute-start(bf16[1024,384]{1,0:T(8,128)(2,1)} %get-tuple-element.119), channel_id=1, source_target_pairs={{0,1},{1,0},{2,3},{3,2},{4,5},{5,4},{6,7},{7,6},{8,9},{9,8},{10,11... | collective-permute-start | bytes 2359304 | tf_op jit(solution)/shard_map/ppermute | solution.py:1259
  53.8 33.0 %collective-permute-start.9 = (bf16[1024,384]{1,0:T(8,128)(2,1)}, bf16[1024,384]{1,0:T(8,128)(2,1)S(1)}, u32[]{:S(2)}, u32[]{:S(2)}) collective-permute-start(bf16[1024,384]{1,0:T(8,128)(2,1)} %get-tuple-element.121), channel_id=1, source_target_pairs={{0,1},{1,0},{2,3},{3,2},{4,5},{5,4},{6,7},{7,6},{8,9},{9,8},{10,11... | collective-permute-start | bytes 2359304 | tf_op jit(solution)/shard_map/ppermute | solution.py:1259
  89.0 24.3 %collective-permute-start.13 = (bf16[12,384,384]{2,1,0:T(8,128)(2,1)}, bf16[12,384,384]{2,1,0:T(8,128)(2,1)S(1)}, u32[]{:S(2)}, u32[]{:S(2)}) collective-permute-start(bf16[12,384,384]{2,1,0:T(8,128)(2,1)} %convert_element_type.146.refs_0_), channel_id=1, source_target_pairs={{0,8},{8,0},{16,24},{24,16},{1,9},{9,1},{17,25},{25,17},{2,10},{10... | collective-permute-start | bytes 10616840 | tf_op jit(solution)/shard_map/ppermute | solution.py:1253
  89.3 29.8 %collective-permute-start.14 = (bf16[12,384,384]{2,1,0:T(8,128)(2,1)}, bf16[12,384,384]{2,1,0:T(8,128)(2,1)}, u32[]{:S(2)}, u32[]{:S(2)}) collective-permute-start(bf16[12,384,384]{2,1,0:T(8,128)(2,1)} %collective-permute-done.12.refs_1_), channel_id=1, source_target_pairs={{0,8},{8,0},{16,24},{24,16},{1,9},{9,1},{17,25},{25,17},{2,10},{10... | collective-permute-start | bytes 10616840 | tf_op jit(solution)/shard_map/ppermute | solution.py:1253
  89.5 20.4 %collective-permute-start.11 = (bf16[1024,384]{1,0:T(8,128)(2,1)S(1)}, bf16[1024,384]{1,0:T(8,128)(2,1)S(1)}, u32[]{:S(2)}, u32[]{:S(2)}) collective-permute-start(bf16[1024,384]{1,0:T(8,128)(2,1)S(1)} %copy-done.41), channel_id=1, source_target_pairs={{0,1},{1,0},{2,3},{3,2},{4,5},{5,4},{6,7},{7,6},{8,9},{9,8},{10,11... | collective-permute-start | bytes 2359304 | tf_op jit(solution)/shard_map/ppermute | solution.py:1259
  90.8 56.6 %collective-permute-start.16 = (bf16[2,512,384]{2,1,0:T(8,128)(2,1)}, bf16[2,512,384]{2,1,0:T(8,128)(2,1)}, u32[]{:S(2)}, u32[]{:S(2)}) collective-permute-start(bf16[2,512,384]{2,1,0:T(8,128)(2,1)} %bitcast.19), channel_id=1, source_target_pairs={{0,6},{1,7},{2,0},{3,1},{4,2},{5,3},{6,4},{7,5},{8,14},{9,15},{10,... | collective-permute-start | bytes 2359304 | tf_op jit(solution)/shard_map/ppermute | solution.py:1259
  94.1 36.5 %collective-permute-start.10 = (bf16[1024,384]{1,0:T(8,128)(2,1)}, bf16[1024,384]{1,0:T(8,128)(2,1)}, u32[]{:S(2)}, u32[]{:S(2)}) collective-permute-start(bf16[1024,384]{1,0:T(8,128)(2,1)} %get-tuple-element.123), channel_id=1, source_target_pairs={{0,1},{1,0},{2,3},{3,2},{4,5},{5,4},{6,7},{7,6},{8,9},{9,8},{10,11... | collective-permute-start | bytes 2359304 | tf_op jit(solution)/shard_map/ppermute | solution.py:1259
  109.9 35.9 %collective-permute-start.15 = (bf16[2,512,384]{2,1,0:T(8,128)(2,1)}, bf16[2,512,384]{2,1,0:T(8,128)(2,1)}, u32[]{:S(2)}, u32[]{:S(2)}) collective-permute-start(bf16[2,512,384]{2,1,0:T(8,128)(2,1)} %bitcast.18), channel_id=1, source_target_pairs={{0,4},{1,5},{2,6},{3,7},{4,0},{5,1},{6,2},{7,3},{8,12},{9,13},{10,... | collective-permute-start | bytes 2359304 | tf_op jit(solution)/shard_map/ppermute | solution.py:1259
  113.3 49.3 %collective-permute-start.17 = (bf16[2,512,384]{2,1,0:T(8,128)(2,1)}, bf16[2,512,384]{2,1,0:T(8,128)(2,1)}, u32[]{:S(2)}, u32[]{:S(2)}) collective-permute-start(bf16[2,512,384]{2,1,0:T(8,128)(2,1)} %bitcast.20), channel_id=1, source_target_pairs={{0,2},{1,3},{2,4},{3,5},{4,6},{5,7},{6,0},{7,1},{8,10},{9,11},{10,... | collective-permute-start | bytes 2359304 | tf_op jit(solution)/shard_map/ppermute | solution.py:1259
  166.2 11.4 %collective-permute-start.18 = (bf16[512,384]{1,0:T(8,128)(2,1)}, bf16[512,384]{1,0:T(8,128)(2,1)}, u32[]{:S(2)}, u32[]{:S(2)}) collective-permute-start(bf16[512,384]{1,0:T(8,128)(2,1)} %slice_bitcast_fusion), channel_id=1, source_target_pairs={{0,16},{8,24},{16,0},{24,8},{1,17},{9,25},{17,1},{25,9},{2,18},{10... | collective-permute-start | bytes 1179656 | tf_op jit(solution)/shard_map/ppermute | solution.py:1253
  179.7 54.5 %collective-permute-start.23 = (bf16[192,6288]{1,0:T(8,128)(2,1)S(1)}, bf16[192,6288]{1,0:T(8,128)(2,1)}, u32[]{:S(2)}, u32[]{:S(2)}) collective-permute-start(bf16[192,6288]{1,0:T(8,128)(2,1)S(1)} %copy-done.3), channel_id=1, source_target_pairs={{0,16},{8,24},{16,0},{24,8},{1,17},{9,25},{17,1},{25,9},{2,18},{10... | collective-permute-start | bytes 7243784 | tf_op jit(solution)/shard_map/ppermute | solution.py:1253
  234.3 26.3 %collective-permute-start.24 = (bf16[192,6288]{1,0:T(8,128)(2,1)}, bf16[192,6288]{1,0:T(8,128)(2,1)S(1)}, u32[]{:S(2)}, u32[]{:S(2)}) collective-permute-start(bf16[192,6288]{1,0:T(8,128)(2,1)} %collective-permute-done.23.refs_1_), channel_id=1, source_target_pairs={{0,8},{8,0},{16,24},{24,16},{1,9},{9,1},{17,25},{25,17},{2,10},{10... | collective-permute-start | bytes 7243784 | tf_op jit(solution)/shard_map/ppermute | solution.py:1253
  234.4 9.7 %collective-permute-start.20 = (bf16[128,768]{0,1:T(8,128)(2,1)S(1)}, bf16[128,768]{0,1:T(8,128)(2,1)S(1)}, u32[]{:S(2)}, u32[]{:S(2)}) collective-permute-start(bf16[128,768]{0,1:T(8,128)(2,1)S(1)} %pad_maximum_fusion.9), channel_id=1, source_target_pairs={{0,2},{1,3},{2,4},{3,5},{4,6},{5,7},{6,0},{7,1},{8,10},{9,11},{10,... | collective-permute-start | bytes 589832 | tf_op jit(solution)/shard_map/ppermute | solution.py:1259
  236.9 17.5 %collective-permute-start.21 = (bf16[128,768]{0,1:T(8,128)(2,1)S(1)}, bf16[128,768]{0,1:T(8,128)(2,1)S(1)}, u32[]{:S(2)}, u32[]{:S(2)}) collective-permute-start(bf16[128,768]{0,1:T(8,128)(2,1)S(1)} %pad_maximum_fusion.9), channel_id=1, source_target_pairs={{0,4},{1,5},{2,6},{3,7},{4,0},{5,1},{6,2},{7,3},{8,12},{9,13},{10,... | collective-permute-start | bytes 589832 | tf_op jit(solution)/shard_map/ppermute | solution.py:1259
  240.7 17.3 %collective-permute-start.22 = (bf16[128,768]{0,1:T(8,128)(2,1)S(1)}, bf16[128,768]{0,1:T(8,128)(2,1)}, u32[]{:S(2)}, u32[]{:S(2)}) collective-permute-start(bf16[128,768]{0,1:T(8,128)(2,1)S(1)} %pad_maximum_fusion.9), channel_id=1, source_target_pairs={{0,6},{1,7},{2,0},{3,1},{4,2},{5,3},{6,4},{7,5},{8,14},{9,15},{10,... | collective-permute-start | bytes 589832 | tf_op jit(solution)/shard_map/ppermute | solution.py:1259
  308.5 9.2 %collective-permute-start.30 = (f32[64,768]{1,0:T(8,128)S(1)}, f32[64,768]{1,0:T(8,128)S(1)}, u32[]{:S(2)}, u32[]{:S(2)}) collective-permute-start(f32[64,768]{1,0:T(8,128)S(1)} %get-tuple-element.278), channel_id=1, source_target_pairs={{0,1},{1,0},{2,3},{3,2},{4,5},{5,4},{6,7},{7,6},{8,9},{9,8},{10,11... | collective-permute-start | bytes 589832 | tf_op jit(solution)/shard_map/ppermute | solution.py:1259
  309.0 10.8 %collective-permute-start.29 = (f32[64,768]{1,0:T(8,128)S(1)}, f32[64,768]{1,0:T(8,128)S(1)}, u32[]{:S(2)}, u32[]{:S(2)}) collective-permute-start(f32[64,768]{1,0:T(8,128)S(1)} %get-tuple-element.279), channel_id=1, source_target_pairs={{0,1},{1,0},{2,3},{3,2},{4,5},{5,4},{6,7},{7,6},{8,9},{9,8},{10,11... | collective-permute-start | bytes 589832 | tf_op jit(solution)/shard_map/ppermute | solution.py:1259
  332.6 59.9 %collective-permute-start.32 = (f32[384,6400]{1,0:T(8,128)}, f32[384,6400]{1,0:T(8,128)}, u32[]{:S(2)}, u32[]{:S(2)}) collective-permute-start(f32[384,6400]{1,0:T(8,128)} %get-tuple-element.148), channel_id=1, source_target_pairs={{0,8},{8,0},{16,24},{24,16},{1,9},{9,1},{17,25},{25,17},{2,10},{10... | collective-permute-start | bytes 29491208 | tf_op jit(solution)/shard_map/ppermute | solution.py:1253
  333.6 17.4 %collective-permute-start.37 = (f32[64,768]{1,0:T(8,128)S(1)}, f32[64,768]{1,0:T(8,128)S(1)}, u32[]{:S(2)}, u32[]{:S(2)}) collective-permute-start(f32[64,768]{1,0:T(8,128)S(1)} %get-tuple-element.281), channel_id=1, source_target_pairs={{0,4},{1,5},{2,6},{3,7},{4,0},{5,1},{6,2},{7,3},{8,12},{9,13},{10,... | collective-permute-start | bytes 589832 | tf_op jit(solution)/shard_map/ppermute | solution.py:1259
  335.7 17.9 %collective-permute-start.36 = (f32[64,768]{1,0:T(8,128)S(1)}, f32[64,768]{1,0:T(8,128)S(1)}, u32[]{:S(2)}, u32[]{:S(2)}) collective-permute-start(f32[64,768]{1,0:T(8,128)S(1)} %get-tuple-element.282), channel_id=1, source_target_pairs={{0,6},{1,7},{2,0},{3,1},{4,2},{5,3},{6,4},{7,5},{8,14},{9,15},{10,... | collective-permute-start | bytes 589832 | tf_op jit(solution)/shard_map/ppermute | solution.py:1259
  337.8 15.9 %collective-permute-start.35 = (f32[64,768]{1,0:T(8,128)S(1)}, f32[64,768]{1,0:T(8,128)S(1)}, u32[]{:S(2)}, u32[]{:S(2)}) collective-permute-start(f32[64,768]{1,0:T(8,128)S(1)} %get-tuple-element.276), channel_id=1, source_target_pairs={{0,1},{1,0},{2,3},{3,2},{4,5},{5,4},{6,7},{7,6},{8,9},{9,8},{10,11... | collective-permute-start | bytes 589832 | tf_op jit(solution)/shard_map/ppermute | solution.py:1259
  381.5 18.3 %collective-permute-start.39 = (f32[16,384,384]{2,1,0:T(8,128)}, f32[16,384,384]{2,1,0:T(8,128)}, u32[]{:S(2)}, u32[]{:S(2)}) collective-permute-start(f32[16,384,384]{2,1,0:T(8,128)} %get-tuple-element.160), channel_id=1, source_target_pairs={{0,8},{8,0},{16,24},{24,16},{1,9},{9,1},{17,25},{25,17},{2,10},{10... | collective-permute-start | bytes 28311560 | tf_op jit(solution)/shard_map/ppermute | solution.py:1253
  398.6 65.7 %collective-permute-start.34 = (f16[192,6400]{1,0:T(8,128)(2,1)}, f16[192,6400]{1,0:T(8,128)(2,1)}, u32[]{:S(2)}, u32[]{:S(2)}) collective-permute-start(f16[192,6400]{1,0:T(8,128)(2,1)} %fusion.8), channel_id=1, source_target_pairs={{0,16},{8,24},{16,0},{24,8},{1,17},{9,25},{17,1},{25,9},{2,18},{10... | collective-permute-start | bytes 7372808 | tf_op jit(solution)/shard_map/ppermute | solution.py:1253
  412.1 62.3 %collective-permute-start.41 = (f16[3088,384]{1,0:T(8,128)(2,1)}, f16[3088,384]{1,0:T(8,128)(2,1)}, u32[]{:S(2)}, u32[]{:S(2)}) collective-permute-start(f16[3088,384]{1,0:T(8,128)(2,1)} %concatenate.148), channel_id=1, source_target_pairs={{0,1},{1,0},{2,3},{3,2},{4,5},{5,4},{6,7},{7,6},{8,9},{9,8},{10,11... | collective-permute-start | bytes 7114760 | tf_op jit(solution)/shard_map/ppermute | solution.py:1259
  460.9 12.8 %collective-permute-start.42 = (bf16[512,384]{1,0:T(8,128)(2,1)S(1)}, bf16[512,384]{1,0:T(8,128)(2,1)S(1)}, u32[]{:S(2)}, u32[]{:S(2)}) collective-permute-start(bf16[512,384]{1,0:T(8,128)(2,1)S(1)} %fusion.15), channel_id=1, source_target_pairs={{0,16},{8,24},{16,0},{24,8},{1,17},{9,25},{17,1},{25,9},{2,18},{10... | collective-permute-start | bytes 1179656 | tf_op jit(solution)/shard_map/ppermute | solution.py:1253
  484.6 9.8 %collective-permute-start.43 = (f32[9,384,384]{2,1,0:T(8,128)}, f32[9,384,384]{2,1,0:T(8,128)}, u32[]{:S(2)}, u32[]{:S(2)}) collective-permute-start(f32[9,384,384]{2,1,0:T(8,128)} %get-tuple-element.179), channel_id=1, source_target_pairs={{0,8},{8,0},{16,24},{24,16},{1,9},{9,1},{17,25},{25,17},{2,10},{10... | collective-permute-start | bytes 15925256 | tf_op jit(solution)/shard_map/ppermute | solution.py:1253
  484.6 9.6 %collective-permute-start.44 = (bf16[1024,192]{1,0:T(8,128)(2,1)S(1)}, bf16[1024,192]{1,0:T(8,128)(2,1)S(1)}, u32[]{:S(2)}, u32[]{:S(2)}) collective-permute-start(bf16[1024,192]{1,0:T(8,128)(2,1)S(1)} %select_bitcast_fusion.1), channel_id=1, source_target_pairs={{0,8},{8,0},{16,24},{24,16},{1,9},{9,1},{17,25},{25,17},{2,10},{10... | collective-permute-start | bytes 1179656 | tf_op jit(solution)/shard_map/ppermute | solution.py:1253
  498.0 31.8 %collective-permute-start.46 = (f16[1744,384]{1,0:T(8,128)(2,1)S(1)}, f16[1744,384]{1,0:T(8,128)(2,1)}, u32[]{:S(2)}, u32[]{:S(2)}) collective-permute-start(f16[1744,384]{1,0:T(8,128)(2,1)S(1)} %concatenate.154), channel_id=1, source_target_pairs={{0,1},{1,0},{2,3},{3,2},{4,5},{5,4},{6,7},{7,6},{8,9},{9,8},{10,11... | collective-permute-start | bytes 4018184 | tf_op jit(solution)/shard_map/ppermute | solution.py:1259
  501.6 19.6 %collective-permute-start.47 = (bf16[3072,128]{1,0:T(8,128)(2,1)S(1)}, bf16[3072,128]{1,0:T(8,128)(2,1)S(1)}, u32[]{:S(2)}, u32[]{:S(2)}) collective-permute-start(bf16[3072,128]{1,0:T(8,128)(2,1)S(1)} %maximum_maximum_fusion.refs_12_), channel_id=1, source_target_pairs={{0,2},{1,3},{2,4},{3,5},{4,6},{5,7},{6,0},{7,1},{8,10},{9,11},{10,... | collective-permute-start | bytes 2359304 | tf_op jit(solution)/shard_map/ppermute | solution.py:1259
  543.0 60.1 %collective-permute-start.48 = (f16[2416,384]{1,0:T(8,128)(2,1)}, f16[2416,384]{1,0:T(8,128)(2,1)S(1)}, u32[]{:S(2)}, u32[]{:S(2)}) collective-permute-start(f16[2416,384]{1,0:T(8,128)(2,1)} %concatenate.156), channel_id=1, source_target_pairs={{0,16},{8,24},{16,0},{24,8},{1,17},{9,25},{17,1},{25,9},{2,18},{10... | collective-permute-start | bytes 5566472 | tf_op jit(solution)/shard_map/ppermute | solution.py:1253
  545.3 50.6 %collective-permute-start.49 = (bf16[3072,128]{1,0:T(8,128)(2,1)S(1)}, bf16[3072,128]{1,0:T(8,128)(2,1)}, u32[]{:S(2)}, u32[]{:S(2)}) collective-permute-start(bf16[3072,128]{1,0:T(8,128)(2,1)S(1)} %maximum_maximum_fusion.refs_12_), channel_id=1, source_target_pairs={{0,4},{1,5},{2,6},{3,7},{4,0},{5,1},{6,2},{7,3},{8,12},{9,13},{10,... | collective-permute-start | bytes 2359304 | tf_op jit(solution)/shard_map/ppermute | solution.py:1259
  546.3 49.5 %collective-permute-start.50 = (bf16[3072,128]{1,0:T(8,128)(2,1)S(1)}, bf16[3072,128]{1,0:T(8,128)(2,1)}, u32[]{:S(2)}, u32[]{:S(2)}) collective-permute-start(bf16[3072,128]{1,0:T(8,128)(2,1)S(1)} %maximum_maximum_fusion.refs_12_), channel_id=1, source_target_pairs={{0,6},{1,7},{2,0},{3,1},{4,2},{5,3},{6,4},{7,5},{8,14},{9,15},{10,... | collective-permute-start | bytes 2359304 | tf_op jit(solution)/shard_map/ppermute | solution.py:1259
  547.0 66.4 %collective-permute-start.51 = (bf16[3072,128]{1,0:T(8,128)(2,1)S(1)}, bf16[3072,128]{1,0:T(8,128)(2,1)}, u32[]{:S(2)}, u32[]{:S(2)}) collective-permute-start(bf16[3072,128]{1,0:T(8,128)(2,1)S(1)} %maximum_maximum_fusion.refs_12_), channel_id=1, source_target_pairs={{0,1},{1,0},{2,3},{3,2},{4,5},{5,4},{6,7},{7,6},{8,9},{9,8},{10,11... | collective-permute-start | bytes 2359304 | tf_op jit(solution)/shard_map/ppermute | solution.py:1259
  595.8 44.5 %collective-permute-start.53 = (bf16[3072,128]{1,0:T(8,128)(2,1)}, bf16[3072,128]{1,0:T(8,128)(2,1)}, u32[]{:S(2)}, u32[]{:S(2)}) collective-permute-start(bf16[3072,128]{1,0:T(8,128)(2,1)} %collective-permute-done.49.refs_9_), channel_id=1, source_target_pairs={{0,1},{1,0},{2,3},{3,2},{4,5},{5,4},{6,7},{7,6},{8,9},{9,8},{10,11... | collective-permute-start | bytes 2359304 | tf_op jit(solution)/shard_map/ppermute | solution.py:1259
  596.9 43.4 %collective-permute-start.54 = (bf16[3072,128]{1,0:T(8,128)(2,1)S(1)}, bf16[3072,128]{1,0:T(8,128)(2,1)}, u32[]{:S(2)}, u32[]{:S(2)}) collective-permute-start(bf16[3072,128]{1,0:T(8,128)(2,1)S(1)} %copy-done.17), channel_id=1, source_target_pairs={{0,1},{1,0},{2,3},{3,2},{4,5},{5,4},{6,7},{7,6},{8,9},{9,8},{10,11... | collective-permute-start | bytes 2359304 | tf_op jit(solution)/shard_map/ppermute | solution.py:1259
  597.9 51.5 %collective-permute-start.55 = (bf16[3072,128]{1,0:T(8,128)(2,1)}, bf16[3072,128]{1,0:T(8,128)(2,1)}, u32[]{:S(2)}, u32[]{:S(2)}) collective-permute-start(bf16[3072,128]{1,0:T(8,128)(2,1)} %collective-permute-done.50.refs_11_), channel_id=1, source_target_pairs={{0,1},{1,0},{2,3},{3,2},{4,5},{5,4},{6,7},{7,6},{8,9},{9,8},{10,11... | collective-permute-start | bytes 2359304 | tf_op jit(solution)/shard_map/ppermute | solution.py:1259
  613.4 14.0 %collective-permute-start.52 = (f16[616,384]{1,0:T(8,128)(2,1)}, f16[616,384]{1,0:T(8,128)(2,1)S(1)}, u32[]{:S(2)}, u32[]{:S(2)}) collective-permute-start(f16[616,384]{1,0:T(8,128)(2,1)} %concatenate.157), channel_id=1, source_target_pairs={{0,2},{1,3},{2,4},{3,5},{4,6},{5,7},{6,0},{7,1},{8,10},{9,11},{10,... | collective-permute-start | bytes 1419272 | tf_op jit(solution)/shard_map/ppermute | solution.py:1259
  613.6 63.7 %collective-permute-start.57 = (f16[616,384]{1,0:T(8,128)(2,1)S(1)}, f16[616,384]{1,0:T(8,128)(2,1)}, u32[]{:S(2)}, u32[]{:S(2)}) collective-permute-start(f16[616,384]{1,0:T(8,128)(2,1)S(1)} %concatenate.159), channel_id=1, source_target_pairs={{0,6},{1,7},{2,0},{3,1},{4,2},{5,3},{6,4},{7,5},{8,14},{9,15},{10,... | collective-permute-start | bytes 1419272 | tf_op jit(solution)/shard_map/ppermute | solution.py:1259
  627.4 51.1 %collective-permute-start.56 = (f16[616,384]{1,0:T(8,128)(2,1)}, f16[616,384]{1,0:T(8,128)(2,1)S(1)}, u32[]{:S(2)}, u32[]{:S(2)}) collective-permute-start(f16[616,384]{1,0:T(8,128)(2,1)} %concatenate.158), channel_id=1, source_target_pairs={{0,4},{1,5},{2,6},{3,7},{4,0},{5,1},{6,2},{7,3},{8,12},{9,13},{10,... | collective-permute-start | bytes 1419272 | tf_op jit(solution)/shard_map/ppermute | solution.py:1259
  707.1 36.0 %collective-permute-start.67 = (f16[688,384]{1,0:T(8,128)(2,1)S(1)}, f16[688,384]{1,0:T(8,128)(2,1)S(1)}, u32[]{:S(2)}, u32[]{:S(2)}) collective-permute-start(f16[688,384]{1,0:T(8,128)(2,1)S(1)} %concatenate.167), channel_id=1, source_target_pairs={{0,2},{1,3},{2,4},{3,5},{4,6},{5,7},{6,0},{7,1},{8,10},{9,11},{10,... | collective-permute-start | bytes 1585160 | tf_op jit(solution)/shard_map/ppermute | solution.py:1259
  707.9 42.5 %collective-permute-start.69 = (f16[688,384]{1,0:T(8,128)(2,1)S(1)}, f16[688,384]{1,0:T(8,128)(2,1)S(1)}, u32[]{:S(2)}, u32[]{:S(2)}) collective-permute-start(f16[688,384]{1,0:T(8,128)(2,1)S(1)} %concatenate.167), channel_id=1, source_target_pairs={{0,4},{1,5},{2,6},{3,7},{4,0},{5,1},{6,2},{7,3},{8,12},{9,13},{10,... | collective-permute-start | bytes 1585160 | tf_op jit(solution)/shard_map/ppermute | solution.py:1259
  712.4 41.6 %collective-permute-start.71 = (f16[688,384]{1,0:T(8,128)(2,1)S(1)}, f16[688,384]{1,0:T(8,128)(2,1)S(1)}, u32[]{:S(2)}, u32[]{:S(2)}) collective-permute-start(f16[688,384]{1,0:T(8,128)(2,1)S(1)} %concatenate.167), channel_id=1, source_target_pairs={{0,6},{1,7},{2,0},{3,1},{4,2},{5,3},{6,4},{7,5},{8,14},{9,15},{10,... | collective-permute-start | bytes 1585160 | tf_op jit(solution)/shard_map/ppermute | solution.py:1259
  714.1 56.3 %collective-permute-start.66 = (f16[688,384]{1,0:T(8,128)(2,1)S(1)}, f16[688,384]{1,0:T(8,128)(2,1)S(1)}, u32[]{:S(2)}, u32[]{:S(2)}) collective-permute-start(f16[688,384]{1,0:T(8,128)(2,1)S(1)} %concatenate.167), channel_id=1, source_target_pairs={{0,1},{1,0},{2,3},{3,2},{4,5},{5,4},{6,7},{7,6},{8,9},{9,8},{10,11... | collective-permute-start | bytes 1585160 | tf_op jit(solution)/shard_map/ppermute | solution.py:1259
  743.1 28.4 %collective-permute-start.68 = (f16[688,384]{1,0:T(8,128)(2,1)S(1)}, f16[688,384]{1,0:T(8,128)(2,1)S(1)}, u32[]{:S(2)}, u32[]{:S(2)}) collective-permute-start(f16[688,384]{1,0:T(8,128)(2,1)S(1)} %collective-permute-done.67), channel_id=1, source_target_pairs={{0,1},{1,0},{2,3},{3,2},{4,5},{5,4},{6,7},{7,6},{8,9},{9,8},{10,11... | collective-permute-start | bytes 1585160 | tf_op jit(solution)/shard_map/ppermute | solution.py:1259
  750.5 22.1 %collective-permute-start.70 = (f16[688,384]{1,0:T(8,128)(2,1)S(1)}, f16[688,384]{1,0:T(8,128)(2,1)S(1)}, u32[]{:S(2)}, u32[]{:S(2)}) collective-permute-start(f16[688,384]{1,0:T(8,128)(2,1)S(1)} %collective-permute-done.69), channel_id=1, source_target_pairs={{0,1},{1,0},{2,3},{3,2},{4,5},{5,4},{6,7},{7,6},{8,9},{9,8},{10,11... | collective-permute-start | bytes 1585160 | tf_op jit(solution)/shard_map/ppermute | solution.py:1259
  754.0 20.9 %collective-permute-start.72 = (f16[688,384]{1,0:T(8,128)(2,1)S(1)}, f16[688,384]{1,0:T(8,128)(2,1)S(1)}, u32[]{:S(2)}, u32[]{:S(2)}) collective-permute-start(f16[688,384]{1,0:T(8,128)(2,1)S(1)} %collective-permute-done.71), channel_id=1, source_target_pairs={{0,1},{1,0},{2,3},{3,2},{4,5},{5,4},{6,7},{7,6},{8,9},{9,8},{10,11... | collective-permute-start | bytes 1585160 | tf_op jit(solution)/shard_map/ppermute | solution.py:1259
  (71 other events, 768.3 us)

commit v4 on v3

--- a/solution.py
+++ b/solution.py
@@ -225,47 +225,64 @@
     )(hit_list, table)
 
 
-def scatter_kernel(piece_count, half, rows_all, starts, *refs):
-    used = len(starts)
-    lists = refs[:used]
-    lex_ref = refs[used]
-    pieces = refs[used + 1 : used + 1 + piece_count]
-    out_ref, square_ref, acc, tail, wide, pair = refs[used + 1 + piece_count :]
+def add_rows(own_ref, their_ref, groups, pieces, acc, tail, wide, pair):
+    half = pieces[0].shape[0] // 3
     chunk = 128
-
-    def clear(start):
-        acc[pl.ds(start, chunk), :] = jnp.zeros((chunk, 128), f32)
-        tail[pl.ds(start, chunk), :] = jnp.zeros((chunk, 128), f32)
-
-    in_chunks(acc.shape[0], chunk, clear)
-    for k in range(piece_count):
-
-        def widen(start, k=k):
-            values = pieces[k][pl.ds(start, chunk), :].astype(f32)
+    for k, piece in enumerate(pieces):
+
+        def widen(start, k=k, piece=piece):
+            values = piece[pl.ds(start, chunk), :].astype(f32)
             wide[pl.ds(k * 2 * half + start, chunk), :] = values
 
-        def widen_pair(start, k=k):
-            values = pieces[k][pl.ds(2 * half + start, chunk), :].astype(f32)
+        def widen_pair(start, k=k, piece=piece):
+            values = piece[pl.ds(2 * half + start, chunk), :].astype(f32)
             pair[pl.ds(k * half + start, chunk), :] = values
 
         in_chunks(2 * half, chunk, widen)
         in_chunks(half, chunk, widen_pair)
     upper = lax.broadcasted_iota(i32, (1, 128), 1) >= 64
-    for which, (side, start) in enumerate(starts):
-        own = upper if side else ~upper
-
-        def go(i, carry, which=which, side=side, start=start, own=own):
-            for u in range(8):
-                entry = lists[which][i * 8 + u]
-                row = entry >> 16
-                p = (entry & 0xFFFF) + start
-                q = (p // half) * half + p + side * half
-                acc[pl.ds(row, 1), :] += wide[pl.ds(q, 1), :]
-                tail[pl.ds(row, 1), :] += jnp.where(own, pair[pl.ds(p, 1), :], 0.0)
-            return carry
-
-        held = lists[which].shape[0] - 8
-        lax.fori_loop(0, (lists[which][held] + 7) // 8, go, 0)
+    for base, total, start in groups:
+        for side, list_ref in enumerate((own_ref, their_ref)):
+            own = upper if side else ~upper
+
+            def go(i, carry, base=base, start=start, side=side, list_ref=list_ref, own=own):
+                for u in range(8):
+                    entry = list_ref[base + i * 8 + u]
+                    row = entry >> 16
+                    p = (entry & 0xFFFF) + start
+                    q = (p // half) * half + p + side * half
+                    acc[pl.ds(row, 1), :] += wide[pl.ds(q, 1), :]
+                    tail[pl.ds(row, 1), :] += jnp.where(own, pair[pl.ds(p, 1), :], 0.0)
+                return carry
+
+            lax.fori_loop(0, (list_ref[base + total + 8] + 7) // 8, go, 0)
+
+
+def scatter_first_kernel(count, groups, own_ref, their_ref, *refs):
+    pieces = refs[:count]
+    acc, tail, wide, pair = refs[count:]
+
+    def clear(start):
+        acc[pl.ds(start, 128), :] = jnp.zeros((128, 128), f32)
+        tail[pl.ds(start, 128), :] = jnp.zeros((128, 128), f32)
+
+    in_chunks(acc.shape[0], 128, clear)
+    add_rows(own_ref, their_ref, groups, pieces, acc, tail, wide, pair)
+
+
+def scatter_last_kernel(
+    count, groups, rows_all, own_ref, their_ref, first_acc, first_tail, lex_ref, stack_ref, *refs
+):
+    pieces = [stack_ref.at[k] for k in range(stack_ref.shape[0])] + list(refs[:count])
+    pieces = [pieces[k] for k in (1, 0, 2, 3)]
+    out_ref, square_ref, acc, tail, wide, pair = refs[count:]
+
+    def carry_over(start):
+        acc[pl.ds(start, 128), :] = first_acc[pl.ds(start, 128), :]
+        tail[pl.ds(start, 128), :] = first_tail[pl.ds(start, 128), :]
+
+    in_chunks(acc.shape[0], 128, carry_over)
+    add_rows(own_ref, their_ref, groups, pieces, acc, tail, wide, pair)
     chunks = rows_all // 128
     rest = rows_all - chunks * 128
 
@@ -292,24 +309,39 @@
     square_ref[0, 0] = total
 
 
-def scatter_rows(hits, lex, pieces, rows_all):
-    lists, starts, start = [], [], 0
-    for own_list, other_list in hits:
-        lists += [own_list, other_list]
-        starts += [(0, start), (1, start)]
-        start += own_list.shape[0] - 16
-    width = lex.shape[0]
+def scatter_first(own_list, their_list, groups, pieces, rows_all):
     half = pieces[0].shape[0] // 3
     count = len(pieces)
     padded = (rows_all // 128 + 1) * 128
     return pl.pallas_call(
-        partial(scatter_kernel, count, half, rows_all, tuple(starts)),
+        partial(scatter_first_kernel, count, groups),
+        out_shape=[jax.ShapeDtypeStruct((padded, 128), f32)] * 2,
+        in_specs=[pl.BlockSpec(memory_space=SMEM)] * 2
+        + [pl.BlockSpec(memory_space=pltpu.VMEM)] * count,
+        out_specs=[pl.BlockSpec(memory_space=pltpu.VMEM)] * 2,
+        scratch_shapes=[
+            pltpu.VMEM((count * 2 * half, 128), f32),
+            pltpu.VMEM((count * half, 128), f32),
+        ],
+        name="scatter_first",
+        cost_estimate=cost(1e10, rows_all * 128 * 8),
+    )(own_list, their_list, *pieces)
+
+
+def scatter_last(own_list, their_list, groups, before, lex, stacked, pieces, rows_all):
+    width = lex.shape[0]
+    half = stacked.shape[1] // 3
+    count = len(pieces)
+    used = count + stacked.shape[0]
+    padded = (rows_all // 128 + 1) * 128
+    return pl.pallas_call(
+        partial(scatter_last_kernel, count, groups, rows_all),
         out_shape=[
             jax.ShapeDtypeStruct((width, rows_all), f32),
             jax.ShapeDtypeStruct((1, 1), f32),
         ],
-        in_specs=[pl.BlockSpec(memory_space=SMEM)] * len(lists)
-        + [pl.BlockSpec(memory_space=pltpu.VMEM)] * (count + 1),
+        in_specs=[pl.BlockSpec(memory_space=SMEM)] * 2
+        + [pl.BlockSpec(memory_space=pltpu.VMEM)] * (count + 4),
         out_specs=[
             pl.BlockSpec(memory_space=pltpu.VMEM),
             pl.BlockSpec(memory_space=SMEM),
@@ -317,12 +349,12 @@
         scratch_shapes=[
             pltpu.VMEM((padded, 128), f32),
             pltpu.VMEM((padded, 128), f32),
-            pltpu.VMEM((count * 2 * half, 128), f32),
-            pltpu.VMEM((count * half, 128), f32),
-        ],
-        name="scatter_rows",
-        cost_estimate=cost(1.5e10, rows_all * width * 8),
-    )(*lists, lex, *pieces)
+            pltpu.VMEM((used * 2 * half, 128), f32),
+            pltpu.VMEM((used * half, 128), f32),
+        ],
+        name="scatter_last",
+        cost_estimate=cost(1e10, rows_all * width * 8),
+    )(own_list, their_list, *before, lex, stacked, *pieces)
 
 
 def norm_parts(inputs):
@@ -1308,31 +1340,37 @@
     targets_all = numbers[:, :, ny * tokens :].reshape(-1)
     lines = sorted(range(1, n1), key=lambda a: -min(a, n1 - a)) + [0]
     piece_order = [(a, b) for b in list(range(1, n0)) + [0] for a in lines]
-    early = (n0 - 1) * n1
     ids_order = [numbers[a, b, : ny * tokens] for a, b in piece_order]
-    looked, hits = [], []
-    for first, last in ((0, early), (early, n0 * n1)):
-        ids_rows = jnp.concatenate(ids_order[first:last])
+    def near_piece(h, sums, *before):
+        part = looked[n1 * (n0 - 1) + h]
+        for b in range(1, n0):
+            moved = over_voc(tie(looked[(b - 1) * n1 + h], *sums[: max(h - 1, 0)]), 0, -b)
+            part = part + tie(moved, *sums, *before)
+        return part.reshape(ny, tokens, cols_y)
+
+    looked, hits, bases, by_one = [], [], [], []
+    step = n1 // 2
+    for first in range(0, n0 * n1, step):
+        ids_rows = jnp.concatenate(ids_order[first : first + step])
         local_ids = ids_rows - vocab_start
         packed_ids = jnp.where(
             (local_ids >= 0) & (local_ids < shard_rows),
             (local_ids << 16) | jnp.arange(ids_rows.shape[0], dtype=i32),
             -1,
         )
-        hits.append(find_hits(tie(packed_ids, upright), shard_rows))
-        looked += lookup(hits[-1], upright, ids_rows.shape[0], last - first)
-
-    def near_piece(h, sums, *before):
-        part = looked[n1 * (n0 - 1) + h]
-        for b in range(1, n0):
-            moved = over_voc(tie(looked[(b - 1) * n1 + h], *sums[: max(h - 1, 0)]), 0, -b)
-            part = part + tie(moved, *sums, *before)
-        return part.reshape(ny, tokens, cols_y)
-
-    by_one = []
-    for h in range(n1 - 1):
+        bases.append(sum(own.shape[0] for own in hits))
+        if first == n0 * n1 - step:
+            by_one.append(near_piece(0, by_one))
+        hits.append(find_hits(tie(packed_ids, upright, *by_one), shard_rows))
+        looked += lookup(hits[-1], upright, ids_rows.shape[0], step)
+    hits = jnp.concatenate(hits)
+    listed = step * ny * tokens
+    early = (n0 - 1) * n1 // step
+
+    for h in range(1, n1 - 1):
         by_one.append(near_piece(h, by_one))
-    slots_y = [tie(part, by_one[1]) for part in slots_y]
+    far_parts = [over_voc(by_one[h], -lines[h], 0) for h in range(n1 - 1)]
+    slots_y = [tie(part, by_one[n1 - 2], far_parts[0]) for part in slots_y]
     slots_core = [over_dp(part, 0, 1) for part in slots_y]
     inverse = (
         jnp.zeros((block_count,), i32).at[block_order].set(jnp.arange(block_count, dtype=i32))
@@ -1343,8 +1381,7 @@
         src.astype(i32), inverse % per_owner, slots_y + slots_core
     )
 
-    far_parts = [over_voc(by_one[h], -lines[h], 0) for h in range(n1 - 1)]
-    by_one.append(near_piece(n1 - 1, by_one, wup, far_parts[0]))
+    by_one.append(near_piece(n1 - 1, by_one, wup))
     mine = by_one[-1]
     for part in far_parts:
         mine = mine + part
@@ -1378,8 +1415,8 @@
         ],
         2,
     ).reshape(2, HEADS, 2 * HD, 2 * HD)
-    their_hits = [over_dp(own, 0, 1) for own in hits]
-    h1, mixed = qkv_forward(tie(x0, *their_hits), wqkv, vectors)
+    their_hits = over_dp(hits, 0, 1)
+    h1, mixed = qkv_forward(tie(x0, their_hits), wqkv, vectors)
     y, distill = attend(seq_lengths, mixed, lift_maps)
     x1, h2, up, act, x2, picked = mlp_forward(x0, y, wo, wup, wdown, vectors, pick_rows)
 
@@ -1421,10 +1458,11 @@
         piece_places, group.T, tie(grad_logits, *by_one[:-1]), cols_own, shard_rows
     )
     lex_arrived = over_dp(lex_theirs, 0, 1)
-    lex_high = jnp.max(mine_high) + jnp.max(over_dp(theirs_high, 0, 1))
+    their_high = over_dp(theirs_high, 0, 1)
+    lex_high = jnp.max(mine_high) + jnp.max(their_high)
     ghp = by_one[-1]
     for part in near_parts:
-        ghp = ghp + tie(part, lex_theirs)
+        ghp = ghp + tie(part, lex_theirs, their_high)
 
     def lex_lines(k):
         lines = slice(k * cols_own, (k + 1) * cols_own)
@@ -1507,7 +1545,7 @@
     moved_a = moved_parts(sent_a, 0)
     rows_sent = jnp.take(arrived, (c_at + 1) % nc, axis=1)
     rows_other = over_dp(rows_sent, 0, 1)
-    if cols_own == 192:
+    if cols_own == 192 and n0 == 2 and n1 == 4:
         packed = jnp.concatenate(
             [
                 rows_mine[:, :128],
@@ -1518,35 +1556,50 @@
         )
     else:
         packed = jnp.stack([rows_mine, rows_other])
-    halves_b = qkv_weights(core, tie(h1, rows_sent, *moved_a), gqkv, y, ga, small)
+    halves_b = qkv_weights(core, tie(h1, packed, *moved_a), gqkv, y, ga, small)
     total_a, high_a = collect(own_a, moved_a, bound_a, halves_b[0])
+    near_raw = [over_voc(packed, k, 0) for k in range(1, n1)]
     own_b, sent_b, bound_b = core_parts(*halves_b, packed)
-    near_raw = [over_voc(packed, k, 0) for k in range(1, n1)]
-    total_b, high_b = collect(own_b, moved_parts(sent_b, 0), bound_b, near_raw[0])
+    total_b, high_b = collect(own_b, moved_parts(sent_b, 0), bound_b)
+    own_a, sent_a = coded_parts((total_a,), high_a, 1)
+    own_b, sent_b = coded_parts((total_b,), high_b, 1)
+    near_rows = [packed] + [tie(part, *sent_b) for part in near_raw]
+    total_a, high_a = collect(own_a, moved_parts(sent_a, 1), high_a, *sent_b)
+    total_b, high_b = collect(own_b, moved_parts(sent_b, 1), high_b)
     total = jnp.concatenate([total_a, total_b], 0)
+    own, sent = coded_parts((total,), jnp.maximum(high_a, high_b), 2)
     high = jnp.maximum(high_a, high_b)
-    own, sent = coded_parts((total,), high, 1)
-    near_rows = [packed] + [tie(part, *sent) for part in near_raw]
-    total, high = collect(own, moved_parts(sent, 1), high)
-    own, sent = coded_parts((total,), high, 2)
-    gathered = [[packed] + [over_voc(packed, 0, k) for k in range(1, n0)]]
-    sent = [tie(part, *near_rows, *gathered[0]) for part in sent]
-    gathered += [[part] + [over_voc(part, 0, k) for k in range(1, n0)] for part in near_rows[1:]]
+    own_x = [over_voc(tie(packed, *sent_b, near_rows[-2]), 0, k) for k in range(1, n0)]
+    sent = [tie(part, *near_rows) for part in sent]
+    far_rows = jnp.stack([tie(part, *own_x) for part in near_rows[1:]])
+    far_x = [over_voc(far_rows, 0, k) for k in range(1, n0)]
     moved_ab = moved_parts(sent, 2)
-    lex = tie(lex, moved_ab[0])
-    if cols_own == 192:
-        pieces = [gathered[a][b] for a, b in piece_order]
-        emb_grads, emb_square = scatter_rows(
-            list(zip(hits, their_hits)), lex, pieces, shard_rows
+
+    if cols_own == 192 and n0 == 2 and n1 == 4:
+        groups = [(base, listed, (g % early) * listed) for g, base in enumerate(bases)]
+        before = scatter_first(
+            hits,
+            their_hits,
+            groups[early:],
+            [tie(near_rows[a], *sent) for a in lines],
+            shard_rows,
+        )
+        lex = tie(lex, *before, moved_ab[0])
+        emb_grads, emb_square = scatter_last(
+            hits, their_hits, groups[:early], before, lex, far_x[0], own_x, shard_rows
         )
         emb_square = emb_square[0, 0]
     else:
+        gathered = [[packed] + own_x]
+        for a in range(1, n1):
+            gathered.append([near_rows[a]] + [part[a - 1] for part in far_x])
         pieces = jnp.stack([gathered[a][b] for a, b in piece_order], 1).reshape(-1, cols_own)
         ids_rows = jnp.concatenate(ids_order)
         local = jnp.concatenate([ids_rows, over_dp(ids_rows, 0, 1)]) - vocab_start
         local = jnp.where((local >= 0) & (local < shard_rows), local, shard_rows)
         emb_grads = lex[:, :shard_rows].T.at[local].add(pieces.astype(f32), mode="drop").T
         emb_square = jnp.sum(emb_grads * emb_grads)
+
     blocks = collect(own, moved_ab, high, emb_grads)[0]
 
     square = emb_square + jnp.sum(blocks * blocks)

time: 829 us -> 787 us (0.949)
  waiting for transfers between devices: 265 us -> 198 us
  Pallas kernels: 291 us -> 304 us
  other arithmetic: 114 us -> 125 us
    ppermute x49 -> x47, waiting for transfers between devices: 237 us -> 169 us  [over_voc(): return lax.ppermute(values, 'vocab', pairs)]
    pallas_call x2 -> x4, Pallas kernels: 19.2 us -> 26.3 us  [lookup(): pl.pallas_call(partial(lookup_kernel, rows_all), out_shape=[jax.ShapeDtyp...]
    pallas_call x1 -> x2, Pallas kernels: 27.9 us -> 31.4 us  [the longest x1 19.8 us: scatter_last(): pl.pallas_call(partial(scatter_last_kernel, count, groups, rows_all), out...]
    ppermute x49 -> x47, starting transfers between devices: 70.8 us -> 68 us  [over_voc(): return lax.ppermute(values, 'vocab', pairs)]
    pallas_call x2 -> x4, Pallas kernels: 25.5 us -> 27.9 us  [find_hits(): pl.pallas_call(partial(hits_kernel, empty_row), out_shape=jax.ShapeDtypeS...]
    convert_element_type x6 -> x7, other arithmetic: 14.7 us -> 16.9 us  [encode(): coded = (values * jnp.exp2(15.0 - level)).astype(jnp.float16)]
  transfers between devices with their start and end apart: 73 -> 71, of which waited for: 37 -> 39; matrix products, arithmetic and copies ran while one was open for 14% -> 18% of each run, Pallas kernels for 25% -> 28%
where the time goes in v4:
time: 787 us; the launch traced here: 782 us
  Pallas kernels  304 us (39%)
  waiting for transfers between devices  198 us (25%)
  other arithmetic  125 us (16%)
  starting transfers between devices  83.8 us (11%)
  local copies, waits for them, and re-layouts  54.1 us (7%)
  between operations  17.5 us (2%)
    ppermute x47, waiting for transfers between devices, over_voc(): return lax.ppermute(values, 'vocab', pairs)  169 us
    ppermute x47, starting transfers between devices, over_voc(): return lax.ppermute(values, 'vocab', pairs)  68 us
    pallas_call x1, Pallas kernels, attend_back(): pl.pallas_call(partial(attend_back_kernel, coefficient, int(later)), grid...  35.9 us
    pallas_call x1, Pallas kernels, shampoo(): pl.pallas_call(partial(shampoo_kernel, count, strip), grid=(slots,), out_...  35.3 us
    ppermute x24, waiting for transfers between devices, over_dp(): return lax.ppermute(values, 'dp', pairs)  28.7 us
    pallas_call x4, Pallas kernels, find_hits(): pl.pallas_call(partial(hits_kernel, empty_row), out_shape=jax.ShapeDtypeS...  27.9 us
    pallas_call x4, Pallas kernels, lookup(): pl.pallas_call(partial(lookup_kernel, rows_all), out_shape=[jax.ShapeDtyp...  26.3 us
    pallas_call x1, Pallas kernels, mlp_back(): pl.pallas_call(mlp_back_kernel, grid=(FSTEPS,), out_shape=[halves, halves...  26.2 us
  transfers between devices with their start and end apart: 71, of which 39 were waited for; matrix products, arithmetic and copies ran while one was open for 18% of the time, Pallas kernels for 28%

profile of v4, /device:TPU:8, one launch (start us, length us, event | category | flops | bytes accessed | tf_op | source)
XLA Modules:
  0.0 781.9 jit_solution(18088628935956711311)
XLA Ops:
  5.0 5.3 convert_element_type.163.refs_0_
  16.8 4.4 collective-permute-start.2
  23.6 7.4 turn_table.1.table_ref
  31.0 7.0 find_hits.4.list_ref
  38.0 6.5 lookup.5
  47.1 7.0 find_hits.6.list_ref
  54.1 6.6 lookup.4
  60.7 7.0 find_hits.5.list_ref
  67.7 6.6 lookup.7
  83.1 7.0 find_hits.7.list_ref
  90.1 6.5 lookup.6
  98.9 10.4 %collective-permute-done.11 = bf16[2,512,384]{2,1,0:T(8,128)(2,1)S(1)} collective-permute-done((bf16[2,512,384]{2,1,0:T(8,128)(2,1)S(1)}, bf16[2,512,384]{2,1,0:T(8,128)(2,1)S(1)}, u32[]{:S(2)}, u32[]{:S(2)}) %collective-permute-start.11) | collective-permute-done | bytes 786464 | tf_op jit(solution)/shard_map/ppermute | solution.py:1291
  117.1 4.5 collective-permute-done.13.refs_2_
  123.4 11.5 %place_blocks.1 = (bf16[768,2304]{1,0:T(8,128)(2,1)}, bf16[768,768]{1,0:T(8,128)(2,1)}, bf16[768,3072]{1,0:T(8,128)(2,1)}, bf16[3072,768]{1,0:T(8,128)(2,1)}) custom-call(s32[48]{0:T(128)} %get-tuple-element.356.src_ref, s32[48]{0:T(128)} %get-tuple-element.355.off_ref, bf16[12,384,384]{2,1,0:T(8,128)(2,1)} %convert_element_type.163.refs_0_, ...), custom_call_target="tpu_custom_call" | custom-call | bytes 566231 | tf_op jit(solution)/shard_map/place_blocks/pallas_call | solution.py:110
  136.6 13.7 %collective-permute-done.16 = bf16[2,512,384]{2,1,0:T(8,128)(2,1)} collective-permute-done((bf16[2,512,384]{2,1,0:T(8,128)(2,1)}, bf16[2,512,384]{2,1,0:T(8,128)(2,1)}, u32[]{:S(2)}, u32[]{:S(2)}) %collective-permute-start.16) | collective-permute-done | bytes 786464 | tf_op jit(solution)/shard_map/ppermute | solution.py:1291
  155.1 8.6 %collective-permute-done.17 = bf16[512,384]{1,0:T(8,128)(2,1)} collective-permute-done((bf16[512,384]{1,0:T(8,128)(2,1)}, bf16[512,384]{1,0:T(8,128)(2,1)}, u32[]{:S(2)}, u32[]{:S(2)}) %collective-permute-start.17) | collective-permute-done | bytes 393248 | tf_op jit(solution)/shard_map/ppermute | solution.py:1285
  169.9 6.2 qkv_forward.1
  176.1 20.0 %attend.1 = (bf16[512,768]{1,0:T(8,128)(2,1)}, f32[8,128]{1,0:T(8,128)}) custom-call(s32[1,4]{1,0:T(1,128)} %len_ref.3, bf16[512,2304]{1,0:T(8,128)(2,1)} %get-tuple-element.149.q_ref.k_ref.v_ref, bf16[512,2304]{1,0:T(8,128)(2,1)} %get-tuple-element.149.q_ref.k_ref.v_ref, bf16[512,2304]{1,0:T(8,128)(2,1)} %get-tuple-element.149.q_ref.k_ref.v_ref, ...), custom_call_target="tpu_custom_call" | custom-call | flops 240000000 | bytes 80000 | tf_op jit(solution)/shard_map/attend/pallas_call | solution.py:495
  196.1 14.8 %mlp_forward.1 = (f32[512,768]{1,0:T(8,128)}, bf16[512,768]{1,0:T(8,128)(2,1)}, f32[512,3072]{1,0:T(8,128)}, bf16[512,3072]{1,0:T(8,128)(2,1)}, f32[512,768]{1,0:T(8,128)}, /*index=5*/bf16[64,768]{1,0:T(8,128)(2,1)}) custom-call(bf16[512,768]{1,0:T(8,128)(2,1)} %pad_maximum_fusion.4.x_ref, bf16[512,768]{1,0:T(8,128)(2,1)} %get-tuple-element.150.y_ref, ...), custom_call_target="tpu_custom_call" | custom-call | flops 108716360 | bytes 600000 | tf_op jit(solution)/shard_map/mlp_forward/pallas_call | solution.py:693
  213.7 5.6 collective-permute-done.18
  227.3 10.0 %collective-permute-done.20 = bf16[128,768]{0,1:T(8,128)(2,1)S(1)} collective-permute-done((bf16[128,768]{0,1:T(8,128)(2,1)S(1)}, bf16[128,768]{0,1:T(8,128)(2,1)S(1)}, u32[]{:S(2)}, u32[]{:S(2)}) %collective-permute-start.20) | collective-permute-done | bytes 196640 | tf_op jit(solution)/shard_map/ppermute | solution.py:1291
  244.7 15.9 %vocabulary_logits.1 = (f32[512,6288]{1,0:T(8,128)}, f32[8,512]{1,0:T(8,128)}) custom-call(s32[4]{0:T(128)} %pad_add_fusion.5.places_ref, bf16[512,768]{1,0:T(8,128)(2,1)} %copy.72.group_ref, s32[512,1]{1,0:T(8,128)} %sub.290.target_ref, bf16[192,6288]{1,0:T(8,128)(2,1)} %copy-done.2, bf16[192,6288]{1,0:T(8,128)(2,1)} %collective-permute-done.22.refs_1_, ...), custom_call_target="tpu_custom_call" | custom-call | flops 98901688 | bytes 400000 | tf_op jit(solution)/shard_map/vocabulary_logits/pallas_call | solution.py:1038
  273.1 15.3 %vocabulary_back.1 = (bf16[512,6400]{1,0:T(8,128)(2,1)}, f32[512,768]{1,0:T(8,128)}) custom-call(s32[4]{0:T(128)} %pad_add_fusion.5.places_ref, f32[512,6288]{1,0:T(8,128)} %get-tuple-element.156.logit_ref, f32[128,512]{1,0:T(8,128)} %select_maximum_fusion.stat_ref, s32[512,1]{1,0:T(8,128)} %sub.290.target_ref, bf16[192,6288]{1,0:T(8,128)(2,1)} %copy-done.2, ...), custom_call_target="tpu_custom_call" | custom-call | flops 98901688 | bytes 600000 | tf_op jit(solution)/shard_map/vocabulary_back/pallas_call | solution.py:1081
  293.4 4.1 collective-permute-done.31
  304.1 11.7 %lexicon.1 = (f32[384,6400]{1,0:T(8,128)}, f32[384,6400]{1,0:T(8,128)}, f32[1,1280]{1,0:T(1,128)}, f32[1,1280]{1,0:T(1,128)}) custom-call(s32[4]{0:T(128)} %pad_add_fusion.5.places_ref, bf16[768,512]{1,0:T(8,128)(2,1)} %bitcast.236, bf16[512,6400]{1,0:T(8,128)(2,1)} %get-tuple-element.160.grad_ref), custom_call_target="tpu_custom_call" | custom-call | flops 100663296 | bytes 600000 | tf_op jit(solution)/shard_map/lexicon/pallas_call | solution.py:1127
  324.1 10.1 %collective-permute-done.34 = f32[64,768]{1,0:T(8,128)S(1)} collective-permute-done((f32[64,768]{1,0:T(8,128)S(1)}, f32[64,768]{1,0:T(8,128)S(1)}, u32[]{:S(2)}, u32[]{:S(2)}) %collective-permute-start.34) | collective-permute-done | bytes 196640 | tf_op jit(solution)/shard_map/ppermute | solution.py:1291
  338.5 26.2 %mlp_back.1 = (f32[16,384,384]{2,1,0:T(8,128)}, f32[16,384,384]{2,1,0:T(8,128)}, f32[1,384]{1,0:T(1,128)}, f32[1,384]{1,0:T(1,128)}, f32[512,768]{1,0:T(8,128)},...) custom-call(s32[1]{0:T(128)} %bitcast.4.core_ref, f32[64,768]{1,0:T(8,128)} %fusion.37.ghp_ref, ...), custom_call_target="tpu_custom_call" | custom-call | flops 193273536 | bytes 1000000 | tf_op jit(solution)/shard_map/mlp_back/pallas_call | solution.py:833
  367.5 6.1 fusion.7
  376.0 3.4 collective-permute-done.38
  381.4 10.4 %multiply_convert_fusion = (f16[16,192,384]{2,1,0:T(8,128)(2,1)S(1)}, f32[16,192,384]{2,1,0:T(8,128)}) fusion(f32[16,384,384]{2,1,0:T(8,128)} %collective-permute-done.37, s32[]{:T(128)S(6)} %select_n.387, f32[16,384,384]{2,1,0:T(8,128)} %get-tuple-element.174, f32[]{:T(128)S(6)} %exp2.159, s32[]{:T(128)S(6)} %select_n.385), kind=kLoop, calls=%fused_computation.32 | loop fusion | flops 4718592 | bytes 25952268 | tf_op jit(solution)/shard_map/convert_element_type | solution.py:1224
  395.5 35.9 %attend_back.1 = (bf16[3,512,768]{2,1,0:T(8,128)(2,1)}, f32[12,64,64]{2,1,0:T(8,128)}, f32[12,64,64]{2,1,0:T(8,128)}) custom-call(s32[1,4]{1,0:T(1,128)} %len_ref.3, bf16[512,2304]{1,0:T(8,128)(2,1)} %get-tuple-element.149.q_ref.k_ref.v_ref, bf16[512,2304]{1,0:T(8,128)(2,1)} %get-tuple-element.149.q_ref.k_ref.v_ref, ...), custom_call_target="tpu_custom_call" | custom-call | flops 240000000 | bytes 80000 | tf_op jit(solution)/shard_map/attend_back/pallas_call | solution.py:607
  431.3 7.9 %qkv_back.1 = (bf16[512,768]{1,0:T(8,128)(2,1)}, f32[16,768]{1,0:T(8,128)}) custom-call(bf16[3,512,768]{2,1,0:T(8,128)(2,1)} %get-tuple-element.180.g_ref, bf16[768,2304]{1,0:T(8,128)(2,1)} %get-tuple-element.148.w_ref, bf16[512,768]{1,0:T(8,128)(2,1)} %pad_maximum_fusion.4.x_ref, f32[512,768]{1,0:T(8,128)} %get-tuple-element.181.gx1_ref, f32[15,768]{1,0:T(8,128)} %vec_ref.7), custom_call_target="tpu_custom_call" | custom-call | flops 36238784 | bytes 200000 | tf_op jit(solution)/shard_map/qkv_back/pallas_call | solution.py:897
  447.3 7.5 fusion.1.lex_ref
  457.8 10.4 %qkv_weights.1 = (f32[9,384,384]{2,1,0:T(8,128)}, f32[9,384,384]{2,1,0:T(8,128)}, f32[1,384]{1,0:T(1,128)}, f32[1,384]{1,0:T(1,128)}) custom-call(s32[1]{0:T(128)} %bitcast.4.core_ref, bf16[512,768]{1,0:T(8,128)(2,1)} %get-tuple-element.185.h_ref, bf16[3,512,768]{2,1,0:T(8,128)(2,1)} %get-tuple-element.180.g_ref, bf16[512,768]{1,0:T(8,128)(2,1)} %get-tuple-element.150.y_ref, ...), custom_call_target="tpu_custom_call" | custom-call | flops 48318384 | bytes 400000 | tf_op jit(solution)/shard_map/qkv_weights/pallas_call | solution.py:949
  471.8 5.4 collective-permute-done.45
  484.7 4.2 convert_element_type.178
  504.1 11.3 %collective-permute-done.46 = f16[1744,384]{1,0:T(8,128)(2,1)S(1)} collective-permute-done((f16[1744,384]{1,0:T(8,128)(2,1)}, f16[1744,384]{1,0:T(8,128)(2,1)S(1)}, u32[]{:S(2)}, u32[]{:S(2)}) %collective-permute-start.46) | collective-permute-done | bytes 1339424 | tf_op jit(solution)/shard_map/ppermute | solution.py:1291
  518.6 3.7 add_add_fusion
  532.2 19.9 %collective-permute-done.49.refs_1_ = bf16[3072,128]{1,0:T(8,128)(2,1)} collective-permute-done((bf16[3072,128]{1,0:T(8,128)(2,1)S(1)}, bf16[3072,128]{1,0:T(8,128)(2,1)}, u32[]{:S(2)}, u32[]{:S(2)}) %collective-permute-start.49) | collective-permute-done | bytes 786464 | tf_op jit(solution)/shard_map/ppermute | solution.py:1291
  581.4 11.6 %scatter_first.1 = (f32[6400,128]{1,0:T(8,128)}, f32[6400,128]{1,0:T(8,128)}) custom-call(s32[8256]{0:T(1024)} %copy-done.22, s32[8256]{0:T(1024)} %copy-done.25, bf16[3072,128]{1,0:T(8,128)(2,1)} %collective-permute-done.42.refs_0_, bf16[3072,128]{1,0:T(8,128)(2,1)} %collective-permute-done.49.refs_1_, bf16[3072,128]{1,0:T(8,128)(2,1)} %collective-permute-done.50.refs_2_, ...), custom_call_target="tpu_custom_call" | custom-call | flops 200000000 | bytes 128778 | tf_op jit(solution)/shard_map/scatter_first/pallas_call | solution.py:316
  593.0 13.9 %collective-permute-done.51 = f16[616,384]{1,0:T(8,128)(2,1)S(1)} collective-permute-done((f16[616,384]{1,0:T(8,128)(2,1)}, f16[616,384]{1,0:T(8,128)(2,1)S(1)}, u32[]{:S(2)}, u32[]{:S(2)}) %collective-permute-start.51) | collective-permute-done | bytes 473120 | tf_op jit(solution)/shard_map/ppermute | solution.py:1291
  608.8 19.8 %scatter_last.1 = (f32[192,6288]{1,0:T(8,128)}, f32[1,1]{1,0:T(1,128)}) custom-call(s32[8256]{0:T(1024)} %copy-done.22, s32[8256]{0:T(1024)} %copy-done.25, f32[6400,128]{1,0:T(8,128)} %get-tuple-element.208.first_acc, f32[6400,128]{1,0:T(8,128)} %get-tuple-element.209.first_tail, f32[192,6400]{1,0:T(8,128)} %fusion.1.lex_ref, ...), custom_call_target="tpu_custom_call" | custom-call | flops 200000000 | bytes 193167 | tf_op jit(solution)/shard_map/scatter_last/pallas_call | solution.py:337
  654.6 9.9 %collective-permute-start.62 = (f32[8,128]{1,0:T(8,128)S(1)}, f32[8,128]{1,0:T(8,128)S(1)}, u32[]{:S(2)}, u32[]{:S(2)}) collective-permute-start(f32[8,128]{1,0:T(8,128)S(1)} %select_reduce_fusion.1), channel_id=1, source_target_pairs={{0,4},{1,5},{2,6},{3,7},{4,0},{5,1},{6,2},{7,3},{8,12},{9,13},{10,... | collective-permute-start | bytes 12296 | tf_op jit(solution)/shard_map/ppermute | solution.py:1291
  668.8 4.1 collective-permute-start.67
  676.0 27.9 %collective-permute-done.65 = f16[688,384]{1,0:T(8,128)(2,1)S(1)} collective-permute-done((f16[688,384]{1,0:T(8,128)(2,1)S(1)}, f16[688,384]{1,0:T(8,128)(2,1)S(1)}, u32[]{:S(2)}, u32[]{:S(2)}) %collective-permute-start.65) | collective-permute-done | bytes 528416 | tf_op jit(solution)/shard_map/ppermute | solution.py:1291
  703.9 7.7 collective-permute-done.67
  714.9 12.2 %fusion.11 = (f32[6288,192]{0,1:T(8,128)}, f32[6288,192]{0,1:T(8,128)}, f32[6288,192]{0,1:T(8,128)}) fusion(f32[192,6288]{1,0:T(8,128)} %get-tuple-element.216, f32[]{:T(128)} %div.104, f32[6288,192]{0,1:T(8,128)} %param.49, f32[]{:T(128)} %bitcast.122, f32[]{:T(128)} %bitcast.120, f32[6288,192]{0,1:T(8,128)} %param.48, f32[6288,192]{0,1:T(8,128)} %param.47), kind=kLoop, calls=%fused_computation.55 | loop fusion | flops 19316736 | bytes 33804300 | tf_op jit(solution)/shard_map/transpose | solution.py:1687
  736.8 35.3 %shampoo.1 = (f32[12,384,384]{2,1,0:T(8,128)}, f32[12,384,384]{2,1,0:T(8,128)}, f32[12,384,384]{2,1,0:T(8,128)}, f32[12,384,384]{2,1,0:T(8,128)}, f32[2,384,384]{2,1,0:T(8,128)}) custom-call(s32[8]{0:T(128)} %stack.250.places_ref, f32[1]{0:T(128)} %bitcast.111.clip_ref, f32[688,384]{1,0:T(8,128)} %convert_element_type.202.refs_0_.refs_8_.refs_16_, ...), custom_call_target="tpu_custom_call" | custom-call | flops 326149088 | bytes 1415577 | tf_op jit(solution)/shard_map/shampoo/pallas_call | solution.py:1187
  (460 shorter events, 236.4 us)
Async XLA Ops:
  3.3 20.3 %collective-permute-start.4 = (bf16[192,6288]{1,0:T(8,128)(2,1)S(1)}, bf16[192,6288]{1,0:T(8,128)(2,1)}, u32[]{:S(2)}, u32[]{:S(2)}) collective-permute-start(bf16[192,6288]{1,0:T(8,128)(2,1)S(1)} %bitcast_convert_fusion.own_ref.refs_0_), channel_id=1, source_target_pairs={{0,8},{8,0},{16,24},{24,16},{1,9},{9,1},{17,25},{25,17},{2,10},{10... | collective-permute-start | bytes 7243784 | tf_op jit(solution)/shard_map/ppermute | solution.py:1285
  10.3 99.8 %collective-permute-start.12 = (bf16[12,384,384]{2,1,0:T(8,128)(2,1)}, bf16[12,384,384]{2,1,0:T(8,128)(2,1)}, u32[]{:S(2)}, u32[]{:S(2)}) collective-permute-start(bf16[12,384,384]{2,1,0:T(8,128)(2,1)} %convert_element_type.163.refs_0_), channel_id=1, source_target_pairs={{0,16},{8,24},{16,0},{24,8},{1,17},{9,25},{17,1},{25,9},{2,18},{10... | collective-permute-start | bytes 10616840 | tf_op jit(solution)/shard_map/ppermute | solution.py:1285
  44.5 29.8 %collective-permute-start.6 = (bf16[1024,384]{1,0:T(8,128)(2,1)}, bf16[1024,384]{1,0:T(8,128)(2,1)S(1)}, u32[]{:S(2)}, u32[]{:S(2)}) collective-permute-start(bf16[1024,384]{1,0:T(8,128)(2,1)} %get-tuple-element.130), channel_id=1, source_target_pairs={{0,1},{1,0},{2,3},{3,2},{4,5},{5,4},{6,7},{7,6},{8,9},{9,8},{10,11... | collective-permute-start | bytes 2359304 | tf_op jit(solution)/shard_map/ppermute | solution.py:1291
  46.5 35.5 %collective-permute-start.8 = (bf16[1024,384]{1,0:T(8,128)(2,1)}, bf16[1024,384]{1,0:T(8,128)(2,1)S(1)}, u32[]{:S(2)}, u32[]{:S(2)}) collective-permute-start(bf16[1024,384]{1,0:T(8,128)(2,1)} %get-tuple-element.135), channel_id=1, source_target_pairs={{0,1},{1,0},{2,3},{3,2},{4,5},{5,4},{6,7},{7,6},{8,9},{9,8},{10,11... | collective-permute-start | bytes 2359304 | tf_op jit(solution)/shard_map/ppermute | solution.py:1291
  74.5 22.1 %collective-permute-start.10 = (bf16[1024,384]{1,0:T(8,128)(2,1)}, bf16[1024,384]{1,0:T(8,128)(2,1)S(1)}, u32[]{:S(2)}, u32[]{:S(2)}) collective-permute-start(bf16[1024,384]{1,0:T(8,128)(2,1)} %get-tuple-element.140), channel_id=1, source_target_pairs={{0,1},{1,0},{2,3},{3,2},{4,5},{5,4},{6,7},{7,6},{8,9},{9,8},{10,11... | collective-permute-start | bytes 2359304 | tf_op jit(solution)/shard_map/ppermute | solution.py:1291
  75.8 33.5 %collective-permute-start.11 = (bf16[2,512,384]{2,1,0:T(8,128)(2,1)S(1)}, bf16[2,512,384]{2,1,0:T(8,128)(2,1)S(1)}, u32[]{:S(2)}, u32[]{:S(2)}) collective-permute-start(bf16[2,512,384]{2,1,0:T(8,128)(2,1)S(1)} %bitcast.261), channel_id=1, source_target_pairs={{0,4},{1,5},{2,6},{3,7},{4,0},{5,1},{6,2},{7,3},{8,12},{9,13},{10,... | collective-permute-start | bytes 2359304 | tf_op jit(solution)/shard_map/ppermute | solution.py:1291
  110.2 11.5 %collective-permute-start.13 = (bf16[12,384,384]{2,1,0:T(8,128)(2,1)}, bf16[12,384,384]{2,1,0:T(8,128)(2,1)S(1)}, u32[]{:S(2)}, u32[]{:S(2)}) collective-permute-start(bf16[12,384,384]{2,1,0:T(8,128)(2,1)} %convert_element_type.163.refs_0_), channel_id=1, source_target_pairs={{0,8},{8,0},{16,24},{24,16},{1,9},{9,1},{17,25},{25,17},{2,10},{10... | collective-permute-start | bytes 10616840 | tf_op jit(solution)/shard_map/ppermute | solution.py:1285
  110.2 11.6 %collective-permute-start.14 = (bf16[12,384,384]{2,1,0:T(8,128)(2,1)}, bf16[12,384,384]{2,1,0:T(8,128)(2,1)}, u32[]{:S(2)}, u32[]{:S(2)}) collective-permute-start(bf16[12,384,384]{2,1,0:T(8,128)(2,1)} %collective-permute-done.12.refs_1_), channel_id=1, source_target_pairs={{0,8},{8,0},{16,24},{24,16},{1,9},{9,1},{17,25},{25,17},{2,10},{10... | collective-permute-start | bytes 10616840 | tf_op jit(solution)/shard_map/ppermute | solution.py:1285
  110.7 24.2 %collective-permute-start.9 = (bf16[1024,384]{1,0:T(8,128)(2,1)}, bf16[1024,384]{1,0:T(8,128)(2,1)}, u32[]{:S(2)}, u32[]{:S(2)}) collective-permute-start(bf16[1024,384]{1,0:T(8,128)(2,1)} %get-tuple-element.137), channel_id=1, source_target_pairs={{0,1},{1,0},{2,3},{3,2},{4,5},{5,4},{6,7},{7,6},{8,9},{9,8},{10,11... | collective-permute-start | bytes 2359304 | tf_op jit(solution)/shard_map/ppermute | solution.py:1291
  111.0 25.5 %collective-permute-start.15 = (bf16[2,512,384]{2,1,0:T(8,128)(2,1)}, bf16[2,512,384]{2,1,0:T(8,128)(2,1)}, u32[]{:S(2)}, u32[]{:S(2)}) collective-permute-start(bf16[2,512,384]{2,1,0:T(8,128)(2,1)} %bitcast.260), channel_id=1, source_target_pairs={{0,6},{1,7},{2,0},{3,1},{4,2},{5,3},{6,4},{7,5},{8,14},{9,15},{10,... | collective-permute-start | bytes 2359304 | tf_op jit(solution)/shard_map/ppermute | solution.py:1291
  113.3 36.9 %collective-permute-start.16 = (bf16[2,512,384]{2,1,0:T(8,128)(2,1)}, bf16[2,512,384]{2,1,0:T(8,128)(2,1)}, u32[]{:S(2)}, u32[]{:S(2)}) collective-permute-start(bf16[2,512,384]{2,1,0:T(8,128)(2,1)} %bitcast.16), channel_id=1, source_target_pairs={{0,2},{1,3},{2,4},{3,5},{4,6},{5,7},{6,0},{7,1},{8,10},{9,11},{10,... | collective-permute-start | bytes 2359304 | tf_op jit(solution)/shard_map/ppermute | solution.py:1291
  153.5 10.2 %collective-permute-start.17 = (bf16[512,384]{1,0:T(8,128)(2,1)}, bf16[512,384]{1,0:T(8,128)(2,1)}, u32[]{:S(2)}, u32[]{:S(2)}) collective-permute-start(bf16[512,384]{1,0:T(8,128)(2,1)} %slice_bitcast_fusion), channel_id=1, source_target_pairs={{0,16},{8,24},{16,0},{24,8},{1,17},{9,25},{17,1},{25,9},{2,18},{10... | collective-permute-start | bytes 1179656 | tf_op jit(solution)/shard_map/ppermute | solution.py:1285
  165.9 53.4 %collective-permute-start.22 = (bf16[192,6288]{1,0:T(8,128)(2,1)S(1)}, bf16[192,6288]{1,0:T(8,128)(2,1)}, u32[]{:S(2)}, u32[]{:S(2)}) collective-permute-start(bf16[192,6288]{1,0:T(8,128)(2,1)S(1)} %copy-done.3), channel_id=1, source_target_pairs={{0,16},{8,24},{16,0},{24,8},{1,17},{9,25},{17,1},{25,9},{2,18},{10... | collective-permute-start | bytes 7243784 | tf_op jit(solution)/shard_map/ppermute | solution.py:1285
  219.3 23.9 %collective-permute-start.23 = (bf16[192,6288]{1,0:T(8,128)(2,1)}, bf16[192,6288]{1,0:T(8,128)(2,1)S(1)}, u32[]{:S(2)}, u32[]{:S(2)}) collective-permute-start(bf16[192,6288]{1,0:T(8,128)(2,1)} %collective-permute-done.22.refs_1_), channel_id=1, source_target_pairs={{0,8},{8,0},{16,24},{24,16},{1,9},{9,1},{17,25},{25,17},{2,10},{10... | collective-permute-start | bytes 7243784 | tf_op jit(solution)/shard_map/ppermute | solution.py:1285
  219.6 17.7 %collective-permute-start.20 = (bf16[128,768]{0,1:T(8,128)(2,1)S(1)}, bf16[128,768]{0,1:T(8,128)(2,1)S(1)}, u32[]{:S(2)}, u32[]{:S(2)}) collective-permute-start(bf16[128,768]{0,1:T(8,128)(2,1)S(1)} %pad_maximum_fusion.9), channel_id=1, source_target_pairs={{0,4},{1,5},{2,6},{3,7},{4,0},{5,1},{6,2},{7,3},{8,12},{9,13},{10,... | collective-permute-start | bytes 589832 | tf_op jit(solution)/shard_map/ppermute | solution.py:1291
  222.6 18.1 %collective-permute-start.21 = (bf16[128,768]{0,1:T(8,128)(2,1)S(1)}, bf16[128,768]{0,1:T(8,128)(2,1)}, u32[]{:S(2)}, u32[]{:S(2)}) collective-permute-start(bf16[128,768]{0,1:T(8,128)(2,1)S(1)} %pad_maximum_fusion.9), channel_id=1, source_target_pairs={{0,6},{1,7},{2,0},{3,1},{4,2},{5,3},{6,4},{7,5},{8,14},{9,15},{10,... | collective-permute-start | bytes 589832 | tf_op jit(solution)/shard_map/ppermute | solution.py:1291
  291.4 9.5 %collective-permute-start.32 = (f32[64,768]{1,0:T(8,128)S(1)}, f32[64,768]{1,0:T(8,128)S(1)}, u32[]{:S(2)}, u32[]{:S(2)}) collective-permute-start(f32[64,768]{1,0:T(8,128)S(1)} %get-tuple-element.301), channel_id=1, source_target_pairs={{0,1},{1,0},{2,3},{3,2},{4,5},{5,4},{6,7},{7,6},{8,9},{9,8},{10,11... | collective-permute-start | bytes 589832 | tf_op jit(solution)/shard_map/ppermute | solution.py:1291
  291.7 11.2 %collective-permute-start.29 = (f32[64,768]{1,0:T(8,128)S(1)}, f32[64,768]{1,0:T(8,128)S(1)}, u32[]{:S(2)}, u32[]{:S(2)}) collective-permute-start(f32[64,768]{1,0:T(8,128)S(1)} %get-tuple-element.303), channel_id=1, source_target_pairs={{0,1},{1,0},{2,3},{3,2},{4,5},{5,4},{6,7},{7,6},{8,9},{9,8},{10,11... | collective-permute-start | bytes 589832 | tf_op jit(solution)/shard_map/ppermute | solution.py:1291
  315.8 51.6 %collective-permute-start.36 = (f32[384,6400]{1,0:T(8,128)}, f32[384,6400]{1,0:T(8,128)}, u32[]{:S(2)}, u32[]{:S(2)}) collective-permute-start(f32[384,6400]{1,0:T(8,128)} %get-tuple-element.161), channel_id=1, source_target_pairs={{0,8},{8,0},{16,24},{24,16},{1,9},{9,1},{17,25},{25,17},{2,10},{10... | collective-permute-start | bytes 29491208 | tf_op jit(solution)/shard_map/ppermute | solution.py:1285
  317.2 17.0 %collective-permute-start.34 = (f32[64,768]{1,0:T(8,128)S(1)}, f32[64,768]{1,0:T(8,128)S(1)}, u32[]{:S(2)}, u32[]{:S(2)}) collective-permute-start(f32[64,768]{1,0:T(8,128)S(1)} %get-tuple-element.304), channel_id=1, source_target_pairs={{0,4},{1,5},{2,6},{3,7},{4,0},{5,1},{6,2},{7,3},{8,12},{9,13},{10,... | collective-permute-start | bytes 589832 | tf_op jit(solution)/shard_map/ppermute | solution.py:1291
  319.2 17.6 %collective-permute-start.30 = (f32[64,768]{1,0:T(8,128)S(1)}, f32[64,768]{1,0:T(8,128)S(1)}, u32[]{:S(2)}, u32[]{:S(2)}) collective-permute-start(f32[64,768]{1,0:T(8,128)S(1)} %get-tuple-element.306), channel_id=1, source_target_pairs={{0,6},{1,7},{2,0},{3,1},{4,2},{5,3},{6,4},{7,5},{8,14},{9,15},{10,... | collective-permute-start | bytes 589832 | tf_op jit(solution)/shard_map/ppermute | solution.py:1291
  321.9 14.9 %collective-permute-start.28 = (f32[64,768]{1,0:T(8,128)S(1)}, f32[64,768]{1,0:T(8,128)S(1)}, u32[]{:S(2)}, u32[]{:S(2)}) collective-permute-start(f32[64,768]{1,0:T(8,128)S(1)} %get-tuple-element.300), channel_id=1, source_target_pairs={{0,1},{1,0},{2,3},{3,2},{4,5},{5,4},{6,7},{7,6},{8,9},{9,8},{10,11... | collective-permute-start | bytes 589832 | tf_op jit(solution)/shard_map/ppermute | solution.py:1291
  364.7 16.7 %collective-permute-start.37 = (f32[16,384,384]{2,1,0:T(8,128)}, f32[16,384,384]{2,1,0:T(8,128)}, u32[]{:S(2)}, u32[]{:S(2)}) collective-permute-start(f32[16,384,384]{2,1,0:T(8,128)} %get-tuple-element.175), channel_id=1, source_target_pairs={{0,8},{8,0},{16,24},{24,16},{1,9},{9,1},{17,25},{25,17},{2,10},{10... | collective-permute-start | bytes 28311560 | tf_op jit(solution)/shard_map/ppermute | solution.py:1285
  373.5 71.9 %collective-permute-start.40 = (f16[192,6400]{1,0:T(8,128)(2,1)}, f16[192,6400]{1,0:T(8,128)(2,1)}, u32[]{:S(2)}, u32[]{:S(2)}) collective-permute-start(f16[192,6400]{1,0:T(8,128)(2,1)} %fusion.7), channel_id=1, source_target_pairs={{0,16},{8,24},{16,0},{24,8},{1,17},{9,25},{17,1},{25,9},{2,18},{10... | collective-permute-start | bytes 7372808 | tf_op jit(solution)/shard_map/ppermute | solution.py:1285
  393.8 64.0 %collective-permute-start.43 = (f16[3088,384]{1,0:T(8,128)(2,1)}, f16[3088,384]{1,0:T(8,128)(2,1)}, u32[]{:S(2)}, u32[]{:S(2)}) collective-permute-start(f16[3088,384]{1,0:T(8,128)(2,1)} %concatenate.163), channel_id=1, source_target_pairs={{0,1},{1,0},{2,3},{3,2},{4,5},{5,4},{6,7},{7,6},{8,9},{9,8},{10,11... | collective-permute-start | bytes 7114760 | tf_op jit(solution)/shard_map/ppermute | solution.py:1291
  443.3 11.6 %collective-permute-start.39 = (bf16[512,384]{1,0:T(8,128)(2,1)S(1)}, bf16[512,384]{1,0:T(8,128)(2,1)S(1)}, u32[]{:S(2)}, u32[]{:S(2)}) collective-permute-start(bf16[512,384]{1,0:T(8,128)(2,1)S(1)} %fusion.29), channel_id=1, source_target_pairs={{0,16},{8,24},{16,0},{24,8},{1,17},{9,25},{17,1},{25,9},{2,18},{10... | collective-permute-start | bytes 1179656 | tf_op jit(solution)/shard_map/ppermute | solution.py:1285
  468.2 11.0 %collective-permute-start.44 = (f32[9,384,384]{2,1,0:T(8,128)}, f32[9,384,384]{2,1,0:T(8,128)}, u32[]{:S(2)}, u32[]{:S(2)}) collective-permute-start(f32[9,384,384]{2,1,0:T(8,128)} %get-tuple-element.192), channel_id=1, source_target_pairs={{0,8},{8,0},{16,24},{24,16},{1,9},{9,1},{17,25},{25,17},{2,10},{10... | collective-permute-start | bytes 15925256 | tf_op jit(solution)/shard_map/ppermute | solution.py:1285
  483.5 31.9 %collective-permute-start.46 = (f16[1744,384]{1,0:T(8,128)(2,1)}, f16[1744,384]{1,0:T(8,128)(2,1)S(1)}, u32[]{:S(2)}, u32[]{:S(2)}) collective-permute-start(f16[1744,384]{1,0:T(8,128)(2,1)} %concatenate.169), channel_id=1, source_target_pairs={{0,1},{1,0},{2,3},{3,2},{4,5},{5,4},{6,7},{7,6},{8,9},{9,8},{10,11... | collective-permute-start | bytes 4018184 | tf_op jit(solution)/shard_map/ppermute | solution.py:1291
  483.9 41.5 %collective-permute-start.42 = (bf16[3072,128]{1,0:T(8,128)(2,1)S(1)}, bf16[3072,128]{1,0:T(8,128)(2,1)}, u32[]{:S(2)}, u32[]{:S(2)}) collective-permute-start(bf16[3072,128]{1,0:T(8,128)(2,1)S(1)} %maximum_maximum_fusion.refs_3_), channel_id=1, source_target_pairs={{0,4},{1,5},{2,6},{3,7},{4,0},{5,1},{6,2},{7,3},{8,12},{9,13},{10,... | collective-permute-start | bytes 2359304 | tf_op jit(solution)/shard_map/ppermute | solution.py:1291
  490.7 61.3 %collective-permute-start.49 = (bf16[3072,128]{1,0:T(8,128)(2,1)S(1)}, bf16[3072,128]{1,0:T(8,128)(2,1)}, u32[]{:S(2)}, u32[]{:S(2)}) collective-permute-start(bf16[3072,128]{1,0:T(8,128)(2,1)S(1)} %maximum_maximum_fusion.refs_3_), channel_id=1, source_target_pairs={{0,2},{1,3},{2,4},{3,5},{4,6},{5,7},{6,0},{7,1},{8,10},{9,11},{10,... | collective-permute-start | bytes 2359304 | tf_op jit(solution)/shard_map/ppermute | solution.py:1291
  490.8 61.2 %collective-permute-start.50 = (bf16[3072,128]{1,0:T(8,128)(2,1)S(1)}, bf16[3072,128]{1,0:T(8,128)(2,1)}, u32[]{:S(2)}, u32[]{:S(2)}) collective-permute-start(bf16[3072,128]{1,0:T(8,128)(2,1)S(1)} %maximum_maximum_fusion.refs_3_), channel_id=1, source_target_pairs={{0,6},{1,7},{2,0},{3,1},{4,2},{5,3},{6,4},{7,5},{8,14},{9,15},{10,... | collective-permute-start | bytes 2359304 | tf_op jit(solution)/shard_map/ppermute | solution.py:1291
  503.1 27.7 %collective-permute-start.47 = (f16[1552,384]{1,0:T(8,128)(2,1)}, f16[1552,384]{1,0:T(8,128)(2,1)}, u32[]{:S(2)}, u32[]{:S(2)}) collective-permute-start(f16[1552,384]{1,0:T(8,128)(2,1)} %concatenate.171), channel_id=1, source_target_pairs={{0,16},{8,24},{16,0},{24,8},{1,17},{9,25},{17,1},{25,9},{2,18},{10... | collective-permute-start | bytes 3575816 | tf_op jit(solution)/shard_map/ppermute | solution.py:1285
  525.4 26.7 %collective-permute-start.52 = (bf16[3072,128]{1,0:T(8,128)(2,1)S(1)}, bf16[3072,128]{1,0:T(8,128)(2,1)}, u32[]{:S(2)}, u32[]{:S(2)}) collective-permute-start(bf16[3072,128]{1,0:T(8,128)(2,1)S(1)} %maximum_maximum_fusion.refs_3_), channel_id=1, source_target_pairs={{0,1},{1,0},{2,3},{3,2},{4,5},{5,4},{6,7},{7,6},{8,9},{9,8},{10,11... | collective-permute-start | bytes 2359304 | tf_op jit(solution)/shard_map/ppermute | solution.py:1291
  529.2 35.3 %collective-permute-start.48 = (f16[880,384]{1,0:T(8,128)(2,1)}, f16[880,384]{1,0:T(8,128)(2,1)}, u32[]{:S(2)}, u32[]{:S(2)}) collective-permute-start(f16[880,384]{1,0:T(8,128)(2,1)} %concatenate.170), channel_id=1, source_target_pairs={{0,16},{8,24},{16,0},{24,8},{1,17},{9,25},{17,1},{25,9},{2,18},{10... | collective-permute-start | bytes 2027528 | tf_op jit(solution)/shard_map/ppermute | solution.py:1285
  555.3 53.5 %collective-permute-start.53 = (bf16[3,3072,128]{2,1,0:T(8,128)(2,1)}, bf16[3,3072,128]{2,1,0:T(8,128)(2,1)}, u32[]{:S(2)}, u32[]{:S(2)}) collective-permute-start(bf16[3,3072,128]{2,1,0:T(8,128)(2,1)} %pad_maximum_fusion), channel_id=1, source_target_pairs={{0,1},{1,0},{2,3},{3,2},{4,5},{5,4},{6,7},{7,6},{8,9},{9,8},{10,11... | collective-permute-start | bytes 7077896 | tf_op jit(solution)/shard_map/ppermute | solution.py:1291
  572.4 34.4 %collective-permute-start.51 = (f16[616,384]{1,0:T(8,128)(2,1)}, f16[616,384]{1,0:T(8,128)(2,1)S(1)}, u32[]{:S(2)}, u32[]{:S(2)}) collective-permute-start(f16[616,384]{1,0:T(8,128)(2,1)} %concatenate.173), channel_id=1, source_target_pairs={{0,2},{1,3},{2,4},{3,5},{4,6},{5,7},{6,0},{7,1},{8,10},{9,11},{10,... | collective-permute-start | bytes 1419272 | tf_op jit(solution)/shard_map/ppermute | solution.py:1291
  575.1 53.5 %collective-permute-start.55 = (f16[616,384]{1,0:T(8,128)(2,1)S(1)}, f16[616,384]{1,0:T(8,128)(2,1)}, u32[]{:S(2)}, u32[]{:S(2)}) collective-permute-start(f16[616,384]{1,0:T(8,128)(2,1)S(1)} %concatenate.175), channel_id=1, source_target_pairs={{0,6},{1,7},{2,0},{3,1},{4,2},{5,3},{6,4},{7,5},{8,14},{9,15},{10,... | collective-permute-start | bytes 1419272 | tf_op jit(solution)/shard_map/ppermute | solution.py:1291
  577.1 52.7 %collective-permute-start.54 = (f16[616,384]{1,0:T(8,128)(2,1)}, f16[616,384]{1,0:T(8,128)(2,1)}, u32[]{:S(2)}, u32[]{:S(2)}) collective-permute-start(f16[616,384]{1,0:T(8,128)(2,1)} %concatenate.174), channel_id=1, source_target_pairs={{0,4},{1,5},{2,6},{3,7},{4,0},{5,1},{6,2},{7,3},{8,12},{9,13},{10,... | collective-permute-start | bytes 1419272 | tf_op jit(solution)/shard_map/ppermute | solution.py:1291
  633.2 8.2 %collective-permute-start.58 = (f32[25,24,384]{2,1,0:T(8,128)S(1)}, f32[25,24,384]{2,1,0:T(8,128)}, u32[]{:S(2)}, u32[]{:S(2)}) collective-permute-start(f32[25,24,384]{2,1,0:T(8,128)S(1)} %get-tuple-element.287), channel_id=1, source_target_pairs={{0,8},{8,0},{16,24},{24,16},{1,9},{9,1},{17,25},{25,17},{2,10},{10... | collective-permute-start | bytes 2764808 | tf_op jit(solution)/shard_map/ppermute | solution.py:1285
  652.7 14.5 %collective-permute-start.63 = (f32[8,128]{1,0:T(8,128)S(1)}, f32[8,128]{1,0:T(8,128)S(1)}, u32[]{:S(2)}, u32[]{:S(2)}) collective-permute-start(f32[8,128]{1,0:T(8,128)S(1)} %select_reduce_fusion.1), channel_id=1, source_target_pairs={{0,6},{1,7},{2,0},{3,1},{4,2},{5,3},{6,4},{7,5},{8,14},{9,15},{10,... | collective-permute-start | bytes 12296 | tf_op jit(solution)/shard_map/ppermute | solution.py:1291
  654.6 12.6 %collective-permute-start.62 = (f32[8,128]{1,0:T(8,128)S(1)}, f32[8,128]{1,0:T(8,128)S(1)}, u32[]{:S(2)}, u32[]{:S(2)}) collective-permute-start(f32[8,128]{1,0:T(8,128)S(1)} %select_reduce_fusion.1), channel_id=1, source_target_pairs={{0,4},{1,5},{2,6},{3,7},{4,0},{5,1},{6,2},{7,3},{8,12},{9,13},{10,... | collective-permute-start | bytes 12296 | tf_op jit(solution)/shard_map/ppermute | solution.py:1291
  668.8 35.2 %collective-permute-start.65 = (f16[688,384]{1,0:T(8,128)(2,1)S(1)}, f16[688,384]{1,0:T(8,128)(2,1)S(1)}, u32[]{:S(2)}, u32[]{:S(2)}) collective-permute-start(f16[688,384]{1,0:T(8,128)(2,1)S(1)} %concatenate.183), channel_id=1, source_target_pairs={{0,2},{1,3},{2,4},{3,5},{4,6},{5,7},{6,0},{7,1},{8,10},{9,11},{10,... | collective-permute-start | bytes 1585160 | tf_op jit(solution)/shard_map/ppermute | solution.py:1291
  668.8 42.8 %collective-permute-start.67 = (f16[688,384]{1,0:T(8,128)(2,1)S(1)}, f16[688,384]{1,0:T(8,128)(2,1)S(1)}, u32[]{:S(2)}, u32[]{:S(2)}) collective-permute-start(f16[688,384]{1,0:T(8,128)(2,1)S(1)} %concatenate.183), channel_id=1, source_target_pairs={{0,4},{1,5},{2,6},{3,7},{4,0},{5,1},{6,2},{7,3},{8,12},{9,13},{10,... | collective-permute-start | bytes 1585160 | tf_op jit(solution)/shard_map/ppermute | solution.py:1291
  672.9 41.9 %collective-permute-start.69 = (f16[688,384]{1,0:T(8,128)(2,1)S(1)}, f16[688,384]{1,0:T(8,128)(2,1)S(1)}, u32[]{:S(2)}, u32[]{:S(2)}) collective-permute-start(f16[688,384]{1,0:T(8,128)(2,1)S(1)} %concatenate.183), channel_id=1, source_target_pairs={{0,6},{1,7},{2,0},{3,1},{4,2},{5,3},{6,4},{7,5},{8,14},{9,15},{10,... | collective-permute-start | bytes 1585160 | tf_op jit(solution)/shard_map/ppermute | solution.py:1291
  674.7 56.6 %collective-permute-start.64 = (f16[688,384]{1,0:T(8,128)(2,1)S(1)}, f16[688,384]{1,0:T(8,128)(2,1)S(1)}, u32[]{:S(2)}, u32[]{:S(2)}) collective-permute-start(f16[688,384]{1,0:T(8,128)(2,1)S(1)} %concatenate.183), channel_id=1, source_target_pairs={{0,1},{1,0},{2,3},{3,2},{4,5},{5,4},{6,7},{7,6},{8,9},{9,8},{10,11... | collective-permute-start | bytes 1585160 | tf_op jit(solution)/shard_map/ppermute | solution.py:1291
  703.9 28.4 %collective-permute-start.66 = (f16[688,384]{1,0:T(8,128)(2,1)S(1)}, f16[688,384]{1,0:T(8,128)(2,1)S(1)}, u32[]{:S(2)}, u32[]{:S(2)}) collective-permute-start(f16[688,384]{1,0:T(8,128)(2,1)S(1)} %collective-permute-done.65), channel_id=1, source_target_pairs={{0,1},{1,0},{2,3},{3,2},{4,5},{5,4},{6,7},{7,6},{8,9},{9,8},{10,11... | collective-permute-start | bytes 1585160 | tf_op jit(solution)/shard_map/ppermute | solution.py:1291
  711.6 21.8 %collective-permute-start.68 = (f16[688,384]{1,0:T(8,128)(2,1)S(1)}, f16[688,384]{1,0:T(8,128)(2,1)S(1)}, u32[]{:S(2)}, u32[]{:S(2)}) collective-permute-start(f16[688,384]{1,0:T(8,128)(2,1)S(1)} %collective-permute-done.67), channel_id=1, source_target_pairs={{0,1},{1,0},{2,3},{3,2},{4,5},{5,4},{6,7},{7,6},{8,9},{9,8},{10,11... | collective-permute-start | bytes 1585160 | tf_op jit(solution)/shard_map/ppermute | solution.py:1291
  714.9 20.9 %collective-permute-start.70 = (f16[688,384]{1,0:T(8,128)(2,1)S(1)}, f16[688,384]{1,0:T(8,128)(2,1)S(1)}, u32[]{:S(2)}, u32[]{:S(2)}) collective-permute-start(f16[688,384]{1,0:T(8,128)(2,1)S(1)} %collective-permute-done.69), channel_id=1, source_target_pairs={{0,1},{1,0},{2,3},{3,2},{4,5},{5,4},{6,7},{7,6},{8,9},{9,8},{10,11... | collective-permute-start | bytes 1585160 | tf_op jit(solution)/shard_map/ppermute | solution.py:1291
  (71 other events, 600.4 us)

commit v5 on v4

--- a/solution.py
+++ b/solution.py
@@ -1159,7 +1159,9 @@
     for k in range(count):
         place = pl.multiple_of(places_ref[k], strip)
         scale = jnp.exp2(tails[k][0:1, :] - 15.0) * clip
-        g_ref[0, pl.ds(place, strip), :] = pieces[k][...] * scale
+        for slot in range(2):
+            values = pieces[k][pl.ds(slot * strip, strip), :] * scale
+            g_ref[slot, pl.ds(place, strip), :] = values
 
         @pl.when(pl.program_id(0) == 0)
         def _(k=k, place=place, scale=scale):
@@ -1167,29 +1169,30 @@
                 values = smalls[k][pl.ds(side * strip, strip), :] * scale
                 small_ref[side, pl.ds(place, strip), :] = values
 
-    grads = split_two(g_ref[0])
-    for old, new, product in ((ls_ref, nl_ref, mm_t), (rs_ref, nr_ref, mm_l)):
-        cross = product(grads[0], grads[1])
-        outer = product(grads[0], grads[0]) + (cross + cross.T)
-        new[0] = SHAMPOO_BETA * old[0] + (1.0 - SHAMPOO_BETA) * outer
-    turned = split_two(three(grads, split_two(rr_ref[0]), mm))
-    direction = three(split_two(lr_ref[0]), turned, mm)
-    weights = w_ref[0]
-    nw_ref[0] = weights - RATE_BLOCKS * (direction + DECAY_RATE * weights)
+    for slot in range(2):
+        grads = split_two(g_ref[slot])
+        for old, new, product in ((ls_ref, nl_ref, mm_t), (rs_ref, nr_ref, mm_l)):
+            cross = product(grads[0], grads[1])
+            outer = product(grads[0], grads[0]) + (cross + cross.T)
+            new[slot] = SHAMPOO_BETA * old[slot] + (1.0 - SHAMPOO_BETA) * outer
+        turned = split_two(three(grads, split_two(rr_ref[slot]), mm))
+        direction = three(split_two(lr_ref[slot]), turned, mm)
+        weights = w_ref[slot]
+        nw_ref[slot] = weights - RATE_BLOCKS * (direction + DECAY_RATE * weights)
 
 
 def shampoo(places, clip, pieces, strip, kept):
     slots = kept[0].shape[0]
     count = len(pieces)
-    block = pl.BlockSpec((1, BS, BS), lambda s: (s, 0, 0))
+    block = pl.BlockSpec((2, BS, BS), lambda s: (s, 0, 0))
     shape = jax.ShapeDtypeStruct((slots, BS, BS), f32)
     small_at, tail_at = slots // 2, (slots + 2) * strip // 16
     return pl.pallas_call(
         partial(shampoo_kernel, count, strip),
-        grid=(slots,),
+        grid=(slots // 2,),
         out_shape=[shape] * 4 + [jax.ShapeDtypeStruct((2, BS, BS), f32)],
         in_specs=[pl.BlockSpec(memory_space=SMEM)] * 2
-        + [pl.BlockSpec((strip, BS), lambda s: (s, 0))] * count
+        + [pl.BlockSpec((2 * strip, BS), lambda s: (s, 0))] * count
         + [pl.BlockSpec((2 * strip, BS), lambda s: (small_at, 0))] * count
         + [pl.BlockSpec((16, BS), lambda s: (tail_at, 0))] * count
         + [block] * 5,

time: 787 us -> 782 us (level)
  waiting for transfers between devices: 198 us -> 184 us
    ppermute x47, waiting for transfers between devices: 169 us -> 157 us  [over_voc(): return lax.ppermute(values, 'vocab', pairs)]
where the time goes in v5:
time: 782 us; the launch traced here: 776 us
  Pallas kernels  306 us (39%)
  waiting for transfers between devices  184 us (24%)
  other arithmetic  125 us (16%)
  starting transfers between devices  89.8 us (11%)
  local copies, waits for them, and re-layouts  54.4 us (7%)
  between operations  17.2 us (2%)
    ppermute x47, waiting for transfers between devices, over_voc(): return lax.ppermute(values, 'vocab', pairs)  157 us
    ppermute x47, starting transfers between devices, over_voc(): return lax.ppermute(values, 'vocab', pairs)  73.9 us
    pallas_call x1, Pallas kernels, attend_back(): pl.pallas_call(partial(attend_back_kernel, coefficient, int(later)), grid...  35.9 us
    pallas_call x1, Pallas kernels, shampoo(): pl.pallas_call(partial(shampoo_kernel, count, strip), grid=(slots // 2,),...  32.7 us
    pallas_call x4, Pallas kernels, lookup(): pl.pallas_call(partial(lookup_kernel, rows_all), out_shape=[jax.ShapeDtyp...  27.9 us
    pallas_call x4, Pallas kernels, find_hits(): pl.pallas_call(partial(hits_kernel, empty_row), out_shape=jax.ShapeDtypeS...  27.9 us
    ppermute x24, waiting for transfers between devices, over_dp(): return lax.ppermute(values, 'dp', pairs)  27.2 us
    pallas_call x1, Pallas kernels, mlp_back(): pl.pallas_call(mlp_back_kernel, grid=(FSTEPS,), out_shape=[halves, halves...  26.2 us
  transfers between devices with their start and end apart: 71, of which 39 were waited for; matrix products, arithmetic and copies ran while one was open for 18% of the time, Pallas kernels for 28%

profile of v5, /device:TPU:8, one launch (start us, length us, event | category | flops | bytes accessed | tf_op | source)
XLA Modules:
  0.0 775.7 jit_solution(14903915980655777918)
XLA Ops:
  5.0 5.3 convert_element_type.163.refs_0_
  16.8 4.4 collective-permute-start.2
  23.6 7.4 turn_table.1.table_ref
  31.0 7.0 find_hits.4.list_ref
  38.0 7.1 lookup.5
  47.7 7.0 find_hits.6.list_ref
  54.7 6.8 lookup.4
  61.5 7.0 find_hits.5.list_ref
  68.5 7.0 lookup.7
  75.8 4.8 collective-permute-start.11
  83.0 7.0 find_hits.7.list_ref
  90.0 6.9 lookup.6
  99.1 10.6 %collective-permute-done.11 = bf16[2,512,384]{2,1,0:T(8,128)(2,1)S(1)} collective-permute-done((bf16[2,512,384]{2,1,0:T(8,128)(2,1)S(1)}, bf16[2,512,384]{2,1,0:T(8,128)(2,1)S(1)}, u32[]{:S(2)}, u32[]{:S(2)}) %collective-permute-start.11) | collective-permute-done | bytes 786464 | tf_op jit(solution)/shard_map/ppermute | solution.py:1294
  123.7 11.5 %place_blocks.1 = (bf16[768,2304]{1,0:T(8,128)(2,1)}, bf16[768,768]{1,0:T(8,128)(2,1)}, bf16[768,3072]{1,0:T(8,128)(2,1)}, bf16[3072,768]{1,0:T(8,128)(2,1)}) custom-call(s32[48]{0:T(128)} %get-tuple-element.356.src_ref, s32[48]{0:T(128)} %get-tuple-element.355.off_ref, bf16[12,384,384]{2,1,0:T(8,128)(2,1)} %convert_element_type.163.refs_0_, ...), custom_call_target="tpu_custom_call" | custom-call | bytes 566231 | tf_op jit(solution)/shard_map/place_blocks/pallas_call | solution.py:110
  136.8 12.2 %collective-permute-done.15 = bf16[2,512,384]{2,1,0:T(8,128)(2,1)} collective-permute-done((bf16[2,512,384]{2,1,0:T(8,128)(2,1)}, bf16[2,512,384]{2,1,0:T(8,128)(2,1)}, u32[]{:S(2)}, u32[]{:S(2)}) %collective-permute-start.15) | collective-permute-done | bytes 786464 | tf_op jit(solution)/shard_map/ppermute | solution.py:1294
  155.9 8.5 %collective-permute-done.17 = bf16[512,384]{1,0:T(8,128)(2,1)} collective-permute-done((bf16[512,384]{1,0:T(8,128)(2,1)}, bf16[512,384]{1,0:T(8,128)(2,1)}, u32[]{:S(2)}, u32[]{:S(2)}) %collective-permute-start.17) | collective-permute-done | bytes 393248 | tf_op jit(solution)/shard_map/ppermute | solution.py:1288
  170.7 6.2 qkv_forward.1
  176.9 20.0 %attend.1 = (bf16[512,768]{1,0:T(8,128)(2,1)}, f32[8,128]{1,0:T(8,128)}) custom-call(s32[1,4]{1,0:T(1,128)} %len_ref.3, bf16[512,2304]{1,0:T(8,128)(2,1)} %get-tuple-element.149.q_ref.k_ref.v_ref, bf16[512,2304]{1,0:T(8,128)(2,1)} %get-tuple-element.149.q_ref.k_ref.v_ref, bf16[512,2304]{1,0:T(8,128)(2,1)} %get-tuple-element.149.q_ref.k_ref.v_ref, ...), custom_call_target="tpu_custom_call" | custom-call | flops 240000000 | bytes 80000 | tf_op jit(solution)/shard_map/attend/pallas_call | solution.py:495
  196.9 14.8 %mlp_forward.1 = (f32[512,768]{1,0:T(8,128)}, bf16[512,768]{1,0:T(8,128)(2,1)}, f32[512,3072]{1,0:T(8,128)}, bf16[512,3072]{1,0:T(8,128)(2,1)}, f32[512,768]{1,0:T(8,128)}, /*index=5*/bf16[64,768]{1,0:T(8,128)(2,1)}) custom-call(bf16[512,768]{1,0:T(8,128)(2,1)} %pad_maximum_fusion.4.x_ref, bf16[512,768]{1,0:T(8,128)(2,1)} %get-tuple-element.150.y_ref, ...), custom_call_target="tpu_custom_call" | custom-call | flops 108716360 | bytes 600000 | tf_op jit(solution)/shard_map/mlp_forward/pallas_call | solution.py:693
  214.4 5.6 collective-permute-done.18
  225.2 10.3 %collective-permute-done.19 = bf16[128,768]{0,1:T(8,128)(2,1)S(1)} collective-permute-done((bf16[128,768]{0,1:T(8,128)(2,1)S(1)}, bf16[128,768]{0,1:T(8,128)(2,1)S(1)}, u32[]{:S(2)}, u32[]{:S(2)}) %collective-permute-start.19) | collective-permute-done | bytes 196640 | tf_op jit(solution)/shard_map/ppermute | solution.py:1294
  235.5 4.0 collective-permute-done.20
  245.2 15.9 %vocabulary_logits.1 = (f32[512,6288]{1,0:T(8,128)}, f32[8,512]{1,0:T(8,128)}) custom-call(s32[4]{0:T(128)} %pad_add_fusion.5.places_ref, bf16[512,768]{1,0:T(8,128)(2,1)} %copy.72.group_ref, s32[512,1]{1,0:T(8,128)} %sub.290.target_ref, bf16[192,6288]{1,0:T(8,128)(2,1)} %copy-done.2, bf16[192,6288]{1,0:T(8,128)(2,1)} %collective-permute-done.22.refs_1_, ...), custom_call_target="tpu_custom_call" | custom-call | flops 98901688 | bytes 400000 | tf_op jit(solution)/shard_map/vocabulary_logits/pallas_call | solution.py:1038
  274.2 15.3 %vocabulary_back.1 = (bf16[512,6400]{1,0:T(8,128)(2,1)}, f32[512,768]{1,0:T(8,128)}) custom-call(s32[4]{0:T(128)} %pad_add_fusion.5.places_ref, f32[512,6288]{1,0:T(8,128)} %get-tuple-element.156.logit_ref, f32[128,512]{1,0:T(8,128)} %select_maximum_fusion.stat_ref, s32[512,1]{1,0:T(8,128)} %sub.290.target_ref, bf16[192,6288]{1,0:T(8,128)(2,1)} %copy-done.2, ...), custom_call_target="tpu_custom_call" | custom-call | flops 98901688 | bytes 600000 | tf_op jit(solution)/shard_map/vocabulary_back/pallas_call | solution.py:1081
  293.9 4.7 collective-permute-done.31
  304.8 11.7 %lexicon.1 = (f32[384,6400]{1,0:T(8,128)}, f32[384,6400]{1,0:T(8,128)}, f32[1,1280]{1,0:T(1,128)}, f32[1,1280]{1,0:T(1,128)}) custom-call(s32[4]{0:T(128)} %pad_add_fusion.5.places_ref, bf16[768,512]{1,0:T(8,128)(2,1)} %bitcast.236, bf16[512,6400]{1,0:T(8,128)(2,1)} %get-tuple-element.160.grad_ref), custom_call_target="tpu_custom_call" | custom-call | flops 100663296 | bytes 600000 | tf_op jit(solution)/shard_map/lexicon/pallas_call | solution.py:1127
  324.7 10.3 %collective-permute-done.34 = f32[64,768]{1,0:T(8,128)S(1)} collective-permute-done((f32[64,768]{1,0:T(8,128)S(1)}, f32[64,768]{1,0:T(8,128)S(1)}, u32[]{:S(2)}, u32[]{:S(2)}) %collective-permute-start.34) | collective-permute-done | bytes 196640 | tf_op jit(solution)/shard_map/ppermute | solution.py:1294
  339.4 26.2 %mlp_back.1 = (f32[16,384,384]{2,1,0:T(8,128)}, f32[16,384,384]{2,1,0:T(8,128)}, f32[1,384]{1,0:T(1,128)}, f32[1,384]{1,0:T(1,128)}, f32[512,768]{1,0:T(8,128)},...) custom-call(s32[1]{0:T(128)} %bitcast.4.core_ref, f32[64,768]{1,0:T(8,128)} %fusion.37.ghp_ref, ...), custom_call_target="tpu_custom_call" | custom-call | flops 193273536 | bytes 1000000 | tf_op jit(solution)/shard_map/mlp_back/pallas_call | solution.py:833
  368.4 6.1 fusion.7
  382.3 10.4 %multiply_convert_fusion = (f16[16,192,384]{2,1,0:T(8,128)(2,1)S(1)}, f32[16,192,384]{2,1,0:T(8,128)}) fusion(f32[16,384,384]{2,1,0:T(8,128)} %collective-permute-done.37, s32[]{:T(128)S(6)} %select_n.387, f32[16,384,384]{2,1,0:T(8,128)} %get-tuple-element.174, f32[]{:T(128)S(6)} %exp2.159, s32[]{:T(128)S(6)} %select_n.385), kind=kLoop, calls=%fused_computation.32 | loop fusion | flops 4718592 | bytes 25952268 | tf_op jit(solution)/shard_map/convert_element_type | solution.py:1227
  396.4 35.9 %attend_back.1 = (bf16[3,512,768]{2,1,0:T(8,128)(2,1)}, f32[12,64,64]{2,1,0:T(8,128)}, f32[12,64,64]{2,1,0:T(8,128)}) custom-call(s32[1,4]{1,0:T(1,128)} %len_ref.3, bf16[512,2304]{1,0:T(8,128)(2,1)} %get-tuple-element.149.q_ref.k_ref.v_ref, bf16[512,2304]{1,0:T(8,128)(2,1)} %get-tuple-element.149.q_ref.k_ref.v_ref, ...), custom_call_target="tpu_custom_call" | custom-call | flops 240000000 | bytes 80000 | tf_op jit(solution)/shard_map/attend_back/pallas_call | solution.py:607
  432.3 7.9 %qkv_back.1 = (bf16[512,768]{1,0:T(8,128)(2,1)}, f32[16,768]{1,0:T(8,128)}) custom-call(bf16[3,512,768]{2,1,0:T(8,128)(2,1)} %get-tuple-element.180.g_ref, bf16[768,2304]{1,0:T(8,128)(2,1)} %get-tuple-element.148.w_ref, bf16[512,768]{1,0:T(8,128)(2,1)} %pad_maximum_fusion.4.x_ref, f32[512,768]{1,0:T(8,128)} %get-tuple-element.181.gx1_ref, f32[15,768]{1,0:T(8,128)} %vec_ref.7), custom_call_target="tpu_custom_call" | custom-call | flops 36238784 | bytes 200000 | tf_op jit(solution)/shard_map/qkv_back/pallas_call | solution.py:897
  448.2 7.5 fusion.1.lex_ref
  458.6 10.4 %qkv_weights.1 = (f32[9,384,384]{2,1,0:T(8,128)}, f32[9,384,384]{2,1,0:T(8,128)}, f32[1,384]{1,0:T(1,128)}, f32[1,384]{1,0:T(1,128)}) custom-call(s32[1]{0:T(128)} %bitcast.4.core_ref, bf16[512,768]{1,0:T(8,128)(2,1)} %get-tuple-element.185.h_ref, bf16[3,512,768]{2,1,0:T(8,128)(2,1)} %get-tuple-element.180.g_ref, bf16[512,768]{1,0:T(8,128)(2,1)} %get-tuple-element.150.y_ref, ...), custom_call_target="tpu_custom_call" | custom-call | flops 48318384 | bytes 400000 | tf_op jit(solution)/shard_map/qkv_weights/pallas_call | solution.py:949
  472.6 5.4 collective-permute-done.45
  485.9 4.2 convert_element_type.178
  505.2 11.0 %collective-permute-done.46 = f16[1744,384]{1,0:T(8,128)(2,1)S(1)} collective-permute-done((f16[1744,384]{1,0:T(8,128)(2,1)}, f16[1744,384]{1,0:T(8,128)(2,1)S(1)}, u32[]{:S(2)}, u32[]{:S(2)}) %collective-permute-start.46) | collective-permute-done | bytes 1339424 | tf_op jit(solution)/shard_map/ppermute | solution.py:1294
  519.4 3.7 add_add_fusion
  533.3 20.0 %collective-permute-done.49.refs_1_ = bf16[3072,128]{1,0:T(8,128)(2,1)} collective-permute-done((bf16[3072,128]{1,0:T(8,128)(2,1)S(1)}, bf16[3072,128]{1,0:T(8,128)(2,1)}, u32[]{:S(2)}, u32[]{:S(2)}) %collective-permute-start.49) | collective-permute-done | bytes 786464 | tf_op jit(solution)/shard_map/ppermute | solution.py:1294
  582.3 12.9 %scatter_first.1 = (f32[6400,128]{1,0:T(8,128)}, f32[6400,128]{1,0:T(8,128)}) custom-call(s32[8256]{0:T(1024)} %copy-done.22, s32[8256]{0:T(1024)} %copy-done.25, bf16[3072,128]{1,0:T(8,128)(2,1)} %collective-permute-done.42.refs_0_, bf16[3072,128]{1,0:T(8,128)(2,1)} %collective-permute-done.49.refs_1_, bf16[3072,128]{1,0:T(8,128)(2,1)} %collective-permute-done.50.refs_2_, ...), custom_call_target="tpu_custom_call" | custom-call | flops 200000000 | bytes 128778 | tf_op jit(solution)/shard_map/scatter_first/pallas_call | solution.py:316
  595.2 12.5 %collective-permute-done.51 = f16[616,384]{1,0:T(8,128)(2,1)S(1)} collective-permute-done((f16[616,384]{1,0:T(8,128)(2,1)}, f16[616,384]{1,0:T(8,128)(2,1)S(1)}, u32[]{:S(2)}, u32[]{:S(2)}) %collective-permute-start.51) | collective-permute-done | bytes 473120 | tf_op jit(solution)/shard_map/ppermute | solution.py:1294
  610.1 21.6 %scatter_last.1 = (f32[192,6288]{1,0:T(8,128)}, f32[1,1]{1,0:T(1,128)}) custom-call(s32[8256]{0:T(1024)} %copy-done.22, s32[8256]{0:T(1024)} %copy-done.25, f32[6400,128]{1,0:T(8,128)} %get-tuple-element.208.first_acc, f32[6400,128]{1,0:T(8,128)} %get-tuple-element.209.first_tail, f32[192,6400]{1,0:T(8,128)} %fusion.1.lex_ref, ...), custom_call_target="tpu_custom_call" | custom-call | flops 200000000 | bytes 193167 | tf_op jit(solution)/shard_map/scatter_last/pallas_call | solution.py:337
  663.2 4.5 collective-permute-start.67
  672.8 25.6 %collective-permute-done.65 = f16[688,384]{1,0:T(8,128)(2,1)S(1)} collective-permute-done((f16[688,384]{1,0:T(8,128)(2,1)S(1)}, f16[688,384]{1,0:T(8,128)(2,1)S(1)}, u32[]{:S(2)}, u32[]{:S(2)}) %collective-permute-start.65) | collective-permute-done | bytes 528416 | tf_op jit(solution)/shard_map/ppermute | solution.py:1294
  698.4 4.3 collective-permute-start.66
  706.2 4.3 collective-permute-start.68
  712.4 12.2 %fusion.11 = (f32[6288,192]{0,1:T(8,128)}, f32[6288,192]{0,1:T(8,128)}, f32[6288,192]{0,1:T(8,128)}) fusion(f32[192,6288]{1,0:T(8,128)} %get-tuple-element.216, f32[]{:T(128)} %div.104, f32[6288,192]{0,1:T(8,128)} %param.49, f32[]{:T(128)} %bitcast.122, f32[]{:T(128)} %bitcast.120, f32[6288,192]{0,1:T(8,128)} %param.48, f32[6288,192]{0,1:T(8,128)} %param.47), kind=kLoop, calls=%fused_computation.55 | loop fusion | flops 19316736 | bytes 33804300 | tf_op jit(solution)/shard_map/transpose | solution.py:1690
  733.6 32.7 %shampoo.1 = (f32[12,384,384]{2,1,0:T(8,128)}, f32[12,384,384]{2,1,0:T(8,128)}, f32[12,384,384]{2,1,0:T(8,128)}, f32[12,384,384]{2,1,0:T(8,128)}, f32[2,384,384]{2,1,0:T(8,128)}) custom-call(s32[8]{0:T(128)} %stack.250.places_ref, f32[1]{0:T(128)} %bitcast.111.clip_ref, f32[688,384]{1,0:T(8,128)} %convert_element_type.202.refs_0_.refs_8_.refs_16_, ...), custom_call_target="tpu_custom_call" | custom-call | flops 326149088 | bytes 1415577 | tf_op jit(solution)/shard_map/shampoo/pallas_call | solution.py:1190
  (460 shorter events, 240.3 us)
Async XLA Ops:
  3.3 20.3 %collective-permute-start.4 = (bf16[192,6288]{1,0:T(8,128)(2,1)S(1)}, bf16[192,6288]{1,0:T(8,128)(2,1)}, u32[]{:S(2)}, u32[]{:S(2)}) collective-permute-start(bf16[192,6288]{1,0:T(8,128)(2,1)S(1)} %bitcast_convert_fusion.own_ref.refs_0_), channel_id=1, source_target_pairs={{0,8},{8,0},{16,24},{24,16},{1,9},{9,1},{17,25},{25,17},{2,10},{10... | collective-permute-start | bytes 7243784 | tf_op jit(solution)/shard_map/ppermute | solution.py:1288
  10.3 100.3 %collective-permute-start.12 = (bf16[12,384,384]{2,1,0:T(8,128)(2,1)}, bf16[12,384,384]{2,1,0:T(8,128)(2,1)}, u32[]{:S(2)}, u32[]{:S(2)}) collective-permute-start(bf16[12,384,384]{2,1,0:T(8,128)(2,1)} %convert_element_type.163.refs_0_), channel_id=1, source_target_pairs={{0,16},{8,24},{16,0},{24,8},{1,17},{9,25},{17,1},{25,9},{2,18},{10... | collective-permute-start | bytes 10616840 | tf_op jit(solution)/shard_map/ppermute | solution.py:1288
  45.1 30.4 %collective-permute-start.6 = (bf16[1024,384]{1,0:T(8,128)(2,1)}, bf16[1024,384]{1,0:T(8,128)(2,1)S(1)}, u32[]{:S(2)}, u32[]{:S(2)}) collective-permute-start(bf16[1024,384]{1,0:T(8,128)(2,1)} %get-tuple-element.130), channel_id=1, source_target_pairs={{0,1},{1,0},{2,3},{3,2},{4,5},{5,4},{6,7},{7,6},{8,9},{9,8},{10,11... | collective-permute-start | bytes 2359304 | tf_op jit(solution)/shard_map/ppermute | solution.py:1294
  46.2 35.7 %collective-permute-start.8 = (bf16[1024,384]{1,0:T(8,128)(2,1)}, bf16[1024,384]{1,0:T(8,128)(2,1)S(1)}, u32[]{:S(2)}, u32[]{:S(2)}) collective-permute-start(bf16[1024,384]{1,0:T(8,128)(2,1)} %get-tuple-element.135), channel_id=1, source_target_pairs={{0,1},{1,0},{2,3},{3,2},{4,5},{5,4},{6,7},{7,6},{8,9},{9,8},{10,11... | collective-permute-start | bytes 2359304 | tf_op jit(solution)/shard_map/ppermute | solution.py:1294
  75.7 21.2 %collective-permute-start.10 = (bf16[1024,384]{1,0:T(8,128)(2,1)}, bf16[1024,384]{1,0:T(8,128)(2,1)S(1)}, u32[]{:S(2)}, u32[]{:S(2)}) collective-permute-start(bf16[1024,384]{1,0:T(8,128)(2,1)} %get-tuple-element.140), channel_id=1, source_target_pairs={{0,1},{1,0},{2,3},{3,2},{4,5},{5,4},{6,7},{7,6},{8,9},{9,8},{10,11... | collective-permute-start | bytes 2359304 | tf_op jit(solution)/shard_map/ppermute | solution.py:1294
  75.8 33.9 %collective-permute-start.11 = (bf16[2,512,384]{2,1,0:T(8,128)(2,1)S(1)}, bf16[2,512,384]{2,1,0:T(8,128)(2,1)S(1)}, u32[]{:S(2)}, u32[]{:S(2)}) collective-permute-start(bf16[2,512,384]{2,1,0:T(8,128)(2,1)S(1)} %bitcast.261), channel_id=1, source_target_pairs={{0,4},{1,5},{2,6},{3,7},{4,0},{5,1},{6,2},{7,3},{8,12},{9,13},{10,... | collective-permute-start | bytes 2359304 | tf_op jit(solution)/shard_map/ppermute | solution.py:1294
  110.6 11.3 %collective-permute-start.13 = (bf16[12,384,384]{2,1,0:T(8,128)(2,1)}, bf16[12,384,384]{2,1,0:T(8,128)(2,1)S(1)}, u32[]{:S(2)}, u32[]{:S(2)}) collective-permute-start(bf16[12,384,384]{2,1,0:T(8,128)(2,1)} %convert_element_type.163.refs_0_), channel_id=1, source_target_pairs={{0,8},{8,0},{16,24},{24,16},{1,9},{9,1},{17,25},{25,17},{2,10},{10... | collective-permute-start | bytes 10616840 | tf_op jit(solution)/shard_map/ppermute | solution.py:1288
  110.6 11.6 %collective-permute-start.14 = (bf16[12,384,384]{2,1,0:T(8,128)(2,1)}, bf16[12,384,384]{2,1,0:T(8,128)(2,1)}, u32[]{:S(2)}, u32[]{:S(2)}) collective-permute-start(bf16[12,384,384]{2,1,0:T(8,128)(2,1)} %collective-permute-done.12.refs_1_), channel_id=1, source_target_pairs={{0,8},{8,0},{16,24},{24,16},{1,9},{9,1},{17,25},{25,17},{2,10},{10... | collective-permute-start | bytes 10616840 | tf_op jit(solution)/shard_map/ppermute | solution.py:1288
  111.1 24.1 %collective-permute-start.9 = (bf16[1024,384]{1,0:T(8,128)(2,1)}, bf16[1024,384]{1,0:T(8,128)(2,1)}, u32[]{:S(2)}, u32[]{:S(2)}) collective-permute-start(bf16[1024,384]{1,0:T(8,128)(2,1)} %get-tuple-element.137), channel_id=1, source_target_pairs={{0,1},{1,0},{2,3},{3,2},{4,5},{5,4},{6,7},{7,6},{8,9},{9,8},{10,11... | collective-permute-start | bytes 2359304 | tf_op jit(solution)/shard_map/ppermute | solution.py:1294
  111.5 37.5 %collective-permute-start.15 = (bf16[2,512,384]{2,1,0:T(8,128)(2,1)}, bf16[2,512,384]{2,1,0:T(8,128)(2,1)}, u32[]{:S(2)}, u32[]{:S(2)}) collective-permute-start(bf16[2,512,384]{2,1,0:T(8,128)(2,1)} %bitcast.260), channel_id=1, source_target_pairs={{0,6},{1,7},{2,0},{3,1},{4,2},{5,3},{6,4},{7,5},{8,14},{9,15},{10,... | collective-permute-start | bytes 2359304 | tf_op jit(solution)/shard_map/ppermute | solution.py:1294
  115.1 35.6 %collective-permute-start.16 = (bf16[2,512,384]{2,1,0:T(8,128)(2,1)}, bf16[2,512,384]{2,1,0:T(8,128)(2,1)}, u32[]{:S(2)}, u32[]{:S(2)}) collective-permute-start(bf16[2,512,384]{2,1,0:T(8,128)(2,1)} %bitcast.16), channel_id=1, source_target_pairs={{0,2},{1,3},{2,4},{3,5},{4,6},{5,7},{6,0},{7,1},{8,10},{9,11},{10,... | collective-permute-start | bytes 2359304 | tf_op jit(solution)/shard_map/ppermute | solution.py:1294
  153.9 10.4 %collective-permute-start.17 = (bf16[512,384]{1,0:T(8,128)(2,1)}, bf16[512,384]{1,0:T(8,128)(2,1)}, u32[]{:S(2)}, u32[]{:S(2)}) collective-permute-start(bf16[512,384]{1,0:T(8,128)(2,1)} %slice_bitcast_fusion), channel_id=1, source_target_pairs={{0,16},{8,24},{16,0},{24,8},{1,17},{9,25},{17,1},{25,9},{2,18},{10... | collective-permute-start | bytes 1179656 | tf_op jit(solution)/shard_map/ppermute | solution.py:1288
  166.5 53.6 %collective-permute-start.22 = (bf16[192,6288]{1,0:T(8,128)(2,1)S(1)}, bf16[192,6288]{1,0:T(8,128)(2,1)}, u32[]{:S(2)}, u32[]{:S(2)}) collective-permute-start(bf16[192,6288]{1,0:T(8,128)(2,1)S(1)} %copy-done.3), channel_id=1, source_target_pairs={{0,16},{8,24},{16,0},{24,8},{1,17},{9,25},{17,1},{25,9},{2,18},{10... | collective-permute-start | bytes 7243784 | tf_op jit(solution)/shard_map/ppermute | solution.py:1288
  220.1 23.7 %collective-permute-start.23 = (bf16[192,6288]{1,0:T(8,128)(2,1)}, bf16[192,6288]{1,0:T(8,128)(2,1)S(1)}, u32[]{:S(2)}, u32[]{:S(2)}) collective-permute-start(bf16[192,6288]{1,0:T(8,128)(2,1)} %collective-permute-done.22.refs_1_), channel_id=1, source_target_pairs={{0,8},{8,0},{16,24},{24,16},{1,9},{9,1},{17,25},{25,17},{2,10},{10... | collective-permute-start | bytes 7243784 | tf_op jit(solution)/shard_map/ppermute | solution.py:1288
  220.3 15.2 %collective-permute-start.19 = (bf16[128,768]{0,1:T(8,128)(2,1)S(1)}, bf16[128,768]{0,1:T(8,128)(2,1)S(1)}, u32[]{:S(2)}, u32[]{:S(2)}) collective-permute-start(bf16[128,768]{0,1:T(8,128)(2,1)S(1)} %pad_maximum_fusion.9), channel_id=1, source_target_pairs={{0,2},{1,3},{2,4},{3,5},{4,6},{5,7},{6,0},{7,1},{8,10},{9,11},{10,... | collective-permute-start | bytes 589832 | tf_op jit(solution)/shard_map/ppermute | solution.py:1294
  222.0 17.5 %collective-permute-start.20 = (bf16[128,768]{0,1:T(8,128)(2,1)S(1)}, bf16[128,768]{0,1:T(8,128)(2,1)S(1)}, u32[]{:S(2)}, u32[]{:S(2)}) collective-permute-start(bf16[128,768]{0,1:T(8,128)(2,1)S(1)} %pad_maximum_fusion.9), channel_id=1, source_target_pairs={{0,4},{1,5},{2,6},{3,7},{4,0},{5,1},{6,2},{7,3},{8,12},{9,13},{10,... | collective-permute-start | bytes 589832 | tf_op jit(solution)/shard_map/ppermute | solution.py:1294
  223.2 18.0 %collective-permute-start.21 = (bf16[128,768]{0,1:T(8,128)(2,1)S(1)}, bf16[128,768]{0,1:T(8,128)(2,1)}, u32[]{:S(2)}, u32[]{:S(2)}) collective-permute-start(bf16[128,768]{0,1:T(8,128)(2,1)S(1)} %pad_maximum_fusion.9), channel_id=1, source_target_pairs={{0,6},{1,7},{2,0},{3,1},{4,2},{5,3},{6,4},{7,5},{8,14},{9,15},{10,... | collective-permute-start | bytes 589832 | tf_op jit(solution)/shard_map/ppermute | solution.py:1294
  290.7 7.9 %collective-permute-start.31 = (f32[64,768]{1,0:T(8,128)S(1)}, f32[64,768]{1,0:T(8,128)S(1)}, u32[]{:S(2)}, u32[]{:S(2)}) collective-permute-start(f32[64,768]{1,0:T(8,128)S(1)} %get-tuple-element.302), channel_id=1, source_target_pairs={{0,1},{1,0},{2,3},{3,2},{4,5},{5,4},{6,7},{7,6},{8,9},{9,8},{10,11... | collective-permute-start | bytes 589832 | tf_op jit(solution)/shard_map/ppermute | solution.py:1294
  291.9 9.6 %collective-permute-start.32 = (f32[64,768]{1,0:T(8,128)S(1)}, f32[64,768]{1,0:T(8,128)S(1)}, u32[]{:S(2)}, u32[]{:S(2)}) collective-permute-start(f32[64,768]{1,0:T(8,128)S(1)} %get-tuple-element.301), channel_id=1, source_target_pairs={{0,1},{1,0},{2,3},{3,2},{4,5},{5,4},{6,7},{7,6},{8,9},{9,8},{10,11... | collective-permute-start | bytes 589832 | tf_op jit(solution)/shard_map/ppermute | solution.py:1294
  292.8 10.8 %collective-permute-start.29 = (f32[64,768]{1,0:T(8,128)S(1)}, f32[64,768]{1,0:T(8,128)S(1)}, u32[]{:S(2)}, u32[]{:S(2)}) collective-permute-start(f32[64,768]{1,0:T(8,128)S(1)} %get-tuple-element.303), channel_id=1, source_target_pairs={{0,1},{1,0},{2,3},{3,2},{4,5},{5,4},{6,7},{7,6},{8,9},{9,8},{10,11... | collective-permute-start | bytes 589832 | tf_op jit(solution)/shard_map/ppermute | solution.py:1294
  316.5 51.9 %collective-permute-start.36 = (f32[384,6400]{1,0:T(8,128)}, f32[384,6400]{1,0:T(8,128)}, u32[]{:S(2)}, u32[]{:S(2)}) collective-permute-start(f32[384,6400]{1,0:T(8,128)} %get-tuple-element.161), channel_id=1, source_target_pairs={{0,8},{8,0},{16,24},{24,16},{1,9},{9,1},{17,25},{25,17},{2,10},{10... | collective-permute-start | bytes 29491208 | tf_op jit(solution)/shard_map/ppermute | solution.py:1288
  318.0 17.0 %collective-permute-start.34 = (f32[64,768]{1,0:T(8,128)S(1)}, f32[64,768]{1,0:T(8,128)S(1)}, u32[]{:S(2)}, u32[]{:S(2)}) collective-permute-start(f32[64,768]{1,0:T(8,128)S(1)} %get-tuple-element.304), channel_id=1, source_target_pairs={{0,4},{1,5},{2,6},{3,7},{4,0},{5,1},{6,2},{7,3},{8,12},{9,13},{10,... | collective-permute-start | bytes 589832 | tf_op jit(solution)/shard_map/ppermute | solution.py:1294
  320.8 16.9 %collective-permute-start.30 = (f32[64,768]{1,0:T(8,128)S(1)}, f32[64,768]{1,0:T(8,128)S(1)}, u32[]{:S(2)}, u32[]{:S(2)}) collective-permute-start(f32[64,768]{1,0:T(8,128)S(1)} %get-tuple-element.306), channel_id=1, source_target_pairs={{0,6},{1,7},{2,0},{3,1},{4,2},{5,3},{6,4},{7,5},{8,14},{9,15},{10,... | collective-permute-start | bytes 589832 | tf_op jit(solution)/shard_map/ppermute | solution.py:1294
  322.6 15.2 %collective-permute-start.28 = (f32[64,768]{1,0:T(8,128)S(1)}, f32[64,768]{1,0:T(8,128)S(1)}, u32[]{:S(2)}, u32[]{:S(2)}) collective-permute-start(f32[64,768]{1,0:T(8,128)S(1)} %get-tuple-element.300), channel_id=1, source_target_pairs={{0,1},{1,0},{2,3},{3,2},{4,5},{5,4},{6,7},{7,6},{8,9},{9,8},{10,11... | collective-permute-start | bytes 589832 | tf_op jit(solution)/shard_map/ppermute | solution.py:1294
  365.6 16.7 %collective-permute-start.37 = (f32[16,384,384]{2,1,0:T(8,128)}, f32[16,384,384]{2,1,0:T(8,128)}, u32[]{:S(2)}, u32[]{:S(2)}) collective-permute-start(f32[16,384,384]{2,1,0:T(8,128)} %get-tuple-element.175), channel_id=1, source_target_pairs={{0,8},{8,0},{16,24},{24,16},{1,9},{9,1},{17,25},{25,17},{2,10},{10... | collective-permute-start | bytes 28311560 | tf_op jit(solution)/shard_map/ppermute | solution.py:1288
  374.4 71.8 %collective-permute-start.40 = (f16[192,6400]{1,0:T(8,128)(2,1)}, f16[192,6400]{1,0:T(8,128)(2,1)}, u32[]{:S(2)}, u32[]{:S(2)}) collective-permute-start(f16[192,6400]{1,0:T(8,128)(2,1)} %fusion.7), channel_id=1, source_target_pairs={{0,16},{8,24},{16,0},{24,8},{1,17},{9,25},{17,1},{25,9},{2,18},{10... | collective-permute-start | bytes 7372808 | tf_op jit(solution)/shard_map/ppermute | solution.py:1288
  394.7 63.9 %collective-permute-start.43 = (f16[3088,384]{1,0:T(8,128)(2,1)}, f16[3088,384]{1,0:T(8,128)(2,1)}, u32[]{:S(2)}, u32[]{:S(2)}) collective-permute-start(f16[3088,384]{1,0:T(8,128)(2,1)} %concatenate.163), channel_id=1, source_target_pairs={{0,1},{1,0},{2,3},{3,2},{4,5},{5,4},{6,7},{7,6},{8,9},{9,8},{10,11... | collective-permute-start | bytes 7114760 | tf_op jit(solution)/shard_map/ppermute | solution.py:1294
  444.5 11.2 %collective-permute-start.39 = (bf16[512,384]{1,0:T(8,128)(2,1)S(1)}, bf16[512,384]{1,0:T(8,128)(2,1)S(1)}, u32[]{:S(2)}, u32[]{:S(2)}) collective-permute-start(bf16[512,384]{1,0:T(8,128)(2,1)S(1)} %fusion.29), channel_id=1, source_target_pairs={{0,16},{8,24},{16,0},{24,8},{1,17},{9,25},{17,1},{25,9},{2,18},{10... | collective-permute-start | bytes 1179656 | tf_op jit(solution)/shard_map/ppermute | solution.py:1288
  469.0 11.0 %collective-permute-start.44 = (f32[9,384,384]{2,1,0:T(8,128)}, f32[9,384,384]{2,1,0:T(8,128)}, u32[]{:S(2)}, u32[]{:S(2)}) collective-permute-start(f32[9,384,384]{2,1,0:T(8,128)} %get-tuple-element.192), channel_id=1, source_target_pairs={{0,8},{8,0},{16,24},{24,16},{1,9},{9,1},{17,25},{25,17},{2,10},{10... | collective-permute-start | bytes 15925256 | tf_op jit(solution)/shard_map/ppermute | solution.py:1288
  484.4 31.9 %collective-permute-start.46 = (f16[1744,384]{1,0:T(8,128)(2,1)}, f16[1744,384]{1,0:T(8,128)(2,1)S(1)}, u32[]{:S(2)}, u32[]{:S(2)}) collective-permute-start(f16[1744,384]{1,0:T(8,128)(2,1)} %concatenate.169), channel_id=1, source_target_pairs={{0,1},{1,0},{2,3},{3,2},{4,5},{5,4},{6,7},{7,6},{8,9},{9,8},{10,11... | collective-permute-start | bytes 4018184 | tf_op jit(solution)/shard_map/ppermute | solution.py:1294
  485.2 41.1 %collective-permute-start.42 = (bf16[3072,128]{1,0:T(8,128)(2,1)S(1)}, bf16[3072,128]{1,0:T(8,128)(2,1)}, u32[]{:S(2)}, u32[]{:S(2)}) collective-permute-start(bf16[3072,128]{1,0:T(8,128)(2,1)S(1)} %maximum_maximum_fusion.refs_3_), channel_id=1, source_target_pairs={{0,4},{1,5},{2,6},{3,7},{4,0},{5,1},{6,2},{7,3},{8,12},{9,13},{10,... | collective-permute-start | bytes 2359304 | tf_op jit(solution)/shard_map/ppermute | solution.py:1294
  491.9 61.4 %collective-permute-start.49 = (bf16[3072,128]{1,0:T(8,128)(2,1)S(1)}, bf16[3072,128]{1,0:T(8,128)(2,1)}, u32[]{:S(2)}, u32[]{:S(2)}) collective-permute-start(bf16[3072,128]{1,0:T(8,128)(2,1)S(1)} %maximum_maximum_fusion.refs_3_), channel_id=1, source_target_pairs={{0,2},{1,3},{2,4},{3,5},{4,6},{5,7},{6,0},{7,1},{8,10},{9,11},{10,... | collective-permute-start | bytes 2359304 | tf_op jit(solution)/shard_map/ppermute | solution.py:1294
  492.0 61.3 %collective-permute-start.50 = (bf16[3072,128]{1,0:T(8,128)(2,1)S(1)}, bf16[3072,128]{1,0:T(8,128)(2,1)}, u32[]{:S(2)}, u32[]{:S(2)}) collective-permute-start(bf16[3072,128]{1,0:T(8,128)(2,1)S(1)} %maximum_maximum_fusion.refs_3_), channel_id=1, source_target_pairs={{0,6},{1,7},{2,0},{3,1},{4,2},{5,3},{6,4},{7,5},{8,14},{9,15},{10,... | collective-permute-start | bytes 2359304 | tf_op jit(solution)/shard_map/ppermute | solution.py:1294
  504.2 27.7 %collective-permute-start.47 = (f16[1552,384]{1,0:T(8,128)(2,1)}, f16[1552,384]{1,0:T(8,128)(2,1)}, u32[]{:S(2)}, u32[]{:S(2)}) collective-permute-start(f16[1552,384]{1,0:T(8,128)(2,1)} %concatenate.171), channel_id=1, source_target_pairs={{0,16},{8,24},{16,0},{24,8},{1,17},{9,25},{17,1},{25,9},{2,18},{10... | collective-permute-start | bytes 3575816 | tf_op jit(solution)/shard_map/ppermute | solution.py:1288
  526.2 27.1 %collective-permute-start.52 = (bf16[3072,128]{1,0:T(8,128)(2,1)S(1)}, bf16[3072,128]{1,0:T(8,128)(2,1)}, u32[]{:S(2)}, u32[]{:S(2)}) collective-permute-start(bf16[3072,128]{1,0:T(8,128)(2,1)S(1)} %maximum_maximum_fusion.refs_3_), channel_id=1, source_target_pairs={{0,1},{1,0},{2,3},{3,2},{4,5},{5,4},{6,7},{7,6},{8,9},{9,8},{10,11... | collective-permute-start | bytes 2359304 | tf_op jit(solution)/shard_map/ppermute | solution.py:1294
  530.5 34.9 %collective-permute-start.48 = (f16[880,384]{1,0:T(8,128)(2,1)}, f16[880,384]{1,0:T(8,128)(2,1)}, u32[]{:S(2)}, u32[]{:S(2)}) collective-permute-start(f16[880,384]{1,0:T(8,128)(2,1)} %concatenate.170), channel_id=1, source_target_pairs={{0,16},{8,24},{16,0},{24,8},{1,17},{9,25},{17,1},{25,9},{2,18},{10... | collective-permute-start | bytes 2027528 | tf_op jit(solution)/shard_map/ppermute | solution.py:1288
  556.6 53.5 %collective-permute-start.53 = (bf16[3,3072,128]{2,1,0:T(8,128)(2,1)}, bf16[3,3072,128]{2,1,0:T(8,128)(2,1)}, u32[]{:S(2)}, u32[]{:S(2)}) collective-permute-start(bf16[3,3072,128]{2,1,0:T(8,128)(2,1)} %pad_maximum_fusion), channel_id=1, source_target_pairs={{0,1},{1,0},{2,3},{3,2},{4,5},{5,4},{6,7},{7,6},{8,9},{9,8},{10,11... | collective-permute-start | bytes 7077896 | tf_op jit(solution)/shard_map/ppermute | solution.py:1294
  573.3 34.4 %collective-permute-start.51 = (f16[616,384]{1,0:T(8,128)(2,1)}, f16[616,384]{1,0:T(8,128)(2,1)S(1)}, u32[]{:S(2)}, u32[]{:S(2)}) collective-permute-start(f16[616,384]{1,0:T(8,128)(2,1)} %concatenate.173), channel_id=1, source_target_pairs={{0,2},{1,3},{2,4},{3,5},{4,6},{5,7},{6,0},{7,1},{8,10},{9,11},{10,... | collective-permute-start | bytes 1419272 | tf_op jit(solution)/shard_map/ppermute | solution.py:1294
  576.0 55.8 %collective-permute-start.55 = (f16[616,384]{1,0:T(8,128)(2,1)S(1)}, f16[616,384]{1,0:T(8,128)(2,1)}, u32[]{:S(2)}, u32[]{:S(2)}) collective-permute-start(f16[616,384]{1,0:T(8,128)(2,1)S(1)} %concatenate.175), channel_id=1, source_target_pairs={{0,6},{1,7},{2,0},{3,1},{4,2},{5,3},{6,4},{7,5},{8,14},{9,15},{10,... | collective-permute-start | bytes 1419272 | tf_op jit(solution)/shard_map/ppermute | solution.py:1294
  578.0 55.0 %collective-permute-start.54 = (f16[616,384]{1,0:T(8,128)(2,1)}, f16[616,384]{1,0:T(8,128)(2,1)}, u32[]{:S(2)}, u32[]{:S(2)}) collective-permute-start(f16[616,384]{1,0:T(8,128)(2,1)} %concatenate.174), channel_id=1, source_target_pairs={{0,4},{1,5},{2,6},{3,7},{4,0},{5,1},{6,2},{7,3},{8,12},{9,13},{10,... | collective-permute-start | bytes 1419272 | tf_op jit(solution)/shard_map/ppermute | solution.py:1294
  636.3 8.2 %collective-permute-start.58 = (f32[25,24,384]{2,1,0:T(8,128)S(1)}, f32[25,24,384]{2,1,0:T(8,128)}, u32[]{:S(2)}, u32[]{:S(2)}) collective-permute-start(f32[25,24,384]{2,1,0:T(8,128)S(1)} %get-tuple-element.287), channel_id=1, source_target_pairs={{0,8},{8,0},{16,24},{24,16},{1,9},{9,1},{17,25},{25,17},{2,10},{10... | collective-permute-start | bytes 2764808 | tf_op jit(solution)/shard_map/ppermute | solution.py:1288
  662.2 36.2 %collective-permute-start.65 = (f16[688,384]{1,0:T(8,128)(2,1)S(1)}, f16[688,384]{1,0:T(8,128)(2,1)S(1)}, u32[]{:S(2)}, u32[]{:S(2)}) collective-permute-start(f16[688,384]{1,0:T(8,128)(2,1)S(1)} %concatenate.183), channel_id=1, source_target_pairs={{0,2},{1,3},{2,4},{3,5},{4,6},{5,7},{6,0},{7,1},{8,10},{9,11},{10,... | collective-permute-start | bytes 1585160 | tf_op jit(solution)/shard_map/ppermute | solution.py:1294
  663.2 42.9 %collective-permute-start.67 = (f16[688,384]{1,0:T(8,128)(2,1)S(1)}, f16[688,384]{1,0:T(8,128)(2,1)S(1)}, u32[]{:S(2)}, u32[]{:S(2)}) collective-permute-start(f16[688,384]{1,0:T(8,128)(2,1)S(1)} %concatenate.183), channel_id=1, source_target_pairs={{0,4},{1,5},{2,6},{3,7},{4,0},{5,1},{6,2},{7,3},{8,12},{9,13},{10,... | collective-permute-start | bytes 1585160 | tf_op jit(solution)/shard_map/ppermute | solution.py:1294
  667.7 42.7 %collective-permute-start.69 = (f16[688,384]{1,0:T(8,128)(2,1)S(1)}, f16[688,384]{1,0:T(8,128)(2,1)S(1)}, u32[]{:S(2)}, u32[]{:S(2)}) collective-permute-start(f16[688,384]{1,0:T(8,128)(2,1)S(1)} %concatenate.183), channel_id=1, source_target_pairs={{0,6},{1,7},{2,0},{3,1},{4,2},{5,3},{6,4},{7,5},{8,14},{9,15},{10,... | collective-permute-start | bytes 1585160 | tf_op jit(solution)/shard_map/ppermute | solution.py:1294
  669.4 59.4 %collective-permute-start.64 = (f16[688,384]{1,0:T(8,128)(2,1)S(1)}, f16[688,384]{1,0:T(8,128)(2,1)S(1)}, u32[]{:S(2)}, u32[]{:S(2)}) collective-permute-start(f16[688,384]{1,0:T(8,128)(2,1)S(1)} %concatenate.183), channel_id=1, source_target_pairs={{0,1},{1,0},{2,3},{3,2},{4,5},{5,4},{6,7},{7,6},{8,9},{9,8},{10,11... | collective-permute-start | bytes 1585160 | tf_op jit(solution)/shard_map/ppermute | solution.py:1294
  698.4 31.5 %collective-permute-start.66 = (f16[688,384]{1,0:T(8,128)(2,1)S(1)}, f16[688,384]{1,0:T(8,128)(2,1)S(1)}, u32[]{:S(2)}, u32[]{:S(2)}) collective-permute-start(f16[688,384]{1,0:T(8,128)(2,1)S(1)} %collective-permute-done.65), channel_id=1, source_target_pairs={{0,1},{1,0},{2,3},{3,2},{4,5},{5,4},{6,7},{7,6},{8,9},{9,8},{10,11... | collective-permute-start | bytes 1585160 | tf_op jit(solution)/shard_map/ppermute | solution.py:1294
  706.2 24.8 %collective-permute-start.68 = (f16[688,384]{1,0:T(8,128)(2,1)S(1)}, f16[688,384]{1,0:T(8,128)(2,1)S(1)}, u32[]{:S(2)}, u32[]{:S(2)}) collective-permute-start(f16[688,384]{1,0:T(8,128)(2,1)S(1)} %collective-permute-done.67), channel_id=1, source_target_pairs={{0,1},{1,0},{2,3},{3,2},{4,5},{5,4},{6,7},{7,6},{8,9},{9,8},{10,11... | collective-permute-start | bytes 1585160 | tf_op jit(solution)/shard_map/ppermute | solution.py:1294
  710.4 22.1 %collective-permute-start.70 = (f16[688,384]{1,0:T(8,128)(2,1)S(1)}, f16[688,384]{1,0:T(8,128)(2,1)S(1)}, u32[]{:S(2)}, u32[]{:S(2)}) collective-permute-start(f16[688,384]{1,0:T(8,128)(2,1)S(1)} %collective-permute-done.69), channel_id=1, source_target_pairs={{0,1},{1,0},{2,3},{3,2},{4,5},{5,4},{6,7},{7,6},{8,9},{9,8},{10,11... | collective-permute-start | bytes 1585160 | tf_op jit(solution)/shard_map/ppermute | solution.py:1294
  (71 other events, 590.5 us)

commit v6 on v5

--- a/solution.py
+++ b/solution.py
@@ -444,7 +444,7 @@
     allow_ref[...] = ((cols <= rows) & (document(rows) == document(cols))).astype(f32)
 
 
-ROWS = 256
+ROWS = 128
 
 
 def attend_kernel(

time: 782 us -> 786 us (level)
  starting transfers between devices: 89.8 us -> 67.3 us
  waiting for transfers between devices: 184 us -> 201 us
  Pallas kernels: 306 us -> 316 us
    ppermute x47, starting transfers between devices: 73.9 us -> 54.1 us  [over_voc(): return lax.ppermute(values, 'vocab', pairs)]
    ppermute x47, waiting for transfers between devices: 157 us -> 172 us  [over_voc(): return lax.ppermute(values, 'vocab', pairs)]
  transfers between devices with their start and end apart: 71 -> 71, of which waited for: 39 -> 40; matrix products, arithmetic and copies ran while one was open for 18% -> 18% of each run, Pallas kernels for 28% -> 29%
where the time goes in v6:
time: 786 us; the launch traced here: 781 us
  Pallas kernels  316 us (40%)
  waiting for transfers between devices  201 us (26%)
  other arithmetic  125 us (16%)
  starting transfers between devices  67.3 us (9%)
  local copies, waits for them, and re-layouts  54.4 us (7%)
  between operations  17.2 us (2%)
    ppermute x47, waiting for transfers between devices, over_voc(): return lax.ppermute(values, 'vocab', pairs)  172 us
    ppermute x47, starting transfers between devices, over_voc(): return lax.ppermute(values, 'vocab', pairs)  54.1 us
    pallas_call x1, Pallas kernels, attend_back(): pl.pallas_call(partial(attend_back_kernel, coefficient, int(later)), grid...  41.1 us
    pallas_call x1, Pallas kernels, shampoo(): pl.pallas_call(partial(shampoo_kernel, count, strip), grid=(slots // 2,),...  32.7 us
    ppermute x24, waiting for transfers between devices, over_dp(): return lax.ppermute(values, 'dp', pairs)  29.9 us
    pallas_call x4, Pallas kernels, lookup(): pl.pallas_call(partial(lookup_kernel, rows_all), out_shape=[jax.ShapeDtyp...  28.6 us
    pallas_call x4, Pallas kernels, find_hits(): pl.pallas_call(partial(hits_kernel, empty_row), out_shape=jax.ShapeDtypeS...  27.9 us
    pallas_call x1, Pallas kernels, mlp_back(): pl.pallas_call(mlp_back_kernel, grid=(FSTEPS,), out_shape=[halves, halves...  26.2 us
  transfers between devices with their start and end apart: 71, of which 40 were waited for; matrix products, arithmetic and copies ran while one was open for 18% of the time, Pallas kernels for 29%

profile of v6, /device:TPU:8, one launch (start us, length us, event | category | flops | bytes accessed | tf_op | source)
XLA Modules:
  0.0 780.9 jit_solution(2162346663843615993)
XLA Ops:
  5.0 5.3 convert_element_type.163.refs_0_
  16.8 4.4 collective-permute-start.2
  23.6 7.4 turn_table.1.table_ref
  31.0 7.0 find_hits.4.list_ref
  38.0 7.1 lookup.5
  47.7 7.0 find_hits.6.list_ref
  54.7 7.2 lookup.4
  61.9 7.0 find_hits.5.list_ref
  68.9 7.2 lookup.7
  76.7 3.6 collective-permute-start.11
  82.7 7.0 find_hits.7.list_ref
  89.7 7.1 lookup.6
  99.0 8.5 %collective-permute-done.11 = bf16[2,512,384]{2,1,0:T(8,128)(2,1)S(1)} collective-permute-done((bf16[2,512,384]{2,1,0:T(8,128)(2,1)S(1)}, bf16[2,512,384]{2,1,0:T(8,128)(2,1)S(1)}, u32[]{:S(2)}, u32[]{:S(2)}) %collective-permute-start.11) | collective-permute-done | bytes 786464 | tf_op jit(solution)/shard_map/ppermute | solution.py:1294
  121.4 11.5 %place_blocks.1 = (bf16[768,2304]{1,0:T(8,128)(2,1)}, bf16[768,768]{1,0:T(8,128)(2,1)}, bf16[768,3072]{1,0:T(8,128)(2,1)}, bf16[3072,768]{1,0:T(8,128)(2,1)}) custom-call(s32[48]{0:T(128)} %get-tuple-element.356.src_ref, s32[48]{0:T(128)} %get-tuple-element.355.off_ref, bf16[12,384,384]{2,1,0:T(8,128)(2,1)} %convert_element_type.163.refs_0_, ...), custom_call_target="tpu_custom_call" | custom-call | bytes 566231 | tf_op jit(solution)/shard_map/place_blocks/pallas_call | solution.py:110
  134.6 15.1 %collective-permute-done.16 = bf16[2,512,384]{2,1,0:T(8,128)(2,1)} collective-permute-done((bf16[2,512,384]{2,1,0:T(8,128)(2,1)}, bf16[2,512,384]{2,1,0:T(8,128)(2,1)}, u32[]{:S(2)}, u32[]{:S(2)}) %collective-permute-start.16) | collective-permute-done | bytes 786464 | tf_op jit(solution)/shard_map/ppermute | solution.py:1294
  154.9 8.5 %collective-permute-done.17 = bf16[512,384]{1,0:T(8,128)(2,1)} collective-permute-done((bf16[512,384]{1,0:T(8,128)(2,1)}, bf16[512,384]{1,0:T(8,128)(2,1)}, u32[]{:S(2)}, u32[]{:S(2)}) %collective-permute-start.17) | collective-permute-done | bytes 393248 | tf_op jit(solution)/shard_map/ppermute | solution.py:1288
  169.8 6.2 qkv_forward.1
  175.9 23.0 %attend.1 = (bf16[512,768]{1,0:T(8,128)(2,1)}, f32[8,128]{1,0:T(8,128)}) custom-call(s32[1,4]{1,0:T(1,128)} %len_ref.3, bf16[512,2304]{1,0:T(8,128)(2,1)} %get-tuple-element.149.q_ref.k_ref.v_ref, bf16[512,2304]{1,0:T(8,128)(2,1)} %get-tuple-element.149.q_ref.k_ref.v_ref, bf16[512,2304]{1,0:T(8,128)(2,1)} %get-tuple-element.149.q_ref.k_ref.v_ref, ...), custom_call_target="tpu_custom_call" | custom-call | flops 240000000 | bytes 80000 | tf_op jit(solution)/shard_map/attend/pallas_call | solution.py:495
  199.0 14.8 %mlp_forward.1 = (f32[512,768]{1,0:T(8,128)}, bf16[512,768]{1,0:T(8,128)(2,1)}, f32[512,3072]{1,0:T(8,128)}, bf16[512,3072]{1,0:T(8,128)(2,1)}, f32[512,768]{1,0:T(8,128)}, /*index=5*/bf16[64,768]{1,0:T(8,128)(2,1)}) custom-call(bf16[512,768]{1,0:T(8,128)(2,1)} %pad_maximum_fusion.4.x_ref, bf16[512,768]{1,0:T(8,128)(2,1)} %get-tuple-element.150.y_ref, ...), custom_call_target="tpu_custom_call" | custom-call | flops 108716360 | bytes 600000 | tf_op jit(solution)/shard_map/mlp_forward/pallas_call | solution.py:693
  215.2 6.9 collective-permute-done.18
  230.2 10.0 %collective-permute-done.20 = bf16[128,768]{0,1:T(8,128)(2,1)S(1)} collective-permute-done((bf16[128,768]{0,1:T(8,128)(2,1)S(1)}, bf16[128,768]{0,1:T(8,128)(2,1)S(1)}, u32[]{:S(2)}, u32[]{:S(2)}) %collective-permute-start.20) | collective-permute-done | bytes 196640 | tf_op jit(solution)/shard_map/ppermute | solution.py:1294
  247.3 15.9 %vocabulary_logits.1 = (f32[512,6288]{1,0:T(8,128)}, f32[8,512]{1,0:T(8,128)}) custom-call(s32[4]{0:T(128)} %pad_add_fusion.5.places_ref, bf16[512,768]{1,0:T(8,128)(2,1)} %copy.72.group_ref, s32[512,1]{1,0:T(8,128)} %sub.290.target_ref, bf16[192,6288]{1,0:T(8,128)(2,1)} %copy-done.2, bf16[192,6288]{1,0:T(8,128)(2,1)} %collective-permute-done.22.refs_1_, ...), custom_call_target="tpu_custom_call" | custom-call | flops 98901688 | bytes 400000 | tf_op jit(solution)/shard_map/vocabulary_logits/pallas_call | solution.py:1038
  275.7 15.3 %vocabulary_back.1 = (bf16[512,6400]{1,0:T(8,128)(2,1)}, f32[512,768]{1,0:T(8,128)}) custom-call(s32[4]{0:T(128)} %pad_add_fusion.5.places_ref, f32[512,6288]{1,0:T(8,128)} %get-tuple-element.156.logit_ref, f32[128,512]{1,0:T(8,128)} %select_maximum_fusion.stat_ref, s32[512,1]{1,0:T(8,128)} %sub.290.target_ref, bf16[192,6288]{1,0:T(8,128)(2,1)} %copy-done.2, ...), custom_call_target="tpu_custom_call" | custom-call | flops 98901688 | bytes 600000 | tf_op jit(solution)/shard_map/vocabulary_back/pallas_call | solution.py:1081
  294.7 5.4 collective-permute-done.31
  307.0 11.7 %lexicon.1 = (f32[384,6400]{1,0:T(8,128)}, f32[384,6400]{1,0:T(8,128)}, f32[1,1280]{1,0:T(1,128)}, f32[1,1280]{1,0:T(1,128)}) custom-call(s32[4]{0:T(128)} %pad_add_fusion.5.places_ref, bf16[768,512]{1,0:T(8,128)(2,1)} %bitcast.236, bf16[512,6400]{1,0:T(8,128)(2,1)} %get-tuple-element.160.grad_ref), custom_call_target="tpu_custom_call" | custom-call | flops 100663296 | bytes 600000 | tf_op jit(solution)/shard_map/lexicon/pallas_call | solution.py:1127
  326.9 9.9 %collective-permute-done.34 = f32[64,768]{1,0:T(8,128)S(1)} collective-permute-done((f32[64,768]{1,0:T(8,128)S(1)}, f32[64,768]{1,0:T(8,128)S(1)}, u32[]{:S(2)}, u32[]{:S(2)}) %collective-permute-start.34) | collective-permute-done | bytes 196640 | tf_op jit(solution)/shard_map/ppermute | solution.py:1294
  341.1 26.2 %mlp_back.1 = (f32[16,384,384]{2,1,0:T(8,128)}, f32[16,384,384]{2,1,0:T(8,128)}, f32[1,384]{1,0:T(1,128)}, f32[1,384]{1,0:T(1,128)}, f32[512,768]{1,0:T(8,128)},...) custom-call(s32[1]{0:T(128)} %bitcast.4.core_ref, f32[64,768]{1,0:T(8,128)} %fusion.37.ghp_ref, ...), custom_call_target="tpu_custom_call" | custom-call | flops 193273536 | bytes 1000000 | tf_op jit(solution)/shard_map/mlp_back/pallas_call | solution.py:833
  370.1 6.1 fusion.7
  377.2 4.8 collective-permute-done.38
  384.0 10.4 %multiply_convert_fusion = (f16[16,192,384]{2,1,0:T(8,128)(2,1)S(1)}, f32[16,192,384]{2,1,0:T(8,128)}) fusion(f32[16,384,384]{2,1,0:T(8,128)} %collective-permute-done.37, s32[]{:T(128)S(6)} %select_n.387, f32[16,384,384]{2,1,0:T(8,128)} %get-tuple-element.174, f32[]{:T(128)S(6)} %exp2.159, s32[]{:T(128)S(6)} %select_n.385), kind=kLoop, calls=%fused_computation.32 | loop fusion | flops 4718592 | bytes 25952268 | tf_op jit(solution)/shard_map/convert_element_type | solution.py:1227
  396.7 41.1 %attend_back.1 = (bf16[3,512,768]{2,1,0:T(8,128)(2,1)}, f32[12,64,64]{2,1,0:T(8,128)}, f32[12,64,64]{2,1,0:T(8,128)}) custom-call(s32[1,4]{1,0:T(1,128)} %len_ref.3, bf16[512,2304]{1,0:T(8,128)(2,1)} %get-tuple-element.149.q_ref.k_ref.v_ref, bf16[512,2304]{1,0:T(8,128)(2,1)} %get-tuple-element.149.q_ref.k_ref.v_ref, ...), custom_call_target="tpu_custom_call" | custom-call | flops 240000000 | bytes 80000 | tf_op jit(solution)/shard_map/attend_back/pallas_call | solution.py:607
  437.8 7.9 %qkv_back.1 = (bf16[512,768]{1,0:T(8,128)(2,1)}, f32[16,768]{1,0:T(8,128)}) custom-call(bf16[3,512,768]{2,1,0:T(8,128)(2,1)} %get-tuple-element.180.g_ref, bf16[768,2304]{1,0:T(8,128)(2,1)} %get-tuple-element.148.w_ref, bf16[512,768]{1,0:T(8,128)(2,1)} %pad_maximum_fusion.4.x_ref, f32[512,768]{1,0:T(8,128)} %get-tuple-element.181.gx1_ref, f32[15,768]{1,0:T(8,128)} %vec_ref.7), custom_call_target="tpu_custom_call" | custom-call | flops 36238784 | bytes 200000 | tf_op jit(solution)/shard_map/qkv_back/pallas_call | solution.py:897
  452.7 7.5 fusion.1.lex_ref
  463.9 10.4 %qkv_weights.1 = (f32[9,384,384]{2,1,0:T(8,128)}, f32[9,384,384]{2,1,0:T(8,128)}, f32[1,384]{1,0:T(1,128)}, f32[1,384]{1,0:T(1,128)}) custom-call(s32[1]{0:T(128)} %bitcast.4.core_ref, bf16[512,768]{1,0:T(8,128)(2,1)} %get-tuple-element.185.h_ref, bf16[3,512,768]{2,1,0:T(8,128)(2,1)} %get-tuple-element.180.g_ref, bf16[512,768]{1,0:T(8,128)(2,1)} %get-tuple-element.150.y_ref, ...), custom_call_target="tpu_custom_call" | custom-call | flops 48318384 | bytes 400000 | tf_op jit(solution)/shard_map/qkv_weights/pallas_call | solution.py:949
  477.9 5.4 collective-permute-done.45
  492.1 4.2 convert_element_type.178
  511.4 10.0 %collective-permute-done.46 = f16[1744,384]{1,0:T(8,128)(2,1)S(1)} collective-permute-done((f16[1744,384]{1,0:T(8,128)(2,1)}, f16[1744,384]{1,0:T(8,128)(2,1)S(1)}, u32[]{:S(2)}, u32[]{:S(2)}) %collective-permute-start.46) | collective-permute-done | bytes 1339424 | tf_op jit(solution)/shard_map/ppermute | solution.py:1294
  524.6 3.7 add_add_fusion
  539.6 19.9 %collective-permute-done.49.refs_1_ = bf16[3072,128]{1,0:T(8,128)(2,1)} collective-permute-done((bf16[3072,128]{1,0:T(8,128)(2,1)S(1)}, bf16[3072,128]{1,0:T(8,128)(2,1)}, u32[]{:S(2)}, u32[]{:S(2)}) %collective-permute-start.49) | collective-permute-done | bytes 786464 | tf_op jit(solution)/shard_map/ppermute | solution.py:1294
  587.5 13.6 %scatter_first.1 = (f32[6400,128]{1,0:T(8,128)}, f32[6400,128]{1,0:T(8,128)}) custom-call(s32[8256]{0:T(1024)} %copy-done.22, s32[8256]{0:T(1024)} %copy-done.25, bf16[3072,128]{1,0:T(8,128)(2,1)} %collective-permute-done.42.refs_0_, bf16[3072,128]{1,0:T(8,128)(2,1)} %collective-permute-done.49.refs_1_, bf16[3072,128]{1,0:T(8,128)(2,1)} %collective-permute-done.50.refs_2_, ...), custom_call_target="tpu_custom_call" | custom-call | flops 200000000 | bytes 128778 | tf_op jit(solution)/shard_map/scatter_first/pallas_call | solution.py:316
  601.0 11.9 %collective-permute-done.51 = f16[616,384]{1,0:T(8,128)(2,1)S(1)} collective-permute-done((f16[616,384]{1,0:T(8,128)(2,1)}, f16[616,384]{1,0:T(8,128)(2,1)S(1)}, u32[]{:S(2)}, u32[]{:S(2)}) %collective-permute-start.51) | collective-permute-done | bytes 473120 | tf_op jit(solution)/shard_map/ppermute | solution.py:1294
  616.2 22.1 %scatter_last.1 = (f32[192,6288]{1,0:T(8,128)}, f32[1,1]{1,0:T(1,128)}) custom-call(s32[8256]{0:T(1024)} %copy-done.22, s32[8256]{0:T(1024)} %copy-done.25, f32[6400,128]{1,0:T(8,128)} %get-tuple-element.208.first_acc, f32[6400,128]{1,0:T(8,128)} %get-tuple-element.209.first_tail, f32[192,6400]{1,0:T(8,128)} %fusion.1.lex_ref, ...), custom_call_target="tpu_custom_call" | custom-call | flops 200000000 | bytes 193167 | tf_op jit(solution)/shard_map/scatter_last/pallas_call | solution.py:337
  662.4 4.1 collective-permute-start.62
  670.8 4.1 collective-permute-start.67
  678.0 28.0 %collective-permute-done.65 = f16[688,384]{1,0:T(8,128)(2,1)S(1)} collective-permute-done((f16[688,384]{1,0:T(8,128)(2,1)S(1)}, f16[688,384]{1,0:T(8,128)(2,1)S(1)}, u32[]{:S(2)}, u32[]{:S(2)}) %collective-permute-start.65) | collective-permute-done | bytes 528416 | tf_op jit(solution)/shard_map/ppermute | solution.py:1294
  705.9 7.7 collective-permute-done.67
  716.9 12.2 %fusion.11 = (f32[6288,192]{0,1:T(8,128)}, f32[6288,192]{0,1:T(8,128)}, f32[6288,192]{0,1:T(8,128)}) fusion(f32[192,6288]{1,0:T(8,128)} %get-tuple-element.216, f32[]{:T(128)} %div.104, f32[6288,192]{0,1:T(8,128)} %param.49, f32[]{:T(128)} %bitcast.122, f32[]{:T(128)} %bitcast.120, f32[6288,192]{0,1:T(8,128)} %param.48, f32[6288,192]{0,1:T(8,128)} %param.47), kind=kLoop, calls=%fused_computation.55 | loop fusion | flops 19316736 | bytes 33804300 | tf_op jit(solution)/shard_map/transpose | solution.py:1690
  738.8 32.7 %shampoo.1 = (f32[12,384,384]{2,1,0:T(8,128)}, f32[12,384,384]{2,1,0:T(8,128)}, f32[12,384,384]{2,1,0:T(8,128)}, f32[12,384,384]{2,1,0:T(8,128)}, f32[2,384,384]{2,1,0:T(8,128)}) custom-call(s32[8]{0:T(128)} %stack.250.places_ref, f32[1]{0:T(128)} %bitcast.111.clip_ref, f32[688,384]{1,0:T(8,128)} %convert_element_type.202.refs_0_.refs_8_.refs_16_, ...), custom_call_target="tpu_custom_call" | custom-call | flops 326149088 | bytes 1415577 | tf_op jit(solution)/shard_map/shampoo/pallas_call | solution.py:1190
  (460 shorter events, 230.3 us)
Async XLA Ops:
  3.3 20.3 %collective-permute-start.4 = (bf16[192,6288]{1,0:T(8,128)(2,1)S(1)}, bf16[192,6288]{1,0:T(8,128)(2,1)}, u32[]{:S(2)}, u32[]{:S(2)}) collective-permute-start(bf16[192,6288]{1,0:T(8,128)(2,1)S(1)} %bitcast_convert_fusion.own_ref.refs_0_), channel_id=1, source_target_pairs={{0,8},{8,0},{16,24},{24,16},{1,9},{9,1},{17,25},{25,17},{2,10},{10... | collective-permute-start | bytes 7243784 | tf_op jit(solution)/shard_map/ppermute | solution.py:1288
  10.3 98.0 %collective-permute-start.12 = (bf16[12,384,384]{2,1,0:T(8,128)(2,1)}, bf16[12,384,384]{2,1,0:T(8,128)(2,1)}, u32[]{:S(2)}, u32[]{:S(2)}) collective-permute-start(bf16[12,384,384]{2,1,0:T(8,128)(2,1)} %convert_element_type.163.refs_0_), channel_id=1, source_target_pairs={{0,16},{8,24},{16,0},{24,8},{1,17},{9,25},{17,1},{25,9},{2,18},{10... | collective-permute-start | bytes 10616840 | tf_op jit(solution)/shard_map/ppermute | solution.py:1288
  45.1 30.9 %collective-permute-start.6 = (bf16[1024,384]{1,0:T(8,128)(2,1)}, bf16[1024,384]{1,0:T(8,128)(2,1)S(1)}, u32[]{:S(2)}, u32[]{:S(2)}) collective-permute-start(bf16[1024,384]{1,0:T(8,128)(2,1)} %get-tuple-element.130), channel_id=1, source_target_pairs={{0,1},{1,0},{2,3},{3,2},{4,5},{5,4},{6,7},{7,6},{8,9},{9,8},{10,11... | collective-permute-start | bytes 2359304 | tf_op jit(solution)/shard_map/ppermute | solution.py:1294
  46.8 34.8 %collective-permute-start.8 = (bf16[1024,384]{1,0:T(8,128)(2,1)}, bf16[1024,384]{1,0:T(8,128)(2,1)S(1)}, u32[]{:S(2)}, u32[]{:S(2)}) collective-permute-start(bf16[1024,384]{1,0:T(8,128)(2,1)} %get-tuple-element.135), channel_id=1, source_target_pairs={{0,1},{1,0},{2,3},{3,2},{4,5},{5,4},{6,7},{7,6},{8,9},{9,8},{10,11... | collective-permute-start | bytes 2359304 | tf_op jit(solution)/shard_map/ppermute | solution.py:1294
  76.2 20.5 %collective-permute-start.10 = (bf16[1024,384]{1,0:T(8,128)(2,1)}, bf16[1024,384]{1,0:T(8,128)(2,1)S(1)}, u32[]{:S(2)}, u32[]{:S(2)}) collective-permute-start(bf16[1024,384]{1,0:T(8,128)(2,1)} %get-tuple-element.140), channel_id=1, source_target_pairs={{0,1},{1,0},{2,3},{3,2},{4,5},{5,4},{6,7},{7,6},{8,9},{9,8},{10,11... | collective-permute-start | bytes 2359304 | tf_op jit(solution)/shard_map/ppermute | solution.py:1294
  76.7 30.7 %collective-permute-start.11 = (bf16[2,512,384]{2,1,0:T(8,128)(2,1)S(1)}, bf16[2,512,384]{2,1,0:T(8,128)(2,1)S(1)}, u32[]{:S(2)}, u32[]{:S(2)}) collective-permute-start(bf16[2,512,384]{2,1,0:T(8,128)(2,1)S(1)} %bitcast.261), channel_id=1, source_target_pairs={{0,4},{1,5},{2,6},{3,7},{4,0},{5,1},{6,2},{7,3},{8,12},{9,13},{10,... | collective-permute-start | bytes 2359304 | tf_op jit(solution)/shard_map/ppermute | solution.py:1294
  108.3 11.3 %collective-permute-start.13 = (bf16[12,384,384]{2,1,0:T(8,128)(2,1)}, bf16[12,384,384]{2,1,0:T(8,128)(2,1)S(1)}, u32[]{:S(2)}, u32[]{:S(2)}) collective-permute-start(bf16[12,384,384]{2,1,0:T(8,128)(2,1)} %convert_element_type.163.refs_0_), channel_id=1, source_target_pairs={{0,8},{8,0},{16,24},{24,16},{1,9},{9,1},{17,25},{25,17},{2,10},{10... | collective-permute-start | bytes 10616840 | tf_op jit(solution)/shard_map/ppermute | solution.py:1288
  108.3 11.6 %collective-permute-start.14 = (bf16[12,384,384]{2,1,0:T(8,128)(2,1)}, bf16[12,384,384]{2,1,0:T(8,128)(2,1)}, u32[]{:S(2)}, u32[]{:S(2)}) collective-permute-start(bf16[12,384,384]{2,1,0:T(8,128)(2,1)} %collective-permute-done.12.refs_1_), channel_id=1, source_target_pairs={{0,8},{8,0},{16,24},{24,16},{1,9},{9,1},{17,25},{25,17},{2,10},{10... | collective-permute-start | bytes 10616840 | tf_op jit(solution)/shard_map/ppermute | solution.py:1288
  108.8 24.1 %collective-permute-start.9 = (bf16[1024,384]{1,0:T(8,128)(2,1)}, bf16[1024,384]{1,0:T(8,128)(2,1)}, u32[]{:S(2)}, u32[]{:S(2)}) collective-permute-start(bf16[1024,384]{1,0:T(8,128)(2,1)} %get-tuple-element.137), channel_id=1, source_target_pairs={{0,1},{1,0},{2,3},{3,2},{4,5},{5,4},{6,7},{7,6},{8,9},{9,8},{10,11... | collective-permute-start | bytes 2359304 | tf_op jit(solution)/shard_map/ppermute | solution.py:1294
  110.5 24.1 %collective-permute-start.15 = (bf16[2,512,384]{2,1,0:T(8,128)(2,1)}, bf16[2,512,384]{2,1,0:T(8,128)(2,1)}, u32[]{:S(2)}, u32[]{:S(2)}) collective-permute-start(bf16[2,512,384]{2,1,0:T(8,128)(2,1)} %bitcast.260), channel_id=1, source_target_pairs={{0,6},{1,7},{2,0},{3,1},{4,2},{5,3},{6,4},{7,5},{8,14},{9,15},{10,... | collective-permute-start | bytes 2359304 | tf_op jit(solution)/shard_map/ppermute | solution.py:1294
  112.7 37.0 %collective-permute-start.16 = (bf16[2,512,384]{2,1,0:T(8,128)(2,1)}, bf16[2,512,384]{2,1,0:T(8,128)(2,1)}, u32[]{:S(2)}, u32[]{:S(2)}) collective-permute-start(bf16[2,512,384]{2,1,0:T(8,128)(2,1)} %bitcast.16), channel_id=1, source_target_pairs={{0,2},{1,3},{2,4},{3,5},{4,6},{5,7},{6,0},{7,1},{8,10},{9,11},{10,... | collective-permute-start | bytes 2359304 | tf_op jit(solution)/shard_map/ppermute | solution.py:1294
  153.0 10.4 %collective-permute-start.17 = (bf16[512,384]{1,0:T(8,128)(2,1)}, bf16[512,384]{1,0:T(8,128)(2,1)}, u32[]{:S(2)}, u32[]{:S(2)}) collective-permute-start(bf16[512,384]{1,0:T(8,128)(2,1)} %slice_bitcast_fusion), channel_id=1, source_target_pairs={{0,16},{8,24},{16,0},{24,8},{1,17},{9,25},{17,1},{25,9},{2,18},{10... | collective-permute-start | bytes 1179656 | tf_op jit(solution)/shard_map/ppermute | solution.py:1288
  165.6 56.6 %collective-permute-start.22 = (bf16[192,6288]{1,0:T(8,128)(2,1)S(1)}, bf16[192,6288]{1,0:T(8,128)(2,1)}, u32[]{:S(2)}, u32[]{:S(2)}) collective-permute-start(bf16[192,6288]{1,0:T(8,128)(2,1)S(1)} %copy-done.3), channel_id=1, source_target_pairs={{0,16},{8,24},{16,0},{24,8},{1,17},{9,25},{17,1},{25,9},{2,18},{10... | collective-permute-start | bytes 7243784 | tf_op jit(solution)/shard_map/ppermute | solution.py:1288
  222.2 23.7 %collective-permute-start.23 = (bf16[192,6288]{1,0:T(8,128)(2,1)}, bf16[192,6288]{1,0:T(8,128)(2,1)S(1)}, u32[]{:S(2)}, u32[]{:S(2)}) collective-permute-start(bf16[192,6288]{1,0:T(8,128)(2,1)} %collective-permute-done.22.refs_1_), channel_id=1, source_target_pairs={{0,8},{8,0},{16,24},{24,16},{1,9},{9,1},{17,25},{25,17},{2,10},{10... | collective-permute-start | bytes 7243784 | tf_op jit(solution)/shard_map/ppermute | solution.py:1288
  222.4 7.8 collective-permute-start.19
  222.5 17.7 %collective-permute-start.20 = (bf16[128,768]{0,1:T(8,128)(2,1)S(1)}, bf16[128,768]{0,1:T(8,128)(2,1)S(1)}, u32[]{:S(2)}, u32[]{:S(2)}) collective-permute-start(bf16[128,768]{0,1:T(8,128)(2,1)S(1)} %pad_maximum_fusion.9), channel_id=1, source_target_pairs={{0,4},{1,5},{2,6},{3,7},{4,0},{5,1},{6,2},{7,3},{8,12},{9,13},{10,... | collective-permute-start | bytes 589832 | tf_op jit(solution)/shard_map/ppermute | solution.py:1294
  225.3 18.0 %collective-permute-start.21 = (bf16[128,768]{0,1:T(8,128)(2,1)S(1)}, bf16[128,768]{0,1:T(8,128)(2,1)}, u32[]{:S(2)}, u32[]{:S(2)}) collective-permute-start(bf16[128,768]{0,1:T(8,128)(2,1)S(1)} %pad_maximum_fusion.9), channel_id=1, source_target_pairs={{0,6},{1,7},{2,0},{3,1},{4,2},{5,3},{6,4},{7,5},{8,14},{9,15},{10,... | collective-permute-start | bytes 589832 | tf_op jit(solution)/shard_map/ppermute | solution.py:1294
  292.3 7.9 %collective-permute-start.31 = (f32[64,768]{1,0:T(8,128)S(1)}, f32[64,768]{1,0:T(8,128)S(1)}, u32[]{:S(2)}, u32[]{:S(2)}) collective-permute-start(f32[64,768]{1,0:T(8,128)S(1)} %get-tuple-element.302), channel_id=1, source_target_pairs={{0,1},{1,0},{2,3},{3,2},{4,5},{5,4},{6,7},{7,6},{8,9},{9,8},{10,11... | collective-permute-start | bytes 589832 | tf_op jit(solution)/shard_map/ppermute | solution.py:1294
  292.7 11.0 %collective-permute-start.32 = (f32[64,768]{1,0:T(8,128)S(1)}, f32[64,768]{1,0:T(8,128)S(1)}, u32[]{:S(2)}, u32[]{:S(2)}) collective-permute-start(f32[64,768]{1,0:T(8,128)S(1)} %get-tuple-element.301), channel_id=1, source_target_pairs={{0,1},{1,0},{2,3},{3,2},{4,5},{5,4},{6,7},{7,6},{8,9},{9,8},{10,11... | collective-permute-start | bytes 589832 | tf_op jit(solution)/shard_map/ppermute | solution.py:1294
  294.4 11.4 %collective-permute-start.29 = (f32[64,768]{1,0:T(8,128)S(1)}, f32[64,768]{1,0:T(8,128)S(1)}, u32[]{:S(2)}, u32[]{:S(2)}) collective-permute-start(f32[64,768]{1,0:T(8,128)S(1)} %get-tuple-element.303), channel_id=1, source_target_pairs={{0,1},{1,0},{2,3},{3,2},{4,5},{5,4},{6,7},{7,6},{8,9},{9,8},{10,11... | collective-permute-start | bytes 589832 | tf_op jit(solution)/shard_map/ppermute | solution.py:1294
  318.6 51.4 %collective-permute-start.36 = (f32[384,6400]{1,0:T(8,128)}, f32[384,6400]{1,0:T(8,128)}, u32[]{:S(2)}, u32[]{:S(2)}) collective-permute-start(f32[384,6400]{1,0:T(8,128)} %get-tuple-element.161), channel_id=1, source_target_pairs={{0,8},{8,0},{16,24},{24,16},{1,9},{9,1},{17,25},{25,17},{2,10},{10... | collective-permute-start | bytes 29491208 | tf_op jit(solution)/shard_map/ppermute | solution.py:1288
  319.8 17.0 %collective-permute-start.34 = (f32[64,768]{1,0:T(8,128)S(1)}, f32[64,768]{1,0:T(8,128)S(1)}, u32[]{:S(2)}, u32[]{:S(2)}) collective-permute-start(f32[64,768]{1,0:T(8,128)S(1)} %get-tuple-element.304), channel_id=1, source_target_pairs={{0,4},{1,5},{2,6},{3,7},{4,0},{5,1},{6,2},{7,3},{8,12},{9,13},{10,... | collective-permute-start | bytes 589832 | tf_op jit(solution)/shard_map/ppermute | solution.py:1294
  321.9 17.5 %collective-permute-start.30 = (f32[64,768]{1,0:T(8,128)S(1)}, f32[64,768]{1,0:T(8,128)S(1)}, u32[]{:S(2)}, u32[]{:S(2)}) collective-permute-start(f32[64,768]{1,0:T(8,128)S(1)} %get-tuple-element.306), channel_id=1, source_target_pairs={{0,6},{1,7},{2,0},{3,1},{4,2},{5,3},{6,4},{7,5},{8,14},{9,15},{10,... | collective-permute-start | bytes 589832 | tf_op jit(solution)/shard_map/ppermute | solution.py:1294
  324.7 14.7 %collective-permute-start.28 = (f32[64,768]{1,0:T(8,128)S(1)}, f32[64,768]{1,0:T(8,128)S(1)}, u32[]{:S(2)}, u32[]{:S(2)}) collective-permute-start(f32[64,768]{1,0:T(8,128)S(1)} %get-tuple-element.300), channel_id=1, source_target_pairs={{0,1},{1,0},{2,3},{3,2},{4,5},{5,4},{6,7},{7,6},{8,9},{9,8},{10,11... | collective-permute-start | bytes 589832 | tf_op jit(solution)/shard_map/ppermute | solution.py:1294
  367.3 16.7 %collective-permute-start.37 = (f32[16,384,384]{2,1,0:T(8,128)}, f32[16,384,384]{2,1,0:T(8,128)}, u32[]{:S(2)}, u32[]{:S(2)}) collective-permute-start(f32[16,384,384]{2,1,0:T(8,128)} %get-tuple-element.175), channel_id=1, source_target_pairs={{0,8},{8,0},{16,24},{24,16},{1,9},{9,1},{17,25},{25,17},{2,10},{10... | collective-permute-start | bytes 28311560 | tf_op jit(solution)/shard_map/ppermute | solution.py:1288
  376.1 74.6 %collective-permute-start.40 = (f16[192,6400]{1,0:T(8,128)(2,1)}, f16[192,6400]{1,0:T(8,128)(2,1)}, u32[]{:S(2)}, u32[]{:S(2)}) collective-permute-start(f16[192,6400]{1,0:T(8,128)(2,1)} %fusion.7), channel_id=1, source_target_pairs={{0,16},{8,24},{16,0},{24,8},{1,17},{9,25},{17,1},{25,9},{2,18},{10... | collective-permute-start | bytes 7372808 | tf_op jit(solution)/shard_map/ppermute | solution.py:1288
  396.3 67.5 %collective-permute-start.43 = (f16[3088,384]{1,0:T(8,128)(2,1)}, f16[3088,384]{1,0:T(8,128)(2,1)}, u32[]{:S(2)}, u32[]{:S(2)}) collective-permute-start(f16[3088,384]{1,0:T(8,128)(2,1)} %concatenate.163), channel_id=1, source_target_pairs={{0,1},{1,0},{2,3},{3,2},{4,5},{5,4},{6,7},{7,6},{8,9},{9,8},{10,11... | collective-permute-start | bytes 7114760 | tf_op jit(solution)/shard_map/ppermute | solution.py:1294
  450.0 11.0 %collective-permute-start.39 = (bf16[512,384]{1,0:T(8,128)(2,1)S(1)}, bf16[512,384]{1,0:T(8,128)(2,1)S(1)}, u32[]{:S(2)}, u32[]{:S(2)}) collective-permute-start(bf16[512,384]{1,0:T(8,128)(2,1)S(1)} %fusion.29), channel_id=1, source_target_pairs={{0,16},{8,24},{16,0},{24,8},{1,17},{9,25},{17,1},{25,9},{2,18},{10... | collective-permute-start | bytes 1179656 | tf_op jit(solution)/shard_map/ppermute | solution.py:1288
  474.3 11.0 %collective-permute-start.44 = (f32[9,384,384]{2,1,0:T(8,128)}, f32[9,384,384]{2,1,0:T(8,128)}, u32[]{:S(2)}, u32[]{:S(2)}) collective-permute-start(f32[9,384,384]{2,1,0:T(8,128)} %get-tuple-element.192), channel_id=1, source_target_pairs={{0,8},{8,0},{16,24},{24,16},{1,9},{9,1},{17,25},{25,17},{2,10},{10... | collective-permute-start | bytes 15925256 | tf_op jit(solution)/shard_map/ppermute | solution.py:1288
  489.6 31.9 %collective-permute-start.46 = (f16[1744,384]{1,0:T(8,128)(2,1)}, f16[1744,384]{1,0:T(8,128)(2,1)S(1)}, u32[]{:S(2)}, u32[]{:S(2)}) collective-permute-start(f16[1744,384]{1,0:T(8,128)(2,1)} %concatenate.169), channel_id=1, source_target_pairs={{0,1},{1,0},{2,3},{3,2},{4,5},{5,4},{6,7},{7,6},{8,9},{9,8},{10,11... | collective-permute-start | bytes 4018184 | tf_op jit(solution)/shard_map/ppermute | solution.py:1294
  491.3 40.2 %collective-permute-start.42 = (bf16[3072,128]{1,0:T(8,128)(2,1)S(1)}, bf16[3072,128]{1,0:T(8,128)(2,1)}, u32[]{:S(2)}, u32[]{:S(2)}) collective-permute-start(bf16[3072,128]{1,0:T(8,128)(2,1)S(1)} %maximum_maximum_fusion.refs_3_), channel_id=1, source_target_pairs={{0,4},{1,5},{2,6},{3,7},{4,0},{5,1},{6,2},{7,3},{8,12},{9,13},{10,... | collective-permute-start | bytes 2359304 | tf_op jit(solution)/shard_map/ppermute | solution.py:1294
  498.2 61.2 %collective-permute-start.49 = (bf16[3072,128]{1,0:T(8,128)(2,1)S(1)}, bf16[3072,128]{1,0:T(8,128)(2,1)}, u32[]{:S(2)}, u32[]{:S(2)}) collective-permute-start(bf16[3072,128]{1,0:T(8,128)(2,1)S(1)} %maximum_maximum_fusion.refs_3_), channel_id=1, source_target_pairs={{0,2},{1,3},{2,4},{3,5},{4,6},{5,7},{6,0},{7,1},{8,10},{9,11},{10,... | collective-permute-start | bytes 2359304 | tf_op jit(solution)/shard_map/ppermute | solution.py:1294
  498.3 61.2 %collective-permute-start.50 = (bf16[3072,128]{1,0:T(8,128)(2,1)S(1)}, bf16[3072,128]{1,0:T(8,128)(2,1)}, u32[]{:S(2)}, u32[]{:S(2)}) collective-permute-start(bf16[3072,128]{1,0:T(8,128)(2,1)S(1)} %maximum_maximum_fusion.refs_3_), channel_id=1, source_target_pairs={{0,6},{1,7},{2,0},{3,1},{4,2},{5,3},{6,4},{7,5},{8,14},{9,15},{10,... | collective-permute-start | bytes 2359304 | tf_op jit(solution)/shard_map/ppermute | solution.py:1294
  510.4 27.7 %collective-permute-start.47 = (f16[1552,384]{1,0:T(8,128)(2,1)}, f16[1552,384]{1,0:T(8,128)(2,1)}, u32[]{:S(2)}, u32[]{:S(2)}) collective-permute-start(f16[1552,384]{1,0:T(8,128)(2,1)} %concatenate.171), channel_id=1, source_target_pairs={{0,16},{8,24},{16,0},{24,8},{1,17},{9,25},{17,1},{25,9},{2,18},{10... | collective-permute-start | bytes 3575816 | tf_op jit(solution)/shard_map/ppermute | solution.py:1288
  531.5 28.0 %collective-permute-start.52 = (bf16[3072,128]{1,0:T(8,128)(2,1)S(1)}, bf16[3072,128]{1,0:T(8,128)(2,1)}, u32[]{:S(2)}, u32[]{:S(2)}) collective-permute-start(bf16[3072,128]{1,0:T(8,128)(2,1)S(1)} %maximum_maximum_fusion.refs_3_), channel_id=1, source_target_pairs={{0,1},{1,0},{2,3},{3,2},{4,5},{5,4},{6,7},{7,6},{8,9},{9,8},{10,11... | collective-permute-start | bytes 2359304 | tf_op jit(solution)/shard_map/ppermute | solution.py:1294
  536.7 34.0 %collective-permute-start.48 = (f16[880,384]{1,0:T(8,128)(2,1)}, f16[880,384]{1,0:T(8,128)(2,1)}, u32[]{:S(2)}, u32[]{:S(2)}) collective-permute-start(f16[880,384]{1,0:T(8,128)(2,1)} %concatenate.170), channel_id=1, source_target_pairs={{0,16},{8,24},{16,0},{24,8},{1,17},{9,25},{17,1},{25,9},{2,18},{10... | collective-permute-start | bytes 2027528 | tf_op jit(solution)/shard_map/ppermute | solution.py:1288
  562.7 53.5 %collective-permute-start.53 = (bf16[3,3072,128]{2,1,0:T(8,128)(2,1)}, bf16[3,3072,128]{2,1,0:T(8,128)(2,1)}, u32[]{:S(2)}, u32[]{:S(2)}) collective-permute-start(bf16[3,3072,128]{2,1,0:T(8,128)(2,1)} %pad_maximum_fusion), channel_id=1, source_target_pairs={{0,1},{1,0},{2,3},{3,2},{4,5},{5,4},{6,7},{7,6},{8,9},{9,8},{10,11... | collective-permute-start | bytes 7077896 | tf_op jit(solution)/shard_map/ppermute | solution.py:1294
  578.5 34.4 %collective-permute-start.51 = (f16[616,384]{1,0:T(8,128)(2,1)}, f16[616,384]{1,0:T(8,128)(2,1)S(1)}, u32[]{:S(2)}, u32[]{:S(2)}) collective-permute-start(f16[616,384]{1,0:T(8,128)(2,1)} %concatenate.173), channel_id=1, source_target_pairs={{0,2},{1,3},{2,4},{3,5},{4,6},{5,7},{6,0},{7,1},{8,10},{9,11},{10,... | collective-permute-start | bytes 1419272 | tf_op jit(solution)/shard_map/ppermute | solution.py:1294
  581.2 57.2 %collective-permute-start.55 = (f16[616,384]{1,0:T(8,128)(2,1)S(1)}, f16[616,384]{1,0:T(8,128)(2,1)}, u32[]{:S(2)}, u32[]{:S(2)}) collective-permute-start(f16[616,384]{1,0:T(8,128)(2,1)S(1)} %concatenate.175), channel_id=1, source_target_pairs={{0,6},{1,7},{2,0},{3,1},{4,2},{5,3},{6,4},{7,5},{8,14},{9,15},{10,... | collective-permute-start | bytes 1419272 | tf_op jit(solution)/shard_map/ppermute | solution.py:1294
  583.2 56.4 %collective-permute-start.54 = (f16[616,384]{1,0:T(8,128)(2,1)}, f16[616,384]{1,0:T(8,128)(2,1)}, u32[]{:S(2)}, u32[]{:S(2)}) collective-permute-start(f16[616,384]{1,0:T(8,128)(2,1)} %concatenate.174), channel_id=1, source_target_pairs={{0,4},{1,5},{2,6},{3,7},{4,0},{5,1},{6,2},{7,3},{8,12},{9,13},{10,... | collective-permute-start | bytes 1419272 | tf_op jit(solution)/shard_map/ppermute | solution.py:1294
  643.0 8.2 %collective-permute-start.58 = (f32[25,24,384]{2,1,0:T(8,128)S(1)}, f32[25,24,384]{2,1,0:T(8,128)}, u32[]{:S(2)}, u32[]{:S(2)}) collective-permute-start(f32[25,24,384]{2,1,0:T(8,128)S(1)} %get-tuple-element.287), channel_id=1, source_target_pairs={{0,8},{8,0},{16,24},{24,16},{1,9},{9,1},{17,25},{25,17},{2,10},{10... | collective-permute-start | bytes 2764808 | tf_op jit(solution)/shard_map/ppermute | solution.py:1288
  670.8 35.2 %collective-permute-start.65 = (f16[688,384]{1,0:T(8,128)(2,1)S(1)}, f16[688,384]{1,0:T(8,128)(2,1)S(1)}, u32[]{:S(2)}, u32[]{:S(2)}) collective-permute-start(f16[688,384]{1,0:T(8,128)(2,1)S(1)} %concatenate.183), channel_id=1, source_target_pairs={{0,2},{1,3},{2,4},{3,5},{4,6},{5,7},{6,0},{7,1},{8,10},{9,11},{10,... | collective-permute-start | bytes 1585160 | tf_op jit(solution)/shard_map/ppermute | solution.py:1294
  670.8 42.8 %collective-permute-start.67 = (f16[688,384]{1,0:T(8,128)(2,1)S(1)}, f16[688,384]{1,0:T(8,128)(2,1)S(1)}, u32[]{:S(2)}, u32[]{:S(2)}) collective-permute-start(f16[688,384]{1,0:T(8,128)(2,1)S(1)} %concatenate.183), channel_id=1, source_target_pairs={{0,4},{1,5},{2,6},{3,7},{4,0},{5,1},{6,2},{7,3},{8,12},{9,13},{10,... | collective-permute-start | bytes 1585160 | tf_op jit(solution)/shard_map/ppermute | solution.py:1294
  674.9 41.9 %collective-permute-start.69 = (f16[688,384]{1,0:T(8,128)(2,1)S(1)}, f16[688,384]{1,0:T(8,128)(2,1)S(1)}, u32[]{:S(2)}, u32[]{:S(2)}) collective-permute-start(f16[688,384]{1,0:T(8,128)(2,1)S(1)} %concatenate.183), channel_id=1, source_target_pairs={{0,6},{1,7},{2,0},{3,1},{4,2},{5,3},{6,4},{7,5},{8,14},{9,15},{10,... | collective-permute-start | bytes 1585160 | tf_op jit(solution)/shard_map/ppermute | solution.py:1294
  676.6 56.6 %collective-permute-start.64 = (f16[688,384]{1,0:T(8,128)(2,1)S(1)}, f16[688,384]{1,0:T(8,128)(2,1)S(1)}, u32[]{:S(2)}, u32[]{:S(2)}) collective-permute-start(f16[688,384]{1,0:T(8,128)(2,1)S(1)} %concatenate.183), channel_id=1, source_target_pairs={{0,1},{1,0},{2,3},{3,2},{4,5},{5,4},{6,7},{7,6},{8,9},{9,8},{10,11... | collective-permute-start | bytes 1585160 | tf_op jit(solution)/shard_map/ppermute | solution.py:1294
  705.9 28.4 %collective-permute-start.66 = (f16[688,384]{1,0:T(8,128)(2,1)S(1)}, f16[688,384]{1,0:T(8,128)(2,1)S(1)}, u32[]{:S(2)}, u32[]{:S(2)}) collective-permute-start(f16[688,384]{1,0:T(8,128)(2,1)S(1)} %collective-permute-done.65), channel_id=1, source_target_pairs={{0,1},{1,0},{2,3},{3,2},{4,5},{5,4},{6,7},{7,6},{8,9},{9,8},{10,11... | collective-permute-start | bytes 1585160 | tf_op jit(solution)/shard_map/ppermute | solution.py:1294
  713.6 21.8 %collective-permute-start.68 = (f16[688,384]{1,0:T(8,128)(2,1)S(1)}, f16[688,384]{1,0:T(8,128)(2,1)S(1)}, u32[]{:S(2)}, u32[]{:S(2)}) collective-permute-start(f16[688,384]{1,0:T(8,128)(2,1)S(1)} %collective-permute-done.67), channel_id=1, source_target_pairs={{0,1},{1,0},{2,3},{3,2},{4,5},{5,4},{6,7},{7,6},{8,9},{9,8},{10,11... | collective-permute-start | bytes 1585160 | tf_op jit(solution)/shard_map/ppermute | solution.py:1294
  716.9 20.9 %collective-permute-start.70 = (f16[688,384]{1,0:T(8,128)(2,1)S(1)}, f16[688,384]{1,0:T(8,128)(2,1)S(1)}, u32[]{:S(2)}, u32[]{:S(2)}) collective-permute-start(f16[688,384]{1,0:T(8,128)(2,1)S(1)} %collective-permute-done.69), channel_id=1, source_target_pairs={{0,1},{1,0},{2,3},{3,2},{4,5},{5,4},{6,7},{7,6},{8,9},{9,8},{10,11... | collective-permute-start | bytes 1585160 | tf_op jit(solution)/shard_map/ppermute | solution.py:1294
  (71 other events, 594.7 us)
